TPU v7x, 32 devices: a whole 2x2x4 slice. The times are simulated.
32 devices in a mesh: outer: 2 (over y), local: 4 (over x, core), tensor: 4 (over z).
Axes of the slice: x: 2, y: 2, z: 4, core: 2. Of those that a mesh axis runs over, the one named last changes fastest.
Arguments:
- tokens: bfloat16 [32, 512, 768], P(('outer', 'local')), may hold values from -6 to 6
- segments: int32 [32, 512], P(('outer', 'local')), may hold values from 0 to 3, never falling along the last dimension, each value on 1 to 256 neighbouring positions
- w_qkv: bfloat16 [3, 768, 768], P(None, None, 'tensor'), may hold values from -0.21875 to 0.21875
- b_qv: float32 [2, 12, 64], P(None, 'tensor'), may hold values from -3 to 3
- w_out: bfloat16 [768, 768], P('tensor'), may hold values from -1.75 to 1.75
- w_in: bfloat16 [768, 3072], P(None, 'tensor'), may hold values from -0.21875 to 0.21875
- b_inner: float32 [48, 64], P('tensor'), may hold values from -3 to 3
- w_down: bfloat16 [3072, 768], P('tensor'), may hold values from -0.109375 to 0.109375
- gains: float32 [2, 768], replicated, may hold values from 0.1 to 1.9
- shifts: float32 [4, 768], replicated, may hold values from -3 to 3
- cotangent: bfloat16 [32, 512, 768], P(('outer', 'local')), may hold values from -6 to 6
Outputs:
- output: bfloat16 [32, 512, 768], P(('outer', 'local'))
- grad_tokens: float32 [32, 512, 768], P(('outer', 'local'))
- grad_w_qkv: float32 [3, 768, 768], P(None, 'local', 'tensor')
- grad_b_qv: float32 [2, 12, 64], P(None, 'tensor', 'local')
- grad_w_out: float32 [768, 768], P('tensor', 'local')
- grad_w_in: float32 [768, 3072], P('local', 'tensor')
- grad_b_inner: float32 [48, 64], P('tensor', 'local')
- grad_w_down: float32 [3072, 768], P('tensor', 'local')
- grad_gains: float32 [2, 768], P(None, 'local')
- grad_shifts: float32 [4, 768], P(None, 'local')
Inputs may be any that keep to these rules, and one draw needn't show every extreme that they name: `segments`: in each row the document numbers never fall; each document holds 1 to 256 tokens and some document holds exactly 256.
All inputs are finite; a program needn't handle non-finite values.
Results may differ from a plain program's by a relative error of at most 0.015.
Values may be sent and summed in bfloat16 or wider, within the bound.
No kernel may reach another device: no remote copies, remote signals or barrier semaphores. Data moves between devices by JAX's collectives and lax.ppermute only.
A program may use at most 192 MiB of HBM per device.

v0:
```python
import math

import jax
import jax.numpy as jnp
from jax import lax
from jax.sharding import PartitionSpec as P

EPSILON = 1e-12
MASKED = -1e30


def normalize(values):
    centre = values - jnp.mean(values, axis=-1, keepdims=True)
    variance = jnp.mean(centre * centre, axis=-1, keepdims=True)
    recip = lax.rsqrt(variance + EPSILON)
    return (centre * recip, recip)


def norm_back(grad_norm, normed, recip):
    first = jnp.mean(grad_norm, axis=-1, keepdims=True)
    second = jnp.mean(grad_norm * normed, axis=-1, keepdims=True)
    return recip * (grad_norm - first - normed * second)


def gelu_slope(values):
    cumul = 0.5 * (1.0 + lax.erf(values * (1.0 / math.sqrt(2.0))))
    return cumul + values * jnp.exp(-0.5 * values * values) * (1.0 / math.sqrt(2.0 * math.pi))


def local(tokens, segments, w_qkv, b_qv, w_out, w_in, b_inner, w_down, gains, shifts, cotangent):
    seq_count, seq_len, model_width = tokens.shape
    tok_rows = seq_count * seq_len
    local_heads = b_qv.shape[1]
    head_size = b_qv.shape[2]
    score_scale = head_size ** (-0.5)
    head_shape = (seq_count, seq_len, local_heads, head_size)
    flat_tokens = tokens.reshape(tok_rows, model_width)
    flat_cot = cotangent.reshape(tok_rows, model_width)
    projected = jnp.einsum("td,cdh->cth", flat_tokens, w_qkv, preferred_element_type=jnp.float32)
    queries = (projected[0] + b_qv[0].reshape(-1)).astype(jnp.bfloat16).reshape(head_shape)
    key_proj = projected[1].astype(jnp.bfloat16).reshape(head_shape)
    values = (projected[2] + b_qv[1].reshape(-1)).astype(jnp.bfloat16).reshape(head_shape)
    allowed = segments[:, None, :, None] == segments[:, None, None, :]

    def scores_now():
        raw_scores = jnp.einsum(
            "sqhe,skhe->shqk", queries, key_proj, preferred_element_type=jnp.float32
        )
        return jnp.where(allowed, raw_scores * score_scale, MASKED)

    scores = scores_now()
    row_max = jnp.max(scores, axis=-1, keepdims=True)
    exp_scores = jnp.exp(scores - row_max)
    row_total = jnp.sum(exp_scores, axis=-1, keepdims=True)
    probs = exp_scores / row_total
    log_total = row_max + jnp.log(row_total)
    context = jnp.einsum(
        "shqk,skhe->sqhe", probs.astype(jnp.bfloat16), values, preferred_element_type=jnp.float32
    )
    context = context.reshape(tok_rows, local_heads * head_size).astype(jnp.bfloat16)
    attn_share = jnp.dot(context, w_out, preferred_element_type=jnp.float32)
    own_tokens = flat_tokens.astype(jnp.float32)
    own_cot = flat_cot.astype(jnp.float32)
    attention = lax.psum(attn_share, "tensor")
    norm_one, recip_one = normalize(own_tokens + attention + shifts[0])
    hidden1 = norm_one * gains[0] + shifts[1]
    hidden_own = hidden1.astype(jnp.bfloat16)
    pre_act = jnp.dot(hidden_own, w_in, preferred_element_type=jnp.float32) + b_inner.reshape(-1)
    activation = jax.nn.gelu(pre_act, approximate=False).astype(jnp.bfloat16)
    feed_share = jnp.dot(activation, w_down, preferred_element_type=jnp.float32)
    feed = lax.psum(feed_share, "tensor")
    norm_two, recip_two = normalize(hidden1 + feed + shifts[2])
    output_own = (norm_two * gains[1] + shifts[3]).astype(jnp.bfloat16)
    grad_gain2 = jnp.sum(own_cot * norm_two, axis=0)
    grad_beta2 = jnp.sum(own_cot, axis=0)
    grad_r2_own = norm_back(own_cot * gains[1], norm_two, recip_two)
    grad_bdown = jnp.sum(grad_r2_own, axis=0)
    grad_r2_low = grad_r2_own.astype(jnp.bfloat16)
    grad_wdown = jnp.einsum(
        "tf,td->fd", activation, grad_r2_low, preferred_element_type=jnp.float32
    )
    grad_act = jnp.einsum("td,fd->tf", grad_r2_low, w_down, preferred_element_type=jnp.float32)
    grad_pre = grad_act * gelu_slope(pre_act)
    grad_binner = jnp.sum(grad_pre, axis=0).reshape(b_inner.shape)
    grad_pre_low = grad_pre.astype(jnp.bfloat16)
    grad_win = jnp.einsum("td,tf->df", hidden_own, grad_pre_low, preferred_element_type=jnp.float32)
    ffn_vectors = jnp.stack([grad_gain2, grad_bdown, grad_beta2])
    entry_share = jnp.einsum("tf,df->td", grad_pre_low, w_in, preferred_element_type=jnp.float32)
    entry_ffn = lax.psum(entry_share, "tensor")
    grad_h1 = grad_r2_own + entry_ffn
    grad_gain1 = jnp.sum(grad_h1 * norm_one, axis=0)
    grad_beta1 = jnp.sum(grad_h1, axis=0)
    grad_r1_own = norm_back(grad_h1 * gains[0], norm_one, recip_one)
    grad_bout = jnp.sum(grad_r1_own, axis=0)
    attn_vectors = jnp.stack([grad_gain1, grad_bout, grad_beta1])
    grad_r1_low = grad_r1_own.astype(jnp.bfloat16)
    grad_wout = jnp.einsum("th,td->hd", context, grad_r1_low, preferred_element_type=jnp.float32)
    grad_context = jnp.einsum("td,hd->th", grad_r1_low, w_out, preferred_element_type=jnp.float32)
    grad_context = grad_context.astype(jnp.bfloat16).reshape(head_shape)
    probs_again = jnp.exp(scores_now() - log_total)
    grad_probs = jnp.einsum(
        "sqhe,skhe->shqk", grad_context, values, preferred_element_type=jnp.float32
    )
    inner_sum = jnp.sum(probs_again * grad_probs, axis=-1, keepdims=True)
    grad_scores = (probs_again * (grad_probs - inner_sum) * score_scale).astype(jnp.bfloat16)
    grad_query = jnp.einsum(
        "shqk,skhe->sqhe", grad_scores, key_proj, preferred_element_type=jnp.float32
    )
    grad_key = jnp.einsum(
        "shqk,sqhe->skhe", grad_scores, queries, preferred_element_type=jnp.float32
    )
    grad_value = jnp.einsum(
        "shqk,sqhe->skhe",
        probs_again.astype(jnp.bfloat16),
        grad_context,
        preferred_element_type=jnp.float32,
    )
    grad_proj = jnp.stack([grad_query, grad_key, grad_value]).reshape(
        3, tok_rows, local_heads * head_size
    )
    grad_bqv = jnp.sum(jnp.stack([grad_proj[0], grad_proj[2]]), axis=1).reshape(b_qv.shape)
    grad_proj_low = grad_proj.astype(jnp.bfloat16)
    grad_wqkv = jnp.einsum(
        "td,cth->cdh", flat_tokens, grad_proj_low, preferred_element_type=jnp.float32
    )
    entry_attn = lax.psum(
        jnp.einsum("cth,cdh->td", grad_proj_low, w_qkv, preferred_element_type=jnp.float32).astype(
            jnp.bfloat16
        ),
        "tensor",
    ).astype(jnp.float32)
    grad_inputs = (grad_r1_own + entry_attn).reshape(seq_count, seq_len, model_width)
    reduced = lax.psum(
        (
            lax.psum_scatter(grad_win, "local", scatter_dimension=0, tiled=True),
            lax.psum_scatter(grad_wdown, "local", scatter_dimension=1, tiled=True),
            lax.psum_scatter(grad_binner, "local", scatter_dimension=1, tiled=True),
            lax.psum_scatter(ffn_vectors, "local", scatter_dimension=1, tiled=True),
            lax.psum_scatter(grad_wqkv, "local", scatter_dimension=1, tiled=True),
            lax.psum_scatter(grad_wout, "local", scatter_dimension=1, tiled=True),
            lax.psum_scatter(grad_bqv, "local", scatter_dimension=2, tiled=True),
            lax.psum_scatter(attn_vectors, "local", scatter_dimension=1, tiled=True),
        ),
        "outer",
    )
    ffn_done = (reduced[0], reduced[1], reduced[2], reduced[3])
    attn_done = (reduced[4], reduced[5], reduced[6], reduced[7])
    grad_gains = jnp.stack([attn_done[3][0], ffn_done[3][0]])
    grad_shifts = jnp.stack([attn_done[3][1], attn_done[3][2], ffn_done[3][1], ffn_done[3][2]])
    return (
        output_own.reshape(seq_count, seq_len, model_width),
        grad_inputs,
        attn_done[0],
        attn_done[2],
        attn_done[1],
        ffn_done[0],
        ffn_done[2],
        ffn_done[1],
        grad_gains,
        grad_shifts,
    )


def solution(mesh):
    placed = (
        P(("outer", "local"), None, None),
        P(("outer", "local"), None),
        P(None, None, "tensor"),
        P(None, "tensor", None),
        P("tensor", None),
        P(None, "tensor"),
        P("tensor", None),
        P("tensor", None),
        P(),
        P(),
        P(("outer", "local"), None, None),
    )
    return jax.shard_map(
        local,
        mesh=mesh,
        in_specs=placed,
        out_specs=(
            P(("outer", "local"), None, None),
            P(("outer", "local"), None, None),
            P(None, "local", "tensor"),
            P(None, "tensor", "local"),
            P("tensor", "local"),
            P("local", "tensor"),
            P("tensor", "local"),
            P("tensor", "local"),
            P(None, "local"),
            P(None, "local"),
        ),
        check_vma=False,
    )
```

profile of v0, /device:TPU:0, one launch (start us, length us, event | category | flops | bytes accessed | tf_op | source)
XLA Modules:
  0.0 1289.6 jit_solution(12005579631688383753)
XLA Ops:
  7.2 4.3 convolution_bitcast_fusion
  12.5 2.0 fusion.116
  15.3 2.7 convert_element_type.75
  18.0 3.4 squeeze.7
  21.4 3.1 squeeze.8
  24.6 7.9 fusion.3
  32.6 7.5 fusion.2
  40.0 7.3 fusion.84
  48.2 3.7 fusion.121
  52.2 225.5 %all-reduce.8.cloned.1.call-done = f32[2048,768]{1,0:T(8,128)} async-done(((f32[2048,768]{1,0:T(8,128)}), f32[2048,768]{1,0:T(8,128)}) %all-reduce.8.cloned.1.call-update) | async-done | bytes 6291472 | tf_op jit(solution)/shard_map/psum | solution.py:64
  277.6 4.6 fusion.115
  283.2 18.0 %fusion.15 = (bf16[2048,768]{1,0:T(8,128)(2,1)S(1)}, f32[2048,768]{1,0:T(8,128)}) fusion(f32[768]{0:T(1024)S(1)} %add.168, bf16[768,768]{1,0:T(8,128)(2,1)S(1)} %copy-done, f32[2048,768]{1,0:T(8,128)S(1)} %get-tuple-element.70, f32[768]{0:T(1024)S(1)} %get-tuple-element.49, f32[768]{0:T(1024)S(1)} %get-tuple-element.53, f32[2048]{0:T(1024)S(1)} %add_rsqrt_fusion.1, ...), kind=kOutput, calls=%fused_computation.17 | convolution fusion | flops 2527592448 | bytes 16933888 | tf_op jit(solution)/shard_map/dot_general | solution.py:68
  301.1 1.7 copy-done.28
  302.8 4.4 fusion.122
  307.3 4.0 convert_reduce_fusion
  311.3 217.9 %all-reduce.10.cloned.1.call-done = f32[2048,768]{1,0:T(8,128)} async-done(((f32[2048,768]{1,0:T(8,128)}), f32[2048,768]{1,0:T(8,128)}) %all-reduce.10.cloned.1.call-update) | async-done | bytes 6291472 | tf_op jit(solution)/shard_map/psum | solution.py:71
  529.2 6.1 fusion.114
  537.2 3.1 fusion.27
  540.3 4.5 fusion.112
  544.8 5.3 fusion.118
  550.1 1.6 copy-done.29
  551.7 4.5 fusion.63
  556.4 221.9 %all-reduce.12.cloned.1.call-done = f32[2048,768]{1,0:T(8,128)} async-done(((f32[2048,768]{1,0:T(8,128)}), f32[2048,768]{1,0:T(8,128)}) %all-reduce.12.cloned.1.call-update) | async-done | bytes 6291472 | tf_op jit(solution)/shard_map/psum | solution.py:89
  778.3 8.7 multiply_reduce_fusion.1
  787.0 5.2 fusion.111
  792.2 2.7 copy-done.2
  794.9 2.3 fusion.81
  797.2 4.9 convolution_convert_fusion
  802.1 2.5 reshape.147
  804.6 6.9 fusion.68
  811.5 6.6 fusion.86
  818.1 2.2 copy.61
  820.3 2.4 stack.48
  823.6 25.7 %fusion.71 = f32[4,512,3,64]{1,3,2,0:T(8,128)} fusion(f32[4,3,512,512]{2,3,1,0:T(8,128)} %fusion.86, f32[4,3,512,512]{2,3,1,0:T(8,128)} %get-tuple-element.77, f32[4,3,512]{2,1,0:T(4,128)} %copy-done.15, pred[4,512,512]{1,2,0:T(8,128)(4,1)} %copy-done.5, bf16[4,512,3,64]{1,0,3,2:T(4,128)(2,1)S(1)} %copy-done.9), kind=kOutput, calls=%fused_computation.97 | convolution fusion | flops 437262848 | bytes 28598272 | tf_op jit(solution)/shard_map/shqk,skhe->sqhe/dot_general | solution.py:106
  849.4 3.6 copy.56
  853.0 3.1 stack.46
  856.1 2.4 convert.16
  858.5 20.1 %fusion.78 = bf16[4,512,3,64]{1,3,2,0:T(8,128)(2,1)} fusion(f32[4,3,512,512]{2,3,1,0:T(8,128)} %fusion.86, f32[4,3,512,512]{2,3,1,0:T(8,128)} %get-tuple-element.77, f32[4,3,512]{2,1,0:T(4,128)S(1)} %copy-done.16, pred[4,512,512]{1,2,0:T(8,128)(4,1)} %copy-done.5, f32[4,512,3,64]{1,0,3,2:T(4,128)} %squeeze.8, f32[3,64]{1,0:T(4,128)S(1)} %copy-done.18), kind=kOutput, calls=%fused_computation.100 | convolution fusion | flops 438442496 | bytes 28599040 | tf_op jit(solution)/shard_map/shqk,sqhe->skhe/dot_general | solution.py:109
  878.7 1.7 copy.58
  880.4 1.5 stack.47
  881.9 5.8 convolution_bitcast_fusion.1
  887.7 4.2 copy.68
  891.9 4.7 reshape.154
  896.7 7.8 fusion.65
  904.9 8.3 fusion.61
  913.2 1.3 stack.57
  920.3 1.7 maximum_reduce_fusion
  925.4 6.0 bitcast_convert_fusion
  931.5 1.7 copy.73
  933.3 1.5 reshape.155
  935.9 25.8 %reduce-scatter.23.cloned.1.call-done = f32[768,192]{0,1:T(8,128)} async-done(((f32[768,768]{0,1:T(8,128)}), f32[768,192]{0,1:T(8,128)}) %reduce-scatter.23.cloned.1.call-update) | async-done | bytes 589840 | tf_op jit(solution)/shard_map/reduce_scatter | solution.py:136
  961.6 35.8 %reduce-scatter.21.cloned.1.call-done = f32[192,768]{1,0:T(8,128)} async-done(((f32[768,768]{1,0:T(8,128)}), f32[192,768]{1,0:T(8,128)}) %reduce-scatter.21.cloned.1.call-update) | async-done | bytes 589840 | tf_op jit(solution)/shard_map/reduce_scatter | solution.py:135
  997.5 21.8 %reduce-scatter.31.cloned.1.call-done = f32[16,12]{1,0:T(8,128)} async-done(((f32[64,12]{1,0:T(8,128)}), f32[16,12]{1,0:T(8,128)}) %reduce-scatter.31.cloned.1.call-update) | async-done | bytes 784
  1020.0 23.3 %reduce-scatter.35.cloned.1.call-done = f32[192,3]{1,0:T(8,128)} async-done(((f32[768,3]{1,0:T(8,128)}), f32[192,3]{1,0:T(8,128)}) %reduce-scatter.35.cloned.1.call-update) | async-done | bytes 2320
  1044.3 20.8 %reduce-scatter.27.cloned.1.call-done = f32[16,6]{1,0:T(8,128)} async-done(((f32[64,6]{1,0:T(8,128)}), f32[16,6]{1,0:T(8,128)}) %reduce-scatter.27.cloned.1.call-update) | async-done | bytes 400
  1066.0 23.0 %reduce-scatter.33.cloned.1.call-done = f32[192,3]{1,0:T(8,128)} async-done(((f32[768,3]{1,0:T(8,128)}), f32[192,3]{1,0:T(8,128)}) %reduce-scatter.33.cloned.1.call-update) | async-done | bytes 2320
  1090.0 8.9 all-reduce
  1100.7 111.8 %all-reduce.14.cloned.1.call-done = bf16[2048,768]{1,0:T(8,128)(2,1)} async-done(((bf16[2048,768]{1,0:T(8,128)(2,1)}), bf16[2048,768]{1,0:T(8,128)(2,1)}) %all-reduce.14.cloned.1.call-update) | async-done | bytes 3145744 | tf_op jit(solution)/shard_map/psum | solution.py:126
  1212.4 7.0 convert_add_fusion
  1219.4 55.7 %all-reduce.16.cloned.1.call-done = (f32[3,192,192]{1,2,0:T(8,128)}, f32[192,192]{1,0:T(8,128)}, f32[192,768]{1,0:T(8,128)}, f32[768,192]{0,1:T(8,128)}) async-done(((f32[3,192,192]{1,2,0:T(8,128)}, f32[192,192]{1,0:T(8,128)}, f32[192,768]{1,0:T(8,128)}, f32[768,192]{0,1:T(8,128)}), (f32[3,192,192]{1,2,0:T(8,128)}, f32[192,192]{1,0:T(8,128)}, f32[192,768]{1,0:T(8,128)}, ...) | async-done | bytes 1769488 | tf_op jit(solution)/shard_map/psum | solution.py:133
  1275.1 2.1 copy.62
  1277.2 1.6 copy.116
  1278.8 1.9 copy.117
  1280.7 1.9 copy.118
  (139 shorter events, 22.9 us)
Async XLA Ops:
  7.2 276.0 %copy-start = (bf16[768,768]{1,0:T(8,128)(2,1)S(1)}, bf16[768,768]{1,0:T(8,128)(2,1)}, u32[]{:S(2)}) copy-start(bf16[768,768]{1,0:T(8,128)(2,1)} %param.16) | copy-start | bytes 3538948
  7.2 270.4 %all-reduce.8.cloned.1.call-start = ((), (), s32[]{:S(2)}) async-start(), calls=%async_computation.8 | async-start | bytes 12582912 | tf_op jit(solution)/shard_map/psum | solution.py:64
  11.5 3.0 copy-start.25
  11.5 3.0 copy-start.14
  15.3 789.3 %copy-start.5 = (pred[4,512,512]{1,2,0:T(8,128)(4,1)}, pred[4,512,512]{1,2,0:T(8,128)(4,1)S(1)}, u32[]{:S(2)}) copy-start(pred[4,512,512]{1,2,0:T(8,128)(4,1)S(1)} %broadcast_compare_fusion) | copy-start | bytes 3145732
  18.0 14.5 %copy-start.8 = (bf16[4,512,3,64]{1,0,3,2:T(4,128)(2,1)}, bf16[4,512,3,64]{1,0,3,2:T(4,128)(2,1)S(1)}, u32[]{:S(2)}) copy-start(bf16[4,512,3,64]{1,0,3,2:T(4,128)(2,1)S(1)} %convert_element_type.75) | copy-start | bytes 2359300
  24.6 8.0 copy-start.17
  32.5 7.5 copy-start.6
  40.0 8.1 copy-start.10
  48.1 3.9 copy-start.23
  48.1 3.9 copy-start.24
  48.1 3.9 copy-start.22
  51.9 477.3 %all-reduce.10.cloned.1.call-start = ((), (), s32[]{:S(2)}) async-start(), calls=%async_computation.9 | async-start | bytes 12582912 | tf_op jit(solution)/shard_map/psum | solution.py:71
  52.1 734.9 %copy-start.12 = (f32[768]{0:T(1024)}, f32[768]{0:T(1024)S(1)}, u32[]{:S(2)}) copy-start(f32[768]{0:T(1024)S(1)} %get-tuple-element.53) | copy-start | bytes 9220
  52.1 477.1 %copy-start.20 = (f32[768]{0:T(1024)}, f32[768]{0:T(1024)S(1)}, u32[]{:S(2)}) copy-start(f32[768]{0:T(1024)S(1)} %get-tuple-element.49) | copy-start | bytes 9220
  282.3 18.9 %copy-start.1 = (f32[2048,768]{1,0:T(8,128)}, f32[2048,768]{1,0:T(8,128)S(1)}, u32[]{:S(2)}) copy-start(f32[2048,768]{1,0:T(8,128)S(1)} %get-tuple-element.70) | copy-start | bytes 18874372
  283.1 19.7 %copy-start.26 = (bf16[768,768]{1,0:T(8,128)(2,1)S(1)}, bf16[768,768]{1,0:T(8,128)(2,1)}, u32[]{:S(2)}) copy-start(bf16[768,768]{1,0:T(8,128)(2,1)} %param.18) | copy-start | bytes 3538948
  301.1 1.7 copy-start.28
  307.3 471.0 %all-reduce.12.cloned.1.call-start = ((), (), s32[]{:S(2)}) async-start(), calls=%async_computation.10 | async-start | bytes 12582912 | tf_op jit(solution)/shard_map/psum | solution.py:89
  535.4 1.9 copy-start.3
  537.2 7.5 slice-start
  540.3 4.5 copy-start.27
  540.3 4.5 slice-start.1
  544.8 5.3 copy-start.4
  550.1 1.6 copy-start.29
  556.3 375.2 %reduce-scatter.29.cloned.1.call-start = ((), (), s32[]{:S(2)}) async-start(), calls=%async_computation.16 | async-start | bytes 983040
  556.4 248.2 %copy-start.15 = (f32[4,3,512]{2,1,0:T(4,128)}, f32[4,3,512]{2,1,0:T(4,128)S(1)}, u32[]{:S(2)}) copy-start(f32[4,3,512]{2,1,0:T(4,128)S(1)} %log_add_fusion) | copy-start | bytes 73732
  792.2 2.7 copy-start.2
  802.1 131.2 %reduce-scatter.25.cloned.1.call-start = ((), (), s32[]{:S(2)}) async-start(), calls=%async_computation.14 | async-start | bytes 2457600
  804.6 6.9 copy-start.7
  818.1 5.5 copy-start.9
  849.3 9.2 copy-start.16
  849.4 9.2 copy-start.18
  896.6 8.2 copy-start.13
  896.6 8.2 copy-start.21
  896.6 65.0 %reduce-scatter.23.cloned.1.call-start = ((), (), s32[]{:S(2)}) async-start(), calls=%async_computation.13 | async-start | bytes 2949120 | tf_op jit(solution)/shard_map/reduce_scatter | solution.py:136
  904.5 92.9 %reduce-scatter.21.cloned.1.call-start = ((), (), s32[]{:S(2)}) async-start(), calls=%async_computation.12 | async-start | bytes 2949120 | tf_op jit(solution)/shard_map/reduce_scatter | solution.py:135
  913.1 9.6 copy-start.19
  913.1 12.3 copy-start.11
  913.2 106.1 %reduce-scatter.31.cloned.1.call-start = ((), (), s32[]{:S(2)}) async-start(), calls=%async_computation.17 | async-start | bytes 40960
  918.5 124.8 %reduce-scatter.35.cloned.1.call-start = ((), (), s32[]{:S(2)}) async-start(), calls=%async_computation.19 | async-start | bytes 491520
  920.3 144.8 %reduce-scatter.27.cloned.1.call-start = ((), (), s32[]{:S(2)}) async-start(), calls=%async_computation.15 | async-start | bytes 40960
  924.3 164.7 %reduce-scatter.33.cloned.1.call-start = ((), (), s32[]{:S(2)}) async-start(), calls=%async_computation.18 | async-start | bytes 491520
  925.4 287.1 %all-reduce.14.cloned.1.call-start = ((), (), s32[]{:S(2)}) async-start(), calls=%async_computation.11 | async-start | bytes 6291456 | tf_op jit(solution)/shard_map/psum | solution.py:126
  931.5 343.6 %all-reduce.16.cloned.1.call-start = ((), (), s32[]{:S(2)}) async-start(), calls=%async_computation.20 | async-start | bytes 3932160 | tf_op jit(solution)/shard_map/psum | solution.py:133
Sparse Core Ops, SparseCore 0:
  52.0 225.5 all-reduce.7
  307.4 221.7 all-reduce.9
  556.4 221.7 all-reduce.11
  802.2 22.2 reduce-scatter.28
  896.7 29.3 reduce-scatter.24
  928.6 33.0 reduce-scatter.22
  964.3 33.0 reduce-scatter.20
  999.9 19.3 reduce-scatter.30
  1022.5 20.8 reduce-scatter.34
  1045.7 19.3 reduce-scatter.26
  1068.2 20.7 reduce-scatter.32
  1091.3 121.0 all-reduce.13
  1215.5 59.5 all-reduce.15
where the time goes:
time: 1300 us; the launch traced here: 1290 us
  waiting for transfers between devices  983 us (76%)
  matrix products  150 us (12%)
  local copies, waits for them, and re-layouts  71.7 us (6%)
  other arithmetic  60.1 us (5%)
  between operations  14.9 us (1%)
    psum x1, waiting for transfers between devices, local(): attention = lax.psum(attn_share, 'tensor')  225 us
    psum x1, waiting for transfers between devices, local(): entry_ffn = lax.psum(entry_share, 'tensor')  222 us
    psum x1, waiting for transfers between devices, local(): feed = lax.psum(feed_share, 'tensor')  218 us
    psum x1, waiting for transfers between devices, local(): lax.psum(jnp.einsum('cth,cdh->td', grad_proj_low, w_qkv, preferred_elemen...  112 us
    unnamed x19, waiting for transfers between devices  89.2 us
    psum x1, waiting for transfers between devices, local(): lax.psum((lax.psum_scatter(grad_win, 'local', scatter_dimension=0, tiled=...  55.7 us
    reduce_scatter x1, waiting for transfers between devices, local(): lax.psum_scatter(grad_win, 'local', scatter_dimension=0, tiled=True)  35.8 us
    unnamed x87, local copies, waits for them, and re-layouts  35.7 us
  transfers between devices with their start and end apart: 13, of which 11 were waited for; matrix products, arithmetic and copies ran while one was open for 12% of the time, Pallas kernels for 0%

commit v1 on v0

v1 whole, which is shorter than its diff:
```python
import math

import jax
import jax.numpy as jnp
from jax import lax
from jax.sharding import PartitionSpec as P

EPSILON = 1e-12
MASKED = -1e30
BF = jnp.bfloat16
F32 = jnp.float32


def normalize(values):
    centre = values - jnp.mean(values, axis=-1, keepdims=True)
    variance = jnp.mean(centre * centre, axis=-1, keepdims=True)
    recip = lax.rsqrt(variance + EPSILON)
    return (centre * recip, recip)


def norm_back(grad_norm, normed, recip):
    first = jnp.mean(grad_norm, axis=-1, keepdims=True)
    second = jnp.mean(grad_norm * normed, axis=-1, keepdims=True)
    return recip * (grad_norm - first - normed * second)


def gelu_slope(values):
    cumul = 0.5 * (1.0 + lax.erf(values * (1.0 / math.sqrt(2.0))))
    return cumul + values * jnp.exp(-0.5 * values * values) * (1.0 / math.sqrt(2.0 * math.pi))


def swap(value, axis, size, bit):
    return lax.ppermute(value, axis, [(i, i ^ bit) for i in range(size)])


def ordered(own, got, bit, axis):
    first = jnp.where(bit == 0, own, got)
    second = jnp.where(bit == 0, got, own)
    return jnp.stack([first, second], axis)


def line_gather(own, size):
    right = [None, lax.ppermute(own, "tensor", [(i, i + 1) for i in range(size - 1)])]
    left = [None, lax.ppermute(own, "tensor", [(i + 1, i) for i in range(size - 1)])]
    for step in range(2, size):
        right.append(lax.ppermute(right[-1], "tensor", [(i, i + 1) for i in range(step - 1, size - 1)]))
        left.append(lax.ppermute(left[-1], "tensor", [(i + 1, i) for i in range(size - step)]))
    place = lax.axis_index("tensor")
    return [own] + [jnp.where(place >= s, right[s], left[size - s]) for s in range(1, size)]


def make(sizes):
    n_outer, n_local, n_tensor = sizes["outer"], sizes["local"], sizes["tensor"]

    def local(tokens, segments, w_qkv, b_qv, w_out, w_in, b_inner, w_down, gains, shifts, cotangent):
        seq_count, seq_len, width = tokens.shape
        heads, head_size = b_qv.shape[1], b_qv.shape[2]
        head_cols = heads * head_size
        hidden_cols = w_in.shape[1]
        rows = seq_count * seq_len
        own_rows = rows // n_tensor
        own_seqs = seq_count // n_tensor
        scale = head_size ** (-0.5)
        z = lax.axis_index("tensor")
        l_index = lax.axis_index("local")
        core, x = l_index & 1, l_index >> 1
        o_index = lax.axis_index("outer")
        y = o_index & 1
        z_from = lambda s: jnp.mod(z - s, n_tensor)
        z_to = lambda s: jnp.mod(z + s, n_tensor)
        cyclic = lambda v, s: lax.ppermute(v, "tensor", [(i, (i + s) % n_tensor) for i in range(n_tensor)])

        def gather(pack):
            piece_rows = pack.shape[0] // 8
            piece = lax.dynamic_slice_in_dim(pack, (core * 4 + y * 2 + x) * piece_rows, piece_rows, 0)
            got = jnp.stack(line_gather(piece, n_tensor)[1:])
            half = width // 2
            a, b = got[..., :half], got[..., half:]
            a = ordered(a, swap(a, "local", n_local, 2), x, 1)
            b = ordered(b, swap(b, "outer", n_outer, 1), y, 1)
            a = ordered(a, swap(a, "outer", n_outer, 1), y, 1)
            b = ordered(b, swap(b, "local", n_local, 2), x, 2)
            both = jnp.concatenate([a, b], -1)
            both = ordered(both, swap(both, "local", n_local, 1), core, 1)
            both = both.reshape(n_tensor - 1, pack.shape[0], width)
            return jnp.concatenate([pack[None], both])

        qkv_rows = w_qkv.transpose(0, 2, 1).reshape(3 * head_cols, width)
        out_all = gather(w_out)
        in_all = gather(w_in)
        down_all = gather(w_down)
        qkv_all = gather(qkv_rows).reshape(n_tensor, 3, head_cols, width)
        biases = jnp.concatenate([b_inner.reshape(-1), b_qv.reshape(-1)])
        bias_all = jnp.stack([biases] + [cyclic(biases, s) for s in range(1, n_tensor)])
        b_inner_all = bias_all[:, :hidden_cols]
        b_qv_all = bias_all[:, hidden_cols:].reshape(n_tensor, 2, head_cols)

        flat_tokens = tokens.reshape(rows, width)
        projected = jnp.einsum("td,cdh->cth", flat_tokens, w_qkv, preferred_element_type=F32)
        shape = (seq_count, seq_len, heads, head_size)
        queries = (projected[0] + b_qv[0].reshape(-1)).astype(BF).reshape(shape)
        keys = projected[1].astype(BF).reshape(shape)
        values = (projected[2] + b_qv[1].reshape(-1)).astype(BF).reshape(shape)
        allowed = segments[:, None, :, None] == segments[:, None, None, :]
        scores = jnp.einsum("sqhe,skhe->shqk", queries, keys, preferred_element_type=F32)
        probs = jax.nn.softmax(jnp.where(allowed, scores * scale, MASKED), axis=-1).astype(BF)
        context = jnp.einsum("shqk,skhe->sqhe", probs, values, preferred_element_type=F32)
        context = context.astype(BF).reshape(n_tensor, own_rows, head_cols)
        pick = lambda v, i: lax.dynamic_index_in_dim(v, i, 0, keepdims=False)
        ctx = [pick(context, z)] + [cyclic(pick(context, z_to(s)), s) for s in range(1, n_tensor)]

        own_tokens = pick(tokens.reshape(n_tensor, own_rows, width), z)
        own_cot = pick(cotangent.reshape(n_tensor, own_rows, width), z).astype(F32)
        ctx_all = jnp.stack(ctx)
        attention = jnp.einsum("sth,shd->td", ctx_all, out_all, preferred_element_type=F32)
        norm_one, recip_one = normalize(own_tokens.astype(F32) + attention + shifts[0])
        hidden1 = norm_one * gains[0] + shifts[1]
        hidden_low = hidden1.astype(BF)
        pre_act = jnp.einsum("td,sdf->stf", hidden_low, in_all, preferred_element_type=F32)
        pre_act = pre_act + b_inner_all[:, None, :]
        activation = jax.nn.gelu(pre_act, approximate=False).astype(BF)
        feed = jnp.einsum("stf,sfd->td", activation, down_all, preferred_element_type=F32)
        norm_two, recip_two = normalize(hidden1 + feed + shifts[2])
        output_own = (norm_two * gains[1] + shifts[3]).astype(BF)

        def spread(own):
            parts = line_gather(own, n_tensor)
            whole = jnp.zeros((n_tensor,) + own.shape, own.dtype)
            for s in range(n_tensor):
                whole = lax.dynamic_update_index_in_dim(whole, parts[s], z_from(s), 0)
            return whole.reshape(seq_count, seq_len, width)

        output = spread(output_own)

        place = x * 4 + core * 2 + y

        def relative(value):
            blocks = value.T.reshape(8, width // 8, own_rows)
            return jnp.stack([pick(blocks, place ^ r) for r in range(8)])

        def scatter(left, right):
            part = left.reshape(2, 2, 2 * (width // 8), own_rows)
            mul = lambda v: jnp.einsum("xdt,stn->xsdn", v, right, preferred_element_type=F32)
            keep, send = mul(part[:, 0]), mul(part[:, 1]).astype(BF)
            total = keep + swap(send, "local", n_local, 1).astype(F32)
            total = total[0] + swap(total[1].astype(BF), "local", n_local, 2).astype(F32)
            half = width // 8
            total = total[:, :half] + swap(total[:, half:].astype(BF), "outer", n_outer, 1).astype(F32)
            mine = total[0]
            for s in range(1, n_tensor):
                mine = mine + cyclic(total[s].astype(BF), n_tensor - s).astype(F32)
            bit = 2
            while bit < n_outer:
                mine = mine + swap(mine.astype(BF), "outer", n_outer, bit).astype(F32)
                bit *= 2
            other = swap(mine.astype(BF), "outer", n_outer, 1).astype(F32)
            return ordered(mine, other, y, 0).reshape(2 * half, mine.shape[-1])

        grad_gain2 = jnp.sum(own_cot * norm_two, axis=0)
        grad_beta2 = jnp.sum(own_cot, axis=0)
        grad_r2 = norm_back(own_cot * gains[1], norm_two, recip_two)
        grad_bdown = jnp.sum(grad_r2, axis=0)
        grad_r2_low = grad_r2.astype(BF)
        done_wdown = scatter(relative(grad_r2_low), activation)
        grad_act = jnp.einsum("td,sfd->stf", grad_r2_low, down_all, preferred_element_type=F32)
        grad_pre = grad_act * gelu_slope(pre_act)
        grad_binner = jnp.sum(grad_pre, axis=1)
        grad_pre_low = grad_pre.astype(BF)
        done_win = scatter(relative(hidden_low), grad_pre_low)
        entry_ffn = jnp.einsum("stf,sdf->td", grad_pre_low, in_all, preferred_element_type=F32)
        grad_h1 = grad_r2 + entry_ffn
        grad_gain1 = jnp.sum(grad_h1 * norm_one, axis=0)
        grad_beta1 = jnp.sum(grad_h1, axis=0)
        grad_r1 = norm_back(grad_h1 * gains[0], norm_one, recip_one)
        grad_bout = jnp.sum(grad_r1, axis=0)
        grad_r1_low = grad_r1.astype(BF)
        done_wout = scatter(relative(grad_r1_low), ctx_all)
        grad_context = jnp.einsum("td,shd->sth", grad_r1_low, out_all, preferred_element_type=F32)
        all_heads = (n_tensor, own_seqs, seq_len, heads, head_size)
        grad_context = grad_context.astype(BF).reshape(all_heads)

        own_proj = jnp.einsum("td,schd->csth", own_tokens, qkv_all, preferred_element_type=F32)
        q = (own_proj[0] + b_qv_all[:, 0, None, :]).astype(BF).reshape(all_heads)
        k = own_proj[1].astype(BF).reshape(all_heads)
        v = (own_proj[2] + b_qv_all[:, 1, None, :]).astype(BF).reshape(all_heads)
        own_segments = pick(segments.reshape(n_tensor, own_seqs, seq_len), z)
        own_allowed = own_segments[None, :, None, :, None] == own_segments[None, :, None, None, :]
        own_scores = jnp.einsum("znqhe,znkhe->znhqk", q, k, preferred_element_type=F32)
        own_probs = jax.nn.softmax(jnp.where(own_allowed, own_scores * scale, MASKED), axis=-1)
        grad_probs = jnp.einsum("znqhe,znkhe->znhqk", grad_context, v, preferred_element_type=F32)
        inner = jnp.sum(own_probs * grad_probs, axis=-1, keepdims=True)
        grad_scores = (own_probs * (grad_probs - inner) * scale).astype(BF)
        grad_q = jnp.einsum("znhqk,znkhe->znqhe", grad_scores, k, preferred_element_type=F32)
        grad_k = jnp.einsum("znhqk,znqhe->znkhe", grad_scores, q, preferred_element_type=F32)
        grad_v = jnp.einsum("znhqk,znqhe->znkhe", own_probs.astype(BF), grad_context, preferred_element_type=F32)
        flat = lambda g: g.reshape(n_tensor, own_rows, head_cols)
        grad_bqv = jnp.stack([jnp.sum(flat(grad_q), 1), jnp.sum(flat(grad_v), 1)], 1)
        grad_proj = jnp.concatenate([flat(grad_q), flat(grad_k), flat(grad_v)], -1).astype(BF)
        qkv_cat = qkv_all.reshape(n_tensor, 3 * head_cols, width)
        entry_attn = jnp.einsum("sth,shd->td", grad_proj, qkv_cat, preferred_element_type=F32)
        grad_tokens = spread((grad_r1 + entry_attn).astype(BF)).astype(F32)
        done_wqkv = scatter(relative(own_tokens), grad_proj)

        slot_vec = jnp.concatenate([grad_binner, grad_bqv.reshape(n_tensor, -1)], 1)
        placed = jnp.zeros_like(slot_vec)
        for s in range(n_tensor):
            placed = lax.dynamic_update_index_in_dim(placed, slot_vec[s], z_from(s), 0)
        common = jnp.stack([grad_gain1, grad_gain2, grad_bout, grad_beta1, grad_bdown, grad_beta2])
        vectors = lax.psum(jnp.concatenate([placed.reshape(-1), common.reshape(-1)]), ("outer", "local", "tensor"))
        slot_sum = pick(vectors[: placed.size].reshape(placed.shape), z)
        common = vectors[placed.size :].reshape(common.shape)
        part = lambda v, n: lax.dynamic_slice_in_dim(v, l_index * (n // n_local), n // n_local, v.ndim - 1)
        binner = part(slot_sum[:hidden_cols].reshape(b_inner.shape), head_size)
        bqv = part(slot_sum[hidden_cols:].reshape(b_qv.shape), head_size)
        common = part(common, width)
        grad_wqkv = done_wqkv.reshape(width // n_local, 3, head_cols).transpose(1, 0, 2)
        return (
            output,
            grad_tokens,
            grad_wqkv,
            bqv,
            done_wout.T,
            done_win,
            binner,
            done_wdown.T,
            common[:2],
            common[2:],
        )

    return local


def solution(mesh):
    placed = (
        P(("outer", "local"), None, None),
        P(("outer", "local"), None),
        P(None, None, "tensor"),
        P(None, "tensor", None),
        P("tensor", None),
        P(None, "tensor"),
        P("tensor", None),
        P("tensor", None),
        P(),
        P(),
        P(("outer", "local"), None, None),
    )
    return jax.shard_map(
        make(dict(mesh.shape)),
        mesh=mesh,
        in_specs=placed,
        out_specs=(
            P(("outer", "local"), None, None),
            P(("outer", "local"), None, None),
            P(None, "local", "tensor"),
            P(None, "tensor", "local"),
            P("tensor", "local"),
            P("local", "tensor"),
            P("tensor", "local"),
            P("tensor", "local"),
            P(None, "local"),
            P(None, "local"),
        ),
        check_vma=False,
    )
```

time: 1300 us -> 609 us (0.47)
  waiting for transfers between devices: 983 us -> 177 us
  starting transfers between devices: 0.79 us -> 130 us
  blocking collectives: 8.85 us -> 40.6 us
  other arithmetic: 60.1 us -> 44.1 us
    psum x5 -> x0, waiting for transfers between devices: 833 us -> none  [the longest x1 225 us: local(): attention = lax.psum(attn_share, 'tensor')]
    ppermute x0 -> x90, waiting for transfers between devices: none -> 177 us  [the longest x12 78.8 us: line_gather(): lax.ppermute(left[-1], 'tensor', [(i + 1, i) for i in range(size - step)])]
    ppermute x0 -> x90, starting transfers between devices: none -> 130 us  [the longest x18 42 us: local(): lax.ppermute(v, 'tensor', [(i, (i + s) % n_tensor) for i in range(n_tenso...]
    unnamed x19 -> x0, waiting for transfers between devices: 89.2 us -> none
    reduce_scatter x2 -> x0, waiting for transfers between devices: 61.6 us -> none  [the longest x1 35.8 us: local(): lax.psum_scatter(grad_win, 'local', scatter_dimension=0, tiled=True)]
    psum x1, blocking collectives: 8.85 us -> 40.6 us  [local(): lax.psum(jnp.concatenate([placed.reshape(-1), common.reshape(-1)]), ('out...]
    dot_general x17 -> x22, matrix products: 148 us -> 118 us  [the longest x8 25 us: scatter(): jnp.einsum('xdt,stn->xsdn', v, right, preferred_element_type=F32)]
    reduce_sum x6 -> x4, other arithmetic: 29.5 us -> 2.04 us  [the longest x1 1.59 us: local(): jnp.sum(flat(grad_v), 1)]
  transfers between devices with their start and end apart: 13 -> 90, of which waited for: 11 -> 36; matrix products, arithmetic and copies ran while one was open for 12% -> 24% of each run, Pallas kernels for 0% -> 0%
where the time goes in v1:
time: 609 us; the launch traced here: 604 us
  waiting for transfers between devices  177 us (29%)
  matrix products  140 us (23%)
  starting transfers between devices  130 us (21%)
  local copies, waits for them, and re-layouts  69.1 us (11%)
  other arithmetic  44.1 us (7%)
  blocking collectives  40.6 us (7%)
    ppermute x12, waiting for transfers between devices, line_gather(): lax.ppermute(left[-1], 'tensor', [(i + 1, i) for i in range(size - step)])  78.8 us
    ppermute x36, waiting for transfers between devices, swap(): return lax.ppermute(value, axis, [(i, i ^ bit) for i in range(size)])  74 us
    ppermute x18, starting transfers between devices, local(): lax.ppermute(v, 'tensor', [(i, (i + s) % n_tensor) for i in range(n_tenso...  42 us
    psum x1, blocking collectives, local(): lax.psum(jnp.concatenate([placed.reshape(-1), common.reshape(-1)]), ('out...  40.6 us
    ppermute x36, starting transfers between devices, swap(): return lax.ppermute(value, axis, [(i, i ^ bit) for i in range(size)])  29.5 us
    ppermute x6, starting transfers between devices, line_gather(): lax.ppermute(own, 'tensor', [(i, i + 1) for i in range(size - 1)])  25.1 us
    dot_general x8, matrix products, scatter(): jnp.einsum('xdt,stn->xsdn', v, right, preferred_element_type=F32)  25 us
    unnamed x181, local copies, waits for them, and re-layouts  22.5 us
  transfers between devices with their start and end apart: 90, of which 36 were waited for; matrix products, arithmetic and copies ran while one was open for 24% of the time, Pallas kernels for 0%

profile of v1, /device:TPU:0, one launch (start us, length us, event | category | flops | bytes accessed | tf_op | source)
XLA Modules:
  0.0 603.9 jit_solution(14907237546093854566)
XLA Ops:
  3.3 6.2 %collective-permute-start.3 = (bf16[24,768]{1,0:T(8,128)(2,1)}, bf16[24,768]{1,0:T(8,128)(2,1)}, u32[]{:S(2)}, u32[]{:S(2)}) collective-permute-start(bf16[24,768]{1,0:T(8,128)(2,1)} %constant_dynamic-slice_fusion.8), channel_id=1, source_target_pairs={{0,1},{1,2},{2,3},{4,5},{5,6},{6,7},{8,9},{9,10},{10,11},{12,13},{... | collective-permute-start | bytes 110600 | tf_op jit(solution)/shard_map/ppermute | solution.py:43
  16.7 2.9 collective-permute-start.27
  20.9 4.2 convolution_bitcast_fusion
  33.2 2.2 squeeze.139
  35.4 3.1 convert_element_type.278
  48.3 11.5 %fusion.209 = (f32[4,3,512]{2,1,0:T(4,128)S(1)}, f32[4,3,512,512]{2,3,1,0:T(8,128)}) fusion(pred[4,512,512]{1,2,0:T(8,128)(4,1)S(1)} %copy-done.31, bf16[4,512,3,64]{1,0,3,2:T(4,128)(2,1)} %convert_element_type.278, f32[4,512,3,64]{1,0,3,2:T(4,128)} %squeeze.139, f32[3,64]{1,0:T(4,128)S(1)} %get-tuple-element.180), kind=kOutput, calls=%fused_computation.445 | convolution fusion | flops 416023040 | bytes 16016128 | tf_op jit(solution)/shard_map/sub | solution.py:106
  59.8 6.0 fusion.103
  70.5 4.5 collective-permute-start.45
  80.5 3.9 collective-permute-done.5
  86.6 5.5 collective-permute-done.6
  97.2 2.4 collective-permute-start.28
  103.0 6.1 %collective-permute-done.47 = bf16[72,768]{1,0:T(8,128)(2,1)S(1)} collective-permute-done((bf16[72,768]{1,0:T(8,128)(2,1)S(1)}, bf16[72,768]{1,0:T(8,128)(2,1)S(1)}, u32[]{:S(2)}, u32[]{:S(2)}) %collective-permute-start.47) | collective-permute-done | bytes 110624 | tf_op jit(solution)/shard_map/ppermute | solution.py:47
  109.1 3.9 collective-permute-start.14
  113.7 4.2 collective-permute-done.10
  126.7 4.3 collective-permute-done.30
  133.0 8.0 %collective-permute-done.16 = bf16[96,768]{1,0:T(8,128)(2,1)S(1)} collective-permute-done((bf16[96,768]{1,0:T(8,128)(2,1)S(1)}, bf16[96,768]{1,0:T(8,128)(2,1)S(1)}, u32[]{:S(2)}, u32[]{:S(2)}) %collective-permute-start.16) | collective-permute-done | bytes 147488 | tf_op jit(solution)/shard_map/ppermute | solution.py:47
  143.7 4.6 collective-permute-done.48
  150.4 4.9 collective-permute-done.31
  158.3 4.0 collective-permute-done.17
  164.8 3.4 collective-permute-done.53
  170.8 3.4 collective-permute-done.36
  176.1 4.9 collective-permute-done.22
  187.9 3.8 collective-permute-done.52
  193.1 8.2 %collective-permute-done.35 = bf16[3,2,96,384]{3,2,0,1:T(8,128)(2,1)S(1)} collective-permute-done((bf16[3,2,96,384]{3,2,0,1:T(8,128)(2,1)S(1)}, bf16[3,2,96,384]{3,2,0,1:T(8,128)(2,1)S(1)}, u32[]{:S(2)}, u32[]{:S(2)}) %collective-permute-start.35) | collective-permute-done | bytes 442400 | tf_op jit(solution)/shard_map/ppermute | solution.py:33
  201.9 4.7 collective-permute-done.37
  217.4 11.1 %fusion.220 = (f32[4,3,512]{2,1,0:T(4,128)S(1)}, f32[4,3,512,512]{2,3,1,0:T(8,128)}) fusion(pred[512,512]{0,1:T(8,128)(4,1)S(1)} %copy-done.37, bf16[4,512,3,64]{1,3,2,0:T(8,128)(2,1)} %bitcast.594, f32[4,512,3,64]{1,3,2,0:T(8,128)} %bitcast.590, f32[4,3,64]{2,1,0:T(4,128)S(1)} %copy-done.57), kind=kOutput, calls=%fused_computation.448 | convolution fusion | flops 416023040 | bytes 15232000 | tf_op jit(solution)/shard_map/sub | solution.py:189
  228.5 2.4 select_bitcast_fusion.1
  232.5 2.3 select_bitcast_fusion.3
  236.4 15.8 %fusion.10 = (bf16[4,512,768]{2,1,0:T(8,128)(2,1)S(1)}, f32[4,768,512]{1,2,0:T(8,128)S(1)}) fusion(f32[4,768]{1,0:T(4,128)S(1)} %copy-done.55, bf16[3,768,768]{2,1,0:T(8,128)(2,1)S(1)} %bitcast.551, bf16[1,768,768]{2,1,0:T(8,128)(2,1)S(1)} %bitcast.607, f32[768]{0:T(1024)S(1)} %copy-done.49, f32[768]{0:T(1024)S(1)} %copy-done.45, ...), kind=kOutput, calls=%fused_computation.17 | convolution fusion | flops 2531131392 | bytes 15751168 | tf_op jit(solution)/shard_map/td,sdf->stf/dot_general | solution.py:119
  252.3 2.8 fusion.219
  257.6 6.0 fusion.223
  263.6 2.7 bitcast_add_fusion.5
  271.3 7.0 %fusion.116 = f32[4,3,512,512]{2,3,1,0:T(8,128)} fusion(bf16[4,512,3,64]{1,3,2,0:T(8,128)(2,1)S(1)} %bitcast.588, f32[4,512,3,64]{1,3,2,0:T(8,128)S(1)} %bitcast.548, f32[4,3,64]{2,1,0:T(4,128)S(1)} %copy-done.43), kind=kOutput, calls=%fused_computation.177 | convolution fusion | flops 403439616 | bytes 14945280 | tf_op jit(solution)/shard_map/znqhe,znkhe->znhqk/dot_general | solution.py:190
  278.3 3.5 bitcast_convert_fusion
  281.8 19.2 %bitcast_convert_fusion.1 = (bf16[4,1,512,3,64]{2,4,3,0,1:T(8,128)(2,1)}, f32[4,3,64,512]{3,2,1,0:T(8,128)}) fusion(bf16[4,512,3,64]{1,3,2,0:T(8,128)(2,1)} %bitcast.595, f32[4,3,512,512]{2,3,1,0:T(8,128)} %fusion.116, f32[4,3,512,512]{2,3,1,0:T(8,128)} %get-tuple-element.169, f32[4,3,512]{2,1,0:T(4,128)S(1)} %get-tuple-element.168), kind=kOutput, calls=%fused_computation.129 | convolution fusion | flops 425073152 | bytes 28336128 | tf_op jit(solution)/shard_map/znhqk,znkhe->znqhe/dot_general | solution.py:193
  301.0 18.8 %fusion.104 = bf16[4,3,64,512]{3,2,1,0:T(8,128)(2,1)} fusion(f32[4,3,512,512]{2,3,1,0:T(8,128)} %fusion.116, f32[4,3,512,512]{2,3,1,0:T(8,128)} %get-tuple-element.169, f32[4,3,512]{2,1,0:T(4,128)S(1)} %get-tuple-element.168, f32[4,512,3,64]{1,3,2,0:T(8,128)S(1)} %bitcast.591, f32[4,3,64]{2,1,0:T(4,128)S(1)} %copy-done.57), kind=kOutput, calls=%fused_computation.154 | convolution fusion | flops 425859584 | bytes 27552768 | tf_op jit(solution)/shard_map/znhqk,znqhe->znkhe/dot_general | solution.py:194
  334.4 2.9 fusion.112
  339.4 4.4 convert_bitcast_fusion.2
  345.4 3.0 bitcast_dynamic-update-slice_fusion.3
  351.0 2.8 convert_bitcast_fusion
  359.8 7.5 %collective-permute-done.70 = bf16[4,192,192]{2,1,0:T(8,128)(2,1)S(1)} collective-permute-done((bf16[4,192,192]{2,1,0:T(8,128)(2,1)S(1)}, bf16[4,192,192]{2,1,0:T(8,128)(2,1)S(1)}, u32[]{:S(2)}, u32[]{:S(2)}) %collective-permute-start.70) | collective-permute-done | bytes 294944 | tf_op jit(solution)/shard_map/ppermute | solution.py:33
  369.6 4.6 collective-permute-done.71
  374.9 4.6 collective-permute-start.72
  382.1 5.2 collective-permute-start.56
  388.6 4.8 convert_bitcast_fusion.1
  395.1 40.6 %psum.7 = f32[9216]{0:T(1024)S(1)} all-reduce(f32[9216]{0:T(1024)S(1)} %pad_maximum_fusion.40), channel_id=1, replica_groups=mesh['outer'=2,'local'=4,'tensor'=4] {'outer','local','tensor'}, use_global_device_ids=true, to_apply=%region_22.23 | all-reduce | flops 9216 | bytes 73728 | tf_op jit(solution)/shard_map/psum | solution.py:209
  435.8 2.9 collective-permute-start.39
  443.2 10.9 %collective-permute-done.39 = bf16[512,768]{1,0:T(8,128)(2,1)} collective-permute-done((bf16[512,768]{1,0:T(8,128)(2,1)}, bf16[512,768]{1,0:T(8,128)(2,1)}, u32[]{:S(2)}, u32[]{:S(2)}) %collective-permute-start.39) | collective-permute-done | bytes 786464 | tf_op jit(solution)/shard_map/ppermute | solution.py:43
  455.6 5.2 collective-permute-done.58
  464.5 3.7 bitcast_add_fusion.2
  469.7 13.6 %collective-permute-done.41 = bf16[512,768]{1,0:T(8,128)(2,1)} collective-permute-done((bf16[512,768]{1,0:T(8,128)(2,1)S(1)}, bf16[512,768]{1,0:T(8,128)(2,1)}, u32[]{:S(2)}, u32[]{:S(2)}) %collective-permute-start.41) | collective-permute-done | bytes 786464 | tf_op jit(solution)/shard_map/ppermute | solution.py:47
  487.7 2.2 collective-permute-start.63
  489.9 3.2 bitcast_add_fusion.1
  493.1 6.9 %collective-permute-done.59 = bf16[512,768]{1,0:T(8,128)(2,1)S(1)} collective-permute-done((bf16[512,768]{1,0:T(8,128)(2,1)}, bf16[512,768]{1,0:T(8,128)(2,1)S(1)}, u32[]{:S(2)}, u32[]{:S(2)}) %collective-permute-start.59) | collective-permute-done | bytes 786464 | tf_op jit(solution)/shard_map/ppermute | solution.py:47
  503.9 11.7 %collective-permute-done.42 = bf16[512,768]{1,0:T(8,128)(2,1)S(1)} collective-permute-done((bf16[512,768]{1,0:T(8,128)(2,1)}, bf16[512,768]{1,0:T(8,128)(2,1)S(1)}, u32[]{:S(2)}, u32[]{:S(2)}) %collective-permute-start.42) | collective-permute-done | bytes 786464 | tf_op jit(solution)/shard_map/ppermute | solution.py:47
  524.1 6.8 %collective-permute-done.64 = bf16[4,96,576]{2,1,0:T(8,128)(2,1)S(1)} collective-permute-done((bf16[4,96,576]{2,1,0:T(8,128)(2,1)S(1)}, bf16[4,96,576]{2,1,0:T(8,128)(2,1)S(1)}, u32[]{:S(2)}, u32[]{:S(2)}) %collective-permute-start.64) | collective-permute-done | bytes 442400 | tf_op jit(solution)/shard_map/ppermute | solution.py:33
  531.0 4.4 collective-permute-start.65
  539.7 3.2 convert_element_type.298
  549.1 10.8 %collective-permute-done.77 = bf16[4,192,768]{2,1,0:T(8,128)(2,1)S(1)} collective-permute-done((bf16[4,192,768]{2,1,0:T(8,128)(2,1)S(1)}, bf16[4,192,768]{2,1,0:T(8,128)(2,1)S(1)}, u32[]{:S(2)}, u32[]{:S(2)}) %collective-permute-start.77) | collective-permute-done | bytes 1179680 | tf_op jit(solution)/shard_map/ppermute | solution.py:33
  566.3 9.7 %collective-permute-start.86 = (bf16[96,768]{1,0:T(8,128)(2,1)S(1)}, bf16[96,768]{1,0:T(8,128)(2,1)S(1)}, u32[]{:S(2)}, u32[]{:S(2)}) collective-permute-start(bf16[96,768]{1,0:T(8,128)(2,1)S(1)} %get-tuple-element.104), channel_id=1, source_target_pairs={{0,3},{1,0},{2,1},{3,2},{4,7},{5,4},{6,5},{7,6},{8,11},{9,8},{10,9... | collective-permute-start | bytes 442376 | tf_op jit(solution)/shard_map/ppermute | solution.py:71
  580.3 2.2 collective-permute-start.79
  585.4 8.5 %collective-permute-done.87 = bf16[96,768]{1,0:T(8,128)(2,1)S(1)} collective-permute-done((bf16[96,768]{1,0:T(8,128)(2,1)S(1)}, bf16[96,768]{1,0:T(8,128)(2,1)S(1)}, u32[]{:S(2)}, u32[]{:S(2)}) %collective-permute-start.87) | collective-permute-done | bytes 147488 | tf_op jit(solution)/shard_map/ppermute | solution.py:71
  594.1 3.4 collective-permute-done.80
  598.1 2.4 collective-permute-done.89
  (515 shorter events, 196.2 us)
Async XLA Ops:
  2.0 75.7 %collective-permute-start.4 = (bf16[24,768]{1,0:T(8,128)(2,1)}, bf16[24,768]{1,0:T(8,128)(2,1)}, u32[]{:S(2)}, u32[]{:S(2)}) collective-permute-start(bf16[24,768]{1,0:T(8,128)(2,1)} %constant_dynamic-slice_fusion.8), channel_id=1, source_target_pairs={{1,0},{2,1},{3,2},{5,4},{6,5},{7,6},{9,8},{10,9},{11,10},{13,12},{... | collective-permute-start | bytes 110600 | tf_op jit(solution)/shard_map/ppermute | solution.py:44
  3.3 75.8 %collective-permute-start.3 = (bf16[24,768]{1,0:T(8,128)(2,1)}, bf16[24,768]{1,0:T(8,128)(2,1)}, u32[]{:S(2)}, u32[]{:S(2)}) collective-permute-start(bf16[24,768]{1,0:T(8,128)(2,1)} %constant_dynamic-slice_fusion.8), channel_id=1, source_target_pairs={{0,1},{1,2},{2,3},{4,5},{5,6},{6,7},{8,9},{9,10},{10,11},{12,13},{... | collective-permute-start | bytes 110600 | tf_op jit(solution)/shard_map/ppermute | solution.py:43
  13.6 54.9 %collective-permute-start.25 = (f32[1152]{0:T(1024)}, f32[1152]{0:T(1024)}, u32[]{:S(2)}, u32[]{:S(2)}) collective-permute-start(f32[1152]{0:T(1024)} %constant_dynamic-update-slice_fusion.1), channel_id=1, source_target_pairs={{0,1},{1,2},{2,3},{3,0},{4,5},{5,6},{6,7},{7,4},{8,9},{9,10},{10,1... | collective-permute-start | bytes 13832 | tf_op jit(solution)/shard_map/ppermute | solution.py:71
  15.1 55.4 %collective-permute-start.26 = (f32[1152]{0:T(1024)}, f32[1152]{0:T(1024)}, u32[]{:S(2)}, u32[]{:S(2)}) collective-permute-start(f32[1152]{0:T(1024)} %constant_dynamic-update-slice_fusion.1), channel_id=1, source_target_pairs={{0,2},{1,3},{2,0},{3,1},{4,6},{5,7},{6,4},{7,5},{8,10},{9,11},{10,... | collective-permute-start | bytes 13832 | tf_op jit(solution)/shard_map/ppermute | solution.py:71
  16.7 59.1 %collective-permute-start.27 = (f32[1152]{0:T(1024)}, f32[1152]{0:T(1024)}, u32[]{:S(2)}, u32[]{:S(2)}) collective-permute-start(f32[1152]{0:T(1024)} %constant_dynamic-update-slice_fusion.1), channel_id=1, source_target_pairs={{0,3},{1,0},{2,1},{3,2},{4,7},{5,4},{6,5},{7,6},{8,11},{9,8},{10,9... | collective-permute-start | bytes 13832 | tf_op jit(solution)/shard_map/ppermute | solution.py:71
  68.5 28.7 %collective-permute-start.46 = (bf16[72,768]{1,0:T(8,128)(2,1)S(1)}, bf16[72,768]{1,0:T(8,128)(2,1)S(1)}, u32[]{:S(2)}, u32[]{:S(2)}) collective-permute-start(bf16[72,768]{1,0:T(8,128)(2,1)S(1)} %constant_dynamic-slice_fusion.5), channel_id=1, source_target_pairs={{1,0},{2,1},{3,2},{5,4},{6,5},{7,6},{9,8},{10,9},{11,10},{13,12},{... | collective-permute-start | bytes 331784 | tf_op jit(solution)/shard_map/ppermute | solution.py:44
  70.5 29.1 %collective-permute-start.45 = (bf16[72,768]{1,0:T(8,128)(2,1)S(1)}, bf16[72,768]{1,0:T(8,128)(2,1)S(1)}, u32[]{:S(2)}, u32[]{:S(2)}) collective-permute-start(bf16[72,768]{1,0:T(8,128)(2,1)S(1)} %constant_dynamic-slice_fusion.5), channel_id=1, source_target_pairs={{0,1},{1,2},{2,3},{4,5},{5,6},{6,7},{8,9},{9,10},{10,11},{12,13},{... | collective-permute-start | bytes 331784 | tf_op jit(solution)/shard_map/ppermute | solution.py:43
  75.8 42.7 %collective-permute-start.29 = (bf16[96,768]{1,0:T(8,128)(2,1)S(1)}, bf16[96,768]{1,0:T(8,128)(2,1)S(1)}, u32[]{:S(2)}, u32[]{:S(2)}) collective-permute-start(bf16[96,768]{1,0:T(8,128)(2,1)S(1)} %copy-done.41), channel_id=1, source_target_pairs={{1,0},{2,1},{3,2},{5,4},{6,5},{7,6},{9,8},{10,9},{11,10},{13,12},{... | collective-permute-start | bytes 442376 | tf_op jit(solution)/shard_map/ppermute | solution.py:44
  92.2 8.7 %collective-permute-start.11 = (bf16[3,24,384]{2,1,0:T(8,128)(2,1)S(1)}, bf16[3,24,384]{2,1,0:T(8,128)(2,1)S(1)}, u32[]{:S(2)}, u32[]{:S(2)}) collective-permute-start(bf16[3,24,384]{2,1,0:T(8,128)(2,1)S(1)} %get-tuple-element.151), channel_id=1, source_target_pairs={{0,16},{16,0},{1,17},{17,1},{2,18},{18,2},{3,19},{19,3},{4,20},{20... | collective-permute-start | bytes 165896 | tf_op jit(solution)/shard_map/ppermute | solution.py:33
  93.8 8.5 %collective-permute-start.9 = (bf16[3,24,384]{2,1,0:T(8,128)(2,1)S(1)}, bf16[3,24,384]{2,1,0:T(8,128)(2,1)S(1)}, u32[]{:S(2)}, u32[]{:S(2)}) collective-permute-start(bf16[3,24,384]{2,1,0:T(8,128)(2,1)S(1)} %get-tuple-element.150), channel_id=1, source_target_pairs={{0,8},{4,12},{8,0},{12,4},{1,9},{5,13},{9,1},{13,5},{2,10},{6,14},... | collective-permute-start | bytes 165896 | tf_op jit(solution)/shard_map/ppermute | solution.py:33
  97.2 22.7 %collective-permute-start.28 = (bf16[96,768]{1,0:T(8,128)(2,1)S(1)}, bf16[96,768]{1,0:T(8,128)(2,1)S(1)}, u32[]{:S(2)}, u32[]{:S(2)}) collective-permute-start(bf16[96,768]{1,0:T(8,128)(2,1)S(1)} %copy-done.41), channel_id=1, source_target_pairs={{0,1},{1,2},{2,3},{4,5},{5,6},{6,7},{8,9},{9,10},{10,11},{12,13},{... | collective-permute-start | bytes 442376 | tf_op jit(solution)/shard_map/ppermute | solution.py:43
  99.6 23.8 %collective-permute-start.15 = (bf16[96,768]{1,0:T(8,128)(2,1)S(1)}, bf16[96,768]{1,0:T(8,128)(2,1)S(1)}, u32[]{:S(2)}, u32[]{:S(2)}) collective-permute-start(bf16[96,768]{1,0:T(8,128)(2,1)S(1)} %constant_dynamic-slice_fusion.7), channel_id=1, source_target_pairs={{1,0},{2,1},{3,2},{5,4},{6,5},{7,6},{9,8},{10,9},{11,10},{13,12},{... | collective-permute-start | bytes 442376 | tf_op jit(solution)/shard_map/ppermute | solution.py:44
  100.9 8.2 %collective-permute-start.47 = (bf16[72,768]{1,0:T(8,128)(2,1)S(1)}, bf16[72,768]{1,0:T(8,128)(2,1)S(1)}, u32[]{:S(2)}, u32[]{:S(2)}) collective-permute-start(bf16[72,768]{1,0:T(8,128)(2,1)S(1)} %collective-permute-done.46), channel_id=1, source_target_pairs={{1,0},{2,1},{5,4},{6,5},{9,8},{10,9},{13,12},{14,13},{17,16},{18,1... | collective-permute-start | bytes 331784 | tf_op jit(solution)/shard_map/ppermute | solution.py:47
  102.2 10.8 %collective-permute-start.49 = (bf16[72,768]{1,0:T(8,128)(2,1)S(1)}, bf16[72,768]{1,0:T(8,128)(2,1)S(1)}, u32[]{:S(2)}, u32[]{:S(2)}) collective-permute-start(bf16[72,768]{1,0:T(8,128)(2,1)S(1)} %collective-permute-done.45), channel_id=1, source_target_pairs={{1,2},{2,3},{5,6},{6,7},{9,10},{10,11},{13,14},{14,15},{17,18},{18... | collective-permute-start | bytes 331784 | tf_op jit(solution)/shard_map/ppermute | solution.py:46
  109.1 16.1 %collective-permute-start.14 = (bf16[96,768]{1,0:T(8,128)(2,1)S(1)}, bf16[96,768]{1,0:T(8,128)(2,1)S(1)}, u32[]{:S(2)}, u32[]{:S(2)}) collective-permute-start(bf16[96,768]{1,0:T(8,128)(2,1)S(1)} %constant_dynamic-slice_fusion.7), channel_id=1, source_target_pairs={{0,1},{1,2},{2,3},{4,5},{5,6},{6,7},{8,9},{9,10},{10,11},{12,13},{... | collective-permute-start | bytes 442376 | tf_op jit(solution)/shard_map/ppermute | solution.py:43
  118.5 64.0 %collective-permute-start.1 = (bf16[512,192]{0,1:T(8,128)(2,1)S(1)}, bf16[512,192]{0,1:T(8,128)(2,1)S(1)}, u32[]{:S(2)}, u32[]{:S(2)}) collective-permute-start(bf16[512,192]{0,1:T(8,128)(2,1)S(1)} %get-tuple-element.90), channel_id=1, source_target_pairs={{0,2},{1,3},{2,0},{3,1},{4,6},{5,7},{6,4},{7,5},{8,10},{9,11},{10,... | collective-permute-start | bytes 589832 | tf_op jit(solution)/shard_map/ppermute | solution.py:71
  119.9 11.1 %collective-permute-start.30 = (bf16[96,768]{1,0:T(8,128)(2,1)S(1)}, bf16[96,768]{1,0:T(8,128)(2,1)S(1)}, u32[]{:S(2)}, u32[]{:S(2)}) collective-permute-start(bf16[96,768]{1,0:T(8,128)(2,1)S(1)} %collective-permute-done.29), channel_id=1, source_target_pairs={{1,0},{2,1},{5,4},{6,5},{9,8},{10,9},{13,12},{14,13},{17,16},{18,1... | collective-permute-start | bytes 442376 | tf_op jit(solution)/shard_map/ppermute | solution.py:47
  122.6 9.7 %collective-permute-start.32 = (bf16[96,768]{1,0:T(8,128)(2,1)S(1)}, bf16[96,768]{1,0:T(8,128)(2,1)S(1)}, u32[]{:S(2)}, u32[]{:S(2)}) collective-permute-start(bf16[96,768]{1,0:T(8,128)(2,1)S(1)} %collective-permute-done.28), channel_id=1, source_target_pairs={{1,2},{2,3},{5,6},{6,7},{9,10},{10,11},{13,14},{14,15},{17,18},{18... | collective-permute-start | bytes 442376 | tf_op jit(solution)/shard_map/ppermute | solution.py:46
  123.4 61.1 %collective-permute-start.2 = (bf16[512,192]{0,1:T(8,128)(2,1)S(1)}, bf16[512,192]{0,1:T(8,128)(2,1)S(1)}, u32[]{:S(2)}, u32[]{:S(2)}) collective-permute-start(bf16[512,192]{0,1:T(8,128)(2,1)S(1)} %get-tuple-element.89), channel_id=1, source_target_pairs={{0,3},{1,0},{2,1},{3,2},{4,7},{5,4},{6,5},{7,6},{8,11},{9,8},{10,9... | collective-permute-start | bytes 589832 | tf_op jit(solution)/shard_map/ppermute | solution.py:71
  125.2 60.7 %collective-permute-start = (bf16[512,192]{0,1:T(8,128)(2,1)S(1)}, bf16[512,192]{0,1:T(8,128)(2,1)S(1)}, u32[]{:S(2)}, u32[]{:S(2)}) collective-permute-start(bf16[512,192]{0,1:T(8,128)(2,1)S(1)} %get-tuple-element.91), channel_id=1, source_target_pairs={{0,1},{1,2},{2,3},{3,0},{4,5},{5,6},{6,7},{7,4},{8,9},{9,10},{10,1... | collective-permute-start | bytes 589832 | tf_op jit(solution)/shard_map/ppermute | solution.py:71
  131.0 10.0 %collective-permute-start.16 = (bf16[96,768]{1,0:T(8,128)(2,1)S(1)}, bf16[96,768]{1,0:T(8,128)(2,1)S(1)}, u32[]{:S(2)}, u32[]{:S(2)}) collective-permute-start(bf16[96,768]{1,0:T(8,128)(2,1)S(1)} %collective-permute-done.15), channel_id=1, source_target_pairs={{1,0},{2,1},{5,4},{6,5},{9,8},{10,9},{13,12},{14,13},{17,16},{18,1... | collective-permute-start | bytes 442376 | tf_op jit(solution)/shard_map/ppermute | solution.py:47
  132.3 9.3 %collective-permute-start.18 = (bf16[96,768]{1,0:T(8,128)(2,1)S(1)}, bf16[96,768]{1,0:T(8,128)(2,1)S(1)}, u32[]{:S(2)}, u32[]{:S(2)}) collective-permute-start(bf16[96,768]{1,0:T(8,128)(2,1)S(1)} %collective-permute-done.14), channel_id=1, source_target_pairs={{1,2},{2,3},{5,6},{6,7},{9,10},{10,11},{13,14},{14,15},{17,18},{18... | collective-permute-start | bytes 442376 | tf_op jit(solution)/shard_map/ppermute | solution.py:46
  181.0 10.7 %collective-permute-start.52 = (bf16[3,2,72,384]{3,2,0,1:T(8,128)(2,1)S(1)}, bf16[3,2,72,384]{3,2,0,1:T(8,128)(2,1)S(1)}, u32[]{:S(2)}, u32[]{:S(2)}) collective-permute-start(bf16[3,2,72,384]{3,2,0,1:T(8,128)(2,1)S(1)} %pad_maximum_fusion.34), channel_id=1, source_target_pairs={{0,16},{16,0},{1,17},{17,1},{2,18},{18,2},{3,19},{19,3},{4,20},{20... | collective-permute-start | bytes 995336 | tf_op jit(solution)/shard_map/ppermute | solution.py:33
  181.9 10.8 %collective-permute-start.54 = (bf16[3,2,72,384]{3,2,1,0:T(8,128)(2,1)S(1)}, bf16[3,2,72,384]{3,2,1,0:T(8,128)(2,1)S(1)}, u32[]{:S(2)}, u32[]{:S(2)}) collective-permute-start(bf16[3,2,72,384]{3,2,1,0:T(8,128)(2,1)S(1)} %pad_maximum_fusion.35), channel_id=1, source_target_pairs={{0,8},{4,12},{8,0},{12,4},{1,9},{5,13},{9,1},{13,5},{2,10},{6,14},... | collective-permute-start | bytes 995336 | tf_op jit(solution)/shard_map/ppermute | solution.py:33
  182.4 18.8 %collective-permute-start.35 = (bf16[3,2,96,384]{3,2,0,1:T(8,128)(2,1)S(1)}, bf16[3,2,96,384]{3,2,0,1:T(8,128)(2,1)S(1)}, u32[]{:S(2)}, u32[]{:S(2)}) collective-permute-start(bf16[3,2,96,384]{3,2,0,1:T(8,128)(2,1)S(1)} %pad_maximum_fusion.31), channel_id=1, source_target_pairs={{0,16},{16,0},{1,17},{17,1},{2,18},{18,2},{3,19},{19,3},{4,20},{20... | collective-permute-start | bytes 1327112 | tf_op jit(solution)/shard_map/ppermute | solution.py:33
  184.5 17.4 %collective-permute-start.23 = (bf16[3,2,96,384]{3,2,0,1:T(8,128)(2,1)S(1)}, bf16[3,2,96,384]{3,2,0,1:T(8,128)(2,1)S(1)}, u32[]{:S(2)}, u32[]{:S(2)}) collective-permute-start(bf16[3,2,96,384]{3,2,0,1:T(8,128)(2,1)S(1)} %pad_maximum_fusion.29), channel_id=1, source_target_pairs={{0,8},{4,12},{8,0},{12,4},{1,9},{5,13},{9,1},{13,5},{2,10},{6,14},... | collective-permute-start | bytes 1327112 | tf_op jit(solution)/shard_map/ppermute | solution.py:33
  185.9 20.7 %collective-permute-start.37 = (bf16[3,2,96,384]{3,2,0,1:T(8,128)(2,1)S(1)}, bf16[3,2,96,384]{3,2,0,1:T(8,128)(2,1)S(1)}, u32[]{:S(2)}, u32[]{:S(2)}) collective-permute-start(bf16[3,2,96,384]{3,2,0,1:T(8,128)(2,1)S(1)} %pad_maximum_fusion.32), channel_id=1, source_target_pairs={{0,8},{4,12},{8,0},{12,4},{1,9},{5,13},{9,1},{13,5},{2,10},{6,14},... | collective-permute-start | bytes 1327112 | tf_op jit(solution)/shard_map/ppermute | solution.py:33
  191.7 16.8 %collective-permute-start.21 = (bf16[3,2,96,384]{3,2,0,1:T(8,128)(2,1)S(1)}, bf16[3,2,96,384]{3,2,0,1:T(8,128)(2,1)S(1)}, u32[]{:S(2)}, u32[]{:S(2)}) collective-permute-start(bf16[3,2,96,384]{3,2,0,1:T(8,128)(2,1)S(1)} %pad_maximum_fusion.28), channel_id=1, source_target_pairs={{0,16},{16,0},{1,17},{17,1},{2,18},{18,2},{3,19},{19,3},{4,20},{20... | collective-permute-start | bytes 1327112 | tf_op jit(solution)/shard_map/ppermute | solution.py:33
  193.0 17.7 %collective-permute-start.55 = (bf16[3,2,2,72,768]{4,3,2,1,0:T(8,128)(2,1)S(1)}, bf16[3,2,2,72,768]{4,3,2,1,0:T(8,128)(2,1)S(1)}, u32[]{:S(2)}, u32[]{:S(2)}) collective-permute-start(bf16[3,2,2,72,768]{4,3,2,1,0:T(8,128)(2,1)S(1)} %maximum_maximum_fusion.2), channel_id=1, source_target_pairs={{0,4},{4,0},{8,12},{12,8},{1,5},{5,1},{9,13},{13,9},{2,6},{6,2},{1... | collective-permute-start | bytes 3981320 | tf_op jit(solution)/shard_map/ppermute | solution.py:33
  208.6 19.9 %collective-permute-start.38 = (bf16[3,2,2,96,768]{4,3,0,1,2:T(8,128)(2,1)}, bf16[3,2,2,96,768]{4,3,0,1,2:T(8,128)(2,1)}, u32[]{:S(2)}, u32[]{:S(2)}) collective-permute-start(bf16[3,2,2,96,768]{4,3,0,1,2:T(8,128)(2,1)} %maximum_maximum_fusion.1), channel_id=1, source_target_pairs={{0,4},{4,0},{8,12},{12,8},{1,5},{5,1},{9,13},{13,9},{2,6},{6,2},{1... | collective-permute-start | bytes 5308424 | tf_op jit(solution)/shard_map/ppermute | solution.py:33
  210.1 21.4 %collective-permute-start.24 = (bf16[3,2,2,96,768]{4,3,0,1,2:T(8,128)(2,1)}, bf16[3,2,2,96,768]{4,3,0,1,2:T(8,128)(2,1)}, u32[]{:S(2)}, u32[]{:S(2)}) collective-permute-start(bf16[3,2,2,96,768]{4,3,0,1,2:T(8,128)(2,1)} %maximum_maximum_fusion), channel_id=1, source_target_pairs={{0,4},{4,0},{8,12},{12,8},{1,5},{5,1},{9,13},{13,9},{2,6},{6,2},{1... | collective-permute-start | bytes 5308424 | tf_op jit(solution)/shard_map/ppermute | solution.py:33
  337.3 16.6 %collective-permute-start.69 = (bf16[2,4,192,192]{3,2,0,1:T(8,128)(2,1)}, bf16[2,4,192,192]{3,2,0,1:T(8,128)(2,1)}, u32[]{:S(2)}, u32[]{:S(2)}) collective-permute-start(bf16[2,4,192,192]{3,2,0,1:T(8,128)(2,1)} %fusion.112), channel_id=1, source_target_pairs={{0,4},{4,0},{8,12},{12,8},{1,5},{5,1},{9,13},{13,9},{2,6},{6,2},{1... | collective-permute-start | bytes 1769480 | tf_op jit(solution)/shard_map/ppermute | solution.py:33
  343.8 118.4 %collective-permute-start.62 = (bf16[2,4,192,576]{3,2,0,1:T(8,128)(2,1)}, bf16[2,4,192,576]{3,2,0,1:T(8,128)(2,1)}, u32[]{:S(2)}, u32[]{:S(2)}) collective-permute-start(bf16[2,4,192,576]{3,2,0,1:T(8,128)(2,1)} %convert_bitcast_fusion.2), channel_id=1, source_target_pairs={{0,4},{4,0},{8,12},{12,8},{1,5},{5,1},{9,13},{13,9},{2,6},{6,2},{1... | collective-permute-start | bytes 5308424 | tf_op jit(solution)/shard_map/ppermute | solution.py:33
  348.4 45.9 %collective-permute-start.57 = (bf16[512,768]{1,0:T(8,128)(2,1)}, bf16[512,768]{1,0:T(8,128)(2,1)}, u32[]{:S(2)}, u32[]{:S(2)}) collective-permute-start(bf16[512,768]{1,0:T(8,128)(2,1)} %get-tuple-element.175), channel_id=1, source_target_pairs={{1,0},{2,1},{3,2},{5,4},{6,5},{7,6},{9,8},{10,9},{11,10},{13,12},{... | collective-permute-start | bytes 2359304 | tf_op jit(solution)/shard_map/ppermute | solution.py:44
  355.7 11.6 %collective-permute-start.70 = (bf16[4,192,192]{2,1,0:T(8,128)(2,1)S(1)}, bf16[4,192,192]{2,1,0:T(8,128)(2,1)S(1)}, u32[]{:S(2)}, u32[]{:S(2)}) collective-permute-start(bf16[4,192,192]{2,1,0:T(8,128)(2,1)S(1)} %fusion.135), channel_id=1, source_target_pairs={{0,8},{4,12},{8,0},{12,4},{1,9},{5,13},{9,1},{13,5},{2,10},{6,14},... | collective-permute-start | bytes 884744 | tf_op jit(solution)/shard_map/ppermute | solution.py:33
  379.6 7.7 %collective-permute-start.74 = (bf16[96,192]{1,0:T(8,128)(2,1)S(1)}, bf16[96,192]{1,0:T(8,128)(2,1)S(1)}, u32[]{:S(2)}, u32[]{:S(2)}) collective-permute-start(bf16[96,192]{1,0:T(8,128)(2,1)S(1)} %get-tuple-element.140), channel_id=1, source_target_pairs={{0,1},{1,2},{2,3},{3,0},{4,5},{5,6},{6,7},{7,4},{8,9},{9,10},{10,1... | collective-permute-start | bytes 110600 | tf_op jit(solution)/shard_map/ppermute | solution.py:71
  382.1 53.7 %collective-permute-start.56 = (bf16[512,768]{1,0:T(8,128)(2,1)}, bf16[512,768]{1,0:T(8,128)(2,1)}, u32[]{:S(2)}, u32[]{:S(2)}) collective-permute-start(bf16[512,768]{1,0:T(8,128)(2,1)} %get-tuple-element.175), channel_id=1, source_target_pairs={{0,1},{1,2},{2,3},{4,5},{5,6},{6,7},{8,9},{9,10},{10,11},{12,13},{... | collective-permute-start | bytes 2359304 | tf_op jit(solution)/shard_map/ppermute | solution.py:43
  387.3 98.0 %collective-permute-start.83 = (bf16[2,4,192,768]{3,2,1,0:T(8,128)(2,1)}, bf16[2,4,192,768]{3,2,1,0:T(8,128)(2,1)S(1)}, u32[]{:S(2)}, u32[]{:S(2)}) collective-permute-start(bf16[2,4,192,768]{3,2,1,0:T(8,128)(2,1)} %convert_bitcast_fusion), channel_id=1, source_target_pairs={{0,4},{4,0},{8,12},{12,8},{1,5},{5,1},{9,13},{13,9},{2,6},{6,2},{1... | collective-permute-start | bytes 7077896 | tf_op jit(solution)/shard_map/ppermute | solution.py:33
  387.3 51.4 %collective-permute-start.40 = (bf16[512,768]{1,0:T(8,128)(2,1)}, bf16[512,768]{1,0:T(8,128)(2,1)S(1)}, u32[]{:S(2)}, u32[]{:S(2)}) collective-permute-start(bf16[512,768]{1,0:T(8,128)(2,1)} %get-tuple-element.66), channel_id=1, source_target_pairs={{1,0},{2,1},{3,2},{5,4},{6,5},{7,6},{9,8},{10,9},{11,10},{13,12},{... | collective-permute-start | bytes 2359304 | tf_op jit(solution)/shard_map/ppermute | solution.py:44
  394.3 44.4 %collective-permute-start.75 = (bf16[96,192]{1,0:T(8,128)(2,1)S(1)}, bf16[96,192]{1,0:T(8,128)(2,1)S(1)}, u32[]{:S(2)}, u32[]{:S(2)}) collective-permute-start(bf16[96,192]{1,0:T(8,128)(2,1)S(1)} %get-tuple-element.55), channel_id=1, source_target_pairs={{0,16},{16,0},{1,17},{17,1},{2,18},{18,2},{3,19},{19,3},{4,20},{20... | collective-permute-start | bytes 110600 | tf_op jit(solution)/shard_map/ppermute | solution.py:33
  435.8 18.3 %collective-permute-start.39 = (bf16[512,768]{1,0:T(8,128)(2,1)}, bf16[512,768]{1,0:T(8,128)(2,1)}, u32[]{:S(2)}, u32[]{:S(2)}) collective-permute-start(bf16[512,768]{1,0:T(8,128)(2,1)} %get-tuple-element.66), channel_id=1, source_target_pairs={{0,1},{1,2},{2,3},{4,5},{5,6},{6,7},{8,9},{9,10},{10,11},{12,13},{... | collective-permute-start | bytes 2359304 | tf_op jit(solution)/shard_map/ppermute | solution.py:43
  438.7 49.0 %collective-permute-start.76 = (bf16[2,4,192,768]{3,2,0,1:T(8,128)(2,1)}, bf16[2,4,192,768]{3,2,0,1:T(8,128)(2,1)}, u32[]{:S(2)}, u32[]{:S(2)}) collective-permute-start(bf16[2,4,192,768]{3,2,0,1:T(8,128)(2,1)} %convert_bitcast_fusion.1), channel_id=1, source_target_pairs={{0,4},{4,0},{8,12},{12,8},{1,5},{5,1},{9,13},{13,9},{2,6},{6,2},{1... | collective-permute-start | bytes 7077896 | tf_op jit(solution)/shard_map/ppermute | solution.py:33
  438.7 22.2 %collective-permute-start.58 = (bf16[512,768]{1,0:T(8,128)(2,1)}, bf16[512,768]{1,0:T(8,128)(2,1)}, u32[]{:S(2)}, u32[]{:S(2)}) collective-permute-start(bf16[512,768]{1,0:T(8,128)(2,1)} %collective-permute-done.57), channel_id=1, source_target_pairs={{1,0},{2,1},{5,4},{6,5},{9,8},{10,9},{13,12},{14,13},{17,16},{18,1... | collective-permute-start | bytes 2359304 | tf_op jit(solution)/shard_map/ppermute | solution.py:47
  454.1 14.3 %collective-permute-start.60 = (bf16[512,768]{1,0:T(8,128)(2,1)}, bf16[512,768]{1,0:T(8,128)(2,1)}, u32[]{:S(2)}, u32[]{:S(2)}) collective-permute-start(bf16[512,768]{1,0:T(8,128)(2,1)} %collective-permute-done.56), channel_id=1, source_target_pairs={{1,2},{2,3},{5,6},{6,7},{9,10},{10,11},{13,14},{14,15},{17,18},{18... | collective-permute-start | bytes 2359304 | tf_op jit(solution)/shard_map/ppermute | solution.py:46
  460.8 22.4 %collective-permute-start.41 = (bf16[512,768]{1,0:T(8,128)(2,1)S(1)}, bf16[512,768]{1,0:T(8,128)(2,1)}, u32[]{:S(2)}, u32[]{:S(2)}) collective-permute-start(bf16[512,768]{1,0:T(8,128)(2,1)S(1)} %collective-permute-done.40), channel_id=1, source_target_pairs={{1,0},{2,1},{5,4},{6,5},{9,8},{10,9},{13,12},{14,13},{17,16},{18,1... | collective-permute-start | bytes 2359304 | tf_op jit(solution)/shard_map/ppermute | solution.py:47
  462.1 21.8 %collective-permute-start.43 = (bf16[512,768]{1,0:T(8,128)(2,1)}, bf16[512,768]{1,0:T(8,128)(2,1)}, u32[]{:S(2)}, u32[]{:S(2)}) collective-permute-start(bf16[512,768]{1,0:T(8,128)(2,1)} %collective-permute-done.39), channel_id=1, source_target_pairs={{1,2},{2,3},{5,6},{6,7},{9,10},{10,11},{13,14},{14,15},{17,18},{18... | collective-permute-start | bytes 2359304 | tf_op jit(solution)/shard_map/ppermute | solution.py:46
  468.4 31.6 %collective-permute-start.59 = (bf16[512,768]{1,0:T(8,128)(2,1)}, bf16[512,768]{1,0:T(8,128)(2,1)S(1)}, u32[]{:S(2)}, u32[]{:S(2)}) collective-permute-start(bf16[512,768]{1,0:T(8,128)(2,1)} %collective-permute-done.58), channel_id=1, source_target_pairs={{1,0},{5,4},{9,8},{13,12},{17,16},{21,20},{25,24},{29,28}} | collective-permute-start | bytes 2359304 | tf_op jit(solution)/shard_map/ppermute | solution.py:47
  483.3 39.4 %collective-permute-start.61 = (bf16[512,768]{1,0:T(8,128)(2,1)}, bf16[512,768]{1,0:T(8,128)(2,1)S(1)}, u32[]{:S(2)}, u32[]{:S(2)}) collective-permute-start(bf16[512,768]{1,0:T(8,128)(2,1)} %collective-permute-done.60), channel_id=1, source_target_pairs={{2,3},{6,7},{10,11},{14,15},{18,19},{22,23},{26,27},{30,31}} | collective-permute-start | bytes 2359304 | tf_op jit(solution)/shard_map/ppermute | solution.py:46
  484.0 31.6 %collective-permute-start.42 = (bf16[512,768]{1,0:T(8,128)(2,1)}, bf16[512,768]{1,0:T(8,128)(2,1)S(1)}, u32[]{:S(2)}, u32[]{:S(2)}) collective-permute-start(bf16[512,768]{1,0:T(8,128)(2,1)} %collective-permute-done.41), channel_id=1, source_target_pairs={{1,0},{5,4},{9,8},{13,12},{17,16},{21,20},{25,24},{29,28}} | collective-permute-start | bytes 2359304 | tf_op jit(solution)/shard_map/ppermute | solution.py:47
  485.3 51.4 %collective-permute-start.44 = (bf16[512,768]{1,0:T(8,128)(2,1)}, bf16[512,768]{1,0:T(8,128)(2,1)S(1)}, u32[]{:S(2)}, u32[]{:S(2)}) collective-permute-start(bf16[512,768]{1,0:T(8,128)(2,1)} %collective-permute-done.43), channel_id=1, source_target_pairs={{2,3},{6,7},{10,11},{14,15},{18,19},{22,23},{26,27},{30,31}} | collective-permute-start | bytes 2359304 | tf_op jit(solution)/shard_map/ppermute | solution.py:46
  487.7 31.2 %collective-permute-start.63 = (bf16[4,192,576]{2,1,0:T(8,128)(2,1)S(1)}, bf16[4,192,576]{2,1,0:T(8,128)(2,1)S(1)}, u32[]{:S(2)}, u32[]{:S(2)}) collective-permute-start(bf16[4,192,576]{2,1,0:T(8,128)(2,1)S(1)} %fusion.115), channel_id=1, source_target_pairs={{0,8},{4,12},{8,0},{12,4},{1,9},{5,13},{9,1},{13,5},{2,10},{6,14},... | collective-permute-start | bytes 2654216 | tf_op jit(solution)/shard_map/ppermute | solution.py:33
  500.0 46.0 %collective-permute-start.84 = (bf16[4,192,768]{2,1,0:T(8,128)(2,1)S(1)}, bf16[4,192,768]{2,1,0:T(8,128)(2,1)S(1)}, u32[]{:S(2)}, u32[]{:S(2)}) collective-permute-start(bf16[4,192,768]{2,1,0:T(8,128)(2,1)S(1)} %fusion.114), channel_id=1, source_target_pairs={{0,8},{4,12},{8,0},{12,4},{1,9},{5,13},{9,1},{13,5},{2,10},{6,14},... | collective-permute-start | bytes 3538952 | tf_op jit(solution)/shard_map/ppermute | solution.py:33
  515.6 44.3 %collective-permute-start.77 = (bf16[4,192,768]{2,1,0:T(8,128)(2,1)S(1)}, bf16[4,192,768]{2,1,0:T(8,128)(2,1)S(1)}, u32[]{:S(2)}, u32[]{:S(2)}) collective-permute-start(bf16[4,192,768]{2,1,0:T(8,128)(2,1)S(1)} %fusion.113), channel_id=1, source_target_pairs={{0,8},{4,12},{8,0},{12,4},{1,9},{5,13},{9,1},{13,5},{2,10},{6,14},... | collective-permute-start | bytes 3538952 | tf_op jit(solution)/shard_map/ppermute | solution.py:33
  519.1 11.7 %collective-permute-start.64 = (bf16[4,96,576]{2,1,0:T(8,128)(2,1)S(1)}, bf16[4,96,576]{2,1,0:T(8,128)(2,1)S(1)}, u32[]{:S(2)}, u32[]{:S(2)}) collective-permute-start(bf16[4,96,576]{2,1,0:T(8,128)(2,1)S(1)} %slice.553), channel_id=1, source_target_pairs={{0,16},{16,0},{1,17},{17,1},{2,18},{18,2},{3,19},{19,3},{4,20},{20... | collective-permute-start | bytes 1327112 | tf_op jit(solution)/shard_map/ppermute | solution.py:33
  531.0 12.0 %collective-permute-start.65 = (bf16[96,576]{1,0:T(8,128)(2,1)S(1)}, bf16[96,576]{1,0:T(8,128)(2,1)S(1)}, u32[]{:S(2)}, u32[]{:S(2)}) collective-permute-start(bf16[96,576]{1,0:T(8,128)(2,1)S(1)} %get-tuple-element.114), channel_id=1, source_target_pairs={{0,3},{1,0},{2,1},{3,2},{4,7},{5,4},{6,5},{7,6},{8,11},{9,8},{10,9... | collective-permute-start | bytes 331784 | tf_op jit(solution)/shard_map/ppermute | solution.py:71
  535.4 8.4 %collective-permute-start.66 = (bf16[96,576]{1,0:T(8,128)(2,1)S(1)}, bf16[96,576]{1,0:T(8,128)(2,1)S(1)}, u32[]{:S(2)}, u32[]{:S(2)}) collective-permute-start(bf16[96,576]{1,0:T(8,128)(2,1)S(1)} %get-tuple-element.116), channel_id=1, source_target_pairs={{0,2},{1,3},{2,0},{3,1},{4,6},{5,7},{6,4},{7,5},{8,10},{9,11},{10,... | collective-permute-start | bytes 331784 | tf_op jit(solution)/shard_map/ppermute | solution.py:71
  547.2 17.4 %collective-permute-start.85 = (bf16[4,96,768]{2,1,0:T(8,128)(2,1)}, bf16[4,96,768]{2,1,0:T(8,128)(2,1)}, u32[]{:S(2)}, u32[]{:S(2)}) collective-permute-start(bf16[4,96,768]{2,1,0:T(8,128)(2,1)} %slice.551), channel_id=1, source_target_pairs={{0,16},{16,0},{1,17},{17,1},{2,18},{18,2},{3,19},{19,3},{4,20},{20... | collective-permute-start | bytes 1769480 | tf_op jit(solution)/shard_map/ppermute | solution.py:33
  561.1 17.9 %collective-permute-start.78 = (bf16[4,96,768]{2,1,0:T(8,128)(2,1)}, bf16[4,96,768]{2,1,0:T(8,128)(2,1)}, u32[]{:S(2)}, u32[]{:S(2)}) collective-permute-start(bf16[4,96,768]{2,1,0:T(8,128)(2,1)} %slice.552), channel_id=1, source_target_pairs={{0,16},{16,0},{1,17},{17,1},{2,18},{18,2},{3,19},{19,3},{4,20},{20... | collective-permute-start | bytes 1769480 | tf_op jit(solution)/shard_map/ppermute | solution.py:33
  566.3 17.2 %collective-permute-start.86 = (bf16[96,768]{1,0:T(8,128)(2,1)S(1)}, bf16[96,768]{1,0:T(8,128)(2,1)S(1)}, u32[]{:S(2)}, u32[]{:S(2)}) collective-permute-start(bf16[96,768]{1,0:T(8,128)(2,1)S(1)} %get-tuple-element.104), channel_id=1, source_target_pairs={{0,3},{1,0},{2,1},{3,2},{4,7},{5,4},{6,5},{7,6},{8,11},{9,8},{10,9... | collective-permute-start | bytes 442376 | tf_op jit(solution)/shard_map/ppermute | solution.py:71
  576.0 17.9 %collective-permute-start.87 = (bf16[96,768]{1,0:T(8,128)(2,1)S(1)}, bf16[96,768]{1,0:T(8,128)(2,1)S(1)}, u32[]{:S(2)}, u32[]{:S(2)}) collective-permute-start(bf16[96,768]{1,0:T(8,128)(2,1)S(1)} %get-tuple-element.106), channel_id=1, source_target_pairs={{0,2},{1,3},{2,0},{3,1},{4,6},{5,7},{6,4},{7,5},{8,10},{9,11},{10,... | collective-permute-start | bytes 442376 | tf_op jit(solution)/shard_map/ppermute | solution.py:71
  577.1 16.9 %collective-permute-start.88 = (bf16[96,768]{1,0:T(8,128)(2,1)S(1)}, bf16[96,768]{1,0:T(8,128)(2,1)S(1)}, u32[]{:S(2)}, u32[]{:S(2)}) collective-permute-start(bf16[96,768]{1,0:T(8,128)(2,1)S(1)} %get-tuple-element.105), channel_id=1, source_target_pairs={{0,1},{1,2},{2,3},{3,0},{4,5},{5,6},{6,7},{7,4},{8,9},{9,10},{10,1... | collective-permute-start | bytes 442376 | tf_op jit(solution)/shard_map/ppermute | solution.py:71
  580.3 13.9 %collective-permute-start.79 = (bf16[96,768]{1,0:T(8,128)(2,1)S(1)}, bf16[96,768]{1,0:T(8,128)(2,1)S(1)}, u32[]{:S(2)}, u32[]{:S(2)}) collective-permute-start(bf16[96,768]{1,0:T(8,128)(2,1)S(1)} %get-tuple-element.107), channel_id=1, source_target_pairs={{0,3},{1,0},{2,1},{3,2},{4,7},{5,4},{6,5},{7,6},{8,11},{9,8},{10,9... | collective-permute-start | bytes 442376 | tf_op jit(solution)/shard_map/ppermute | solution.py:71
  582.5 15.0 %collective-permute-start.80 = (bf16[96,768]{1,0:T(8,128)(2,1)S(1)}, bf16[96,768]{1,0:T(8,128)(2,1)S(1)}, u32[]{:S(2)}, u32[]{:S(2)}) collective-permute-start(bf16[96,768]{1,0:T(8,128)(2,1)S(1)} %get-tuple-element.109), channel_id=1, source_target_pairs={{0,2},{1,3},{2,0},{3,1},{4,6},{5,7},{6,4},{7,5},{8,10},{9,11},{10,... | collective-permute-start | bytes 442376 | tf_op jit(solution)/shard_map/ppermute | solution.py:71
  583.5 14.0 %collective-permute-start.81 = (bf16[96,768]{1,0:T(8,128)(2,1)S(1)}, bf16[96,768]{1,0:T(8,128)(2,1)S(1)}, u32[]{:S(2)}, u32[]{:S(2)}) collective-permute-start(bf16[96,768]{1,0:T(8,128)(2,1)S(1)} %get-tuple-element.108), channel_id=1, source_target_pairs={{0,1},{1,2},{2,3},{3,0},{4,5},{5,6},{6,7},{7,4},{8,9},{9,10},{10,1... | collective-permute-start | bytes 442376 | tf_op jit(solution)/shard_map/ppermute | solution.py:71
  (100 other events, 702.6 us)

commit v2 on v1

v2 whole, which is shorter than its diff:
```python
import functools
import math

import jax
import jax.numpy as jnp
from jax import lax
from jax.experimental import pallas as pl
from jax.experimental.pallas import tpu as pltpu
from jax.sharding import PartitionSpec as P

EPSILON = 1e-12
MASKED = -1e30
BF = jnp.bfloat16
F32 = jnp.float32
SHORT = pl.CostEstimate(flops=1000, bytes_accessed=1000, transcendentals=0)
ROWS_BY_ROWS = (((1,), (1,)), ((), ()))


def dot(left, right):
    return jnp.dot(left, right, preferred_element_type=F32)


def dot_t(left, right):
    return lax.dot_general(left, right, ROWS_BY_ROWS, preferred_element_type=F32)


def normalize(values):
    centre = values - jnp.mean(values, axis=-1, keepdims=True)
    variance = jnp.mean(centre * centre, axis=-1, keepdims=True)
    recip = lax.rsqrt(variance + EPSILON)
    return (centre * recip, recip)


def norm_back(grad_norm, normed, recip):
    first = jnp.mean(grad_norm, axis=-1, keepdims=True)
    second = jnp.mean(grad_norm * normed, axis=-1, keepdims=True)
    return recip * (grad_norm - first - normed * second)


def col_sum(value):
    return jnp.sum(value, axis=0, keepdims=True)


def softmax_columns(raw, allowed):
    scores = jnp.where(allowed, raw, MASKED)
    grown = jnp.exp(scores - jnp.max(scores, axis=0, keepdims=True))
    return grown, 1.0 / jnp.sum(grown, axis=0, keepdims=True)


def column(row):
    return jnp.broadcast_to(row, (8, row.shape[1])).T[:, :1]


def store_relative(out_ref, value, at_ref):
    flipped = value.T.astype(BF)
    block = flipped.shape[0] // 8
    for i in range(8):
        spot = (((i >> 1) & 1) ^ at_ref[0]) * 4 + ((i >> 2) ^ at_ref[1]) * 2 + ((i & 1) ^ at_ref[2])
        out_ref[pl.ds(pl.multiple_of(spot * block, block), block)] = flipped[i * block : (i + 1) * block]


def call(kernel, name, at, grid, in_specs, out_specs, out_shape, scratch=()):
    return pl.pallas_call(
        kernel,
        grid_spec=pltpu.PrefetchScalarGridSpec(
            num_scalar_prefetch=1, grid=grid, in_specs=in_specs, out_specs=out_specs, scratch_shapes=list(scratch)
        ),
        out_shape=out_shape,
        cost_estimate=SHORT,
        name=name,
    )


def const(*shape):
    return pl.BlockSpec(shape, lambda i, at: (0,) * len(shape))


def slot(*shape):
    return pl.BlockSpec((1, *shape), lambda i, at: (i,) + (0,) * len(shape))


def attend_kernel(heads, scale, at_ref, x_ref, w_ref, bias_ref, seg_ref, extra_ref, *out_refs):
    x = x_ref[0]
    size = w_ref.shape[1] // heads
    q_t = ((dot_t(w_ref[0], x) + column(bias_ref[0:1])).astype(BF) * scale).astype(BF)
    k = dot_t(x, w_ref[1]).astype(BF)
    v_t = (dot_t(w_ref[2], x) + column(bias_ref[1:2])).astype(BF)
    row = seg_ref[pl.ds(pl.program_id(0), 1)].astype(F32)
    allowed = column(row) == row
    parts = []
    for h in range(heads):
        at = slice(h * size, (h + 1) * size)
        grown, inv = softmax_columns(dot(k[:, at], q_t[at]), allowed)
        parts.append(dot(v_t[at], grown.astype(BF)) * inv)
    context = jnp.concatenate(parts, 0).T.astype(BF)
    count = len(out_refs)
    ahead = lax.rem(pl.program_id(0) + count - at_ref[3], count)
    for s, out_ref in enumerate(out_refs):
        @pl.when(ahead == s)
        def _():
            out_ref[: context.shape[0]] = context
            out_ref[context.shape[0] :] = extra_ref[...]


def attend(at, tokens, w_rows, bias, segments, heads, extra):
    seqs, length, width = tokens.shape
    cols = w_rows.shape[1]
    return call(
        functools.partial(attend_kernel, heads, (cols // heads) ** -0.5), "attend", at, (seqs,),
        [slot(length, width), const(3, cols, width), const(2, cols), const(seqs, length), const(*extra.shape)],
        [const(length + extra.shape[0], cols)] * seqs,
        [jax.ShapeDtypeStruct((length + extra.shape[0], cols), BF)] * seqs,
    )(at, tokens, w_rows, bias, segments, extra)


def fetch_copies(core, own_ref, mine_ref, theirs_ref, held, sems):
    slots = held.shape[0]
    copies = [[pltpu.make_async_copy(own_ref.at[c], held.at[0, c], sems.at[0, c]) for c in range(2)]]
    for s in range(1, slots):
        copies.append([
            pltpu.make_async_copy(mine_ref.at[:, s - 1], held.at[s, core], sems.at[s, 0]),
            pltpu.make_async_copy(theirs_ref.at[:, s - 1], held.at[s, 1 - core], sems.at[s, 1]),
        ])
    return copies


def fetch_slot(at_ref, refs, held, sems):
    step = pl.program_id(0)
    copies = fetch_copies(at_ref[0], *refs, held, sems)

    @pl.when(step == 0)
    def _():
        for pair in copies:
            for copy in pair:
                copy.start()

    for s, pair in enumerate(copies):
        @pl.when(step == s)
        def _():
            for copy in pair:
                copy.wait()

    return held[step].reshape(8 * held.shape[3], held.shape[4])


def pieces(weight):
    own, mine, theirs = weight
    piece = own.shape[0] // 8
    split = lambda v: v.reshape(4, -1, piece, own.shape[1])
    return own.reshape(2, 4, piece, own.shape[1]), split(mine), split(theirs)


def held_scratch(slots, weight):
    rows, width = weight[0].shape
    return [pltpu.VMEM((slots, 2, 4, rows // 8, width), BF), pltpu.SemaphoreType.DMA((slots, 2))]


def here(*shape):
    return pl.BlockSpec((1, *shape), lambda i, at: (at[3],) + (0,) * len(shape))


FAR = pl.BlockSpec(memory_space=pl.ANY)


def rise_kernel(slots, at_ref, *refs):
    ctx_refs = refs[:slots]
    (w_out_ref, x_ref, gains_ref, shifts_ref, own_ref, mine_ref, theirs_ref, bias_ref,
     hidden_ref, low_ref, norm_ref, recip_ref, act_ref, slope_ref, x_rel_ref, hidden_rel_ref, held, sems) = refs[slots:]
    step = pl.program_id(0)
    weight = fetch_slot(at_ref, (own_ref, mine_ref, theirs_ref), held, sems)

    @pl.when(step == 0)
    def _():
        rows = low_ref.shape[0]
        attention = dot(ctx_refs[0][:rows], w_out_ref[0])
        for s in range(1, slots):
            attention += dot(ctx_refs[s][:rows], w_out_ref[s])
        own = x_ref[0].astype(F32)
        norm, recip = normalize(own + attention + shifts_ref[0:1])
        hidden = norm * gains_ref[0:1] + shifts_ref[1:2]
        norm_ref[...] = norm
        recip_ref[...] = recip
        hidden_ref[...] = hidden
        low_ref[...] = hidden.astype(BF)
        store_relative(x_rel_ref, own, at_ref)
        store_relative(hidden_rel_ref, hidden, at_ref)

    pre = dot(low_ref[...], weight) + bias_ref[0]
    cumul = 0.5 * (1.0 + lax.erf(pre * (1.0 / math.sqrt(2.0))))
    act_ref[0] = (pre * cumul).astype(BF)
    slope_ref[0] = (cumul + pre * jnp.exp(-0.5 * pre * pre) * (1.0 / math.sqrt(2.0 * math.pi))).astype(BF)


def rise(at, ctx, w_out, x, gains, shifts, w_in, bias):
    slots, cols, rows = len(ctx), ctx[0].shape[1], x.shape[1]
    width, hidden = w_in[0].shape
    return call(
        functools.partial(rise_kernel, slots), "rise", at, (slots,),
        [const(*ctx[0].shape)] * slots
        + [
            const(slots, cols, width), here(rows, width), const(*gains.shape),
            const(*shifts.shape), FAR, FAR, FAR, slot(1, hidden),
        ],
        [
            const(rows, width), const(rows, width), const(rows, width), const(rows, 1),
            slot(rows, hidden), slot(rows, hidden), const(width, rows), const(width, rows),
        ],
        [
            jax.ShapeDtypeStruct((rows, width), F32),
            jax.ShapeDtypeStruct((rows, width), BF),
            jax.ShapeDtypeStruct((rows, width), F32),
            jax.ShapeDtypeStruct((rows, 1), F32),
            jax.ShapeDtypeStruct((slots, rows, hidden), BF),
            jax.ShapeDtypeStruct((slots, rows, hidden), BF),
            jax.ShapeDtypeStruct((width, rows), BF),
            jax.ShapeDtypeStruct((width, rows), BF),
        ],
        held_scratch(slots, w_in),
    )(at, *ctx, w_out, x, gains, shifts, *pieces(w_in), bias[:, None, :])


def store_parts(keep_ref, send_ref, x_first, first, whole):
    block, last = keep_ref.shape[2], first + whole.shape[1]
    low = whole.astype(BF)
    for i in range(4):
        spot = jnp.where(x_first, i, 3 - i) if i in (1, 2) else i
        keep_ref[spot, 0, :, first:last] = low[i * block : (i + 1) * block]
        send_ref[spot, 0, :, first:last] = low[(4 + i) * block : (5 + i) * block]


def fall_kernel(slots, at_ref, act_ref, own_ref, mine_ref, theirs_ref, hidden_ref, cot_ref, gains_ref, shifts_ref,
                out_ref, grad_ref, low_ref, vec_ref, keep_ref, send_ref, sum_ref, rel_ref, held, sems):
    s = pl.program_id(0)
    copies = fetch_copies(at_ref[0], own_ref, mine_ref, theirs_ref, held, sems)

    @pl.when(s == 0)
    def _():
        for pair in copies:
            for copy in pair:
                copy.start()

    for i, pair in enumerate(copies):
        @pl.when(s == i)
        def _():
            for copy in pair:
                copy.wait()
            share = dot(act_ref[0], held[i].reshape(8 * held.shape[3], held.shape[4]))
            if i:
                sum_ref[...] += share
            else:
                sum_ref[...] = share

    @pl.when(s == slots - 1)
    def _():
        norm, recip = normalize(hidden_ref[...] + sum_ref[...] + shifts_ref[2:3])
        out_ref[...] = (norm * gains_ref[1:2] + shifts_ref[3:4]).astype(BF)
        cot = cot_ref[0].astype(F32)
        grad = norm_back(cot * gains_ref[1:2], norm, recip)
        grad_ref[...] = grad
        low_ref[...] = grad.astype(BF)
        store_relative(rel_ref, grad, at_ref)
        vec_ref[0:1] = col_sum(cot * norm)
        vec_ref[1:2] = col_sum(grad)
        vec_ref[2:3] = col_sum(cot)

    @pl.when(s >= slots)
    def _():
        store_parts(keep_ref, send_ref, s - slots < slots // 2, 0, dot(rel_ref[...], act_ref[0]))


def part_specs(slots, block, cols, start=0):
    spec = pl.BlockSpec((4, 1, block, cols), lambda i, at: (0, lax.max(i - start, 0), 0, 0))
    return [spec] * 2, [jax.ShapeDtypeStruct((4, slots, block, cols), BF)] * 2


def fall(at, act, w_down, hidden, cot, gains, shifts):
    slots, rows, inner = act.shape
    width = w_down[0].shape[1]
    specs, shapes = part_specs(slots, width // 8, inner, slots)
    return call(
        functools.partial(fall_kernel, slots), "fall", at, (2 * slots,),
        [
            pl.BlockSpec((1, rows, inner), lambda i, at: (lax.rem(i, slots), 0, 0)), FAR, FAR, FAR, const(rows, width),
            here(rows, width), const(*gains.shape), const(*shifts.shape),
        ],
        [const(rows, width), const(rows, width), const(rows, width), const(3, width), *specs],
        [
            jax.ShapeDtypeStruct((rows, width), BF),
            jax.ShapeDtypeStruct((rows, width), F32),
            jax.ShapeDtypeStruct((rows, width), BF),
            jax.ShapeDtypeStruct((3, width), F32),
            *shapes,
        ],
        [pltpu.VMEM((rows, width), F32), pltpu.VMEM((width, rows), BF)] + held_scratch(slots, w_down),
    )(at, act, *pieces(w_down), hidden, cot, gains, shifts)


def back_kernel(slots, at_ref, grad2_ref, low2_ref, own2_ref, mine2_ref, theirs2_ref, slope_ref, own1_ref, mine1_ref,
                theirs1_ref, norm_ref, recip_ref, gains_ref, hidden_rel_ref, bias_ref, grad_ref, low_ref, rel_ref, vec_ref,
                keep_ref, send_ref, sum_ref, held2, sems2, held1, sems1):
    s = pl.program_id(0)
    w_down = fetch_slot(at_ref, (own2_ref, mine2_ref, theirs2_ref), held2, sems2)
    w_in = fetch_slot(at_ref, (own1_ref, mine1_ref, theirs1_ref), held1, sems1)
    pre = dot_t(low2_ref[...], w_down) * slope_ref[0].astype(F32)
    bias_ref[0] = col_sum(pre)
    pre_low = pre.astype(BF)
    store_parts(keep_ref, send_ref, s < slots // 2, 0, dot(hidden_rel_ref[...], pre_low))
    share = dot_t(pre_low, w_in)

    @pl.when(s == 0)
    def _():
        sum_ref[...] = share

    @pl.when(s > 0)
    def _():
        sum_ref[...] += share

    @pl.when(s == slots - 1)
    def _():
        norm = norm_ref[...]
        grad_h = grad2_ref[...] + sum_ref[...]
        grad = norm_back(grad_h * gains_ref[0:1], norm, recip_ref[...])
        grad_ref[...] = grad
        low_ref[...] = grad.astype(BF)
        store_relative(rel_ref, grad, at_ref)
        vec_ref[0:1] = col_sum(grad_h * norm)
        vec_ref[1:2] = col_sum(grad)
        vec_ref[2:3] = col_sum(grad_h)


def back(at, grad2, low2, w_down, slope, w_in, norm, recip, gains, hidden_rel):
    slots, rows, inner = slope.shape
    width = grad2.shape[1]
    specs, shapes = part_specs(slots, width // 8, inner)
    return call(
        functools.partial(back_kernel, slots), "back", at, (slots,),
        [
            const(rows, width), const(rows, width), FAR, FAR, FAR, slot(rows, inner), FAR, FAR, FAR,
            const(rows, width), const(rows, 1), const(*gains.shape), const(width, rows),
        ],
        [slot(1, inner), const(rows, width), const(rows, width), const(width, rows), const(3, width), *specs],
        [
            jax.ShapeDtypeStruct((slots, 1, inner), F32),
            jax.ShapeDtypeStruct((rows, width), F32),
            jax.ShapeDtypeStruct((rows, width), BF),
            jax.ShapeDtypeStruct((width, rows), BF),
            jax.ShapeDtypeStruct((3, width), F32),
            *shapes,
        ],
        [pltpu.VMEM((rows, width), F32)] + held_scratch(slots, w_down) + held_scratch(slots, w_in),
    )(at, grad2, low2, *pieces(w_down), slope, *pieces(w_in), norm, recip, gains, hidden_rel)


def attend_back_kernel(first, slots, heads, scale, at_ref, x_ref, low_ref, grad_ref, *refs):
    ctx_refs = refs[:slots]
    (own_ref, mine_ref, theirs_ref, bias_ref, w_out_ref, seg_ref, x_rel_ref, grad_rel_ref,
     vec_ref, tok_ref, keep_ref, send_ref, sum_ref, q_ref, k_ref, v_ref, proj_ref, held, sems) = refs[slots:]
    s = pl.program_id(0)
    half = mine_ref.shape[-1]
    mine_at = pl.ds(pl.multiple_of(at_ref[0] * half, half), half)
    theirs_at = pl.ds(pl.multiple_of((1 - at_ref[0]) * half, half), half)
    copies = []
    for i in range(slots):
        if first + i == 0:
            copies.append([
                pltpu.make_async_copy(own_ref.at[:2], held.at[i, :2], sems.at[i, 0]),
                pltpu.make_async_copy(own_ref.at[2:], held.at[i, 2:], sems.at[i, 1]),
            ])
        else:
            copies.append([
                pltpu.make_async_copy(mine_ref.at[:, first + i - 1], held.at[i, :, :, mine_at], sems.at[i, 0]),
                pltpu.make_async_copy(theirs_ref.at[:, first + i - 1], held.at[i, :, :, theirs_at], sems.at[i, 1]),
            ])

    @pl.when(s == 0)
    def _():
        for pair in copies:
            for copy in pair:
                copy.start()

    for i, pair in enumerate(copies):
        @pl.when(s == i)
        def _():
            for copy in pair:
                copy.wait()
            store_parts(
                keep_ref, send_ref, i < slots // 2, proj_ref.shape[1], dot(grad_rel_ref[...], ctx_refs[i][: x_ref.shape[1]])
            )

    x, low = x_ref[0], low_ref[...]
    cols = w_out_ref.shape[1]
    size = cols // heads
    weight = held[s].reshape(3, cols, x.shape[1])
    q_t = (dot_t(weight[0], x) + column(bias_ref[0, 0:1])).astype(BF)
    q_scaled = (q_t * scale).astype(BF)
    q = q_t.T
    k_t = dot_t(weight[1], x).astype(BF)
    k = k_t.T
    v = (dot_t(x, weight[2]) + bias_ref[0, 1:2]).astype(BF)
    gc_t = dot_t(w_out_ref[0], low).astype(BF)
    gc = gc_t.T
    row = seg_ref[pl.ds(at_ref[3], 1)].astype(F32)
    allowed = column(row) == row
    for h in range(heads):
        at = slice(h * size, (h + 1) * size)
        grown, inv = softmax_columns(dot(k[:, at], q_scaled[at]), allowed)
        probs = grown * inv
        grad_probs = dot(v[:, at], gc_t[at])
        inner = jnp.sum(probs * grad_probs, axis=0, keepdims=True)
        grad_scores = (probs * (grad_probs - inner) * scale).astype(BF)
        q_ref[at] = dot(k_t[at], grad_scores)
        k_ref[:, at] = dot(grad_scores, q[:, at])
        v_ref[:, at] = dot(probs.astype(BF), gc[:, at])
    grad_q = q_ref[...].T
    grad_v = v_ref[...]
    vec_ref[0, 0:1] = col_sum(grad_q)
    vec_ref[0, 1:2] = col_sum(grad_v)
    parts = [grad_q.astype(BF), k_ref[...].astype(BF), grad_v.astype(BF)]
    for c in range(3):
        proj_ref[:, c * cols : (c + 1) * cols] = parts[c]
    proj = proj_ref[...]
    share = dot(proj, weight.reshape(3 * cols, x.shape[1]))
    store_parts(keep_ref, send_ref, s < slots // 2, 0, dot(x_rel_ref[...], proj))

    @pl.when(s == 0)
    def _():
        sum_ref[...] = share + grad_ref[...]

    @pl.when(s > 0)
    def _():
        sum_ref[...] += share

    @pl.when(s == slots - 1)
    def _():
        tok_ref[...] = sum_ref[...].astype(tok_ref.dtype)


def attend_back(at, first, x, low, grad, ctx, w_qkv, bias, heads, w_out, segments, x_rel, grad_rel, kind):
    slots, cols = len(ctx), w_out.shape[1]
    rows, width = x.shape[1:]
    own, mine, theirs = w_qkv
    piece, half = mine.shape[-2:]
    split = lambda v: v.reshape(4, -1, piece, half)
    later = lambda *shape: pl.BlockSpec((1, *shape), lambda i, at: (i + first,) + (0,) * len(shape))
    specs, shapes = part_specs(slots, width // 8, 4 * cols)
    return call(
        functools.partial(attend_back_kernel, first, slots, heads, (cols // heads) ** -0.5), "attend_back", at, (slots,),
        [here(rows, width), const(rows, width), const(rows, width)]
        + [const(*ctx[0].shape)] * slots
        + [
            FAR, FAR, FAR, later(2, cols), later(cols, width), const(*segments.shape), const(width, rows), const(width, rows),
        ],
        [slot(2, cols), const(rows, width), *specs],
        [
            jax.ShapeDtypeStruct((slots, 2, cols), F32),
            jax.ShapeDtypeStruct((rows, width), kind),
            *shapes,
        ],
        [
            pltpu.VMEM((rows, width), F32), pltpu.VMEM((cols, rows), F32), pltpu.VMEM((rows, cols), F32),
            pltpu.VMEM((rows, cols), F32), pltpu.VMEM((rows, 3 * cols), BF),
            pltpu.VMEM((slots, 4, piece, width), BF), pltpu.SemaphoreType.DMA((slots, 2)),
        ],
    )(at, x, low, grad, *ctx, own.reshape(4, piece, width), split(mine), split(theirs), bias, w_out, segments, x_rel, grad_rel)


def place_kernel(slots, at_ref, *refs):
    sources, (out_ref, held, sems) = refs[:-3], refs[-3:]
    here = at_ref[3]

    def each(step, act):
        for s in range(slots):
            for source, wanted in ((s, here - step == s),) + (((slots - 1 + s, step - here == s),) if s else ()):
                @pl.when(wanted)
                def _():
                    act(pltpu.make_async_copy(sources[source], held.at[step], sems.at[step]))

    step = pl.program_id(0)

    @pl.when(step == 0)
    def _():
        for j in range(slots):
            each(j, lambda copy: copy.start())

    pltpu.make_async_copy(sources[0], held.at[step], sems.at[step]).wait()
    out_ref[0] = held[step].astype(out_ref.dtype)


def place(at, own, behind, ahead, kind):
    slots = len(behind) + 1
    values = [own, *behind, *ahead]
    return call(
        functools.partial(place_kernel, slots), "place", at, (slots,),
        [FAR] * len(values), slot(*own.shape),
        jax.ShapeDtypeStruct((slots, *own.shape), kind),
        [pltpu.VMEM((slots, *own.shape), own.dtype), pltpu.SemaphoreType.DMA((slots,))],
    )(at, *values)


def swap(value, axis, size, bit):
    return lax.ppermute(value, axis, [(i, i ^ bit) for i in range(size)])


def ordered(own, got, bit, axis):
    first = jnp.where(bit == 0, own, got)
    second = jnp.where(bit == 0, got, own)
    return jnp.stack([first, second], axis)


def in_three(value):
    high = value.astype(BF)
    rest = value - high.astype(F32)
    middle = rest.astype(BF)
    return jnp.stack([high, middle, (rest - middle.astype(F32)).astype(BF)])


class Order:
    def __init__(self):
        self.last = ()

    def hold(self, values, *waits):
        leaves, tree = jax.tree.flatten(values)
        held = lax.optimization_barrier((leaves, self.last, waits))[0]
        return jax.tree.unflatten(tree, held)

    def done(self, *values):
        self.last = tuple(values)

    def run(self, made, *waits):
        self.last = waits
        made = self.hold(made)
        self.last = tuple(jax.tree.leaves(made)[:1])
        return made


def make(sizes):
    n_outer, n_local, n_tensor = sizes["outer"], sizes["local"], sizes["tensor"]

    def local(tokens, segments, w_qkv, b_qv, w_out, w_in, b_inner, w_down, gains, shifts, cotangent):
        seq_count, seq_len, width = tokens.shape
        heads, head_size = b_qv.shape[1], b_qv.shape[2]
        head_cols = heads * head_size
        hidden_cols = w_in.shape[1]
        z = lax.axis_index("tensor")
        l_index = lax.axis_index("local")
        core, x = l_index & 1, l_index >> 1
        y = lax.axis_index("outer") & 1
        z_from = lambda s: jnp.mod(z - s, n_tensor)
        z_to = lambda s: jnp.mod(z + s, n_tensor)
        cyclic = lambda v, s: lax.ppermute(v, "tensor", [(i, (i + s) % n_tensor) for i in range(n_tensor)])
        pick = lambda v, i: lax.dynamic_index_in_dim(v, i, 0, keepdims=False)
        others = range(1, n_tensor)
        by_x = lambda v: swap(v, "local", n_local, 2)
        by_y = lambda v: swap(v, "outer", n_outer, 1)
        by_core = lambda v: swap(v, "local", n_local, 1)
        at = jnp.stack([core, x, y, z]).astype(jnp.int32)
        order = Order()
        hold, done, run = order.hold, order.done, order.run

        place8 = core * 4 + y * 2 + x
        half = width // 2

        def piece_of(weight):
            n = weight.shape[0] // 8
            return lax.dynamic_slice_in_dim(weight, place8 * n, n, 0)

        def halves(parts, rows):
            return jnp.stack([p[rows, :half] for p in parts]), jnp.stack([p[rows, half:] for p in parts])

        def plane_two(a, b, a1, b1):
            return ordered(a, a1, x, 0), ordered(b, b1, y, 0)

        def plane_three(a, b, a1, b1, rows):
            a, a1, b, b1 = (v[:, :, rows] for v in (a, a1, b, b1))
            return jnp.concatenate([ordered(a, a1, y, 0), ordered(b, b1, x, 1)], -1)

        qkv_rows = w_qkv.transpose(0, 2, 1)
        flat_qkv = qkv_rows.reshape(3 * head_cols, width)

        first = jnp.concatenate([piece_of(w_out), piece_of(w_in), piece_of(w_down)])
        first_z = [cyclic(first, s) for s in others]
        done(first)
        biases = jnp.concatenate([b_inner.reshape(-1), b_qv.reshape(-1)])
        bias_rows = -(-biases.size // head_cols)
        bias_pack = in_three(jnp.pad(hold(biases), (0, bias_rows * head_cols - biases.size)).reshape(bias_rows, head_cols))
        bias_pack = jnp.pad(bias_pack.reshape(3 * bias_rows, head_cols), ((0, -3 * bias_rows % 16), (0, 0)))

        context = attend(at, hold(tokens), qkv_rows, b_qv.reshape(2, head_cols), segments, heads, bias_pack)
        (ctx_own, *ctx_send), first_z = run((context, first_z))
        ctx_z = [cyclic(v, s) for v, s in zip(ctx_send, others)]
        cut, end = w_out.shape[0] // 8, (w_out.shape[0] + w_in.shape[0]) // 8
        a, b = halves(first_z, slice(0, end))
        a1, b1 = by_x(a), by_y(b)
        c, d = halves(first_z, slice(end, None))
        piece_qkv = lax.dynamic_slice(
            hold(flat_qkv), ((y * 2 + x) * (flat_qkv.shape[0] // 4), core * half), (flat_qkv.shape[0] // 4, half)
        )
        done(c, d, piece_qkv, a1, b1)
        a, b = plane_two(*hold((a, b, a1, b1)))
        a1, b1 = by_y(a), by_x(b)
        done(a, b, *ctx_z)
        ctx_z = hold(ctx_z)
        c1, d1 = by_x(hold(c)), by_y(hold(d))
        bias_got = jnp.stack([p[seq_len : seq_len + 3 * bias_rows] for p in ctx_z]).astype(F32)
        bias_got = bias_got.reshape(n_tensor - 1, 3, bias_rows * head_cols)
        bias_got = bias_got[:, 0] + bias_got[:, 1] + bias_got[:, 2]
        bias_all = jnp.concatenate([biases[None], bias_got[:, : biases.size]])
        b_inner_all = bias_all[:, :hidden_cols]
        b_qv_all = bias_all[:, hidden_cols:].reshape(n_tensor, 2, head_cols)
        done(b_inner_all, a1, b1)
        a, b, a1, b1 = hold((a, b, a1, b1))
        in_both = plane_three(a, b, a1, b1, slice(cut, None))
        in_core = by_core(in_both)
        out_both = plane_three(a, b, a1, b1, slice(0, cut))
        out_core = by_core(out_both)
        third_z = [cyclic(hold(piece_qkv), s) for s in others]
        done(in_both, out_both, c1, d1)
        c, d = plane_two(*hold((c, d, c1, d1)))
        c1, d1 = by_y(c), by_x(d)
        done(c, d, out_core, in_core)
        out_got = ordered(*hold((out_both, out_core)), core, 0).transpose(3, 0, 1, 2, 4, 5)
        out_all = jnp.concatenate([w_out[None], out_got.reshape(n_tensor - 1, *w_out.shape)])
        in_parts = (w_in, in_both, in_core)
        done(out_all, in_core)
        ctx = [ctx_own, *ctx_z]
        made = rise(at, hold(ctx), out_all, tokens, gains, shifts, in_parts, b_inner_all)
        made, c1, d1, third_z = run((made, c1, d1, third_z))
        hidden1, hidden_low, norm_one, recip_one, activation, slope, tokens_rel, hidden_rel = made
        down_both = plane_three(c, d, c1, d1, slice(None))
        down_core = by_core(down_both)
        e = jnp.stack(third_z)
        e1 = by_x(e)
        done(down_both, down_core, e)
        down_parts = (w_down, down_both, down_core)
        made = fall(at, hold(activation), down_parts, hidden1, cotangent, gains, shifts)
        made, e1 = run((made, e1))
        output_own, grad_r2, grad_r2_low, vec_two, keep1, send1 = made

        steps = [(i, i + 1) for i in range(n_tensor - 1)]
        back_steps = [(i + 1, i) for i in range(n_tensor - 1)]

        def hop(right, left, step):
            return (
                lax.ppermute(right, "tensor", steps[step:]),
                lax.ppermute(left, "tensor", back_steps[: len(steps) - step]),
            )

        block = width // 8

        class Part:
            def __init__(self, slots, *arrays):
                self.parts = [v[:, slots].reshape(2, 2, -1, *v.shape[2:]) for v in arrays]

            def total(self, *index):
                terms = [p[index].astype(F32) for p in self.parts]
                return functools.reduce(lambda u, v: u + v, terms).astype(BF)

            def take(self, got):
                self.parts = [p[0] for p in self.parts]
                self.parts.append(got.reshape(self.parts[0].shape))

            def totals(self):
                return [self.total(i) for i in range(self.parts[0].shape[0])]

        def pair_of(keep, got):
            count = keep.shape[1]
            return Part(slice(0, count // 2), keep, got), Part(slice(count // 2, count), keep, got)

        def plane(by_first, by_second):
            flying = []
            for move, group in ((by_x, by_first), (by_y, by_second)):
                sends = [p.total(1) for p in group]
                flat = jnp.concatenate([v.reshape(-1, *v.shape[-2:]) for v in sends])
                done(*order.last, flat)
                flying.append(move(flat))
            return flying

        def landed(flying, *groups):
            for flat, group in zip(flying, groups):
                first = 0
                for p in group:
                    size = math.prod(p.parts[0].shape[:-2]) // 2
                    p.take(flat[first : first + size])
                    first += size

        def z_units(total):
            return [cyclic(total[s], n_tensor - s) for s in others]

        def last_sum(mine, got):
            mine = mine.astype(F32)
            for v in got:
                mine = mine + v.astype(F32)
            bit = 2
            while bit < n_outer:
                mine = mine + swap(mine.astype(BF), "outer", n_outer, bit).astype(F32)
                bit *= 2
            return mine

        def whole_rows(mine, got):
            return ordered(mine, got.astype(F32), y, 0).reshape(2 * block, mine.shape[-1])

        out_1 = hop(output_own, output_own, 0)
        core1 = by_core(send1)
        e = ordered(e, e1, x, 0)
        e1 = by_y(e)
        done(e, core1)
        h1 = pair_of(*hold((keep1, core1)))
        flight = plane([h1[0]], [h1[1]])
        made = back(
            at, hold(grad_r2), grad_r2_low, down_parts, slope, in_parts, norm_one, recip_one, gains, hidden_rel
        )
        made, e1, out_1, flight = run((made, e1, out_1, flight))
        grad_binner, grad_r1, grad_r1_low, grad_r1_rel, vec_one, keep2, send2 = made
        out_2 = hop(*out_1, 1)
        core2 = by_core(send2)
        qkv_both = ordered(e, e1, y, 0)
        qkv_core = by_core(qkv_both)
        qkv_parts = (flat_qkv, qkv_both, qkv_core)
        landed(flight, [h1[0]], [h1[1]])
        done(qkv_both, core2)
        h2 = pair_of(*hold((keep2, core2)))
        groups = [h2[0], h1[1]], [h2[1], h1[0]]
        flight = plane(*groups)
        done(*order.last, qkv_core)
        two = n_tensor // 2
        made = attend_back(
            at, 0, tokens, hold(grad_r1_low), grad_r1, ctx[:two], qkv_parts, b_qv_all, heads, out_all, segments,
            tokens_rel, grad_r1_rel, F32,
        )
        made, out_2, flight = run((made, out_2, flight))
        bqv_a, tok_a, keep_a, send_a = made
        out_3 = hop(*out_2, 2)
        core_a = by_core(send_a)
        landed(flight, *groups)
        total1 = h1[0].totals() + h1[1].totals()
        done(*total1, core_a)
        ha = pair_of(*hold((keep_a, core_a)))
        groups = [ha[0], h2[1]], [ha[1], h2[0]]
        flight = plane(*groups)
        made = attend_back(
            at, two, tokens, hold(grad_r1_low), tok_a, ctx[two:], qkv_parts, b_qv_all, heads, out_all, segments,
            tokens_rel, grad_r1_rel, BF,
        )
        made, out_3, flight = run((made, out_3, flight))
        bqv_b, tok_own, keep_b, send_b = made
        tok_1 = hop(tok_own, tok_own, 0)
        core_b = by_core(send_b)
        landed(flight, *groups)
        grad_bqv = jnp.concatenate([bqv_a, bqv_b])

        slot_vec = jnp.concatenate([grad_binner.reshape(n_tensor, -1), grad_bqv.reshape(n_tensor, -1)], 1)
        placed = jnp.zeros_like(slot_vec)
        for s in range(n_tensor):
            placed = lax.dynamic_update_index_in_dim(placed, slot_vec[s], z_from(s), 0)
        common = jnp.stack([vec_one[0], vec_two[0], vec_one[1], vec_one[2], vec_two[1], vec_two[2]])
        vectors = [jnp.concatenate([placed.reshape(-1), common.reshape(-1)])]
        rounds = [
            (axis, size, 1 << i)
            for axis, size in (("local", n_local), ("outer", n_outer), ("tensor", n_tensor))
            for i in range(size.bit_length() - 1)
        ]

        def vector_round(count=1):
            for _ in range(count):
                if len(vectors) > 1:
                    vectors[:] = [vectors[0] + hold(vectors[1])]
                if rounds:
                    vectors.append(swap(vectors[0], *rounds.pop(0)))

        total2 = h2[0].totals() + h2[1].totals()
        total12 = [jnp.stack(pair) for pair in zip(total1, total2)]
        z12 = z_units(total12)
        done(*total12, core_b)
        hb = pair_of(*hold((keep_b, core_b)))
        groups = [hb[0], ha[1]], [hb[1], ha[0]]
        flight = plane(*groups)
        outs = hold((output_own, out_1, out_2, out_3))
        output = place(at, outs[0], [v[0] for v in outs[1:]], [v[1] for v in outs[1:]], BF)
        output, tok_1 = run((output.reshape(seq_count, seq_len, width), tok_1))
        tok_2 = hop(*tok_1, 1)
        vector_round()
        done(*order.last, *flight)
        landed(hold(flight), *groups)
        groups = [hb[1]], [hb[0]]
        flight = plane(*groups)
        done(*order.last, *z12, *vectors)
        mine12 = last_sum(total12[0], hold(z12))
        got12 = by_y(mine12.astype(BF))
        vector_round()
        done(mine12, *flight)
        landed(hold(flight), *groups)
        total3 = hold([t for part in (*ha, *hb) for t in part.totals()])
        z3 = z_units(total3)
        done(*total3, *tok_2, *vectors)
        tok_3 = hop(*hold(tok_2), 2)
        vector_round()
        done(got12, *vectors)
        vector_round()
        got12 = hold(got12)
        done_wdown = whole_rows(mine12[0], got12[0])
        done_win = whole_rows(mine12[1], got12[1])
        done(done_wdown, done_win, *z3)
        mine3 = last_sum(total3[0], hold(z3))
        got3 = by_y(mine3.astype(BF))
        done(mine3, got3, *vectors)
        vector_round()
        done_last = whole_rows(mine3, hold(got3))
        done(done_last, *tok_3)
        grad_tokens = place(at, *hold((tok_own, (tok_1[0], tok_2[0], tok_3[0]), (tok_1[1], tok_2[1], tok_3[1]))), F32)
        grad_tokens = grad_tokens.reshape(seq_count, seq_len, width)
        vector_round(len(rounds) + 1)
        vectors = vectors[0]
        slot_sum = pick(vectors[: placed.size].reshape(placed.shape), z)
        common = vectors[placed.size :].reshape(common.shape)
        part = lambda v, n: lax.dynamic_slice_in_dim(v, l_index * (n // n_local), n // n_local, v.ndim - 1)
        binner = part(slot_sum[:hidden_cols].reshape(b_inner.shape), head_size)
        bqv = part(slot_sum[hidden_cols:].reshape(b_qv.shape), head_size)
        common = part(common, width)
        grad_wqkv = done_last[:, : 3 * head_cols].reshape(width // n_local, 3, head_cols).transpose(1, 0, 2)
        return (
            output,
            grad_tokens,
            grad_wqkv,
            bqv,
            done_last[:, 3 * head_cols :].T,
            done_win,
            binner,
            done_wdown.T,
            common[:2],
            common[2:],
        )

    return local


def solution(mesh):
    placed = (
        P(("outer", "local"), None, None),
        P(("outer", "local"), None),
        P(None, None, "tensor"),
        P(None, "tensor", None),
        P("tensor", None),
        P(None, "tensor"),
        P("tensor", None),
        P("tensor", None),
        P(),
        P(),
        P(("outer", "local"), None, None),
    )
    return jax.shard_map(
        make(dict(mesh.shape)),
        mesh=mesh,
        in_specs=placed,
        out_specs=(
            P(("outer", "local"), None, None),
            P(("outer", "local"), None, None),
            P(None, "local", "tensor"),
            P(None, "tensor", "local"),
            P("tensor", "local"),
            P("local", "tensor"),
            P("tensor", "local"),
            P("tensor", "local"),
            P(None, "local"),
            P(None, "local"),
        ),
        check_vma=False,
    )
```

time: 609 us -> 345 us (0.57)
  matrix products: 140 us -> 0 us
  waiting for transfers between devices: 177 us -> 65.4 us
  Pallas kernels: 0 us -> 107 us
  blocking collectives: 40.6 us -> 0 us
  starting transfers between devices: 130 us -> 89.9 us
  local copies, waits for them, and re-layouts: 69.1 us -> 34.4 us
    dot_general x22 -> x0, matrix products: 118 us -> none  [the longest x8 25 us: scatter(): jnp.einsum('xdt,stn->xsdn', v, right, preferred_element_type=F32)]
    pallas_call x0 -> x8, Pallas kernels: none -> 107 us  [the longest x2 37.4 us: attend_back(): call(functools.partial(attend_back_kernel, first, slots, heads, (cols //...]
    ppermute x36 -> x12, waiting for transfers between devices: 89.7 us -> 13.9 us  [the longest x6 13.9 us: hop(): lax.ppermute(left, 'tensor', back_steps[:len(steps) - step])]
    ppermute x36 -> x35, waiting for transfers between devices: 74 us -> 23.4 us  [swap(): return lax.ppermute(value, axis, [(i, i ^ bit) for i in range(size)])]
    psum x1 -> x0, blocking collectives: 40.6 us -> none  [local(): lax.psum(jnp.concatenate([placed.reshape(-1), common.reshape(-1)]), ('out...]
    ppermute x36 -> x12, starting transfers between devices: 58.7 us -> 23.3 us  [the longest x6 15.2 us: hop(): lax.ppermute(right, 'tensor', steps[step:])]
    sub x2 -> x0, matrix products: 22.6 us -> none  [the longest x1 11.5 us: local(): jax.nn.softmax(jnp.where(allowed, scores * scale, MASKED), axis=-1)]
    ppermute x18 -> x15, waiting for transfers between devices: 12.8 us -> 28.1 us  [local(): lax.ppermute(v, 'tensor', [(i, (i + s) % n_tensor) for i in range(n_tenso...]
  transfers between devices with their start and end apart: 90 -> 62, of which waited for: 36 -> 12; matrix products, arithmetic and copies ran while one was open for 24% -> 18% of each run, Pallas kernels for 0% -> 30%
where the time goes in v2:
time: 345 us; the launch traced here: 339 us
  Pallas kernels  107 us (31%)
  starting transfers between devices  89.9 us (26%)
  waiting for transfers between devices  65.4 us (19%)
  other arithmetic  40.1 us (12%)
  local copies, waits for them, and re-layouts  34.4 us (10%)
    ppermute x15, starting transfers between devices, local(): lax.ppermute(v, 'tensor', [(i, (i + s) % n_tensor) for i in range(n_tenso...  39.9 us
    pallas_call x2, Pallas kernels, attend_back(): call(functools.partial(attend_back_kernel, first, slots, heads, (cols //...  37.4 us
    ppermute x15, waiting for transfers between devices, local(): lax.ppermute(v, 'tensor', [(i, (i + s) % n_tensor) for i in range(n_tenso...  28.1 us
    ppermute x35, starting transfers between devices, swap(): return lax.ppermute(value, axis, [(i, i ^ bit) for i in range(size)])  26.6 us
    ppermute x35, waiting for transfers between devices, swap(): return lax.ppermute(value, axis, [(i, i ^ bit) for i in range(size)])  23.4 us
    pallas_call x1, Pallas kernels, back(): call(functools.partial(back_kernel, slots), 'back', at, (slots,), [const(...  18.9 us
    pallas_call x1, Pallas kernels, fall(): call(functools.partial(fall_kernel, slots), 'fall', at, (2 * slots,), [pl...  15.5 us
    ppermute x6, starting transfers between devices, hop(): lax.ppermute(right, 'tensor', steps[step:])  15.2 us
  transfers between devices with their start and end apart: 62, of which 12 were waited for; matrix products, arithmetic and copies ran while one was open for 18% of the time, Pallas kernels for 30%

profile of v2, /device:TPU:0, one launch (start us, length us, event | category | flops | bytes accessed | tf_op | source)
XLA Modules:
  0.0 338.9 jit_solution(17705248887396549414)
XLA Ops:
  2.5 3.1 collective-permute-start
  5.5 2.6 collective-permute-start.1
  8.1 1.3 collective-permute-start.2
  13.1 13.2 %attend.1 = (bf16[544,192]{1,0:T(8,128)(2,1)}, bf16[544,192]{1,0:T(8,128)(2,1)}, bf16[544,192]{1,0:T(8,128)(2,1)}, bf16[544,192]{1,0:T(8,128)(2,1)}) custom-call(s32[4]{0:T(128)} %pad_add_fusion.at_ref, bf16[4,512,768]{2,1,0:T(8,128)(2,1)} %x_ref.4, bf16[3,192,768]{2,1,0:T(8,128)(2,1)} %bitcast.296, f32[2,192]{1,0:T(2,128)} %reshape.854.bias_ref, ...), custom_call_target="tpu_custom_call" | custom-call | flops 1000 | bytes 1000 | tf_op jit(solution)/shard_map/attend/pallas_call | solution.py:108
  26.3 3.4 %collective-permute-done.1 = bf16[216,768]{1,0:T(8,128)(2,1)S(1)} collective-permute-done((bf16[216,768]{1,0:T(8,128)(2,1)S(1)}, bf16[216,768]{1,0:T(8,128)(2,1)S(1)}, u32[]{:S(2)}, u32[]{:S(2)}) %collective-permute-start.1) | collective-permute-done | bytes 331808 | tf_op jit(solution)/shard_map/ppermute | solution.py:550
  29.9 1.6 collective-permute-start.7
  31.6 1.6 collective-permute-start.6
  33.1 7.6 %collective-permute-start.3 = (bf16[544,192]{1,0:T(8,128)(2,1)}, bf16[544,192]{1,0:T(8,128)(2,1)S(1)}, u32[]{:S(2)}, u32[]{:S(2)}) collective-permute-start(bf16[544,192]{1,0:T(8,128)(2,1)} %get-tuple-element.182), channel_id=1, source_target_pairs={{0,1},{1,2},{2,3},{3,0},{4,5},{5,6},{6,7},{7,4},{8,9},{9,10},{10,1... | collective-permute-start | bytes 626696 | tf_op jit(solution)/shard_map/ppermute | solution.py:550
  40.8 1.6 collective-permute-start.4
  43.2 1.6 dynamic_slice.28
  47.7 2.0 collective-permute-done.3.refs_1_
  49.7 9.6 %collective-permute-done.4.refs_2_.refs_0_ = bf16[544,192]{1,0:T(8,128)(2,1)S(1)} collective-permute-done((bf16[544,192]{1,0:T(8,128)(2,1)S(1)}, bf16[544,192]{1,0:T(8,128)(2,1)S(1)}, u32[]{:S(2)}, u32[]{:S(2)}) %collective-permute-start.4) | collective-permute-done | bytes 208928 | tf_op jit(solution)/shard_map/ppermute | solution.py:550
  66.0 5.8 %collective-permute-start.16 = (bf16[144,384]{1,0:T(8,128)(2,1)}, bf16[144,384]{1,0:T(8,128)(2,1)}, u32[]{:S(2)}, u32[]{:S(2)}) collective-permute-start(bf16[144,384]{1,0:T(8,128)(2,1)} %dynamic_slice.28), channel_id=1, source_target_pairs={{0,1},{1,2},{2,3},{3,0},{4,5},{5,6},{6,7},{7,4},{8,9},{9,10},{10,1... | collective-permute-start | bytes 331784 | tf_op jit(solution)/shard_map/ppermute | solution.py:550
  71.7 2.4 collective-permute-start.17
  74.2 4.4 %collective-permute-start.18 = (bf16[144,384]{1,0:T(8,128)(2,1)}, bf16[144,384]{1,0:T(8,128)(2,1)}, u32[]{:S(2)}, u32[]{:S(2)}) collective-permute-start(bf16[144,384]{1,0:T(8,128)(2,1)} %dynamic_slice.28), channel_id=1, source_target_pairs={{0,3},{1,0},{2,1},{3,2},{4,7},{5,4},{6,5},{7,6},{8,11},{9,8},{10,9... | collective-permute-start | bytes 331784 | tf_op jit(solution)/shard_map/ppermute | solution.py:550
  83.9 13.1 %rise.1 = (f32[512,768]{1,0:T(8,128)}, bf16[512,768]{1,0:T(8,128)(2,1)}, f32[512,768]{1,0:T(8,128)}, f32[512,1]{1,0:T(8,128)}, bf16[4,512,768]{2,1,0:T(8,128)(2,...) custom-call(s32[4]{0:T(128)} %pad_add_fusion.at_ref, ...), custom_call_target="tpu_custom_call" | custom-call | flops 1000 | bytes 1000 | tf_op jit(solution)/shard_map/rise/pallas_call | solution.py:197
  100.6 1.6 collective-permute-start.20
  102.2 1.3 copy.49
  103.5 1.3 copy.50
  104.8 15.5 %fall.1 = (bf16[512,768]{1,0:T(8,128)(2,1)}, f32[512,768]{1,0:T(8,128)}, bf16[512,768]{1,0:T(8,128)(2,1)}, f32[3,768]{1,0:T(4,128)}, bf16[4,4,96,768]{3,2,1,0:T(8,128)(2,1)}, /*index=5*/bf16[4,4,96,768]{3,2,1,0:T(8,128)(2,1)}) custom-call(s32[4]{0:T(128)} %pad_add_fusion.at_ref, bf16[4,512,768]{2,1,0:T(8,128)(2,1)} %get-tuple-element.226.act_ref, ...), custom_call_target="tpu_custom_call" | custom-call | flops 1000 | bytes 1000 | tf_op jit(solution)/shard_map/fall/pallas_call | solution.py:280
  120.5 2.4 collective-permute-start.23
  122.9 1.5 collective-permute-start.24
  125.6 1.5 collective-permute-start.22
  127.1 1.5 add_convert_fusion.2
  130.6 18.9 %back.1 = (f32[4,1,768]{2,1,0:T(1,128)}, f32[512,768]{1,0:T(8,128)}, bf16[512,768]{1,0:T(8,128)(2,1)}, bf16[768,512]{1,0:T(8,128)(2,1)}, f32[3,768]{1,0:T(4,128)...) custom-call(s32[4]{0:T(128)} %pad_add_fusion.at_ref, f32[512,768]{1,0:T(8,128)} %get-tuple-element.241.grad2_ref, ...), custom_call_target="tpu_custom_call" | custom-call | flops 1000 | bytes 1000 | tf_op jit(solution)/shard_map/back/pallas_call | solution.py:335
  149.5 5.9 %collective-permute-done.26 = bf16[4,96,768]{2,1,0:T(8,128)(2,1)S(1)} collective-permute-done((bf16[4,96,768]{2,1,0:T(8,128)(2,1)}, bf16[4,96,768]{2,1,0:T(8,128)(2,1)S(1)}, u32[]{:S(2)}, u32[]{:S(2)}) %collective-permute-start.26) | collective-permute-done | bytes 589856 | tf_op jit(solution)/shard_map/ppermute | solution.py:501
  157.4 1.8 fusion.2
  162.6 1.4 collective-permute-start.32
  166.2 1.6 collective-permute-start.29
  167.8 1.3 collective-permute-start.30
  170.9 18.8 %attend_back.2 = (f32[2,2,192]{2,1,0:T(2,128)}, f32[512,768]{1,0:T(8,128)}, bf16[4,2,96,768]{3,2,1,0:T(8,128)(2,1)}, bf16[4,2,96,768]{3,2,1,0:T(8,128)(2,1)}) custom-call(s32[4]{0:T(128)} %pad_add_fusion.at_ref, bf16[4,512,768]{2,1,0:T(8,128)(2,1)} %x_ref.4, bf16[512,768]{1,0:T(8,128)(2,1)} %get-tuple-element.280.low_ref, ...), custom_call_target="tpu_custom_call" | custom-call | flops 1000 | bytes 1000 | tf_op jit(solution)/shard_map/attend_back/pallas_call | solution.py:446
  190.3 1.6 collective-permute-start.34
  191.9 1.5 collective-permute-start.35
  193.4 1.5 fusion
  199.2 18.5 %attend_back.3 = (f32[2,2,192]{2,1,0:T(2,128)}, bf16[512,768]{1,0:T(8,128)(2,1)}, bf16[4,2,96,768]{3,2,1,0:T(8,128)(2,1)}, bf16[4,2,96,768]{3,2,1,0:T(8,128)(2,1)}) custom-call(s32[4]{0:T(128)} %pad_add_fusion.at_ref, bf16[4,512,768]{2,1,0:T(8,128)(2,1)} %x_ref.4, bf16[512,768]{1,0:T(8,128)(2,1)} %get-tuple-element.280.low_ref, ...), custom_call_target="tpu_custom_call" | custom-call | flops 1000 | bytes 1000 | tf_op jit(solution)/shard_map/attend_back/pallas_call | solution.py:446
  217.8 2.6 fusion.21
  220.5 7.3 %collective-permute-start.39 = (bf16[512,768]{1,0:T(8,128)(2,1)}, bf16[512,768]{1,0:T(8,128)(2,1)}, u32[]{:S(2)}, u32[]{:S(2)}) collective-permute-start(bf16[512,768]{1,0:T(8,128)(2,1)} %get-tuple-element.331.refs_0_), channel_id=1, source_target_pairs={{0,1},{1,2},{2,3},{4,5},{5,6},{6,7},{8,9},{9,10},{10,11},{12,13},{... | collective-permute-start | bytes 2359304 | tf_op jit(solution)/shard_map/ppermute | solution.py:644
  229.8 2.6 fusion.35
  233.1 2.7 collective-permute-start.49
  244.9 1.4 dynamic_update_slice.13
  246.3 1.4 dynamic_update_slice.14
  247.6 1.4 dynamic_update_slice.15
  249.0 1.4 dynamic_update_slice.16
  250.3 1.3 reshape.876
  251.7 1.4 constant_dynamic-update-slice_fusion.1
  253.0 2.3 collective-permute-start.48
  255.4 2.0 collective-permute-start.47
  257.4 1.4 constant_dynamic-update-slice_fusion.2
  258.8 4.0 %place.2 = bf16[4,512,768]{2,1,0:T(8,128)(2,1)} custom-call(s32[4]{0:T(128)} %pad_add_fusion.at_ref, bf16[512,768]{1,0:T(8,128)(2,1)} %get-tuple-element.294.refs_0_, bf16[512,768]{1,0:T(8,128)(2,1)} %collective-permute-done.23.refs_1_, bf16[512,768]{1,0:T(8,128)(2,1)} %collective-permute-done.29.refs_2_, bf16[512,768]{1,0:T(8,128)(2,1)} %collective-permute-done.34.refs_3_, ...), custom_call_target="tpu_custom_call" | custom-call | flops 1000 | bytes 1000 | tf_op jit(solution)/shard_map/place/pallas_call | solution.py:492
  262.7 1.6 collective-permute-start.41
  264.3 1.3 collective-permute-start.42
  267.7 2.5 collective-permute-done.48
  273.4 1.6 collective-permute-start.51
  275.1 1.4 fusion.49
  276.5 1.5 collective-permute-start.57
  278.0 1.6 fusion.28
  279.6 13.3 %collective-permute-done.42.refs_5_ = bf16[512,768]{1,0:T(8,128)(2,1)} collective-permute-done((bf16[512,768]{1,0:T(8,128)(2,1)}, bf16[512,768]{1,0:T(8,128)(2,1)}, u32[]{:S(2)}, u32[]{:S(2)}) %collective-permute-start.42) | collective-permute-done | bytes 786464 | tf_op jit(solution)/shard_map/ppermute | solution.py:645
  293.0 1.8 collective-permute-start.58
  294.9 3.0 collective-permute-start.55
  298.6 1.3 collective-permute-start.53
  300.9 9.4 %collective-permute-done.55 = bf16[96,768]{1,0:T(8,128)(2,1)S(1)} collective-permute-done((bf16[96,768]{1,0:T(8,128)(2,1)S(1)}, bf16[96,768]{1,0:T(8,128)(2,1)S(1)}, u32[]{:S(2)}, u32[]{:S(2)}) %collective-permute-start.55) | collective-permute-done | bytes 147488 | tf_op jit(solution)/shard_map/ppermute | solution.py:550
  311.7 13.8 %collective-permute-done.60 = f32[9216]{0:T(1024)S(1)} collective-permute-done((f32[9216]{0:T(1024)S(1)}, f32[9216]{0:T(1024)S(1)}, u32[]{:S(2)}, u32[]{:S(2)}) %collective-permute-start.60) | collective-permute-done | bytes 36896 | tf_op jit(solution)/shard_map/ppermute | solution.py:501
  327.9 2.5 collective-permute-done.61
  333.6 4.8 %place.3 = f32[4,512,768]{2,1,0:T(8,128)} custom-call(s32[4]{0:T(128)} %pad_add_fusion.at_ref, bf16[512,768]{1,0:T(8,128)(2,1)} %get-tuple-element.331.refs_0_, bf16[512,768]{1,0:T(8,128)(2,1)} %collective-permute-done.39.refs_1_, bf16[512,768]{1,0:T(8,128)(2,1)} %collective-permute-done.41.refs_2_, bf16[512,768]{1,0:T(8,128)(2,1)} %copy-done.25, ...), custom_call_target="tpu_custom_call" | custom-call | flops 1000 | bytes 1000 | tf_op jit(solution)/shard_map/place/pallas_call | solution.py:492
  (300 shorter events, 67.9 us)
Async XLA Ops:
  2.5 23.8 %collective-permute-start = (bf16[216,768]{1,0:T(8,128)(2,1)S(1)}, bf16[216,768]{1,0:T(8,128)(2,1)S(1)}, u32[]{:S(2)}, u32[]{:S(2)}) collective-permute-start(bf16[216,768]{1,0:T(8,128)(2,1)S(1)} %pad_maximum_fusion.16), channel_id=1, source_target_pairs={{0,1},{1,2},{2,3},{3,0},{4,5},{5,6},{6,7},{7,4},{8,9},{9,10},{10,1... | collective-permute-start | bytes 995336 | tf_op jit(solution)/shard_map/ppermute | solution.py:550
  5.5 24.2 %collective-permute-start.1 = (bf16[216,768]{1,0:T(8,128)(2,1)S(1)}, bf16[216,768]{1,0:T(8,128)(2,1)S(1)}, u32[]{:S(2)}, u32[]{:S(2)}) collective-permute-start(bf16[216,768]{1,0:T(8,128)(2,1)S(1)} %pad_maximum_fusion.16), channel_id=1, source_target_pairs={{0,2},{1,3},{2,0},{3,1},{4,6},{5,7},{6,4},{7,5},{8,10},{9,11},{10,... | collective-permute-start | bytes 995336 | tf_op jit(solution)/shard_map/ppermute | solution.py:550
  8.1 21.6 %collective-permute-start.2 = (bf16[216,768]{1,0:T(8,128)(2,1)S(1)}, bf16[216,768]{1,0:T(8,128)(2,1)S(1)}, u32[]{:S(2)}, u32[]{:S(2)}) collective-permute-start(bf16[216,768]{1,0:T(8,128)(2,1)S(1)} %pad_maximum_fusion.16), channel_id=1, source_target_pairs={{0,3},{1,0},{2,1},{3,2},{4,7},{5,4},{6,5},{7,6},{8,11},{9,8},{10,9... | collective-permute-start | bytes 995336 | tf_op jit(solution)/shard_map/ppermute | solution.py:550
  26.3 33.5 %copy-start.38 = (f32[1,1152]{1,0:T(1,128)}, f32[1,1152]{1,0:T(1,128)S(1)}, u32[]{:S(2)}) copy-start(f32[1,1152]{1,0:T(1,128)S(1)} %broadcast_in_dim.18) | copy-start | bytes 13828
  29.9 16.3 %collective-permute-start.7 = (bf16[3,120,384]{2,1,0:T(8,128)(2,1)S(1)}, bf16[3,120,384]{2,1,0:T(8,128)(2,1)S(1)}, u32[]{:S(2)}, u32[]{:S(2)}) collective-permute-start(bf16[3,120,384]{2,1,0:T(8,128)(2,1)S(1)} %pad_maximum_fusion.23), channel_id=1, source_target_pairs={{0,16},{16,0},{1,17},{17,1},{2,18},{18,2},{3,19},{19,3},{4,20},{20... | collective-permute-start | bytes 829448 | tf_op jit(solution)/shard_map/ppermute | solution.py:501
  31.6 14.7 %collective-permute-start.6 = (bf16[3,120,384]{2,1,0:T(8,128)(2,1)S(1)}, bf16[3,120,384]{2,1,0:T(8,128)(2,1)S(1)}, u32[]{:S(2)}, u32[]{:S(2)}) collective-permute-start(bf16[3,120,384]{2,1,0:T(8,128)(2,1)S(1)} %pad_maximum_fusion.22), channel_id=1, source_target_pairs={{0,8},{4,12},{8,0},{12,4},{1,9},{5,13},{9,1},{13,5},{2,10},{6,14},... | collective-permute-start | bytes 829448 | tf_op jit(solution)/shard_map/ppermute | solution.py:501
  33.1 16.6 %collective-permute-start.3 = (bf16[544,192]{1,0:T(8,128)(2,1)}, bf16[544,192]{1,0:T(8,128)(2,1)S(1)}, u32[]{:S(2)}, u32[]{:S(2)}) collective-permute-start(bf16[544,192]{1,0:T(8,128)(2,1)} %get-tuple-element.182), channel_id=1, source_target_pairs={{0,1},{1,2},{2,3},{3,0},{4,5},{5,6},{6,7},{7,4},{8,9},{9,10},{10,1... | collective-permute-start | bytes 626696 | tf_op jit(solution)/shard_map/ppermute | solution.py:550
  40.8 18.5 %collective-permute-start.4 = (bf16[544,192]{1,0:T(8,128)(2,1)S(1)}, bf16[544,192]{1,0:T(8,128)(2,1)S(1)}, u32[]{:S(2)}, u32[]{:S(2)}) collective-permute-start(bf16[544,192]{1,0:T(8,128)(2,1)S(1)} %copy-done.47), channel_id=1, source_target_pairs={{0,2},{1,3},{2,0},{3,1},{4,6},{5,7},{6,4},{7,5},{8,10},{9,11},{10,... | collective-permute-start | bytes 626696 | tf_op jit(solution)/shard_map/ppermute | solution.py:550
  42.4 16.9 %collective-permute-start.5 = (bf16[544,192]{1,0:T(8,128)(2,1)S(1)}, bf16[544,192]{1,0:T(8,128)(2,1)S(1)}, u32[]{:S(2)}, u32[]{:S(2)}) collective-permute-start(bf16[544,192]{1,0:T(8,128)(2,1)S(1)} %copy-done.46), channel_id=1, source_target_pairs={{0,3},{1,0},{2,1},{3,2},{4,7},{5,4},{6,5},{7,6},{8,11},{9,8},{10,9... | collective-permute-start | bytes 626696 | tf_op jit(solution)/shard_map/ppermute | solution.py:550
  46.4 13.4 %collective-permute-start.9 = (bf16[2,3,120,384]{3,2,1,0:T(8,128)(2,1)S(1)}, bf16[2,3,120,384]{3,2,1,0:T(8,128)(2,1)S(1)}, u32[]{:S(2)}, u32[]{:S(2)}) collective-permute-start(bf16[2,3,120,384]{3,2,1,0:T(8,128)(2,1)S(1)} %pad_maximum_fusion.11), channel_id=1, source_target_pairs={{0,8},{4,12},{8,0},{12,4},{1,9},{5,13},{9,1},{13,5},{2,10},{6,14},... | collective-permute-start | bytes 1658888 | tf_op jit(solution)/shard_map/ppermute | solution.py:501
  47.1 13.2 %collective-permute-start.8 = (bf16[2,3,120,384]{3,2,1,0:T(8,128)(2,1)S(1)}, bf16[2,3,120,384]{3,2,1,0:T(8,128)(2,1)S(1)}, u32[]{:S(2)}, u32[]{:S(2)}) collective-permute-start(bf16[2,3,120,384]{3,2,1,0:T(8,128)(2,1)S(1)} %pad_maximum_fusion.10), channel_id=1, source_target_pairs={{0,16},{16,0},{1,17},{17,1},{2,18},{18,2},{3,19},{19,3},{4,20},{20... | collective-permute-start | bytes 1658888 | tf_op jit(solution)/shard_map/ppermute | solution.py:501
  61.5 18.1 %copy-start = (bf16[2,2,3,96,768]{4,3,2,1,0:T(8,128)(2,1)}, bf16[2,2,3,96,768]{4,3,2,1,0:T(8,128)(2,1)S(1)}, u32[]{:S(2)}) copy-start(bf16[2,2,3,96,768]{4,3,2,1,0:T(8,128)(2,1)S(1)} %maximum_maximum_fusion) | copy-start | bytes 5308420
  61.5 19.6 %collective-permute-start.13 = (bf16[2,2,3,96,768]{4,3,2,1,0:T(8,128)(2,1)S(1)}, bf16[2,2,3,96,768]{4,3,2,1,0:T(8,128)(2,1)S(1)}, u32[]{:S(2)}, u32[]{:S(2)}) collective-permute-start(bf16[2,2,3,96,768]{4,3,2,1,0:T(8,128)(2,1)S(1)} %maximum_maximum_fusion), channel_id=1, source_target_pairs={{0,4},{4,0},{8,12},{12,8},{1,5},{5,1},{9,13},{13,9},{2,6},{6,2},{1... | collective-permute-start | bytes 5308424 | tf_op jit(solution)/shard_map/ppermute | solution.py:501
  62.2 11.9 %collective-permute-start.12 = (bf16[3,96,384]{2,1,0:T(8,128)(2,1)}, bf16[3,96,384]{2,1,0:T(8,128)(2,1)S(1)}, u32[]{:S(2)}, u32[]{:S(2)}) collective-permute-start(bf16[3,96,384]{2,1,0:T(8,128)(2,1)} %pad_maximum_fusion.25), channel_id=1, source_target_pairs={{0,16},{16,0},{1,17},{17,1},{2,18},{18,2},{3,19},{19,3},{4,20},{20... | collective-permute-start | bytes 663560 | tf_op jit(solution)/shard_map/ppermute | solution.py:501
  62.7 15.9 %collective-permute-start.11 = (bf16[3,96,384]{2,1,0:T(8,128)(2,1)}, bf16[3,96,384]{2,1,0:T(8,128)(2,1)S(1)}, u32[]{:S(2)}, u32[]{:S(2)}) collective-permute-start(bf16[3,96,384]{2,1,0:T(8,128)(2,1)} %pad_maximum_fusion.24), channel_id=1, source_target_pairs={{0,8},{4,12},{8,0},{12,4},{1,9},{5,13},{9,1},{13,5},{2,10},{6,14},... | collective-permute-start | bytes 663560 | tf_op jit(solution)/shard_map/ppermute | solution.py:501
  66.0 31.0 %collective-permute-start.16 = (bf16[144,384]{1,0:T(8,128)(2,1)}, bf16[144,384]{1,0:T(8,128)(2,1)}, u32[]{:S(2)}, u32[]{:S(2)}) collective-permute-start(bf16[144,384]{1,0:T(8,128)(2,1)} %dynamic_slice.28), channel_id=1, source_target_pairs={{0,1},{1,2},{2,3},{3,0},{4,5},{5,6},{6,7},{7,4},{8,9},{9,10},{10,1... | collective-permute-start | bytes 331784 | tf_op jit(solution)/shard_map/ppermute | solution.py:550
  71.7 25.3 %collective-permute-start.17 = (bf16[144,384]{1,0:T(8,128)(2,1)}, bf16[144,384]{1,0:T(8,128)(2,1)}, u32[]{:S(2)}, u32[]{:S(2)}) collective-permute-start(bf16[144,384]{1,0:T(8,128)(2,1)} %dynamic_slice.28), channel_id=1, source_target_pairs={{0,2},{1,3},{2,0},{3,1},{4,6},{5,7},{6,4},{7,5},{8,10},{9,11},{10,... | collective-permute-start | bytes 331784 | tf_op jit(solution)/shard_map/ppermute | solution.py:550
  74.2 22.8 %collective-permute-start.18 = (bf16[144,384]{1,0:T(8,128)(2,1)}, bf16[144,384]{1,0:T(8,128)(2,1)}, u32[]{:S(2)}, u32[]{:S(2)}) collective-permute-start(bf16[144,384]{1,0:T(8,128)(2,1)} %dynamic_slice.28), channel_id=1, source_target_pairs={{0,3},{1,0},{2,1},{3,2},{4,7},{5,4},{6,5},{7,6},{8,11},{9,8},{10,9... | collective-permute-start | bytes 331784 | tf_op jit(solution)/shard_map/ppermute | solution.py:550
  78.6 1.9 collective-permute-start.10
  80.6 16.5 %collective-permute-start.15 = (bf16[2,3,96,384]{3,2,1,0:T(8,128)(2,1)}, bf16[2,3,96,384]{3,2,1,0:T(8,128)(2,1)}, u32[]{:S(2)}, u32[]{:S(2)}) collective-permute-start(bf16[2,3,96,384]{3,2,1,0:T(8,128)(2,1)} %pad_maximum_fusion.13), channel_id=1, source_target_pairs={{0,8},{4,12},{8,0},{12,4},{1,9},{5,13},{9,1},{13,5},{2,10},{6,14},... | collective-permute-start | bytes 1327112 | tf_op jit(solution)/shard_map/ppermute | solution.py:501
  81.1 15.9 %collective-permute-start.14 = (bf16[2,3,96,384]{3,2,1,0:T(8,128)(2,1)}, bf16[2,3,96,384]{3,2,1,0:T(8,128)(2,1)S(1)}, u32[]{:S(2)}, u32[]{:S(2)}) collective-permute-start(bf16[2,3,96,384]{3,2,1,0:T(8,128)(2,1)} %pad_maximum_fusion.12), channel_id=1, source_target_pairs={{0,16},{16,0},{1,17},{17,1},{2,18},{18,2},{3,19},{19,3},{4,20},{20... | collective-permute-start | bytes 1327112 | tf_op jit(solution)/shard_map/ppermute | solution.py:501
  99.3 4.2 %collective-permute-start.19 = (bf16[2,2,3,96,768]{4,3,2,0,1:T(8,128)(2,1)S(1)}, bf16[2,2,3,96,768]{4,3,2,0,1:T(8,128)(2,1)S(1)}, u32[]{:S(2)}, u32[]{:S(2)}) collective-permute-start(bf16[2,2,3,96,768]{4,3,2,0,1:T(8,128)(2,1)S(1)} %maximum_maximum_fusion.1), channel_id=1, source_target_pairs={{0,4},{4,0},{8,12},{12,8},{1,5},{5,1},{9,13},{13,9},{2,6},{6,2},{1... | collective-permute-start | bytes 5308424 | tf_op jit(solution)/shard_map/ppermute | solution.py:501
  100.6 19.7 %collective-permute-start.20 = (bf16[3,144,384]{2,1,0:T(8,128)(2,1)S(1)}, bf16[3,144,384]{2,1,0:T(8,128)(2,1)S(1)}, u32[]{:S(2)}, u32[]{:S(2)}) collective-permute-start(bf16[3,144,384]{2,1,0:T(8,128)(2,1)S(1)} %pad_maximum_fusion.17), channel_id=1, source_target_pairs={{0,8},{4,12},{8,0},{12,4},{1,9},{5,13},{9,1},{13,5},{2,10},{6,14},... | collective-permute-start | bytes 995336 | tf_op jit(solution)/shard_map/ppermute | solution.py:501
  120.4 6.7 %collective-permute-start.21 = (bf16[4,4,96,768]{3,2,1,0:T(8,128)(2,1)}, bf16[4,4,96,768]{3,2,1,0:T(8,128)(2,1)S(1)}, u32[]{:S(2)}, u32[]{:S(2)}) collective-permute-start(bf16[4,4,96,768]{3,2,1,0:T(8,128)(2,1)} %get-tuple-element.237), channel_id=1, source_target_pairs={{0,4},{4,0},{8,12},{12,8},{1,5},{5,1},{9,13},{13,9},{2,6},{6,2},{1... | collective-permute-start | bytes 7077896 | tf_op jit(solution)/shard_map/ppermute | solution.py:501
  120.5 29.0 %collective-permute-start.23 = (bf16[512,768]{1,0:T(8,128)(2,1)}, bf16[512,768]{1,0:T(8,128)(2,1)}, u32[]{:S(2)}, u32[]{:S(2)}) collective-permute-start(bf16[512,768]{1,0:T(8,128)(2,1)} %get-tuple-element.294.refs_0_), channel_id=1, source_target_pairs={{0,1},{1,2},{2,3},{4,5},{5,6},{6,7},{8,9},{9,10},{10,11},{12,13},{... | collective-permute-start | bytes 2359304 | tf_op jit(solution)/shard_map/ppermute | solution.py:644
  122.9 26.6 %collective-permute-start.24 = (bf16[512,768]{1,0:T(8,128)(2,1)}, bf16[512,768]{1,0:T(8,128)(2,1)}, u32[]{:S(2)}, u32[]{:S(2)}) collective-permute-start(bf16[512,768]{1,0:T(8,128)(2,1)} %get-tuple-element.294.refs_0_), channel_id=1, source_target_pairs={{1,0},{2,1},{3,2},{5,4},{6,5},{7,6},{9,8},{10,9},{11,10},{13,12},{... | collective-permute-start | bytes 2359304 | tf_op jit(solution)/shard_map/ppermute | solution.py:645
  125.6 23.9 %collective-permute-start.22 = (bf16[2,3,144,384]{3,2,1,0:T(8,128)(2,1)S(1)}, bf16[2,3,144,384]{3,2,1,0:T(8,128)(2,1)S(1)}, u32[]{:S(2)}, u32[]{:S(2)}) collective-permute-start(bf16[2,3,144,384]{3,2,1,0:T(8,128)(2,1)S(1)} %pad_maximum_fusion.4), channel_id=1, source_target_pairs={{0,16},{16,0},{1,17},{17,1},{2,18},{18,2},{3,19},{19,3},{4,20},{20... | collective-permute-start | bytes 1990664 | tf_op jit(solution)/shard_map/ppermute | solution.py:501
  128.9 20.6 %collective-permute-start.25 = (bf16[4,96,768]{2,1,0:T(8,128)(2,1)}, bf16[4,96,768]{2,1,0:T(8,128)(2,1)S(1)}, u32[]{:S(2)}, u32[]{:S(2)}) collective-permute-start(bf16[4,96,768]{2,1,0:T(8,128)(2,1)} %bitcast.58), channel_id=1, source_target_pairs={{0,8},{4,12},{8,0},{12,4},{1,9},{5,13},{9,1},{13,5},{2,10},{6,14},... | collective-permute-start | bytes 1769480 | tf_op jit(solution)/shard_map/ppermute | solution.py:501
  130.0 25.4 %collective-permute-start.26 = (bf16[4,96,768]{2,1,0:T(8,128)(2,1)}, bf16[4,96,768]{2,1,0:T(8,128)(2,1)S(1)}, u32[]{:S(2)}, u32[]{:S(2)}) collective-permute-start(bf16[4,96,768]{2,1,0:T(8,128)(2,1)} %bitcast.59), channel_id=1, source_target_pairs={{0,16},{16,0},{1,17},{17,1},{2,18},{18,2},{3,19},{19,3},{4,20},{20... | collective-permute-start | bytes 1769480 | tf_op jit(solution)/shard_map/ppermute | solution.py:501
  155.5 4.7 %collective-permute-start.27 = (bf16[4,4,96,768]{3,2,1,0:T(8,128)(2,1)}, bf16[4,4,96,768]{3,2,1,0:T(8,128)(2,1)S(1)}, u32[]{:S(2)}, u32[]{:S(2)}) collective-permute-start(bf16[4,4,96,768]{3,2,1,0:T(8,128)(2,1)} %get-tuple-element.258), channel_id=1, source_target_pairs={{0,4},{4,0},{8,12},{12,8},{1,5},{5,1},{9,13},{13,9},{2,6},{6,2},{1... | collective-permute-start | bytes 7077896 | tf_op jit(solution)/shard_map/ppermute | solution.py:501
  156.5 13.4 %collective-permute-start.28 = (bf16[2,2,3,144,384]{4,3,2,1,0:T(8,128)(2,1)S(1)}, bf16[2,2,3,144,384]{4,3,2,1,0:T(8,128)(2,1)S(1)}, u32[]{:S(2)}, u32[]{:S(2)}) collective-permute-start(bf16[2,2,3,144,384]{4,3,2,1,0:T(8,128)(2,1)S(1)} %pad_maximum_fusion), channel_id=1, source_target_pairs={{0,4},{4,0},{8,12},{12,8},{1,5},{5,1},{9,13},{13,9},{2,6},{6,2},{1... | collective-permute-start | bytes 3981320 | tf_op jit(solution)/shard_map/ppermute | solution.py:501
  162.6 27.7 %collective-permute-start.32 = (bf16[6,96,768]{2,1,0:T(8,128)(2,1)}, bf16[6,96,768]{2,1,0:T(8,128)(2,1)S(1)}, u32[]{:S(2)}, u32[]{:S(2)}) collective-permute-start(bf16[6,96,768]{2,1,0:T(8,128)(2,1)} %pad_maximum_fusion.3), channel_id=1, source_target_pairs={{0,16},{16,0},{1,17},{17,1},{2,18},{18,2},{3,19},{19,3},{4,20},{20... | collective-permute-start | bytes 2654216 | tf_op jit(solution)/shard_map/ppermute | solution.py:501
  165.0 25.3 %collective-permute-start.31 = (bf16[6,96,768]{2,1,0:T(8,128)(2,1)}, bf16[6,96,768]{2,1,0:T(8,128)(2,1)}, u32[]{:S(2)}, u32[]{:S(2)}) collective-permute-start(bf16[6,96,768]{2,1,0:T(8,128)(2,1)} %pad_maximum_fusion.2), channel_id=1, source_target_pairs={{0,8},{4,12},{8,0},{12,4},{1,9},{5,13},{9,1},{13,5},{2,10},{6,14},... | collective-permute-start | bytes 2654216 | tf_op jit(solution)/shard_map/ppermute | solution.py:501
  166.2 23.6 %collective-permute-start.29 = (bf16[512,768]{1,0:T(8,128)(2,1)}, bf16[512,768]{1,0:T(8,128)(2,1)}, u32[]{:S(2)}, u32[]{:S(2)}) collective-permute-start(bf16[512,768]{1,0:T(8,128)(2,1)} %collective-permute-done.23.refs_1_), channel_id=1, source_target_pairs={{1,2},{2,3},{5,6},{6,7},{9,10},{10,11},{13,14},{14,15},{17,18},{18... | collective-permute-start | bytes 2359304 | tf_op jit(solution)/shard_map/ppermute | solution.py:644
  167.8 22.5 %collective-permute-start.30 = (bf16[512,768]{1,0:T(8,128)(2,1)}, bf16[512,768]{1,0:T(8,128)(2,1)}, u32[]{:S(2)}, u32[]{:S(2)}) collective-permute-start(bf16[512,768]{1,0:T(8,128)(2,1)} %collective-permute-done.24.refs_4_), channel_id=1, source_target_pairs={{1,0},{2,1},{5,4},{6,5},{9,8},{10,9},{13,12},{14,13},{17,16},{18,1... | collective-permute-start | bytes 2359304 | tf_op jit(solution)/shard_map/ppermute | solution.py:645
  190.3 4.7 %collective-permute-start.33 = (bf16[4,2,96,768]{3,2,1,0:T(8,128)(2,1)}, bf16[4,2,96,768]{3,2,1,0:T(8,128)(2,1)S(1)}, u32[]{:S(2)}, u32[]{:S(2)}) collective-permute-start(bf16[4,2,96,768]{3,2,1,0:T(8,128)(2,1)} %get-tuple-element.276), channel_id=1, source_target_pairs={{0,4},{4,0},{8,12},{12,8},{1,5},{5,1},{9,13},{13,9},{2,6},{6,2},{1... | collective-permute-start | bytes 3538952 | tf_op jit(solution)/shard_map/ppermute | solution.py:501
  190.3 27.4 %collective-permute-start.34 = (bf16[512,768]{1,0:T(8,128)(2,1)}, bf16[512,768]{1,0:T(8,128)(2,1)}, u32[]{:S(2)}, u32[]{:S(2)}) collective-permute-start(bf16[512,768]{1,0:T(8,128)(2,1)} %collective-permute-done.29.refs_2_), channel_id=1, source_target_pairs={{2,3},{6,7},{10,11},{14,15},{18,19},{22,23},{26,27},{30,31}} | collective-permute-start | bytes 2359304 | tf_op jit(solution)/shard_map/ppermute | solution.py:644
  191.9 25.8 %collective-permute-start.35 = (bf16[512,768]{1,0:T(8,128)(2,1)}, bf16[512,768]{1,0:T(8,128)(2,1)}, u32[]{:S(2)}, u32[]{:S(2)}) collective-permute-start(bf16[512,768]{1,0:T(8,128)(2,1)} %collective-permute-done.30.refs_5_), channel_id=1, source_target_pairs={{1,0},{5,4},{9,8},{13,12},{17,16},{21,20},{25,24},{29,28}} | collective-permute-start | bytes 2359304 | tf_op jit(solution)/shard_map/ppermute | solution.py:645
  196.0 21.7 %collective-permute-start.37 = (bf16[4,96,768]{2,1,0:T(8,128)(2,1)}, bf16[4,96,768]{2,1,0:T(8,128)(2,1)}, u32[]{:S(2)}, u32[]{:S(2)}) collective-permute-start(bf16[4,96,768]{2,1,0:T(8,128)(2,1)} %pad_maximum_fusion.6), channel_id=1, source_target_pairs={{0,16},{16,0},{1,17},{17,1},{2,18},{18,2},{3,19},{19,3},{4,20},{20... | collective-permute-start | bytes 1769480 | tf_op jit(solution)/shard_map/ppermute | solution.py:501
  197.7 20.1 %collective-permute-start.36 = (bf16[4,96,768]{2,1,0:T(8,128)(2,1)}, bf16[4,96,768]{2,1,0:T(8,128)(2,1)}, u32[]{:S(2)}, u32[]{:S(2)}) collective-permute-start(bf16[4,96,768]{2,1,0:T(8,128)(2,1)} %pad_maximum_fusion.5), channel_id=1, source_target_pairs={{0,8},{4,12},{8,0},{12,4},{1,9},{5,13},{9,1},{13,5},{2,10},{6,14},... | collective-permute-start | bytes 1769480 | tf_op jit(solution)/shard_map/ppermute | solution.py:501
  217.8 20.6 %collective-permute-start.38 = (bf16[4,2,96,768]{3,2,1,0:T(8,128)(2,1)}, bf16[4,2,96,768]{3,2,1,0:T(8,128)(2,1)}, u32[]{:S(2)}, u32[]{:S(2)}) collective-permute-start(bf16[4,2,96,768]{3,2,1,0:T(8,128)(2,1)} %get-tuple-element.290), channel_id=1, source_target_pairs={{0,4},{4,0},{8,12},{12,8},{1,5},{5,1},{9,13},{13,9},{2,6},{6,2},{1... | collective-permute-start | bytes 3538952 | tf_op jit(solution)/shard_map/ppermute | solution.py:501
  220.5 32.5 %collective-permute-start.39 = (bf16[512,768]{1,0:T(8,128)(2,1)}, bf16[512,768]{1,0:T(8,128)(2,1)}, u32[]{:S(2)}, u32[]{:S(2)}) collective-permute-start(bf16[512,768]{1,0:T(8,128)(2,1)} %get-tuple-element.331.refs_0_), channel_id=1, source_target_pairs={{0,1},{1,2},{2,3},{4,5},{5,6},{6,7},{8,9},{9,10},{10,11},{12,13},{... | collective-permute-start | bytes 2359304 | tf_op jit(solution)/shard_map/ppermute | solution.py:644
  227.8 27.6 %collective-permute-start.40 = (bf16[512,768]{1,0:T(8,128)(2,1)}, bf16[512,768]{1,0:T(8,128)(2,1)}, u32[]{:S(2)}, u32[]{:S(2)}) collective-permute-start(bf16[512,768]{1,0:T(8,128)(2,1)} %get-tuple-element.331.refs_0_), channel_id=1, source_target_pairs={{1,0},{2,1},{3,2},{5,4},{6,5},{7,6},{9,8},{10,9},{11,10},{13,12},{... | collective-permute-start | bytes 2359304 | tf_op jit(solution)/shard_map/ppermute | solution.py:645
  233.1 33.7 %collective-permute-start.49 = (bf16[2,96,768]{2,1,0:T(8,128)(2,1)}, bf16[2,96,768]{2,1,0:T(8,128)(2,1)}, u32[]{:S(2)}, u32[]{:S(2)}) collective-permute-start(bf16[2,96,768]{2,1,0:T(8,128)(2,1)} %pad_maximum_fusion.21), channel_id=1, source_target_pairs={{0,1},{1,2},{2,3},{3,0},{4,5},{5,6},{6,7},{7,4},{8,9},{9,10},{10,1... | collective-permute-start | bytes 884744 | tf_op jit(solution)/shard_map/ppermute | solution.py:550
  240.4 18.4 %collective-permute-start.44 = (bf16[3,96,768]{2,1,0:T(8,128)(2,1)}, bf16[3,96,768]{2,1,0:T(8,128)(2,1)}, u32[]{:S(2)}, u32[]{:S(2)}) collective-permute-start(bf16[3,96,768]{2,1,0:T(8,128)(2,1)} %pad_maximum_fusion.15), channel_id=1, source_target_pairs={{0,16},{16,0},{1,17},{17,1},{2,18},{18,2},{3,19},{19,3},{4,20},{20... | collective-permute-start | bytes 1327112 | tf_op jit(solution)/shard_map/ppermute | solution.py:501
  242.5 20.3 %collective-permute-start.43 = (bf16[3,96,768]{2,1,0:T(8,128)(2,1)}, bf16[3,96,768]{2,1,0:T(8,128)(2,1)}, u32[]{:S(2)}, u32[]{:S(2)}) collective-permute-start(bf16[3,96,768]{2,1,0:T(8,128)(2,1)} %pad_maximum_fusion.14), channel_id=1, source_target_pairs={{0,8},{4,12},{8,0},{12,4},{1,9},{5,13},{9,1},{13,5},{2,10},{6,14},... | collective-permute-start | bytes 1327112 | tf_op jit(solution)/shard_map/ppermute | solution.py:501
  253.0 17.2 %collective-permute-start.48 = (bf16[2,96,768]{2,1,0:T(8,128)(2,1)}, bf16[2,96,768]{2,1,0:T(8,128)(2,1)}, u32[]{:S(2)}, u32[]{:S(2)}) collective-permute-start(bf16[2,96,768]{2,1,0:T(8,128)(2,1)} %pad_maximum_fusion.20), channel_id=1, source_target_pairs={{0,2},{1,3},{2,0},{3,1},{4,6},{5,7},{6,4},{7,5},{8,10},{9,11},{10,... | collective-permute-start | bytes 884744 | tf_op jit(solution)/shard_map/ppermute | solution.py:550
  255.4 17.3 %collective-permute-start.47 = (bf16[2,96,768]{2,1,0:T(8,128)(2,1)}, bf16[2,96,768]{2,1,0:T(8,128)(2,1)}, u32[]{:S(2)}, u32[]{:S(2)}) collective-permute-start(bf16[2,96,768]{2,1,0:T(8,128)(2,1)} %pad_maximum_fusion.19), channel_id=1, source_target_pairs={{0,3},{1,0},{2,1},{3,2},{4,7},{5,4},{6,5},{7,6},{8,11},{9,8},{10,9... | collective-permute-start | bytes 884744 | tf_op jit(solution)/shard_map/ppermute | solution.py:550
  258.8 5.6 %collective-permute-start.50 = (f32[9216]{0:T(1024)}, f32[9216]{0:T(1024)}, u32[]{:S(2)}, u32[]{:S(2)}) collective-permute-start(f32[9216]{0:T(1024)} %constant_dynamic-update-slice_fusion.2), channel_id=1, source_target_pairs={{0,4},{4,0},{8,12},{12,8},{1,5},{5,1},{9,13},{13,9},{2,6},{6,2},{1... | collective-permute-start | bytes 110600 | tf_op jit(solution)/shard_map/ppermute | solution.py:501
  262.7 16.9 %collective-permute-start.41 = (bf16[512,768]{1,0:T(8,128)(2,1)}, bf16[512,768]{1,0:T(8,128)(2,1)}, u32[]{:S(2)}, u32[]{:S(2)}) collective-permute-start(bf16[512,768]{1,0:T(8,128)(2,1)} %collective-permute-done.39.refs_1_), channel_id=1, source_target_pairs={{1,2},{2,3},{5,6},{6,7},{9,10},{10,11},{13,14},{14,15},{17,18},{18... | collective-permute-start | bytes 2359304 | tf_op jit(solution)/shard_map/ppermute | solution.py:644
  264.3 28.6 %collective-permute-start.42 = (bf16[512,768]{1,0:T(8,128)(2,1)}, bf16[512,768]{1,0:T(8,128)(2,1)}, u32[]{:S(2)}, u32[]{:S(2)}) collective-permute-start(bf16[512,768]{1,0:T(8,128)(2,1)} %collective-permute-done.40.refs_4_), channel_id=1, source_target_pairs={{1,0},{2,1},{5,4},{6,5},{9,8},{10,9},{13,12},{14,13},{17,16},{18,1... | collective-permute-start | bytes 2359304 | tf_op jit(solution)/shard_map/ppermute | solution.py:645
  266.9 9.6 %collective-permute-start.45 = (bf16[1,96,768]{2,1,0:T(8,128)(2,1)S(1)}, bf16[1,96,768]{2,1,0:T(8,128)(2,1)S(1)}, u32[]{:S(2)}, u32[]{:S(2)}) collective-permute-start(bf16[1,96,768]{2,1,0:T(8,128)(2,1)S(1)} %get-tuple-element.383), channel_id=1, source_target_pairs={{0,8},{4,12},{8,0},{12,4},{1,9},{5,13},{9,1},{13,5},{2,10},{6,14},... | collective-permute-start | bytes 442376 | tf_op jit(solution)/shard_map/ppermute | solution.py:501
  270.2 7.8 %collective-permute-start.46 = (bf16[1,96,768]{2,1,0:T(8,128)(2,1)S(1)}, bf16[1,96,768]{2,1,0:T(8,128)(2,1)S(1)}, u32[]{:S(2)}, u32[]{:S(2)}) collective-permute-start(bf16[1,96,768]{2,1,0:T(8,128)(2,1)S(1)} %get-tuple-element.382), channel_id=1, source_target_pairs={{0,16},{16,0},{1,17},{17,1},{2,18},{18,2},{3,19},{19,3},{4,20},{20... | collective-permute-start | bytes 442376 | tf_op jit(solution)/shard_map/ppermute | solution.py:501
  273.4 6.2 %collective-permute-start.51 = (f32[9216]{0:T(1024)S(1)}, f32[9216]{0:T(1024)S(1)}, u32[]{:S(2)}, u32[]{:S(2)}) collective-permute-start(f32[9216]{0:T(1024)S(1)} %add.616), channel_id=1, source_target_pairs={{0,8},{4,12},{8,0},{12,4},{1,9},{5,13},{9,1},{13,5},{2,10},{6,14},... | collective-permute-start | bytes 110600 | tf_op jit(solution)/shard_map/ppermute | solution.py:501
  276.5 21.5 %collective-permute-start.57 = (bf16[2,96,768]{2,1,0:T(8,128)(2,1)S(1)}, bf16[2,96,768]{2,1,0:T(8,128)(2,1)S(1)}, u32[]{:S(2)}, u32[]{:S(2)}) collective-permute-start(bf16[2,96,768]{2,1,0:T(8,128)(2,1)S(1)} %get-tuple-element.352), channel_id=1, source_target_pairs={{0,16},{16,0},{1,17},{17,1},{2,18},{18,2},{3,19},{19,3},{4,20},{20... | collective-permute-start | bytes 884744 | tf_op jit(solution)/shard_map/ppermute | solution.py:501
  293.0 5.7 %collective-permute-start.58 = (f32[9216]{0:T(1024)S(1)}, f32[9216]{0:T(1024)S(1)}, u32[]{:S(2)}, u32[]{:S(2)}) collective-permute-start(f32[9216]{0:T(1024)S(1)} %add.617), channel_id=1, source_target_pairs={{0,16},{16,0},{1,17},{17,1},{2,18},{18,2},{3,19},{19,3},{4,20},{20... | collective-permute-start | bytes 110600 | tf_op jit(solution)/shard_map/ppermute | solution.py:501
  294.7 6.2 %collective-permute-start.54 = (bf16[96,768]{1,0:T(8,128)(2,1)S(1)}, bf16[96,768]{1,0:T(8,128)(2,1)S(1)}, u32[]{:S(2)}, u32[]{:S(2)}) collective-permute-start(bf16[96,768]{1,0:T(8,128)(2,1)S(1)} %get-tuple-element.318), channel_id=1, source_target_pairs={{0,3},{1,0},{2,1},{3,2},{4,7},{5,4},{6,5},{7,6},{8,11},{9,8},{10,9... | collective-permute-start | bytes 442376 | tf_op jit(solution)/shard_map/ppermute | solution.py:550
  294.9 15.4 %collective-permute-start.55 = (bf16[96,768]{1,0:T(8,128)(2,1)S(1)}, bf16[96,768]{1,0:T(8,128)(2,1)S(1)}, u32[]{:S(2)}, u32[]{:S(2)}) collective-permute-start(bf16[96,768]{1,0:T(8,128)(2,1)S(1)} %get-tuple-element.319), channel_id=1, source_target_pairs={{0,2},{1,3},{2,0},{3,1},{4,6},{5,7},{6,4},{7,5},{8,10},{9,11},{10,... | collective-permute-start | bytes 442376 | tf_op jit(solution)/shard_map/ppermute | solution.py:550
  297.9 12.4 %collective-permute-start.56 = (bf16[96,768]{1,0:T(8,128)(2,1)S(1)}, bf16[96,768]{1,0:T(8,128)(2,1)S(1)}, u32[]{:S(2)}, u32[]{:S(2)}) collective-permute-start(bf16[96,768]{1,0:T(8,128)(2,1)S(1)} %get-tuple-element.320), channel_id=1, source_target_pairs={{0,1},{1,2},{2,3},{3,0},{4,5},{5,6},{6,7},{7,4},{8,9},{9,10},{10,1... | collective-permute-start | bytes 442376 | tf_op jit(solution)/shard_map/ppermute | solution.py:550
  297.9 32.5 %collective-permute-start.52 = (bf16[512,768]{1,0:T(8,128)(2,1)}, bf16[512,768]{1,0:T(8,128)(2,1)S(1)}, u32[]{:S(2)}, u32[]{:S(2)}) collective-permute-start(bf16[512,768]{1,0:T(8,128)(2,1)} %collective-permute-done.41.refs_2_), channel_id=1, source_target_pairs={{2,3},{6,7},{10,11},{14,15},{18,19},{22,23},{26,27},{30,31}} | collective-permute-start | bytes 2359304 | tf_op jit(solution)/shard_map/ppermute | solution.py:644
  298.6 31.8 %collective-permute-start.53 = (bf16[512,768]{1,0:T(8,128)(2,1)}, bf16[512,768]{1,0:T(8,128)(2,1)S(1)}, u32[]{:S(2)}, u32[]{:S(2)}) collective-permute-start(bf16[512,768]{1,0:T(8,128)(2,1)} %collective-permute-done.42.refs_5_), channel_id=1, source_target_pairs={{1,0},{5,4},{9,8},{13,12},{17,16},{21,20},{25,24},{29,28}} | collective-permute-start | bytes 2359304 | tf_op jit(solution)/shard_map/ppermute | solution.py:645
  310.4 15.0 %collective-permute-start.59 = (bf16[96,768]{1,0:T(8,128)(2,1)S(1)}, bf16[96,768]{1,0:T(8,128)(2,1)S(1)}, u32[]{:S(2)}, u32[]{:S(2)}) collective-permute-start(bf16[96,768]{1,0:T(8,128)(2,1)S(1)} %get-tuple-element.350), channel_id=1, source_target_pairs={{0,16},{16,0},{1,17},{17,1},{2,18},{18,2},{3,19},{19,3},{4,20},{20... | collective-permute-start | bytes 442376 | tf_op jit(solution)/shard_map/ppermute | solution.py:501
  310.8 14.6 %collective-permute-start.60 = (f32[9216]{0:T(1024)S(1)}, f32[9216]{0:T(1024)S(1)}, u32[]{:S(2)}, u32[]{:S(2)}) collective-permute-start(f32[9216]{0:T(1024)S(1)} %add.621), channel_id=1, source_target_pairs={{0,1},{1,0},{2,3},{3,2},{4,5},{5,4},{6,7},{7,6},{8,9},{9,8},{10,11... | collective-permute-start | bytes 110600 | tf_op jit(solution)/shard_map/ppermute | solution.py:501
  325.5 4.9 %collective-permute-start.61 = (f32[9216]{0:T(1024)S(1)}, f32[9216]{0:T(1024)S(1)}, u32[]{:S(2)}, u32[]{:S(2)}) collective-permute-start(f32[9216]{0:T(1024)S(1)} %add.622), channel_id=1, source_target_pairs={{0,2},{1,3},{2,0},{3,1},{4,6},{5,7},{6,4},{7,5},{8,10},{9,11},{10,... | collective-permute-start | bytes 110600 | tf_op jit(solution)/shard_map/ppermute | solution.py:501
  (46 other events, 256.0 us)

commit v3 on v2

--- a/solution.py
+++ b/solution.py
@@ -13,6 +13,7 @@
 BF = jnp.bfloat16
 F32 = jnp.float32
 SHORT = pl.CostEstimate(flops=1000, bytes_accessed=1000, transcendentals=0)
+ROOM = {'attend': 36, 'rise': 36, 'fall': 36, 'back': 36, 'attend_back': 48}
 ROWS_BY_ROWS = (((1,), (1,)), ((), ()))
 
 
@@ -67,6 +68,7 @@
         ),
         out_shape=out_shape,
         cost_estimate=SHORT,
+        compiler_params=pltpu.CompilerParams(vmem_limit_bytes=ROOM.get(name, 60) * 2**20),
         name=name,
     )
 
@@ -93,13 +95,14 @@
         grown, inv = softmax_columns(dot(k[:, at], q_t[at]), allowed)
         parts.append(dot(v_t[at], grown.astype(BF)) * inv)
     context = jnp.concatenate(parts, 0).T.astype(BF)
-    count = len(out_refs)
+    count, rows, cols = len(out_refs), context.shape[0] // 2, context.shape[1]
     ahead = lax.rem(pl.program_id(0) + count - at_ref[3], count)
     for s, out_ref in enumerate(out_refs):
         @pl.when(ahead == s)
         def _():
-            out_ref[: context.shape[0]] = context
-            out_ref[context.shape[0] :] = extra_ref[...]
+            out_ref[:rows, :cols] = context[:rows]
+            out_ref[:rows, cols:] = context[rows:]
+            out_ref[rows:] = extra_ref[...]
 
 
 def attend(at, tokens, w_rows, bias, segments, heads, extra):
@@ -108,8 +111,8 @@
     return call(
         functools.partial(attend_kernel, heads, (cols // heads) ** -0.5), "attend", at, (seqs,),
         [slot(length, width), const(3, cols, width), const(2, cols), const(seqs, length), const(*extra.shape)],
-        [const(length + extra.shape[0], cols)] * seqs,
-        [jax.ShapeDtypeStruct((length + extra.shape[0], cols), BF)] * seqs,
+        [const(length // 2 + extra.shape[0], 2 * cols)] * seqs,
+        [jax.ShapeDtypeStruct((length // 2 + extra.shape[0], 2 * cols), BF)] * seqs,
     )(at, tokens, w_rows, bias, segments, extra)
 
 
@@ -171,10 +174,14 @@
 
     @pl.when(step == 0)
     def _():
-        rows = low_ref.shape[0]
-        attention = dot(ctx_refs[0][:rows], w_out_ref[0])
-        for s in range(1, slots):
-            attention += dot(ctx_refs[s][:rows], w_out_ref[s])
+        rows, cols = low_ref.shape[0] // 2, w_out_ref.shape[1]
+        sides = []
+        for side in (slice(0, cols), slice(cols, None)):
+            share = dot(ctx_refs[0][:rows, side], w_out_ref[0])
+            for s in range(1, slots):
+                share += dot(ctx_refs[s][:rows, side], w_out_ref[s])
+            sides.append(share)
+        attention = jnp.concatenate(sides)
         own = x_ref[0].astype(F32)
         norm, recip = normalize(own + attention + shifts_ref[0:1])
         hidden = norm * gains_ref[0:1] + shifts_ref[1:2]
@@ -192,7 +199,7 @@
 
 
 def rise(at, ctx, w_out, x, gains, shifts, w_in, bias):
-    slots, cols, rows = len(ctx), ctx[0].shape[1], x.shape[1]
+    slots, cols, rows = len(ctx), w_out.shape[1], x.shape[1]
     width, hidden = w_in[0].shape
     return call(
         functools.partial(rise_kernel, slots), "rise", at, (slots,),
@@ -244,11 +251,14 @@
         def _():
             for copy in pair:
                 copy.wait()
-            share = dot(act_ref[0], held[i].reshape(8 * held.shape[3], held.shape[4]))
-            if i:
-                sum_ref[...] += share
-            else:
-                sum_ref[...] = share
+
+    @pl.when(s == 0)
+    def _():
+        sum_ref[...] = jnp.zeros_like(sum_ref)
+
+    @pl.when(s < slots)
+    def _():
+        sum_ref[...] += dot(act_ref[0], held[s].reshape(8 * held.shape[3], held.shape[4]))
 
     @pl.when(s == slots - 1)
     def _():
@@ -354,7 +364,7 @@
 def attend_back_kernel(first, slots, heads, scale, at_ref, x_ref, low_ref, grad_ref, *refs):
     ctx_refs = refs[:slots]
     (own_ref, mine_ref, theirs_ref, bias_ref, w_out_ref, seg_ref, x_rel_ref, grad_rel_ref,
-     vec_ref, tok_ref, keep_ref, send_ref, sum_ref, q_ref, k_ref, v_ref, proj_ref, held, sems) = refs[slots:]
+     vec_ref, tok_ref, keep_ref, send_ref, sum_ref, q_ref, k_ref, v_ref, ctx_ref, proj_ref, held, sems) = refs[slots:]
     s = pl.program_id(0)
     half = mine_ref.shape[-1]
     mine_at = pl.ds(pl.multiple_of(at_ref[0] * half, half), half)
@@ -383,10 +393,11 @@
         def _():
             for copy in pair:
                 copy.wait()
-            store_parts(
-                keep_ref, send_ref, i < slots // 2, proj_ref.shape[1], dot(grad_rel_ref[...], ctx_refs[i][: x_ref.shape[1]])
-            )
-
+            rows, cols = ctx_ref.shape[0] // 2, ctx_ref.shape[1]
+            ctx_ref[:rows] = ctx_refs[i][:rows, :cols]
+            ctx_ref[rows:] = ctx_refs[i][:rows, cols:]
+
+    store_parts(keep_ref, send_ref, s < slots // 2, proj_ref.shape[1], dot(grad_rel_ref[...], ctx_ref[...]))
     x, low = x_ref[0], low_ref[...]
     cols = w_out_ref.shape[1]
     size = cols // heads
@@ -458,7 +469,7 @@
         ],
         [
             pltpu.VMEM((rows, width), F32), pltpu.VMEM((cols, rows), F32), pltpu.VMEM((rows, cols), F32),
-            pltpu.VMEM((rows, cols), F32), pltpu.VMEM((rows, 3 * cols), BF),
+            pltpu.VMEM((rows, cols), F32), pltpu.VMEM((rows, cols), BF), pltpu.VMEM((rows, 3 * cols), BF),
             pltpu.VMEM((slots, 4, piece, width), BF), pltpu.SemaphoreType.DMA((slots, 2)),
         ],
     )(at, x, low, grad, *ctx, own.reshape(4, piece, width), split(mine), split(theirs), bias, w_out, segments, x_rel, grad_rel)
@@ -484,6 +495,34 @@
 
     pltpu.make_async_copy(sources[0], held.at[step], sems.at[step]).wait()
     out_ref[0] = held[step].astype(out_ref.dtype)
+
+
+def place_end_kernel(slots, at_ref, own_ref, behind_ref, ahead_ref, whole_ref, out_ref, held, sem):
+    here = at_ref[3]
+    for source, wanted in ((ahead_ref, here == 0), (behind_ref, here == slots - 1), (own_ref, lax.rem(here, slots - 1) > 0)):
+        @pl.when(wanted)
+        def _():
+            copy = pltpu.make_async_copy(source, held, sem)
+            copy.start()
+            copy.wait()
+
+    out_ref[0] = held[...].astype(out_ref.dtype)
+
+
+def place_end(at, own, behind, ahead, whole):
+    slots = whole.shape[0]
+    spot = lambda i, at: (jnp.where(at[3] == 0, slots - 1, jnp.where(at[3] == slots - 1, 0, at[3])), 0, 0)
+    return pl.pallas_call(
+        functools.partial(place_end_kernel, slots),
+        grid_spec=pltpu.PrefetchScalarGridSpec(
+            num_scalar_prefetch=1, grid=(1,), in_specs=[FAR] * 4, out_specs=pl.BlockSpec((1, *own.shape), spot),
+            scratch_shapes=[pltpu.VMEM(own.shape, own.dtype), pltpu.SemaphoreType.DMA],
+        ),
+        out_shape=jax.ShapeDtypeStruct(whole.shape, whole.dtype),
+        input_output_aliases={4: 0},
+        cost_estimate=SHORT,
+        name="place_end",
+    )(at, own, behind, ahead, whole)
 
 
 def place(at, own, behind, ahead, kind):
@@ -580,29 +619,31 @@
         first = jnp.concatenate([piece_of(w_out), piece_of(w_in), piece_of(w_down)])
         first_z = [cyclic(first, s) for s in others]
         done(first)
+        piece_qkv = lax.dynamic_slice(
+            hold(flat_qkv), ((y * 2 + x) * (flat_qkv.shape[0] // 4), core * half), (flat_qkv.shape[0] // 4, half)
+        )
         biases = jnp.concatenate([b_inner.reshape(-1), b_qv.reshape(-1)])
-        bias_rows = -(-biases.size // head_cols)
-        bias_pack = in_three(jnp.pad(hold(biases), (0, bias_rows * head_cols - biases.size)).reshape(bias_rows, head_cols))
-        bias_pack = jnp.pad(bias_pack.reshape(3 * bias_rows, head_cols), ((0, -3 * bias_rows % 16), (0, 0)))
-
-        context = attend(at, hold(tokens), qkv_rows, b_qv.reshape(2, head_cols), segments, heads, bias_pack)
+        bias_rows = -(-biases.size // half)
+        bias_pack = in_three(jnp.pad(hold(biases), (0, bias_rows * half - biases.size)).reshape(bias_rows, half))
+        bias_pack = jnp.pad(bias_pack.reshape(3 * bias_rows, half), ((0, -3 * bias_rows % 16), (0, 0)))
+        extra = jnp.concatenate([bias_pack, piece_qkv])
+
+        context = attend(at, hold(tokens), qkv_rows, b_qv.reshape(2, head_cols), segments, heads, extra)
         (ctx_own, *ctx_send), first_z = run((context, first_z))
         ctx_z = [cyclic(v, s) for v, s in zip(ctx_send, others)]
         cut, end = w_out.shape[0] // 8, (w_out.shape[0] + w_in.shape[0]) // 8
         a, b = halves(first_z, slice(0, end))
         a1, b1 = by_x(a), by_y(b)
         c, d = halves(first_z, slice(end, None))
-        piece_qkv = lax.dynamic_slice(
-            hold(flat_qkv), ((y * 2 + x) * (flat_qkv.shape[0] // 4), core * half), (flat_qkv.shape[0] // 4, half)
-        )
-        done(c, d, piece_qkv, a1, b1)
+        done(c, d, a1, b1)
         a, b = plane_two(*hold((a, b, a1, b1)))
         a1, b1 = by_y(a), by_x(b)
         done(a, b, *ctx_z)
         ctx_z = hold(ctx_z)
         c1, d1 = by_x(hold(c)), by_y(hold(d))
-        bias_got = jnp.stack([p[seq_len : seq_len + 3 * bias_rows] for p in ctx_z]).astype(F32)
-        bias_got = bias_got.reshape(n_tensor - 1, 3, bias_rows * head_cols)
+        top = seq_len // 2
+        bias_got = jnp.stack([p[top : top + 3 * bias_rows] for p in ctx_z]).astype(F32)
+        bias_got = bias_got.reshape(n_tensor - 1, 3, bias_rows * half)
         bias_got = bias_got[:, 0] + bias_got[:, 1] + bias_got[:, 2]
         bias_all = jnp.concatenate([biases[None], bias_got[:, : biases.size]])
         b_inner_all = bias_all[:, :hidden_cols]
@@ -613,7 +654,6 @@
         in_core = by_core(in_both)
         out_both = plane_three(a, b, a1, b1, slice(0, cut))
         out_core = by_core(out_both)
-        third_z = [cyclic(hold(piece_qkv), s) for s in others]
         done(in_both, out_both, c1, d1)
         c, d = plane_two(*hold((c, d, c1, d1)))
         c1, d1 = by_y(c), by_x(d)
@@ -621,15 +661,17 @@
         out_got = ordered(*hold((out_both, out_core)), core, 0).transpose(3, 0, 1, 2, 4, 5)
         out_all = jnp.concatenate([w_out[None], out_got.reshape(n_tensor - 1, *w_out.shape)])
         in_parts = (w_in, in_both, in_core)
-        done(out_all, in_core)
+        e = jnp.stack([p[-piece_qkv.shape[0] :] for p in ctx_z])
+        e1 = by_x(e)
+        done(out_all, in_core, e)
         ctx = [ctx_own, *ctx_z]
         made = rise(at, hold(ctx), out_all, tokens, gains, shifts, in_parts, b_inner_all)
-        made, c1, d1, third_z = run((made, c1, d1, third_z))
+        made, c1, d1, e1 = run((made, c1, d1, e1))
         hidden1, hidden_low, norm_one, recip_one, activation, slope, tokens_rel, hidden_rel = made
         down_both = plane_three(c, d, c1, d1, slice(None))
         down_core = by_core(down_both)
-        e = jnp.stack(third_z)
-        e1 = by_x(e)
+        e = ordered(e, e1, x, 0)
+        e1 = by_y(e)
         done(down_both, down_core, e)
         down_parts = (w_down, down_both, down_core)
         made = fall(at, hold(activation), down_parts, hidden1, cotangent, gains, shifts)
@@ -683,13 +725,15 @@
                     p.take(flat[first : first + size])
                     first += size
 
-        def z_units(total):
-            return [cyclic(total[s], n_tensor - s) for s in others]
-
-        def last_sum(mine, got):
-            mine = mine.astype(F32)
-            for v in got:
-                mine = mine + v.astype(F32)
+        z_near = lambda v: swap(v, "tensor", n_tensor, 1)
+        z_far = lambda v: swap(v, "tensor", n_tensor, 2)
+        odd = (z & 1) == 1
+
+        def after_near(values, got):
+            first, second = jnp.where(odd, got[1], got[0]), jnp.where(odd, got[0], got[1])
+            return values[0].astype(F32) + first.astype(F32), values[1].astype(F32) + second.astype(F32)
+
+        def outer_rest(mine):
             bit = 2
             while bit < n_outer:
                 mine = mine + swap(mine.astype(BF), "outer", n_outer, bit).astype(F32)
@@ -701,27 +745,25 @@
 
         out_1 = hop(output_own, output_own, 0)
         core1 = by_core(send1)
-        e = ordered(e, e1, x, 0)
-        e1 = by_y(e)
-        done(e, core1)
+        qkv_both = ordered(e, e1, y, 0)
+        qkv_core = by_core(qkv_both)
+        qkv_parts = (flat_qkv, qkv_both, qkv_core)
+        done(qkv_both, core1)
         h1 = pair_of(*hold((keep1, core1)))
         flight = plane([h1[0]], [h1[1]])
         made = back(
             at, hold(grad_r2), grad_r2_low, down_parts, slope, in_parts, norm_one, recip_one, gains, hidden_rel
         )
-        made, e1, out_1, flight = run((made, e1, out_1, flight))
+        made, qkv_core, out_1, flight = run((made, qkv_core, out_1, flight))
+        qkv_parts = (flat_qkv, qkv_both, qkv_core)
         grad_binner, grad_r1, grad_r1_low, grad_r1_rel, vec_one, keep2, send2 = made
         out_2 = hop(*out_1, 1)
         core2 = by_core(send2)
-        qkv_both = ordered(e, e1, y, 0)
-        qkv_core = by_core(qkv_both)
-        qkv_parts = (flat_qkv, qkv_both, qkv_core)
         landed(flight, [h1[0]], [h1[1]])
-        done(qkv_both, core2)
+        done(core2)
         h2 = pair_of(*hold((keep2, core2)))
         groups = [h2[0], h1[1]], [h2[1], h1[0]]
         flight = plane(*groups)
-        done(*order.last, qkv_core)
         two = n_tensor // 2
         made = attend_back(
             at, 0, tokens, hold(grad_r1_low), grad_r1, ctx[:two], qkv_parts, b_qv_all, heads, out_all, segments,
@@ -733,7 +775,8 @@
         core_a = by_core(send_a)
         landed(flight, *groups)
         total1 = h1[0].totals() + h1[1].totals()
-        done(*total1, core_a)
+        near1 = z_near(jnp.stack([total1[1], total1[3]]))
+        done(core_a)
         ha = pair_of(*hold((keep_a, core_a)))
         groups = [ha[0], h2[1]], [ha[1], h2[0]]
         flight = plane(*groups)
@@ -741,82 +784,87 @@
             at, two, tokens, hold(grad_r1_low), tok_a, ctx[two:], qkv_parts, b_qv_all, heads, out_all, segments,
             tokens_rel, grad_r1_rel, BF,
         )
-        made, out_3, flight = run((made, out_3, flight))
+        made, out_3, flight, near1 = run((made, out_3, flight, near1))
         bqv_b, tok_own, keep_b, send_b = made
         tok_1 = hop(tok_own, tok_own, 0)
         core_b = by_core(send_b)
         landed(flight, *groups)
+
         grad_bqv = jnp.concatenate([bqv_a, bqv_b])
-
-        slot_vec = jnp.concatenate([grad_binner.reshape(n_tensor, -1), grad_bqv.reshape(n_tensor, -1)], 1)
-        placed = jnp.zeros_like(slot_vec)
-        for s in range(n_tensor):
-            placed = lax.dynamic_update_index_in_dim(placed, slot_vec[s], z_from(s), 0)
-        common = jnp.stack([vec_one[0], vec_two[0], vec_one[1], vec_one[2], vec_two[1], vec_two[2]])
-        vectors = [jnp.concatenate([placed.reshape(-1), common.reshape(-1)])]
-        rounds = [
-            (axis, size, 1 << i)
-            for axis, size in (("local", n_local), ("outer", n_outer), ("tensor", n_tensor))
-            for i in range(size.bit_length() - 1)
+        slot_vec = [
+            jnp.concatenate([grad_binner[s].reshape(-1, half), grad_bqv[s].reshape(-1, half)]) for s in range(n_tensor)
         ]
-
-        def vector_round(count=1):
-            for _ in range(count):
-                if len(vectors) > 1:
-                    vectors[:] = [vectors[0] + hold(vectors[1])]
-                if rounds:
-                    vectors.append(swap(vectors[0], *rounds.pop(0)))
-
-        total2 = h2[0].totals() + h2[1].totals()
-        total12 = [jnp.stack(pair) for pair in zip(total1, total2)]
-        z12 = z_units(total12)
-        done(*total12, core_b)
+        common = jnp.concatenate([vec_one, vec_two]).reshape(-1, half)
+        n_slot = slot_vec[0].shape[0]
+        vec_got = z_near(jnp.concatenate([slot_vec[1], slot_vec[3], common]))
+        done(core_b)
         hb = pair_of(*hold((keep_b, core_b)))
         groups = [hb[0], ha[1]], [hb[1], ha[0]]
         flight = plane(*groups)
+        total2 = h2[0].totals() + h2[1].totals()
+        near2 = jnp.stack([total2[1], total2[3]])
+        mine1, far1 = after_near((total1[0], total1[2]), near1)
         outs = hold((output_own, out_1, out_2, out_3))
         output = place(at, outs[0], [v[0] for v in outs[1:]], [v[1] for v in outs[1:]], BF)
-        output, tok_1 = run((output.reshape(seq_count, seq_len, width), tok_1))
+        output = output.reshape(seq_count, seq_len, width)
+        output, tok_1, flight, vec_got = run((output, tok_1, flight, vec_got))
         tok_2 = hop(*tok_1, 1)
-        vector_round()
-        done(*order.last, *flight)
-        landed(hold(flight), *groups)
+        landed(flight, *groups)
         groups = [hb[1]], [hb[0]]
         flight = plane(*groups)
-        done(*order.last, *z12, *vectors)
-        mine12 = last_sum(total12[0], hold(z12))
+        near2 = z_near(hold(near2))
+        vec_got = vec_got[: 2 * n_slot].reshape(2, n_slot, half), vec_got[2 * n_slot :]
+        vec_0, vec_2 = after_near((slot_vec[0], slot_vec[2]), vec_got[0])
+        common = common + vec_got[1]
+        vec_send = jnp.concatenate([vec_2, common])
+        done(vec_send, *flight)
+        landed(hold(flight), *groups)
+        total3 = [t for part in (*ha, *hb) for t in part.totals()]
+        near3 = z_near(jnp.stack([total3[1], total3[3]]))
+        vec_got = z_far(hold(vec_send))
+        done(*total3, near2)
+        mine2, far2 = after_near((total2[0], total2[2]), hold(near2))
+        far12 = z_far(jnp.stack([far1, far2]).astype(BF))
+        done(far2, *tok_2, vec_got, near3)
+        tok_3 = hop(*hold(tok_2), 2)
+        mine3, far3 = after_near((total3[0], total3[2]), hold(near3))
+        far3 = z_far(far3.astype(BF))
+        vectors = jnp.concatenate([vec_0, common]) + hold(vec_got)
+        vec_got = by_core(vectors)
+        done(far3, far12, vec_got)
+        mine12 = outer_rest(jnp.stack([mine1, mine2]) + hold(far12).astype(F32))
         got12 = by_y(mine12.astype(BF))
-        vector_round()
-        done(mine12, *flight)
-        landed(hold(flight), *groups)
-        total3 = hold([t for part in (*ha, *hb) for t in part.totals()])
-        z3 = z_units(total3)
-        done(*total3, *tok_2, *vectors)
-        tok_3 = hop(*hold(tok_2), 2)
-        vector_round()
-        done(got12, *vectors)
-        vector_round()
-        got12 = hold(got12)
+        vectors = vectors + hold(vec_got)
+        vec_got = by_x(vectors)
+        mine3 = outer_rest(mine3 + hold(far3).astype(F32))
+        got3 = by_y(mine3.astype(BF))
+        tok_held = hold((tok_own, (tok_1[0], tok_2[0], tok_2[0]), (tok_1[1], tok_2[1], tok_2[1])))
+        grad_tokens = place(at, *tok_held, F32)
+        done(grad_tokens, got12, got3, vec_got)
+        got12, got3, vec_got = hold((got12, got3, vec_got))
+        vectors = vectors + vec_got
+        vec_got = by_y(vectors)
         done_wdown = whole_rows(mine12[0], got12[0])
         done_win = whole_rows(mine12[1], got12[1])
-        done(done_wdown, done_win, *z3)
-        mine3 = last_sum(total3[0], hold(z3))
-        got3 = by_y(mine3.astype(BF))
-        done(mine3, got3, *vectors)
-        vector_round()
-        done_last = whole_rows(mine3, hold(got3))
-        done(done_last, *tok_3)
-        grad_tokens = place(at, *hold((tok_own, (tok_1[0], tok_2[0], tok_3[0]), (tok_1[1], tok_2[1], tok_3[1]))), F32)
-        grad_tokens = grad_tokens.reshape(seq_count, seq_len, width)
-        vector_round(len(rounds) + 1)
-        vectors = vectors[0]
-        slot_sum = pick(vectors[: placed.size].reshape(placed.shape), z)
-        common = vectors[placed.size :].reshape(common.shape)
+        done(done_wdown, done_win, vec_got)
+        got3 = hold(got3)
+        done_last = whole_rows(mine3, got3)
+        vectors = vectors + hold(vec_got)
+        bit = 2
+        while bit < n_outer:
+            vectors = vectors + swap(vectors, "outer", n_outer, bit)
+            bit *= 2
+        slot_sum = vectors[:n_slot].reshape(-1)
+        common = vectors[n_slot:].reshape(6, width)
+        common = jnp.stack([common[i] for i in (0, 3, 1, 2, 4, 5)])
         part = lambda v, n: lax.dynamic_slice_in_dim(v, l_index * (n // n_local), n // n_local, v.ndim - 1)
         binner = part(slot_sum[:hidden_cols].reshape(b_inner.shape), head_size)
         bqv = part(slot_sum[hidden_cols:].reshape(b_qv.shape), head_size)
         common = part(common, width)
         grad_wqkv = done_last[:, : 3 * head_cols].reshape(width // n_local, 3, head_cols).transpose(1, 0, 2)
+        done(grad_wqkv, common, binner, bqv, *tok_3)
+        grad_tokens = place_end(at, *hold((tok_own, tok_3[0], tok_3[1], grad_tokens)))
+        grad_tokens = grad_tokens.reshape(seq_count, seq_len, width)
         return (
             output,
             grad_tokens,

time: 345 us -> 315 us (0.913)
  Pallas kernels: 107 us -> 92.5 us
  local copies, waits for them, and re-layouts: 34.4 us -> 20.7 us
    ppermute x15 -> x6, starting transfers between devices: 39.9 us -> 17.2 us  [local(): lax.ppermute(v, 'tensor', [(i, (i + s) % n_tensor) for i in range(n_tenso...]
    ppermute x35 -> x40, waiting for transfers between devices: 23.4 us -> 42.6 us  [swap(): return lax.ppermute(value, axis, [(i, i ^ bit) for i in range(size)])]
    ppermute x35 -> x40, starting transfers between devices: 26.6 us -> 44.4 us  [swap(): return lax.ppermute(value, axis, [(i, i ^ bit) for i in range(size)])]
    ppermute x6, waiting for transfers between devices: 13.9 us -> 4.6 us  [hop(): lax.ppermute(left, 'tensor', back_steps[:len(steps) - step])]
    ppermute x15 -> x6, waiting for transfers between devices: 28.1 us -> 19.8 us  [local(): lax.ppermute(v, 'tensor', [(i, (i + s) % n_tensor) for i in range(n_tenso...]
    dynamic_update_slice x4 -> x0, local copies, waits for them, and re-layouts: 5.41 us -> none  [local(): placed = lax.dynamic_update_index_in_dim(placed, slot_vec[s], z_from(s), 0)]
    pallas_call x1, Pallas kernels: 15.5 us -> 11 us  [fall(): call(functools.partial(fall_kernel, slots), 'fall', at, (2 * slots,), [pl...]
    pallas_call x1, Pallas kernels: 18.9 us -> 14.6 us  [back(): call(functools.partial(back_kernel, slots), 'back', at, (slots,), [const(...]
  transfers between devices with their start and end apart: 62 -> 58, of which waited for: 12 -> 17; matrix products, arithmetic and copies ran while one was open for 18% -> 13% of each run, Pallas kernels for 30% -> 29%
where the time goes in v3:
time: 315 us; the launch traced here: 309 us
  Pallas kernels  92.5 us (29%)
  starting transfers between devices  87.4 us (28%)
  waiting for transfers between devices  67 us (21%)
  other arithmetic  39.2 us (12%)
  local copies, waits for them, and re-layouts  20.7 us (7%)
    ppermute x40, starting transfers between devices, swap(): return lax.ppermute(value, axis, [(i, i ^ bit) for i in range(size)])  44.4 us
    ppermute x40, waiting for transfers between devices, swap(): return lax.ppermute(value, axis, [(i, i ^ bit) for i in range(size)])  42.6 us
    pallas_call x2, Pallas kernels, attend_back(): call(functools.partial(attend_back_kernel, first, slots, heads, (cols //...  33.6 us
    ppermute x6, waiting for transfers between devices, local(): lax.ppermute(v, 'tensor', [(i, (i + s) % n_tensor) for i in range(n_tenso...  19.8 us
    ppermute x6, starting transfers between devices, hop(): lax.ppermute(right, 'tensor', steps[step:])  17.6 us
    ppermute x6, starting transfers between devices, local(): lax.ppermute(v, 'tensor', [(i, (i + s) % n_tensor) for i in range(n_tenso...  17.2 us
    convert_element_type x10, other arithmetic, total(): return functools.reduce(lambda u, v: u + v, terms).astype(BF)  15.8 us
    pallas_call x1, Pallas kernels, back(): call(functools.partial(back_kernel, slots), 'back', at, (slots,), [const(...  14.6 us
  transfers between devices with their start and end apart: 58, of which 17 were waited for; matrix products, arithmetic and copies ran while one was open for 13% of the time, Pallas kernels for 29%

profile of v3, /device:TPU:0, one launch (start us, length us, event | category | flops | bytes accessed | tf_op | source)
XLA Modules:
  0.0 309.4 jit_solution(16207084334926403449)
XLA Ops:
  3.3 3.0 collective-permute-start
  6.3 2.6 collective-permute-start.1
  8.9 1.3 collective-permute-start.2
  12.1 1.9 copy-done
  14.0 10.9 %attend.1 = (bf16[416,384]{1,0:T(8,128)(2,1)S(1)}, bf16[416,384]{1,0:T(8,128)(2,1)S(1)}, bf16[416,384]{1,0:T(8,128)(2,1)S(1)}, bf16[416,384]{1,0:T(8,128)(2,1)S(1)}) custom-call(s32[4]{0:T(128)S(1)} %pad_add_fusion.at_ref, bf16[4,512,768]{2,1,0:T(8,128)(2,1)S(1)} %copy-done, bf16[3,192,768]{2,1,0:T(8,128)(2,1)S(1)} %bitcast.310, ...), custom_call_target="tpu_custom_call" | custom-call | flops 1000 | bytes 1000 | tf_op jit(solution)/shard_map/attend/pallas_call | solution.py:111
  25.6 5.1 %collective-permute-done.1 = bf16[216,768]{1,0:T(8,128)(2,1)S(1)} collective-permute-done((bf16[216,768]{1,0:T(8,128)(2,1)}, bf16[216,768]{1,0:T(8,128)(2,1)S(1)}, u32[]{:S(2)}, u32[]{:S(2)}) %collective-permute-start.1) | collective-permute-done | bytes 331808 | tf_op jit(solution)/shard_map/ppermute | solution.py:589
  30.9 1.6 collective-permute-start.7
  32.5 1.6 collective-permute-start.6
  34.1 7.6 %collective-permute-start.3 = (bf16[416,384]{1,0:T(8,128)(2,1)S(1)}, bf16[416,384]{1,0:T(8,128)(2,1)S(1)}, u32[]{:S(2)}, u32[]{:S(2)}) collective-permute-start(bf16[416,384]{1,0:T(8,128)(2,1)S(1)} %get-tuple-element.182), channel_id=1, source_target_pairs={{0,1},{1,2},{2,3},{3,0},{4,5},{5,6},{6,7},{7,4},{8,9},{9,10},{10,1... | collective-permute-start | bytes 958472 | tf_op jit(solution)/shard_map/ppermute | solution.py:589
  41.7 1.6 collective-permute-start.4
  48.0 3.3 %collective-permute-done.3.refs_1_ = bf16[416,384]{1,0:T(8,128)(2,1)S(1)} collective-permute-done((bf16[416,384]{1,0:T(8,128)(2,1)S(1)}, bf16[416,384]{1,0:T(8,128)(2,1)S(1)}, u32[]{:S(2)}, u32[]{:S(2)}) %collective-permute-start.3) | collective-permute-done | bytes 319520 | tf_op jit(solution)/shard_map/ppermute | solution.py:589
  51.3 11.3 %collective-permute-done.4.refs_2_.refs_0_ = bf16[416,384]{1,0:T(8,128)(2,1)S(1)} collective-permute-done((bf16[416,384]{1,0:T(8,128)(2,1)S(1)}, bf16[416,384]{1,0:T(8,128)(2,1)S(1)}, u32[]{:S(2)}, u32[]{:S(2)}) %collective-permute-start.4) | collective-permute-done | bytes 319520 | tf_op jit(solution)/shard_map/ppermute | solution.py:589
  67.5 1.6 collective-permute-start.16
  71.1 2.5 collective-permute-done.12
  73.7 1.6 collective-permute-done.11
  76.0 1.6 collective-permute-start.14
  79.5 10.5 %rise.1 = (f32[512,768]{1,0:T(8,128)S(1)}, bf16[512,768]{1,0:T(8,128)(2,1)}, f32[512,768]{1,0:T(8,128)S(1)}, f32[512,1]{1,0:T(8,128)S(1)}, bf16[4,512,768]{2,1,0...) custom-call(s32[4]{0:T(128)S(1)} %pad_add_fusion.at_ref, ...), custom_call_target="tpu_custom_call" | custom-call | flops 1000 | bytes 1000 | tf_op jit(solution)/shard_map/rise/pallas_call | solution.py:204
  92.9 2.4 collective-permute-done.17
  95.5 11.0 %fall.1 = (bf16[512,768]{1,0:T(8,128)(2,1)S(1)}, f32[512,768]{1,0:T(8,128)S(1)}, bf16[512,768]{1,0:T(8,128)(2,1)S(1)}, f32[3,768]{1,0:T(4,128)S(1)}, bf16[4,4,96...) custom-call(s32[4]{0:T(128)S(1)} %pad_add_fusion.at_ref, ...), custom_call_target="tpu_custom_call" | custom-call | flops 1000 | bytes 1000 | tf_op jit(solution)/shard_map/fall/pallas_call | solution.py:290
  106.5 2.7 collective-permute-done.18
  110.1 10.3 %collective-permute-start.21 = (bf16[512,768]{1,0:T(8,128)(2,1)S(1)}, bf16[512,768]{1,0:T(8,128)(2,1)}, u32[]{:S(2)}, u32[]{:S(2)}) collective-permute-start(bf16[512,768]{1,0:T(8,128)(2,1)S(1)} %get-tuple-element.290.refs_0_), channel_id=1, source_target_pairs={{0,1},{1,2},{2,3},{4,5},{5,6},{6,7},{8,9},{9,10},{10,11},{12,13},{... | collective-permute-start | bytes 2359304 | tf_op jit(solution)/shard_map/ppermute | solution.py:686
  120.4 1.5 collective-permute-start.22
  121.9 1.5 add_convert_fusion.2
  123.5 1.6 collective-permute-start.23
  125.5 14.6 %back.1 = (f32[4,1,768]{2,1,0:T(1,128)S(1)}, f32[512,768]{1,0:T(8,128)S(1)}, bf16[512,768]{1,0:T(8,128)(2,1)S(1)}, bf16[768,512]{1,0:T(8,128)(2,1)S(1)}, f32[3,7...) custom-call(s32[4]{0:T(128)S(1)} %pad_add_fusion.at_ref, ...), custom_call_target="tpu_custom_call" | custom-call | flops 1000 | bytes 1000 | tf_op jit(solution)/shard_map/back/pallas_call | solution.py:345
  140.2 1.5 collective-permute-done.22.refs_4_
  141.9 2.5 fusion.2
  144.4 2.3 collective-permute-done.25
  146.7 1.5 add_convert_fusion
  152.3 1.6 collective-permute-start.26
  153.8 1.3 collective-permute-start.27
  156.4 16.8 %attend_back.2 = (f32[2,2,192]{2,1,0:T(2,128)S(1)}, f32[512,768]{1,0:T(8,128)}, bf16[4,2,96,768]{3,2,1,0:T(8,128)(2,1)S(1)}, bf16[4,2,96,768]{3,2,1,0:T(8,128)(2,1)}) custom-call(s32[4]{0:T(128)S(1)} %pad_add_fusion.at_ref, bf16[4,512,768]{2,1,0:T(8,128)(2,1)} %x_ref.4, bf16[512,768]{1,0:T(8,128)(2,1)S(1)} %get-tuple-element.276.low_ref, ...), custom_call_target="tpu_custom_call" | custom-call | flops 1000 | bytes 1000 | tf_op jit(solution)/shard_map/attend_back/pallas_call | solution.py:457
  173.2 3.1 collective-permute-done.27.refs_5_
  176.3 1.5 collective-permute-start.31
  177.9 1.5 collective-permute-start.32
  179.4 1.6 fusion
  181.3 1.6 collective-permute-start.34
  183.5 1.5 fusion.41
  185.1 3.6 %collective-permute-start.35 = (bf16[2,96,768]{2,1,0:T(8,128)(2,1)S(1)}, bf16[2,96,768]{2,1,0:T(8,128)(2,1)}, u32[]{:S(2)}, u32[]{:S(2)}) collective-permute-start(bf16[2,96,768]{2,1,0:T(8,128)(2,1)S(1)} %pad_maximum_fusion.18), channel_id=1, source_target_pairs={{0,1},{1,0},{2,3},{3,2},{4,5},{5,4},{6,7},{7,6},{8,9},{9,8},{10,11... | collective-permute-start | bytes 884744 | tf_op jit(solution)/shard_map/ppermute | solution.py:540
  188.7 16.8 %attend_back.3 = (f32[2,2,192]{2,1,0:T(2,128)S(1)}, bf16[512,768]{1,0:T(8,128)(2,1)S(1)}, bf16[4,2,96,768]{3,2,1,0:T(8,128)(2,1)S(1)}, bf16[4,2,96,768]{3,2,1,0:T(8,128)(2,1)}) custom-call(s32[4]{0:T(128)S(1)} %pad_add_fusion.at_ref, bf16[4,512,768]{2,1,0:T(8,128)(2,1)} %x_ref.4, bf16[512,768]{1,0:T(8,128)(2,1)S(1)} %copy-done.9, ...), custom_call_target="tpu_custom_call" | custom-call | flops 1000 | bytes 1000 | tf_op jit(solution)/shard_map/attend_back/pallas_call | solution.py:457
  207.6 2.9 collective-permute-start.37
  211.8 2.5 fusion.36
  218.0 1.3 collective-permute-start.39
  219.6 2.7 collective-permute-start.41
  222.3 1.6 convert_add_fusion.10
  224.7 4.0 %place.2 = bf16[4,512,768]{2,1,0:T(8,128)(2,1)} custom-call(s32[4]{0:T(128)} %copy-done.34, bf16[512,768]{1,0:T(8,128)(2,1)} %copy-done.31, bf16[512,768]{1,0:T(8,128)(2,1)} %collective-permute-done.21.refs_1_, bf16[512,768]{1,0:T(8,128)(2,1)} %collective-permute-done.26.refs_2_, bf16[512,768]{1,0:T(8,128)(2,1)} %collective-permute-done.31.refs_3_, ...), custom_call_target="tpu_custom_call" | custom-call | flops 1000 | bytes 1000 | tf_op jit(solution)/shard_map/place/pallas_call | solution.py:531
  228.7 4.1 %collective-permute-done.41 = f32[18,384]{1,0:T(8,128)S(1)} collective-permute-done((f32[18,384]{1,0:T(8,128)S(1)}, f32[18,384]{1,0:T(8,128)S(1)}, u32[]{:S(2)}, u32[]{:S(2)}) %collective-permute-start.41) | collective-permute-done | bytes 27680 | tf_op jit(solution)/shard_map/ppermute | solution.py:540
  232.9 1.4 fusion.19
  235.4 1.5 collective-permute-start.45
  238.6 1.3 collective-permute-start.43
  240.8 1.3 collective-permute-done.46
  244.2 4.4 %collective-permute-start.47 = (f32[15,384]{1,0:T(8,128)S(1)}, f32[15,384]{1,0:T(8,128)S(1)}, u32[]{:S(2)}, u32[]{:S(2)}) collective-permute-start(f32[15,384]{1,0:T(8,128)S(1)} %pad_maximum_fusion.27), channel_id=1, source_target_pairs={{0,2},{1,3},{2,0},{3,1},{4,6},{5,7},{6,4},{7,5},{8,10},{9,11},{10,... | collective-permute-start | bytes 69128 | tf_op jit(solution)/shard_map/ppermute | solution.py:540
  248.6 1.7 convert_add_fusion.9
  250.5 2.0 collective-permute-start.52
  252.5 21.2 %collective-permute-done.47 = f32[15,384]{1,0:T(8,128)S(1)} collective-permute-done((f32[15,384]{1,0:T(8,128)S(1)}, f32[15,384]{1,0:T(8,128)S(1)}, u32[]{:S(2)}, u32[]{:S(2)}) %collective-permute-start.47) | collective-permute-done | bytes 23072 | tf_op jit(solution)/shard_map/ppermute | solution.py:540
  273.8 3.3 %collective-permute-start.51 = (bf16[96,768]{1,0:T(8,128)(2,1)S(1)}, bf16[96,768]{1,0:T(8,128)(2,1)S(1)}, u32[]{:S(2)}, u32[]{:S(2)}) collective-permute-start(bf16[96,768]{1,0:T(8,128)(2,1)S(1)} %fusion.17), channel_id=1, source_target_pairs={{0,2},{1,3},{2,0},{3,1},{4,6},{5,7},{6,4},{7,5},{8,10},{9,11},{10,... | collective-permute-start | bytes 442376 | tf_op jit(solution)/shard_map/ppermute | solution.py:540
  277.1 1.3 collective-permute-done.52
  278.4 1.7 collective-permute-done.51
  280.9 4.6 %collective-permute-start.54 = (bf16[2,96,768]{2,1,0:T(8,128)(2,1)}, bf16[2,96,768]{2,1,0:T(8,128)(2,1)}, u32[]{:S(2)}, u32[]{:S(2)}) collective-permute-start(bf16[2,96,768]{2,1,0:T(8,128)(2,1)} %get-tuple-element.354), channel_id=1, source_target_pairs={{0,16},{16,0},{1,17},{17,1},{2,18},{18,2},{3,19},{19,3},{4,20},{20... | collective-permute-start | bytes 884744 | tf_op jit(solution)/shard_map/ppermute | solution.py:540
  287.1 1.3 collective-permute-start.50
  288.4 4.8 %place.3.whole_ref = f32[4,512,768]{2,1,0:T(8,128)} custom-call(s32[4]{0:T(128)} %copy-done.34, bf16[512,768]{1,0:T(8,128)(2,1)} %copy-done.5, bf16[512,768]{1,0:T(8,128)(2,1)} %collective-permute-done.37.refs_1_, bf16[512,768]{1,0:T(8,128)(2,1)} %copy-done.38, bf16[512,768]{1,0:T(8,128)(2,1)} %copy-done.38, ...), custom_call_target="tpu_custom_call" | custom-call | flops 1000 | bytes 1000 | tf_op jit(solution)/shard_map/place/pallas_call | solution.py:531
  293.3 2.0 collective-permute-start.57
  301.2 1.7 copy.65
  305.9 3.0 place_end.1
  (308 shorter events, 55.2 us)
Async XLA Ops:
  3.3 22.3 %collective-permute-start = (bf16[216,768]{1,0:T(8,128)(2,1)}, bf16[216,768]{1,0:T(8,128)(2,1)S(1)}, u32[]{:S(2)}, u32[]{:S(2)}) collective-permute-start(bf16[216,768]{1,0:T(8,128)(2,1)} %pad_maximum_fusion.16), channel_id=1, source_target_pairs={{0,1},{1,2},{2,3},{3,0},{4,5},{5,6},{6,7},{7,4},{8,9},{9,10},{10,1... | collective-permute-start | bytes 995336 | tf_op jit(solution)/shard_map/ppermute | solution.py:589
  6.3 24.4 %collective-permute-start.1 = (bf16[216,768]{1,0:T(8,128)(2,1)}, bf16[216,768]{1,0:T(8,128)(2,1)S(1)}, u32[]{:S(2)}, u32[]{:S(2)}) collective-permute-start(bf16[216,768]{1,0:T(8,128)(2,1)} %pad_maximum_fusion.16), channel_id=1, source_target_pairs={{0,2},{1,3},{2,0},{3,1},{4,6},{5,7},{6,4},{7,5},{8,10},{9,11},{10,... | collective-permute-start | bytes 995336 | tf_op jit(solution)/shard_map/ppermute | solution.py:589
  8.9 21.8 %collective-permute-start.2 = (bf16[216,768]{1,0:T(8,128)(2,1)}, bf16[216,768]{1,0:T(8,128)(2,1)S(1)}, u32[]{:S(2)}, u32[]{:S(2)}) collective-permute-start(bf16[216,768]{1,0:T(8,128)(2,1)} %pad_maximum_fusion.16), channel_id=1, source_target_pairs={{0,3},{1,0},{2,1},{3,2},{4,7},{5,4},{6,5},{7,6},{8,11},{9,8},{10,9... | collective-permute-start | bytes 995336 | tf_op jit(solution)/shard_map/ppermute | solution.py:589
  12.1 176.6 %copy-start.34 = (s32[4]{0:T(128)}, s32[4]{0:T(128)S(1)}, u32[]{:S(2)}) copy-start(s32[4]{0:T(128)S(1)} %pad_add_fusion.at_ref) | copy-start | bytes 52
  30.9 14.2 %collective-permute-start.7 = (bf16[3,120,384]{2,1,0:T(8,128)(2,1)S(1)}, bf16[3,120,384]{2,1,0:T(8,128)(2,1)S(1)}, u32[]{:S(2)}, u32[]{:S(2)}) collective-permute-start(bf16[3,120,384]{2,1,0:T(8,128)(2,1)S(1)} %pad_maximum_fusion.23), channel_id=1, source_target_pairs={{0,16},{16,0},{1,17},{17,1},{2,18},{18,2},{3,19},{19,3},{4,20},{20... | collective-permute-start | bytes 829448 | tf_op jit(solution)/shard_map/ppermute | solution.py:540
  32.5 12.6 %collective-permute-start.6 = (bf16[3,120,384]{2,1,0:T(8,128)(2,1)S(1)}, bf16[3,120,384]{2,1,0:T(8,128)(2,1)S(1)}, u32[]{:S(2)}, u32[]{:S(2)}) collective-permute-start(bf16[3,120,384]{2,1,0:T(8,128)(2,1)S(1)} %pad_maximum_fusion.22), channel_id=1, source_target_pairs={{0,8},{4,12},{8,0},{12,4},{1,9},{5,13},{9,1},{13,5},{2,10},{6,14},... | collective-permute-start | bytes 829448 | tf_op jit(solution)/shard_map/ppermute | solution.py:540
  34.1 17.2 %collective-permute-start.3 = (bf16[416,384]{1,0:T(8,128)(2,1)S(1)}, bf16[416,384]{1,0:T(8,128)(2,1)S(1)}, u32[]{:S(2)}, u32[]{:S(2)}) collective-permute-start(bf16[416,384]{1,0:T(8,128)(2,1)S(1)} %get-tuple-element.182), channel_id=1, source_target_pairs={{0,1},{1,2},{2,3},{3,0},{4,5},{5,6},{6,7},{7,4},{8,9},{9,10},{10,1... | collective-permute-start | bytes 958472 | tf_op jit(solution)/shard_map/ppermute | solution.py:589
  41.7 21.0 %collective-permute-start.4 = (bf16[416,384]{1,0:T(8,128)(2,1)S(1)}, bf16[416,384]{1,0:T(8,128)(2,1)S(1)}, u32[]{:S(2)}, u32[]{:S(2)}) collective-permute-start(bf16[416,384]{1,0:T(8,128)(2,1)S(1)} %get-tuple-element.183), channel_id=1, source_target_pairs={{0,2},{1,3},{2,0},{3,1},{4,6},{5,7},{6,4},{7,5},{8,10},{9,11},{10,... | collective-permute-start | bytes 958472 | tf_op jit(solution)/shard_map/ppermute | solution.py:589
  43.3 19.4 %collective-permute-start.5 = (bf16[416,384]{1,0:T(8,128)(2,1)S(1)}, bf16[416,384]{1,0:T(8,128)(2,1)S(1)}, u32[]{:S(2)}, u32[]{:S(2)}) collective-permute-start(bf16[416,384]{1,0:T(8,128)(2,1)S(1)} %get-tuple-element.184), channel_id=1, source_target_pairs={{0,3},{1,0},{2,1},{3,2},{4,7},{5,4},{6,5},{7,6},{8,11},{9,8},{10,9... | collective-permute-start | bytes 958472 | tf_op jit(solution)/shard_map/ppermute | solution.py:589
  46.0 16.9 %collective-permute-start.9 = (bf16[2,3,120,384]{3,2,1,0:T(8,128)(2,1)}, bf16[2,3,120,384]{3,2,1,0:T(8,128)(2,1)}, u32[]{:S(2)}, u32[]{:S(2)}) collective-permute-start(bf16[2,3,120,384]{3,2,1,0:T(8,128)(2,1)} %pad_maximum_fusion.11), channel_id=1, source_target_pairs={{0,8},{4,12},{8,0},{12,4},{1,9},{5,13},{9,1},{13,5},{2,10},{6,14},... | collective-permute-start | bytes 1658888 | tf_op jit(solution)/shard_map/ppermute | solution.py:540
  47.5 15.4 %collective-permute-start.8 = (bf16[2,3,120,384]{3,2,1,0:T(8,128)(2,1)}, bf16[2,3,120,384]{3,2,1,0:T(8,128)(2,1)}, u32[]{:S(2)}, u32[]{:S(2)}) collective-permute-start(bf16[2,3,120,384]{3,2,1,0:T(8,128)(2,1)} %pad_maximum_fusion.10), channel_id=1, source_target_pairs={{0,16},{16,0},{1,17},{17,1},{2,18},{18,2},{3,19},{19,3},{4,20},{20... | collective-permute-start | bytes 1658888 | tf_op jit(solution)/shard_map/ppermute | solution.py:540
  51.3 16.1 %copy-start.19 = (bf16[416,384]{1,0:T(8,128)(2,1)}, bf16[416,384]{1,0:T(8,128)(2,1)S(1)}, u32[]{:S(2)}) copy-start(bf16[416,384]{1,0:T(8,128)(2,1)S(1)} %collective-permute-done.3.refs_1_) | copy-start | bytes 958468
  65.6 12.0 %collective-permute-start.13 = (bf16[2,2,3,96,768]{4,3,2,1,0:T(8,128)(2,1)S(1)}, bf16[2,2,3,96,768]{4,3,2,1,0:T(8,128)(2,1)S(1)}, u32[]{:S(2)}, u32[]{:S(2)}) collective-permute-start(bf16[2,2,3,96,768]{4,3,2,1,0:T(8,128)(2,1)S(1)} %maximum_maximum_fusion), channel_id=1, source_target_pairs={{0,4},{4,0},{8,12},{12,8},{1,5},{5,1},{9,13},{13,9},{2,6},{6,2},{1... | collective-permute-start | bytes 5308424 | tf_op jit(solution)/shard_map/ppermute | solution.py:540
  66.4 7.3 %collective-permute-start.12 = (bf16[3,96,384]{2,1,0:T(8,128)(2,1)S(1)}, bf16[3,96,384]{2,1,0:T(8,128)(2,1)S(1)}, u32[]{:S(2)}, u32[]{:S(2)}) collective-permute-start(bf16[3,96,384]{2,1,0:T(8,128)(2,1)S(1)} %copy-done.42), channel_id=1, source_target_pairs={{0,16},{16,0},{1,17},{17,1},{2,18},{18,2},{3,19},{19,3},{4,20},{20... | collective-permute-start | bytes 663560 | tf_op jit(solution)/shard_map/ppermute | solution.py:540
  66.9 8.3 %collective-permute-start.11 = (bf16[3,96,384]{2,1,0:T(8,128)(2,1)S(1)}, bf16[3,96,384]{2,1,0:T(8,128)(2,1)S(1)}, u32[]{:S(2)}, u32[]{:S(2)}) collective-permute-start(bf16[3,96,384]{2,1,0:T(8,128)(2,1)S(1)} %pad_maximum_fusion.24), channel_id=1, source_target_pairs={{0,8},{4,12},{8,0},{12,4},{1,9},{5,13},{9,1},{13,5},{2,10},{6,14},... | collective-permute-start | bytes 663560 | tf_op jit(solution)/shard_map/ppermute | solution.py:540
  67.5 22.5 %collective-permute-start.16 = (bf16[3,144,384]{2,1,0:T(8,128)(2,1)S(1)}, bf16[3,144,384]{2,1,0:T(8,128)(2,1)S(1)}, u32[]{:S(2)}, u32[]{:S(2)}) collective-permute-start(bf16[3,144,384]{2,1,0:T(8,128)(2,1)S(1)} %pad_maximum_fusion.17), channel_id=1, source_target_pairs={{0,8},{4,12},{8,0},{12,4},{1,9},{5,13},{9,1},{13,5},{2,10},{6,14},... | collective-permute-start | bytes 995336 | tf_op jit(solution)/shard_map/ppermute | solution.py:540
  71.1 6.6 %collective-permute-start.10 = (bf16[2,2,3,24,768]{4,3,2,0,1:T(8,128)(2,1)S(1)}, bf16[2,2,3,24,768]{4,3,2,0,1:T(8,128)(2,1)S(1)}, u32[]{:S(2)}, u32[]{:S(2)}) collective-permute-start(bf16[2,2,3,24,768]{4,3,2,0,1:T(8,128)(2,1)S(1)} %maximum_maximum_fusion.2), channel_id=1, source_target_pairs={{0,4},{4,0},{8,12},{12,8},{1,5},{5,1},{9,13},{13,9},{2,6},{6,2},{1... | collective-permute-start | bytes 1327112 | tf_op jit(solution)/shard_map/ppermute | solution.py:540
  75.3 15.1 %collective-permute-start.15 = (bf16[2,3,96,384]{3,2,1,0:T(8,128)(2,1)S(1)}, bf16[2,3,96,384]{3,2,1,0:T(8,128)(2,1)S(1)}, u32[]{:S(2)}, u32[]{:S(2)}) collective-permute-start(bf16[2,3,96,384]{3,2,1,0:T(8,128)(2,1)S(1)} %pad_maximum_fusion.13), channel_id=1, source_target_pairs={{0,8},{4,12},{8,0},{12,4},{1,9},{5,13},{9,1},{13,5},{2,10},{6,14},... | collective-permute-start | bytes 1327112 | tf_op jit(solution)/shard_map/ppermute | solution.py:540
  76.0 14.4 %collective-permute-start.14 = (bf16[2,3,96,384]{3,2,1,0:T(8,128)(2,1)S(1)}, bf16[2,3,96,384]{3,2,1,0:T(8,128)(2,1)S(1)}, u32[]{:S(2)}, u32[]{:S(2)}) collective-permute-start(bf16[2,3,96,384]{3,2,1,0:T(8,128)(2,1)S(1)} %pad_maximum_fusion.12), channel_id=1, source_target_pairs={{0,16},{16,0},{1,17},{17,1},{2,18},{18,2},{3,19},{19,3},{4,20},{20... | collective-permute-start | bytes 1327112 | tf_op jit(solution)/shard_map/ppermute | solution.py:540
  91.6 3.8 %collective-permute-start.17 = (bf16[2,2,3,96,768]{4,3,2,0,1:T(8,128)(2,1)S(1)}, bf16[2,2,3,96,768]{4,3,2,0,1:T(8,128)(2,1)S(1)}, u32[]{:S(2)}, u32[]{:S(2)}) collective-permute-start(bf16[2,2,3,96,768]{4,3,2,0,1:T(8,128)(2,1)S(1)} %maximum_maximum_fusion.1), channel_id=1, source_target_pairs={{0,4},{4,0},{8,12},{12,8},{1,5},{5,1},{9,13},{13,9},{2,6},{6,2},{1... | collective-permute-start | bytes 5308424 | tf_op jit(solution)/shard_map/ppermute | solution.py:540
  91.8 17.4 %collective-permute-start.18 = (bf16[2,3,144,384]{3,2,1,0:T(8,128)(2,1)S(1)}, bf16[2,3,144,384]{3,2,1,0:T(8,128)(2,1)S(1)}, u32[]{:S(2)}, u32[]{:S(2)}) collective-permute-start(bf16[2,3,144,384]{3,2,1,0:T(8,128)(2,1)S(1)} %pad_maximum_fusion.4), channel_id=1, source_target_pairs={{0,16},{16,0},{1,17},{17,1},{2,18},{18,2},{3,19},{19,3},{4,20},{20... | collective-permute-start | bytes 1990664 | tf_op jit(solution)/shard_map/ppermute | solution.py:540
  106.5 15.4 %copy-start.12 = (bf16[4,4,96,768]{3,2,1,0:T(8,128)(2,1)}, bf16[4,4,96,768]{3,2,1,0:T(8,128)(2,1)S(1)}, u32[]{:S(2)}) copy-start(bf16[4,4,96,768]{3,2,1,0:T(8,128)(2,1)S(1)} %get-tuple-element.235) | copy-start | bytes 7077892
  109.2 12.7 %collective-permute-start.19 = (bf16[4,4,96,768]{3,2,1,0:T(8,128)(2,1)S(1)}, bf16[4,4,96,768]{3,2,1,0:T(8,128)(2,1)}, u32[]{:S(2)}, u32[]{:S(2)}) collective-permute-start(bf16[4,4,96,768]{3,2,1,0:T(8,128)(2,1)S(1)} %get-tuple-element.233), channel_id=1, source_target_pairs={{0,4},{4,0},{8,12},{12,8},{1,5},{5,1},{9,13},{13,9},{2,6},{6,2},{1... | collective-permute-start | bytes 7077896 | tf_op jit(solution)/shard_map/ppermute | solution.py:540
  109.6 16.0 %copy-start.23 = (f32[512,768]{1,0:T(8,128)S(1)}, f32[512,768]{1,0:T(8,128)}, u32[]{:S(2)}) copy-start(f32[512,768]{1,0:T(8,128)} %copy-done.22) | copy-start | bytes 4718596
  109.6 32.2 %collective-permute-start.20 = (bf16[2,2,3,144,384]{4,3,2,1,0:T(8,128)(2,1)S(1)}, bf16[2,2,3,144,384]{4,3,2,1,0:T(8,128)(2,1)S(1)}, u32[]{:S(2)}, u32[]{:S(2)}) collective-permute-start(bf16[2,2,3,144,384]{4,3,2,1,0:T(8,128)(2,1)S(1)} %pad_maximum_fusion), channel_id=1, source_target_pairs={{0,4},{4,0},{8,12},{12,8},{1,5},{5,1},{9,13},{13,9},{2,6},{6,2},{1... | collective-permute-start | bytes 3981320 | tf_op jit(solution)/shard_map/ppermute | solution.py:540
  110.1 30.1 %collective-permute-start.21 = (bf16[512,768]{1,0:T(8,128)(2,1)S(1)}, bf16[512,768]{1,0:T(8,128)(2,1)}, u32[]{:S(2)}, u32[]{:S(2)}) collective-permute-start(bf16[512,768]{1,0:T(8,128)(2,1)S(1)} %get-tuple-element.290.refs_0_), channel_id=1, source_target_pairs={{0,1},{1,2},{2,3},{4,5},{5,6},{6,7},{8,9},{9,10},{10,11},{12,13},{... | collective-permute-start | bytes 2359304 | tf_op jit(solution)/shard_map/ppermute | solution.py:686
  120.4 21.3 %collective-permute-start.22 = (bf16[512,768]{1,0:T(8,128)(2,1)S(1)}, bf16[512,768]{1,0:T(8,128)(2,1)}, u32[]{:S(2)}, u32[]{:S(2)}) collective-permute-start(bf16[512,768]{1,0:T(8,128)(2,1)S(1)} %get-tuple-element.290.refs_0_), channel_id=1, source_target_pairs={{1,0},{2,1},{3,2},{5,4},{6,5},{7,6},{9,8},{10,9},{11,10},{13,12},{... | collective-permute-start | bytes 2359304 | tf_op jit(solution)/shard_map/ppermute | solution.py:687
  123.5 18.3 %collective-permute-start.23 = (bf16[4,96,768]{2,1,0:T(8,128)(2,1)S(1)}, bf16[4,96,768]{2,1,0:T(8,128)(2,1)S(1)}, u32[]{:S(2)}, u32[]{:S(2)}) collective-permute-start(bf16[4,96,768]{2,1,0:T(8,128)(2,1)S(1)} %bitcast.330), channel_id=1, source_target_pairs={{0,8},{4,12},{8,0},{12,4},{1,9},{5,13},{9,1},{13,5},{2,10},{6,14},... | collective-permute-start | bytes 1769480 | tf_op jit(solution)/shard_map/ppermute | solution.py:540
  125.0 16.7 %collective-permute-start.24 = (bf16[4,96,768]{2,1,0:T(8,128)(2,1)S(1)}, bf16[4,96,768]{2,1,0:T(8,128)(2,1)S(1)}, u32[]{:S(2)}, u32[]{:S(2)}) collective-permute-start(bf16[4,96,768]{2,1,0:T(8,128)(2,1)S(1)} %bitcast.329), channel_id=1, source_target_pairs={{0,16},{16,0},{1,17},{17,1},{2,18},{18,2},{3,19},{19,3},{4,20},{20... | collective-permute-start | bytes 1769480 | tf_op jit(solution)/shard_map/ppermute | solution.py:540
  140.2 15.1 %copy-start.8 = (bf16[512,768]{1,0:T(8,128)(2,1)}, bf16[512,768]{1,0:T(8,128)(2,1)S(1)}, u32[]{:S(2)}) copy-start(bf16[512,768]{1,0:T(8,128)(2,1)S(1)} %get-tuple-element.276.low_ref) | copy-start | bytes 2359300
  141.8 4.9 %collective-permute-start.25 = (bf16[4,4,96,768]{3,2,1,0:T(8,128)(2,1)}, bf16[4,4,96,768]{3,2,1,0:T(8,128)(2,1)}, u32[]{:S(2)}, u32[]{:S(2)}) collective-permute-start(bf16[4,4,96,768]{3,2,1,0:T(8,128)(2,1)} %get-tuple-element.253), channel_id=1, source_target_pairs={{0,4},{4,0},{8,12},{12,8},{1,5},{5,1},{9,13},{13,9},{2,6},{6,2},{1... | collective-permute-start | bytes 7077896 | tf_op jit(solution)/shard_map/ppermute | solution.py:540
  149.3 27.0 %collective-permute-start.29 = (bf16[6,96,768]{2,1,0:T(8,128)(2,1)}, bf16[6,96,768]{2,1,0:T(8,128)(2,1)}, u32[]{:S(2)}, u32[]{:S(2)}) collective-permute-start(bf16[6,96,768]{2,1,0:T(8,128)(2,1)} %pad_maximum_fusion.3), channel_id=1, source_target_pairs={{0,16},{16,0},{1,17},{17,1},{2,18},{18,2},{3,19},{19,3},{4,20},{20... | collective-permute-start | bytes 2654216 | tf_op jit(solution)/shard_map/ppermute | solution.py:540
  151.2 25.1 %collective-permute-start.28 = (bf16[6,96,768]{2,1,0:T(8,128)(2,1)}, bf16[6,96,768]{2,1,0:T(8,128)(2,1)}, u32[]{:S(2)}, u32[]{:S(2)}) collective-permute-start(bf16[6,96,768]{2,1,0:T(8,128)(2,1)} %pad_maximum_fusion.2), channel_id=1, source_target_pairs={{0,8},{4,12},{8,0},{12,4},{1,9},{5,13},{9,1},{13,5},{2,10},{6,14},... | collective-permute-start | bytes 2654216 | tf_op jit(solution)/shard_map/ppermute | solution.py:540
  152.3 20.9 %collective-permute-start.26 = (bf16[512,768]{1,0:T(8,128)(2,1)}, bf16[512,768]{1,0:T(8,128)(2,1)}, u32[]{:S(2)}, u32[]{:S(2)}) collective-permute-start(bf16[512,768]{1,0:T(8,128)(2,1)} %collective-permute-done.21.refs_1_), channel_id=1, source_target_pairs={{1,2},{2,3},{5,6},{6,7},{9,10},{10,11},{13,14},{14,15},{17,18},{18... | collective-permute-start | bytes 2359304 | tf_op jit(solution)/shard_map/ppermute | solution.py:686
  153.8 22.5 %collective-permute-start.27 = (bf16[512,768]{1,0:T(8,128)(2,1)}, bf16[512,768]{1,0:T(8,128)(2,1)}, u32[]{:S(2)}, u32[]{:S(2)}) collective-permute-start(bf16[512,768]{1,0:T(8,128)(2,1)} %collective-permute-done.22.refs_4_), channel_id=1, source_target_pairs={{1,0},{2,1},{5,4},{6,5},{9,8},{10,9},{13,12},{14,13},{17,16},{18,1... | collective-permute-start | bytes 2359304 | tf_op jit(solution)/shard_map/ppermute | solution.py:687
  176.3 4.7 %collective-permute-start.30 = (bf16[4,2,96,768]{3,2,1,0:T(8,128)(2,1)}, bf16[4,2,96,768]{3,2,1,0:T(8,128)(2,1)S(1)}, u32[]{:S(2)}, u32[]{:S(2)}) collective-permute-start(bf16[4,2,96,768]{3,2,1,0:T(8,128)(2,1)} %get-tuple-element.270), channel_id=1, source_target_pairs={{0,4},{4,0},{8,12},{12,8},{1,5},{5,1},{9,13},{13,9},{2,6},{6,2},{1... | collective-permute-start | bytes 3538952 | tf_op jit(solution)/shard_map/ppermute | solution.py:540
  176.3 30.2 %collective-permute-start.31 = (bf16[512,768]{1,0:T(8,128)(2,1)}, bf16[512,768]{1,0:T(8,128)(2,1)}, u32[]{:S(2)}, u32[]{:S(2)}) collective-permute-start(bf16[512,768]{1,0:T(8,128)(2,1)} %collective-permute-done.26.refs_2_), channel_id=1, source_target_pairs={{2,3},{6,7},{10,11},{14,15},{18,19},{22,23},{26,27},{30,31}} | collective-permute-start | bytes 2359304 | tf_op jit(solution)/shard_map/ppermute | solution.py:686
  177.9 28.6 %collective-permute-start.32 = (bf16[512,768]{1,0:T(8,128)(2,1)}, bf16[512,768]{1,0:T(8,128)(2,1)}, u32[]{:S(2)}, u32[]{:S(2)}) collective-permute-start(bf16[512,768]{1,0:T(8,128)(2,1)} %collective-permute-done.27.refs_5_), channel_id=1, source_target_pairs={{1,0},{5,4},{9,8},{13,12},{17,16},{21,20},{25,24},{29,28}} | collective-permute-start | bytes 2359304 | tf_op jit(solution)/shard_map/ppermute | solution.py:687
  181.3 25.2 %collective-permute-start.34 = (bf16[4,96,768]{2,1,0:T(8,128)(2,1)S(1)}, bf16[4,96,768]{2,1,0:T(8,128)(2,1)S(1)}, u32[]{:S(2)}, u32[]{:S(2)}) collective-permute-start(bf16[4,96,768]{2,1,0:T(8,128)(2,1)S(1)} %pad_maximum_fusion.6), channel_id=1, source_target_pairs={{0,16},{16,0},{1,17},{17,1},{2,18},{18,2},{3,19},{19,3},{4,20},{20... | collective-permute-start | bytes 1769480 | tf_op jit(solution)/shard_map/ppermute | solution.py:540
  182.9 23.6 %collective-permute-start.33 = (bf16[4,96,768]{2,1,0:T(8,128)(2,1)S(1)}, bf16[4,96,768]{2,1,0:T(8,128)(2,1)}, u32[]{:S(2)}, u32[]{:S(2)}) collective-permute-start(bf16[4,96,768]{2,1,0:T(8,128)(2,1)S(1)} %pad_maximum_fusion.5), channel_id=1, source_target_pairs={{0,8},{4,12},{8,0},{12,4},{1,9},{5,13},{9,1},{13,5},{2,10},{6,14},... | collective-permute-start | bytes 1769480 | tf_op jit(solution)/shard_map/ppermute | solution.py:540
  185.1 21.4 %collective-permute-start.35 = (bf16[2,96,768]{2,1,0:T(8,128)(2,1)S(1)}, bf16[2,96,768]{2,1,0:T(8,128)(2,1)}, u32[]{:S(2)}, u32[]{:S(2)}) collective-permute-start(bf16[2,96,768]{2,1,0:T(8,128)(2,1)S(1)} %pad_maximum_fusion.18), channel_id=1, source_target_pairs={{0,1},{1,0},{2,3},{3,2},{4,5},{5,4},{6,7},{7,6},{8,9},{9,8},{10,11... | collective-permute-start | bytes 884744 | tf_op jit(solution)/shard_map/ppermute | solution.py:540
  207.3 7.0 %collective-permute-start.36 = (bf16[4,2,96,768]{3,2,1,0:T(8,128)(2,1)}, bf16[4,2,96,768]{3,2,1,0:T(8,128)(2,1)}, u32[]{:S(2)}, u32[]{:S(2)}) collective-permute-start(bf16[4,2,96,768]{3,2,1,0:T(8,128)(2,1)} %get-tuple-element.284), channel_id=1, source_target_pairs={{0,4},{4,0},{8,12},{12,8},{1,5},{5,1},{9,13},{13,9},{2,6},{6,2},{1... | collective-permute-start | bytes 3538952 | tf_op jit(solution)/shard_map/ppermute | solution.py:540
  207.6 25.2 %collective-permute-start.37 = (bf16[512,768]{1,0:T(8,128)(2,1)S(1)}, bf16[512,768]{1,0:T(8,128)(2,1)}, u32[]{:S(2)}, u32[]{:S(2)}) collective-permute-start(bf16[512,768]{1,0:T(8,128)(2,1)S(1)} %get-tuple-element.334.refs_0_.own_ref), channel_id=1, source_target_pairs={{0,1},{1,2},{2,3},{4,5},{5,6},{6,7},{8,9},{9,10},{10,11},{12,13},{... | collective-permute-start | bytes 2359304 | tf_op jit(solution)/shard_map/ppermute | solution.py:686
  210.5 22.4 %collective-permute-start.38 = (bf16[512,768]{1,0:T(8,128)(2,1)S(1)}, bf16[512,768]{1,0:T(8,128)(2,1)}, u32[]{:S(2)}, u32[]{:S(2)}) collective-permute-start(bf16[512,768]{1,0:T(8,128)(2,1)S(1)} %get-tuple-element.334.refs_0_.own_ref), channel_id=1, source_target_pairs={{1,0},{2,1},{3,2},{5,4},{6,5},{7,6},{9,8},{10,9},{11,10},{13,12},{... | collective-permute-start | bytes 2359304 | tf_op jit(solution)/shard_map/ppermute | solution.py:687
  216.3 16.5 %collective-permute-start.40 = (bf16[3,96,768]{2,1,0:T(8,128)(2,1)}, bf16[3,96,768]{2,1,0:T(8,128)(2,1)}, u32[]{:S(2)}, u32[]{:S(2)}) collective-permute-start(bf16[3,96,768]{2,1,0:T(8,128)(2,1)} %pad_maximum_fusion.15), channel_id=1, source_target_pairs={{0,16},{16,0},{1,17},{17,1},{2,18},{18,2},{3,19},{19,3},{4,20},{20... | collective-permute-start | bytes 1327112 | tf_op jit(solution)/shard_map/ppermute | solution.py:540
  218.0 14.9 %collective-permute-start.39 = (bf16[3,96,768]{2,1,0:T(8,128)(2,1)}, bf16[3,96,768]{2,1,0:T(8,128)(2,1)S(1)}, u32[]{:S(2)}, u32[]{:S(2)}) collective-permute-start(bf16[3,96,768]{2,1,0:T(8,128)(2,1)} %pad_maximum_fusion.14), channel_id=1, source_target_pairs={{0,8},{4,12},{8,0},{12,4},{1,9},{5,13},{9,1},{13,5},{2,10},{6,14},... | collective-permute-start | bytes 1327112 | tf_op jit(solution)/shard_map/ppermute | solution.py:540
  219.6 13.3 %collective-permute-start.41 = (f32[18,384]{1,0:T(8,128)S(1)}, f32[18,384]{1,0:T(8,128)S(1)}, u32[]{:S(2)}, u32[]{:S(2)}) collective-permute-start(f32[18,384]{1,0:T(8,128)S(1)} %concatenate.76), channel_id=1, source_target_pairs={{0,1},{1,0},{2,3},{3,2},{4,5},{5,4},{6,7},{7,6},{8,9},{9,8},{10,11... | collective-permute-start | bytes 82952 | tf_op jit(solution)/shard_map/ppermute | solution.py:540
  232.9 15.7 %copy-start.47 = (bf16[4,96,768]{2,1,0:T(8,128)(2,1)S(1)}, bf16[4,96,768]{2,1,0:T(8,128)(2,1)}, u32[]{:S(2)}) copy-start(bf16[4,96,768]{2,1,0:T(8,128)(2,1)} %copy-done.46) | copy-start | bytes 1769476
  235.4 5.3 %collective-permute-start.45 = (bf16[1,96,768]{2,1,0:T(8,128)(2,1)S(1)}, bf16[1,96,768]{2,1,0:T(8,128)(2,1)S(1)}, u32[]{:S(2)}, u32[]{:S(2)}) collective-permute-start(bf16[1,96,768]{2,1,0:T(8,128)(2,1)S(1)} %get-tuple-element.373), channel_id=1, source_target_pairs={{0,8},{4,12},{8,0},{12,4},{1,9},{5,13},{9,1},{13,5},{2,10},{6,14},... | collective-permute-start | bytes 442376 | tf_op jit(solution)/shard_map/ppermute | solution.py:540
  237.0 5.1 %collective-permute-start.46 = (bf16[1,96,768]{2,1,0:T(8,128)(2,1)S(1)}, bf16[1,96,768]{2,1,0:T(8,128)(2,1)S(1)}, u32[]{:S(2)}, u32[]{:S(2)}) collective-permute-start(bf16[1,96,768]{2,1,0:T(8,128)(2,1)S(1)} %get-tuple-element.372), channel_id=1, source_target_pairs={{0,16},{16,0},{1,17},{17,1},{2,18},{18,2},{3,19},{19,3},{4,20},{20... | collective-permute-start | bytes 442376 | tf_op jit(solution)/shard_map/ppermute | solution.py:540
  237.7 10.9 %collective-permute-start.44 = (bf16[2,96,768]{2,1,0:T(8,128)(2,1)}, bf16[2,96,768]{2,1,0:T(8,128)(2,1)S(1)}, u32[]{:S(2)}, u32[]{:S(2)}) collective-permute-start(bf16[2,96,768]{2,1,0:T(8,128)(2,1)} %pad_maximum_fusion.19), channel_id=1, source_target_pairs={{0,1},{1,0},{2,3},{3,2},{4,5},{5,4},{6,7},{7,6},{8,9},{9,8},{10,11... | collective-permute-start | bytes 884744 | tf_op jit(solution)/shard_map/ppermute | solution.py:540
  237.9 35.8 %collective-permute-start.42 = (bf16[512,768]{1,0:T(8,128)(2,1)}, bf16[512,768]{1,0:T(8,128)(2,1)S(1)}, u32[]{:S(2)}, u32[]{:S(2)}) collective-permute-start(bf16[512,768]{1,0:T(8,128)(2,1)} %collective-permute-done.37.refs_1_), channel_id=1, source_target_pairs={{1,2},{2,3},{5,6},{6,7},{9,10},{10,11},{13,14},{14,15},{17,18},{18... | collective-permute-start | bytes 2359304 | tf_op jit(solution)/shard_map/ppermute | solution.py:686
  238.6 35.1 %collective-permute-start.43 = (bf16[512,768]{1,0:T(8,128)(2,1)}, bf16[512,768]{1,0:T(8,128)(2,1)S(1)}, u32[]{:S(2)}, u32[]{:S(2)}) collective-permute-start(bf16[512,768]{1,0:T(8,128)(2,1)} %collective-permute-done.38.refs_4_), channel_id=1, source_target_pairs={{1,0},{2,1},{5,4},{6,5},{9,8},{10,9},{13,12},{14,13},{17,16},{18,1... | collective-permute-start | bytes 2359304 | tf_op jit(solution)/shard_map/ppermute | solution.py:687
  244.2 29.4 %collective-permute-start.47 = (f32[15,384]{1,0:T(8,128)S(1)}, f32[15,384]{1,0:T(8,128)S(1)}, u32[]{:S(2)}, u32[]{:S(2)}) collective-permute-start(f32[15,384]{1,0:T(8,128)S(1)} %pad_maximum_fusion.27), channel_id=1, source_target_pairs={{0,2},{1,3},{2,0},{3,1},{4,6},{5,7},{6,4},{7,5},{8,10},{9,11},{10,... | collective-permute-start | bytes 69128 | tf_op jit(solution)/shard_map/ppermute | solution.py:540
  250.4 23.3 %collective-permute-start.48 = (bf16[2,96,768]{2,1,0:T(8,128)(2,1)S(1)}, bf16[2,96,768]{2,1,0:T(8,128)(2,1)S(1)}, u32[]{:S(2)}, u32[]{:S(2)}) collective-permute-start(bf16[2,96,768]{2,1,0:T(8,128)(2,1)S(1)} %pad_maximum_fusion.20), channel_id=1, source_target_pairs={{0,1},{1,0},{2,3},{3,2},{4,5},{5,4},{6,7},{7,6},{8,9},{9,8},{10,11... | collective-permute-start | bytes 884744 | tf_op jit(solution)/shard_map/ppermute | solution.py:540
  250.5 28.0 %collective-permute-start.52 = (bf16[2,96,768]{2,1,0:T(8,128)(2,1)S(1)}, bf16[2,96,768]{2,1,0:T(8,128)(2,1)S(1)}, u32[]{:S(2)}, u32[]{:S(2)}) collective-permute-start(bf16[2,96,768]{2,1,0:T(8,128)(2,1)S(1)} %pad_maximum_fusion.21), channel_id=1, source_target_pairs={{0,2},{1,3},{2,0},{3,1},{4,6},{5,7},{6,4},{7,5},{8,10},{9,11},{10,... | collective-permute-start | bytes 884744 | tf_op jit(solution)/shard_map/ppermute | solution.py:540
  273.8 6.4 %collective-permute-start.51 = (bf16[96,768]{1,0:T(8,128)(2,1)S(1)}, bf16[96,768]{1,0:T(8,128)(2,1)S(1)}, u32[]{:S(2)}, u32[]{:S(2)}) collective-permute-start(bf16[96,768]{1,0:T(8,128)(2,1)S(1)} %fusion.17), channel_id=1, source_target_pairs={{0,2},{1,3},{2,0},{3,1},{4,6},{5,7},{6,4},{7,5},{8,10},{9,11},{10,... | collective-permute-start | bytes 442376 | tf_op jit(solution)/shard_map/ppermute | solution.py:540
  277.0 1.4 collective-permute-start.53
  280.9 12.3 %collective-permute-start.54 = (bf16[2,96,768]{2,1,0:T(8,128)(2,1)}, bf16[2,96,768]{2,1,0:T(8,128)(2,1)}, u32[]{:S(2)}, u32[]{:S(2)}) collective-permute-start(bf16[2,96,768]{2,1,0:T(8,128)(2,1)} %get-tuple-element.354), channel_id=1, source_target_pairs={{0,16},{16,0},{1,17},{17,1},{2,18},{18,2},{3,19},{19,3},{4,20},{20... | collective-permute-start | bytes 884744 | tf_op jit(solution)/shard_map/ppermute | solution.py:540
  286.3 7.0 %collective-permute-start.55 = (bf16[96,768]{1,0:T(8,128)(2,1)}, bf16[96,768]{1,0:T(8,128)(2,1)S(1)}, u32[]{:S(2)}, u32[]{:S(2)}) collective-permute-start(bf16[96,768]{1,0:T(8,128)(2,1)} %get-tuple-element.352), channel_id=1, source_target_pairs={{0,16},{16,0},{1,17},{17,1},{2,18},{18,2},{3,19},{19,3},{4,20},{20... | collective-permute-start | bytes 442376 | tf_op jit(solution)/shard_map/ppermute | solution.py:540
  286.3 7.0 %collective-permute-start.56 = (f32[15,384]{1,0:T(8,128)S(1)}, f32[15,384]{1,0:T(8,128)S(1)}, u32[]{:S(2)}, u32[]{:S(2)}) collective-permute-start(f32[15,384]{1,0:T(8,128)S(1)} %add.591), channel_id=1, source_target_pairs={{0,8},{4,12},{8,0},{12,4},{1,9},{5,13},{9,1},{13,5},{2,10},{6,14},... | collective-permute-start | bytes 69128 | tf_op jit(solution)/shard_map/ppermute | solution.py:540
  286.4 18.6 %collective-permute-start.49 = (bf16[512,768]{1,0:T(8,128)(2,1)S(1)}, bf16[512,768]{1,0:T(8,128)(2,1)S(1)}, u32[]{:S(2)}, u32[]{:S(2)}) collective-permute-start(bf16[512,768]{1,0:T(8,128)(2,1)S(1)} %collective-permute-done.42.refs_2_.refs_3_), channel_id=1, source_target_pairs={{2,3},{6,7},{10,11},{14,15},{18,19},{22,23},{26,27},{30,31}} | collective-permute-start | bytes 2359304 | tf_op jit(solution)/shard_map/ppermute | solution.py:686
  287.1 17.9 %collective-permute-start.50 = (bf16[512,768]{1,0:T(8,128)(2,1)S(1)}, bf16[512,768]{1,0:T(8,128)(2,1)}, u32[]{:S(2)}, u32[]{:S(2)}) collective-permute-start(bf16[512,768]{1,0:T(8,128)(2,1)S(1)} %collective-permute-done.43.refs_5_.refs_6_), channel_id=1, source_target_pairs={{1,0},{5,4},{9,8},{13,12},{17,16},{21,20},{25,24},{29,28}} | collective-permute-start | bytes 2359304 | tf_op jit(solution)/shard_map/ppermute | solution.py:687
  293.3 4.8 %collective-permute-start.57 = (f32[15,384]{1,0:T(8,128)S(1)}, f32[15,384]{1,0:T(8,128)S(1)}, u32[]{:S(2)}, u32[]{:S(2)}) collective-permute-start(f32[15,384]{1,0:T(8,128)S(1)} %add.592), channel_id=1, source_target_pairs={{0,16},{16,0},{1,17},{17,1},{2,18},{18,2},{3,19},{19,3},{4,20},{20... | collective-permute-start | bytes 69128 | tf_op jit(solution)/shard_map/ppermute | solution.py:540
  (45 other events, 228.6 us)

commit v4 on v3

--- a/solution.py
+++ b/solution.py
@@ -804,15 +804,14 @@
         total2 = h2[0].totals() + h2[1].totals()
         near2 = jnp.stack([total2[1], total2[3]])
         mine1, far1 = after_near((total1[0], total1[2]), near1)
-        outs = hold((output_own, out_1, out_2, out_3))
-        output = place(at, outs[0], [v[0] for v in outs[1:]], [v[1] for v in outs[1:]], BF)
-        output = output.reshape(seq_count, seq_len, width)
-        output, tok_1, flight, vec_got = run((output, tok_1, flight, vec_got))
+        far1 = far1.astype(BF)
+        done(*order.last, near2, far1, *tok_1, *flight, vec_got)
+        tok_1, flight, vec_got, near2, far1 = hold((tok_1, flight, vec_got, near2, far1))
         tok_2 = hop(*tok_1, 1)
+        near2 = z_near(near2)
         landed(flight, *groups)
         groups = [hb[1]], [hb[0]]
         flight = plane(*groups)
-        near2 = z_near(hold(near2))
         vec_got = vec_got[: 2 * n_slot].reshape(2, n_slot, half), vec_got[2 * n_slot :]
         vec_0, vec_2 = after_near((slot_vec[0], slot_vec[2]), vec_got[0])
         common = common + vec_got[1]
@@ -824,30 +823,38 @@
         vec_got = z_far(hold(vec_send))
         done(*total3, near2)
         mine2, far2 = after_near((total2[0], total2[2]), hold(near2))
-        far12 = z_far(jnp.stack([far1, far2]).astype(BF))
-        done(far2, *tok_2, vec_got, near3)
-        tok_3 = hop(*hold(tok_2), 2)
-        mine3, far3 = after_near((total3[0], total3[2]), hold(near3))
+        far12 = jnp.stack([far1, far2.astype(BF)])
+        done(far12, *tok_2)
+        tok_2, far12 = hold((tok_2, far12))
+        tok_3 = hop(*tok_2, 2)
+        far12 = z_far(far12)
+        grad_tokens = place(at, tok_own, (tok_1[0], tok_2[0], tok_2[0]), (tok_1[1], tok_2[1], tok_2[1]), F32)
+        grad_tokens, near3 = run((grad_tokens, near3))
+        mine3, far3 = after_near((total3[0], total3[2]), near3)
         far3 = z_far(far3.astype(BF))
+        done(far12, far3)
+        done(hold(far12))
+        mine12 = outer_rest(jnp.stack([mine1, mine2]) + hold(far12).astype(F32))
+        got12 = by_y(mine12.astype(BF))
+        done(mine12)
+        output = place(at, output_own, (out_1[0], out_2[0], out_3[0]), (out_1[1], out_2[1], hold(out_3[1])), BF)
+        output = output.reshape(seq_count, seq_len, width)
+        done(output, vec_got)
         vectors = jnp.concatenate([vec_0, common]) + hold(vec_got)
         vec_got = by_core(vectors)
-        done(far3, far12, vec_got)
-        mine12 = outer_rest(jnp.stack([mine1, mine2]) + hold(far12).astype(F32))
-        got12 = by_y(mine12.astype(BF))
+        mine3 = outer_rest(mine3 + hold(far3).astype(F32))
+        got3 = by_y(mine3.astype(BF))
+        done(mine3, vec_got)
         vectors = vectors + hold(vec_got)
         vec_got = by_x(vectors)
-        mine3 = outer_rest(mine3 + hold(far3).astype(F32))
-        got3 = by_y(mine3.astype(BF))
-        tok_held = hold((tok_own, (tok_1[0], tok_2[0], tok_2[0]), (tok_1[1], tok_2[1], tok_2[1])))
-        grad_tokens = place(at, *tok_held, F32)
-        done(grad_tokens, got12, got3, vec_got)
-        got12, got3, vec_got = hold((got12, got3, vec_got))
+        done(got12)
+        got12 = hold(got12)
+        done_wdown = whole_rows(mine12[0], got12[0])
+        done_win = whole_rows(mine12[1], got12[1])
+        done(done_wdown, done_win, got3, vec_got)
+        got3, vec_got = hold((got3, vec_got))
         vectors = vectors + vec_got
         vec_got = by_y(vectors)
-        done_wdown = whole_rows(mine12[0], got12[0])
-        done_win = whole_rows(mine12[1], got12[1])
-        done(done_wdown, done_win, vec_got)
-        got3 = hold(got3)
         done_last = whole_rows(mine3, got3)
         vectors = vectors + hold(vec_got)
         bit = 2

time: 315 us -> 307 us (0.975)
  starting transfers between devices: 87.4 us -> 83.2 us
    ppermute x6, waiting for transfers between devices: 4.6 us -> 19.7 us  [hop(): lax.ppermute(left, 'tensor', back_steps[:len(steps) - step])]
    ppermute x40, waiting for transfers between devices: 42.6 us -> 28.1 us  [swap(): return lax.ppermute(value, axis, [(i, i ^ bit) for i in range(size)])]
    ppermute x40, starting transfers between devices: 44.4 us -> 39.2 us  [swap(): return lax.ppermute(value, axis, [(i, i ^ bit) for i in range(size)])]
    unnamed x115 -> x123, local copies, waits for them, and re-layouts: 13.6 us -> 12.7 us
  transfers between devices with their start and end apart: 58 -> 58, of which waited for: 17 -> 20; matrix products, arithmetic and copies ran while one was open for 13% -> 13% of each run, Pallas kernels for 29% -> 30%
where the time goes in v4:
time: 307 us; the launch traced here: 303 us
  Pallas kernels  92.9 us (30%)
  starting transfers between devices  83.2 us (27%)
  waiting for transfers between devices  66.6 us (22%)
  other arithmetic  37.5 us (12%)
  local copies, waits for them, and re-layouts  20 us (7%)
    ppermute x40, starting transfers between devices, swap(): return lax.ppermute(value, axis, [(i, i ^ bit) for i in range(size)])  39.2 us
    pallas_call x2, Pallas kernels, attend_back(): call(functools.partial(attend_back_kernel, first, slots, heads, (cols //...  33.8 us
    ppermute x40, waiting for transfers between devices, swap(): return lax.ppermute(value, axis, [(i, i ^ bit) for i in range(size)])  28.1 us
    ppermute x6, waiting for transfers between devices, hop(): lax.ppermute(left, 'tensor', back_steps[:len(steps) - step])  19.7 us
    ppermute x6, waiting for transfers between devices, local(): lax.ppermute(v, 'tensor', [(i, (i + s) % n_tensor) for i in range(n_tenso...  18.7 us
    ppermute x6, starting transfers between devices, hop(): lax.ppermute(right, 'tensor', steps[step:])  18.5 us
    ppermute x6, starting transfers between devices, local(): lax.ppermute(v, 'tensor', [(i, (i + s) % n_tensor) for i in range(n_tenso...  17.2 us
    pallas_call x1, Pallas kernels, back(): call(functools.partial(back_kernel, slots), 'back', at, (slots,), [const(...  14.7 us
  transfers between devices with their start and end apart: 58, of which 20 were waited for; matrix products, arithmetic and copies ran while one was open for 13% of the time, Pallas kernels for 30%

profile of v4, /device:TPU:0, one launch (start us, length us, event | category | flops | bytes accessed | tf_op | source)
XLA Modules:
  0.0 302.8 jit_solution(5485392170387350673)
XLA Ops:
  2.6 3.1 %collective-permute-start = (bf16[216,768]{1,0:T(8,128)(2,1)S(1)}, bf16[216,768]{1,0:T(8,128)(2,1)S(1)}, u32[]{:S(2)}, u32[]{:S(2)}) collective-permute-start(bf16[216,768]{1,0:T(8,128)(2,1)S(1)} %pad_maximum_fusion.16), channel_id=1, source_target_pairs={{0,1},{1,2},{2,3},{3,0},{4,5},{5,6},{6,7},{7,4},{8,9},{9,10},{10,1... | collective-permute-start | bytes 995336 | tf_op jit(solution)/shard_map/ppermute | solution.py:589
  5.6 2.6 collective-permute-start.1
  8.2 1.3 collective-permute-start.2
  12.3 1.9 copy-done
  14.2 10.9 %attend.1 = (bf16[416,384]{1,0:T(8,128)(2,1)S(1)}, bf16[416,384]{1,0:T(8,128)(2,1)S(1)}, bf16[416,384]{1,0:T(8,128)(2,1)S(1)}, bf16[416,384]{1,0:T(8,128)(2,1)S(1)}) custom-call(s32[4]{0:T(128)S(1)} %pad_add_fusion.at_ref, bf16[4,512,768]{2,1,0:T(8,128)(2,1)S(1)} %copy-done, bf16[3,192,768]{2,1,0:T(8,128)(2,1)S(1)} %bitcast.296, ...), custom_call_target="tpu_custom_call" | custom-call | flops 1000 | bytes 1000 | tf_op jit(solution)/shard_map/attend/pallas_call | solution.py:111
  25.9 4.0 %collective-permute-done.1 = bf16[216,768]{1,0:T(8,128)(2,1)S(1)} collective-permute-done((bf16[216,768]{1,0:T(8,128)(2,1)S(1)}, bf16[216,768]{1,0:T(8,128)(2,1)S(1)}, u32[]{:S(2)}, u32[]{:S(2)}) %collective-permute-start.1) | collective-permute-done | bytes 331808 | tf_op jit(solution)/shard_map/ppermute | solution.py:589
  30.0 1.6 collective-permute-start.7
  31.6 1.6 collective-permute-start.6
  33.2 7.6 %collective-permute-start.3 = (bf16[416,384]{1,0:T(8,128)(2,1)S(1)}, bf16[416,384]{1,0:T(8,128)(2,1)S(1)}, u32[]{:S(2)}, u32[]{:S(2)}) collective-permute-start(bf16[416,384]{1,0:T(8,128)(2,1)S(1)} %get-tuple-element.168), channel_id=1, source_target_pairs={{0,1},{1,2},{2,3},{3,0},{4,5},{5,6},{6,7},{7,4},{8,9},{9,10},{10,1... | collective-permute-start | bytes 958472 | tf_op jit(solution)/shard_map/ppermute | solution.py:589
  40.9 1.6 collective-permute-start.4
  47.1 3.4 %collective-permute-done.3.refs_1_ = bf16[416,384]{1,0:T(8,128)(2,1)S(1)} collective-permute-done((bf16[416,384]{1,0:T(8,128)(2,1)S(1)}, bf16[416,384]{1,0:T(8,128)(2,1)S(1)}, u32[]{:S(2)}, u32[]{:S(2)}) %collective-permute-start.3) | collective-permute-done | bytes 319520 | tf_op jit(solution)/shard_map/ppermute | solution.py:589
  50.5 11.3 %collective-permute-done.4.refs_2_.refs_0_ = bf16[416,384]{1,0:T(8,128)(2,1)S(1)} collective-permute-done((bf16[416,384]{1,0:T(8,128)(2,1)S(1)}, bf16[416,384]{1,0:T(8,128)(2,1)S(1)}, u32[]{:S(2)}, u32[]{:S(2)}) %collective-permute-start.4) | collective-permute-done | bytes 319520 | tf_op jit(solution)/shard_map/ppermute | solution.py:589
  62.1 1.2 select_bitcast_fusion.11
  66.5 1.6 collective-permute-start.16
  70.1 2.6 collective-permute-done.12
  72.7 1.6 collective-permute-done.11
  75.0 1.6 collective-permute-start.14
  78.5 10.5 %rise.1 = (f32[512,768]{1,0:T(8,128)S(1)}, bf16[512,768]{1,0:T(8,128)(2,1)}, f32[512,768]{1,0:T(8,128)S(1)}, f32[512,1]{1,0:T(8,128)S(1)}, bf16[4,512,768]{2,1,0...) custom-call(s32[4]{0:T(128)S(1)} %pad_add_fusion.at_ref, ...), custom_call_target="tpu_custom_call" | custom-call | flops 1000 | bytes 1000 | tf_op jit(solution)/shard_map/rise/pallas_call | solution.py:204
  91.9 2.4 collective-permute-done.17
  94.4 11.1 %fall.1 = (bf16[512,768]{1,0:T(8,128)(2,1)S(1)}, f32[512,768]{1,0:T(8,128)S(1)}, bf16[512,768]{1,0:T(8,128)(2,1)S(1)}, f32[3,768]{1,0:T(4,128)S(1)}, bf16[4,4,96...) custom-call(s32[4]{0:T(128)S(1)} %pad_add_fusion.at_ref, ...), custom_call_target="tpu_custom_call" | custom-call | flops 1000 | bytes 1000 | tf_op jit(solution)/shard_map/fall/pallas_call | solution.py:290
  105.6 2.6 collective-permute-done.18
  109.1 10.2 %collective-permute-start.21 = (bf16[512,768]{1,0:T(8,128)(2,1)S(1)}, bf16[512,768]{1,0:T(8,128)(2,1)}, u32[]{:S(2)}, u32[]{:S(2)}) collective-permute-start(bf16[512,768]{1,0:T(8,128)(2,1)S(1)} %get-tuple-element.216.refs_0_), channel_id=1, source_target_pairs={{0,1},{1,2},{2,3},{4,5},{5,6},{6,7},{8,9},{9,10},{10,11},{12,13},{... | collective-permute-start | bytes 2359304 | tf_op jit(solution)/shard_map/ppermute | solution.py:686
  119.3 1.5 collective-permute-start.22
  121.2 1.6 collective-permute-start.23
  123.3 14.7 %back.1 = (f32[4,1,768]{2,1,0:T(1,128)S(1)}, f32[512,768]{1,0:T(8,128)S(1)}, bf16[512,768]{1,0:T(8,128)(2,1)S(1)}, bf16[768,512]{1,0:T(8,128)(2,1)S(1)}, f32[3,7...) custom-call(s32[4]{0:T(128)S(1)} %pad_add_fusion.at_ref, ...), custom_call_target="tpu_custom_call" | custom-call | flops 1000 | bytes 1000 | tf_op jit(solution)/shard_map/back/pallas_call | solution.py:345
  138.0 2.6 collective-permute-done.22.refs_4_
  140.8 2.2 fusion.2
  143.0 2.5 collective-permute-done.25
  149.9 1.6 collective-permute-start.26
  151.5 1.3 collective-permute-start.27
  154.0 16.9 %attend_back.2 = (f32[2,2,192]{2,1,0:T(2,128)S(1)}, f32[512,768]{1,0:T(8,128)}, bf16[4,2,96,768]{3,2,1,0:T(8,128)(2,1)S(1)}, bf16[4,2,96,768]{3,2,1,0:T(8,128)(2,1)}) custom-call(s32[4]{0:T(128)S(1)} %pad_add_fusion.at_ref, bf16[4,512,768]{2,1,0:T(8,128)(2,1)} %x_ref.4, bf16[512,768]{1,0:T(8,128)(2,1)S(1)} %get-tuple-element.261.low_ref, ...), custom_call_target="tpu_custom_call" | custom-call | flops 1000 | bytes 1000 | tf_op jit(solution)/shard_map/attend_back/pallas_call | solution.py:457
  170.9 3.0 %collective-permute-done.27.refs_5_ = bf16[512,768]{1,0:T(8,128)(2,1)} collective-permute-done((bf16[512,768]{1,0:T(8,128)(2,1)}, bf16[512,768]{1,0:T(8,128)(2,1)}, u32[]{:S(2)}, u32[]{:S(2)}) %collective-permute-start.27) | collective-permute-done | bytes 786464 | tf_op jit(solution)/shard_map/ppermute | solution.py:687
  174.0 1.6 collective-permute-start.31
  175.6 1.5 collective-permute-start.32
  177.1 1.6 fusion
  179.0 1.6 collective-permute-start.34
  181.3 1.5 fusion.37
  182.8 3.6 %collective-permute-start.35 = (bf16[2,96,768]{2,1,0:T(8,128)(2,1)S(1)}, bf16[2,96,768]{2,1,0:T(8,128)(2,1)S(1)}, u32[]{:S(2)}, u32[]{:S(2)}) collective-permute-start(bf16[2,96,768]{2,1,0:T(8,128)(2,1)S(1)} %pad_maximum_fusion.18), channel_id=1, source_target_pairs={{0,1},{1,0},{2,3},{3,2},{4,5},{5,4},{6,7},{7,6},{8,9},{9,8},{10,11... | collective-permute-start | bytes 884744 | tf_op jit(solution)/shard_map/ppermute | solution.py:540
  186.4 16.9 %attend_back.3 = (f32[2,2,192]{2,1,0:T(2,128)S(1)}, bf16[512,768]{1,0:T(8,128)(2,1)S(1)}, bf16[4,2,96,768]{3,2,1,0:T(8,128)(2,1)S(1)}, bf16[4,2,96,768]{3,2,1,0:T(8,128)(2,1)}) custom-call(s32[4]{0:T(128)S(1)} %pad_add_fusion.at_ref, bf16[4,512,768]{2,1,0:T(8,128)(2,1)} %x_ref.4, bf16[512,768]{1,0:T(8,128)(2,1)S(1)} %copy-done.9, ...), custom_call_target="tpu_custom_call" | custom-call | flops 1000 | bytes 1000 | tf_op jit(solution)/shard_map/attend_back/pallas_call | solution.py:457
  205.5 2.9 collective-permute-start.36
  208.4 1.3 collective-permute-start.37
  209.6 1.9 fusion.28
  216.7 2.7 collective-permute-start.41
  219.5 1.9 fusion.14
  222.2 8.5 %collective-permute-done.41 = f32[18,384]{1,0:T(8,128)S(1)} collective-permute-done((f32[18,384]{1,0:T(8,128)S(1)}, f32[18,384]{1,0:T(8,128)S(1)}, u32[]{:S(2)}, u32[]{:S(2)}) %collective-permute-start.41) | collective-permute-done | bytes 27680 | tf_op jit(solution)/shard_map/ppermute | solution.py:540
  230.8 2.0 fusion.13
  232.7 1.5 fusion.22
  234.2 1.6 collective-permute-start.43
  237.1 1.3 collective-permute-start.46
  239.5 1.4 collective-permute-done.44
  242.7 2.3 collective-permute-start.50
  245.0 1.7 fusion.12
  246.7 1.9 convert_add_fusion.9
  249.4 14.0 %collective-permute-done.46.refs_5_.refs_6_ = bf16[512,768]{1,0:T(8,128)(2,1)S(1)} collective-permute-done((bf16[512,768]{1,0:T(8,128)(2,1)}, bf16[512,768]{1,0:T(8,128)(2,1)S(1)}, u32[]{:S(2)}, u32[]{:S(2)}) %collective-permute-start.46) | collective-permute-done | bytes 786464 | tf_op jit(solution)/shard_map/ppermute | solution.py:687
  263.4 2.9 collective-permute-start.52
  266.3 1.6 collective-permute-start.48
  267.9 4.8 %place.3.whole_ref = f32[4,512,768]{2,1,0:T(8,128)} custom-call(s32[4]{0:T(128)} %copy-done.34, bf16[512,768]{1,0:T(8,128)(2,1)} %copy-done.5, bf16[512,768]{1,0:T(8,128)(2,1)} %collective-permute-done.36.refs_1_, bf16[512,768]{1,0:T(8,128)(2,1)} %copy-done.38, bf16[512,768]{1,0:T(8,128)(2,1)} %copy-done.38, ...), custom_call_target="tpu_custom_call" | custom-call | flops 1000 | bytes 1000 | tf_op jit(solution)/shard_map/place/pallas_call | solution.py:531
  272.8 1.3 collective-permute-start.49
  274.8 3.1 %collective-permute-start.51 = (bf16[96,768]{1,0:T(8,128)(2,1)}, bf16[96,768]{1,0:T(8,128)(2,1)S(1)}, u32[]{:S(2)}, u32[]{:S(2)}) collective-permute-start(bf16[96,768]{1,0:T(8,128)(2,1)} %fusion.10), channel_id=1, source_target_pairs={{0,2},{1,3},{2,0},{3,1},{4,6},{5,7},{6,4},{7,5},{8,10},{9,11},{10,... | collective-permute-start | bytes 442376 | tf_op jit(solution)/shard_map/ppermute | solution.py:540
  279.5 1.4 collective-permute-start.56
  280.9 4.1 %place.2 = bf16[4,512,768]{2,1,0:T(8,128)(2,1)} custom-call(s32[4]{0:T(128)} %copy-done.34, bf16[512,768]{1,0:T(8,128)(2,1)} %copy-done.31, bf16[512,768]{1,0:T(8,128)(2,1)} %collective-permute-done.21.refs_1_, bf16[512,768]{1,0:T(8,128)(2,1)} %collective-permute-done.26.refs_2_, bf16[512,768]{1,0:T(8,128)(2,1)} %collective-permute-done.31.refs_3_, ...), custom_call_target="tpu_custom_call" | custom-call | flops 1000 | bytes 1000 | tf_op jit(solution)/shard_map/place/pallas_call | solution.py:531
  288.6 1.5 collective-permute-done.55
  290.1 1.4 collective-permute-done.53
  299.2 3.0 %place_end.1 = f32[4,512,768]{2,1,0:T(8,128)} custom-call(s32[4]{0:T(128)} %copy-done.34, bf16[512,768]{1,0:T(8,128)(2,1)} %copy-done.5, bf16[512,768]{1,0:T(8,128)(2,1)} %collective-permute-done.48.behind_ref, bf16[512,768]{1,0:T(8,128)(2,1)} %copy-done.46, f32[4,512,768]{2,1,0:T(8,128)} %place.3.whole_ref), custom_call_target="tpu_custom_call", output_to_operand_aliasing={{}: (4, {})} | custom-call | flops 1000 | bytes 1000 | tf_op jit(solution)/shard_map/place_end/pallas_call | solution.py:515
  (316 shorter events, 56.0 us)
Async XLA Ops:
  2.6 23.3 %collective-permute-start = (bf16[216,768]{1,0:T(8,128)(2,1)S(1)}, bf16[216,768]{1,0:T(8,128)(2,1)S(1)}, u32[]{:S(2)}, u32[]{:S(2)}) collective-permute-start(bf16[216,768]{1,0:T(8,128)(2,1)S(1)} %pad_maximum_fusion.16), channel_id=1, source_target_pairs={{0,1},{1,2},{2,3},{3,0},{4,5},{5,6},{6,7},{7,4},{8,9},{9,10},{10,1... | collective-permute-start | bytes 995336 | tf_op jit(solution)/shard_map/ppermute | solution.py:589
  5.6 24.2 %collective-permute-start.1 = (bf16[216,768]{1,0:T(8,128)(2,1)S(1)}, bf16[216,768]{1,0:T(8,128)(2,1)S(1)}, u32[]{:S(2)}, u32[]{:S(2)}) collective-permute-start(bf16[216,768]{1,0:T(8,128)(2,1)S(1)} %pad_maximum_fusion.16), channel_id=1, source_target_pairs={{0,2},{1,3},{2,0},{3,1},{4,6},{5,7},{6,4},{7,5},{8,10},{9,11},{10,... | collective-permute-start | bytes 995336 | tf_op jit(solution)/shard_map/ppermute | solution.py:589
  8.2 21.6 %collective-permute-start.2 = (bf16[216,768]{1,0:T(8,128)(2,1)S(1)}, bf16[216,768]{1,0:T(8,128)(2,1)S(1)}, u32[]{:S(2)}, u32[]{:S(2)}) collective-permute-start(bf16[216,768]{1,0:T(8,128)(2,1)S(1)} %pad_maximum_fusion.16), channel_id=1, source_target_pairs={{0,3},{1,0},{2,1},{3,2},{4,7},{5,4},{6,5},{7,6},{8,11},{9,8},{10,9... | collective-permute-start | bytes 995336 | tf_op jit(solution)/shard_map/ppermute | solution.py:589
  12.3 174.1 %copy-start.34 = (s32[4]{0:T(128)}, s32[4]{0:T(128)S(1)}, u32[]{:S(2)}) copy-start(s32[4]{0:T(128)S(1)} %pad_add_fusion.at_ref) | copy-start | bytes 52
  30.0 14.9 %collective-permute-start.7 = (bf16[3,120,384]{2,1,0:T(8,128)(2,1)S(1)}, bf16[3,120,384]{2,1,0:T(8,128)(2,1)S(1)}, u32[]{:S(2)}, u32[]{:S(2)}) collective-permute-start(bf16[3,120,384]{2,1,0:T(8,128)(2,1)S(1)} %pad_maximum_fusion.23), channel_id=1, source_target_pairs={{0,16},{16,0},{1,17},{17,1},{2,18},{18,2},{3,19},{19,3},{4,20},{20... | collective-permute-start | bytes 829448 | tf_op jit(solution)/shard_map/ppermute | solution.py:540
  31.6 13.2 %collective-permute-start.6 = (bf16[3,120,384]{2,1,0:T(8,128)(2,1)S(1)}, bf16[3,120,384]{2,1,0:T(8,128)(2,1)S(1)}, u32[]{:S(2)}, u32[]{:S(2)}) collective-permute-start(bf16[3,120,384]{2,1,0:T(8,128)(2,1)S(1)} %pad_maximum_fusion.22), channel_id=1, source_target_pairs={{0,8},{4,12},{8,0},{12,4},{1,9},{5,13},{9,1},{13,5},{2,10},{6,14},... | collective-permute-start | bytes 829448 | tf_op jit(solution)/shard_map/ppermute | solution.py:540
  33.2 17.2 %collective-permute-start.3 = (bf16[416,384]{1,0:T(8,128)(2,1)S(1)}, bf16[416,384]{1,0:T(8,128)(2,1)S(1)}, u32[]{:S(2)}, u32[]{:S(2)}) collective-permute-start(bf16[416,384]{1,0:T(8,128)(2,1)S(1)} %get-tuple-element.168), channel_id=1, source_target_pairs={{0,1},{1,2},{2,3},{3,0},{4,5},{5,6},{6,7},{7,4},{8,9},{9,10},{10,1... | collective-permute-start | bytes 958472 | tf_op jit(solution)/shard_map/ppermute | solution.py:589
  40.9 21.0 %collective-permute-start.4 = (bf16[416,384]{1,0:T(8,128)(2,1)S(1)}, bf16[416,384]{1,0:T(8,128)(2,1)S(1)}, u32[]{:S(2)}, u32[]{:S(2)}) collective-permute-start(bf16[416,384]{1,0:T(8,128)(2,1)S(1)} %get-tuple-element.169), channel_id=1, source_target_pairs={{0,2},{1,3},{2,0},{3,1},{4,6},{5,7},{6,4},{7,5},{8,10},{9,11},{10,... | collective-permute-start | bytes 958472 | tf_op jit(solution)/shard_map/ppermute | solution.py:589
  42.4 19.4 %collective-permute-start.5 = (bf16[416,384]{1,0:T(8,128)(2,1)S(1)}, bf16[416,384]{1,0:T(8,128)(2,1)S(1)}, u32[]{:S(2)}, u32[]{:S(2)}) collective-permute-start(bf16[416,384]{1,0:T(8,128)(2,1)S(1)} %get-tuple-element.170), channel_id=1, source_target_pairs={{0,3},{1,0},{2,1},{3,2},{4,7},{5,4},{6,5},{7,6},{8,11},{9,8},{10,9... | collective-permute-start | bytes 958472 | tf_op jit(solution)/shard_map/ppermute | solution.py:589
  45.0 17.0 %collective-permute-start.9 = (bf16[2,3,120,384]{3,2,1,0:T(8,128)(2,1)S(1)}, bf16[2,3,120,384]{3,2,1,0:T(8,128)(2,1)}, u32[]{:S(2)}, u32[]{:S(2)}) collective-permute-start(bf16[2,3,120,384]{3,2,1,0:T(8,128)(2,1)S(1)} %pad_maximum_fusion.11), channel_id=1, source_target_pairs={{0,8},{4,12},{8,0},{12,4},{1,9},{5,13},{9,1},{13,5},{2,10},{6,14},... | collective-permute-start | bytes 1658888 | tf_op jit(solution)/shard_map/ppermute | solution.py:540
  46.6 15.5 %collective-permute-start.8 = (bf16[2,3,120,384]{3,2,1,0:T(8,128)(2,1)}, bf16[2,3,120,384]{3,2,1,0:T(8,128)(2,1)}, u32[]{:S(2)}, u32[]{:S(2)}) collective-permute-start(bf16[2,3,120,384]{3,2,1,0:T(8,128)(2,1)} %pad_maximum_fusion.10), channel_id=1, source_target_pairs={{0,16},{16,0},{1,17},{17,1},{2,18},{18,2},{3,19},{19,3},{4,20},{20... | collective-permute-start | bytes 1658888 | tf_op jit(solution)/shard_map/ppermute | solution.py:540
  50.5 16.0 %copy-start.19 = (bf16[416,384]{1,0:T(8,128)(2,1)}, bf16[416,384]{1,0:T(8,128)(2,1)S(1)}, u32[]{:S(2)}) copy-start(bf16[416,384]{1,0:T(8,128)(2,1)S(1)} %collective-permute-done.3.refs_1_) | copy-start | bytes 958468
  64.7 12.0 %collective-permute-start.13 = (bf16[2,2,3,96,768]{4,3,2,1,0:T(8,128)(2,1)S(1)}, bf16[2,2,3,96,768]{4,3,2,1,0:T(8,128)(2,1)S(1)}, u32[]{:S(2)}, u32[]{:S(2)}) collective-permute-start(bf16[2,2,3,96,768]{4,3,2,1,0:T(8,128)(2,1)S(1)} %maximum_maximum_fusion), channel_id=1, source_target_pairs={{0,4},{4,0},{8,12},{12,8},{1,5},{5,1},{9,13},{13,9},{2,6},{6,2},{1... | collective-permute-start | bytes 5308424 | tf_op jit(solution)/shard_map/ppermute | solution.py:540
  65.4 7.3 %collective-permute-start.12 = (bf16[3,96,384]{2,1,0:T(8,128)(2,1)S(1)}, bf16[3,96,384]{2,1,0:T(8,128)(2,1)S(1)}, u32[]{:S(2)}, u32[]{:S(2)}) collective-permute-start(bf16[3,96,384]{2,1,0:T(8,128)(2,1)S(1)} %copy-done.45), channel_id=1, source_target_pairs={{0,16},{16,0},{1,17},{17,1},{2,18},{18,2},{3,19},{19,3},{4,20},{20... | collective-permute-start | bytes 663560 | tf_op jit(solution)/shard_map/ppermute | solution.py:540
  65.9 8.3 %collective-permute-start.11 = (bf16[3,96,384]{2,1,0:T(8,128)(2,1)S(1)}, bf16[3,96,384]{2,1,0:T(8,128)(2,1)S(1)}, u32[]{:S(2)}, u32[]{:S(2)}) collective-permute-start(bf16[3,96,384]{2,1,0:T(8,128)(2,1)S(1)} %copy-done.44), channel_id=1, source_target_pairs={{0,8},{4,12},{8,0},{12,4},{1,9},{5,13},{9,1},{13,5},{2,10},{6,14},... | collective-permute-start | bytes 663560 | tf_op jit(solution)/shard_map/ppermute | solution.py:540
  66.5 22.5 %collective-permute-start.16 = (bf16[3,144,384]{2,1,0:T(8,128)(2,1)S(1)}, bf16[3,144,384]{2,1,0:T(8,128)(2,1)S(1)}, u32[]{:S(2)}, u32[]{:S(2)}) collective-permute-start(bf16[3,144,384]{2,1,0:T(8,128)(2,1)S(1)} %pad_maximum_fusion.17), channel_id=1, source_target_pairs={{0,8},{4,12},{8,0},{12,4},{1,9},{5,13},{9,1},{13,5},{2,10},{6,14},... | collective-permute-start | bytes 995336 | tf_op jit(solution)/shard_map/ppermute | solution.py:540
  70.0 6.6 %collective-permute-start.10 = (bf16[2,2,3,24,768]{4,3,2,0,1:T(8,128)(2,1)S(1)}, bf16[2,2,3,24,768]{4,3,2,0,1:T(8,128)(2,1)S(1)}, u32[]{:S(2)}, u32[]{:S(2)}) collective-permute-start(bf16[2,2,3,24,768]{4,3,2,0,1:T(8,128)(2,1)S(1)} %maximum_maximum_fusion.2), channel_id=1, source_target_pairs={{0,4},{4,0},{8,12},{12,8},{1,5},{5,1},{9,13},{13,9},{2,6},{6,2},{1... | collective-permute-start | bytes 1327112 | tf_op jit(solution)/shard_map/ppermute | solution.py:540
  74.3 15.2 %collective-permute-start.15 = (bf16[2,3,96,384]{3,2,1,0:T(8,128)(2,1)S(1)}, bf16[2,3,96,384]{3,2,1,0:T(8,128)(2,1)S(1)}, u32[]{:S(2)}, u32[]{:S(2)}) collective-permute-start(bf16[2,3,96,384]{3,2,1,0:T(8,128)(2,1)S(1)} %pad_maximum_fusion.13), channel_id=1, source_target_pairs={{0,8},{4,12},{8,0},{12,4},{1,9},{5,13},{9,1},{13,5},{2,10},{6,14},... | collective-permute-start | bytes 1327112 | tf_op jit(solution)/shard_map/ppermute | solution.py:540
  75.0 14.4 %collective-permute-start.14 = (bf16[2,3,96,384]{3,2,1,0:T(8,128)(2,1)S(1)}, bf16[2,3,96,384]{3,2,1,0:T(8,128)(2,1)S(1)}, u32[]{:S(2)}, u32[]{:S(2)}) collective-permute-start(bf16[2,3,96,384]{3,2,1,0:T(8,128)(2,1)S(1)} %pad_maximum_fusion.12), channel_id=1, source_target_pairs={{0,16},{16,0},{1,17},{17,1},{2,18},{18,2},{3,19},{19,3},{4,20},{20... | collective-permute-start | bytes 1327112 | tf_op jit(solution)/shard_map/ppermute | solution.py:540
  90.5 3.8 %collective-permute-start.17 = (bf16[2,2,3,96,768]{4,3,2,0,1:T(8,128)(2,1)S(1)}, bf16[2,2,3,96,768]{4,3,2,0,1:T(8,128)(2,1)S(1)}, u32[]{:S(2)}, u32[]{:S(2)}) collective-permute-start(bf16[2,2,3,96,768]{4,3,2,0,1:T(8,128)(2,1)S(1)} %maximum_maximum_fusion.1), channel_id=1, source_target_pairs={{0,4},{4,0},{8,12},{12,8},{1,5},{5,1},{9,13},{13,9},{2,6},{6,2},{1... | collective-permute-start | bytes 5308424 | tf_op jit(solution)/shard_map/ppermute | solution.py:540
  90.8 17.4 %collective-permute-start.18 = (bf16[2,3,144,384]{3,2,1,0:T(8,128)(2,1)S(1)}, bf16[2,3,144,384]{3,2,1,0:T(8,128)(2,1)S(1)}, u32[]{:S(2)}, u32[]{:S(2)}) collective-permute-start(bf16[2,3,144,384]{3,2,1,0:T(8,128)(2,1)S(1)} %pad_maximum_fusion.4), channel_id=1, source_target_pairs={{0,16},{16,0},{1,17},{17,1},{2,18},{18,2},{3,19},{19,3},{4,20},{20... | collective-permute-start | bytes 1990664 | tf_op jit(solution)/shard_map/ppermute | solution.py:540
  105.5 15.3 %copy-start.12 = (bf16[4,4,96,768]{3,2,1,0:T(8,128)(2,1)}, bf16[4,4,96,768]{3,2,1,0:T(8,128)(2,1)S(1)}, u32[]{:S(2)}) copy-start(bf16[4,4,96,768]{3,2,1,0:T(8,128)(2,1)S(1)} %get-tuple-element.221) | copy-start | bytes 7077892
  108.2 12.7 %collective-permute-start.19 = (bf16[4,4,96,768]{3,2,1,0:T(8,128)(2,1)S(1)}, bf16[4,4,96,768]{3,2,1,0:T(8,128)(2,1)S(1)}, u32[]{:S(2)}, u32[]{:S(2)}) collective-permute-start(bf16[4,4,96,768]{3,2,1,0:T(8,128)(2,1)S(1)} %get-tuple-element.219), channel_id=1, source_target_pairs={{0,4},{4,0},{8,12},{12,8},{1,5},{5,1},{9,13},{13,9},{2,6},{6,2},{1... | collective-permute-start | bytes 7077896 | tf_op jit(solution)/shard_map/ppermute | solution.py:540
  108.5 14.8 %copy-start.23 = (f32[512,768]{1,0:T(8,128)S(1)}, f32[512,768]{1,0:T(8,128)}, u32[]{:S(2)}) copy-start(f32[512,768]{1,0:T(8,128)} %copy-done.22) | copy-start | bytes 4718596
  108.5 32.1 %collective-permute-start.20 = (bf16[2,2,3,144,384]{4,3,2,1,0:T(8,128)(2,1)S(1)}, bf16[2,2,3,144,384]{4,3,2,1,0:T(8,128)(2,1)S(1)}, u32[]{:S(2)}, u32[]{:S(2)}) collective-permute-start(bf16[2,2,3,144,384]{4,3,2,1,0:T(8,128)(2,1)S(1)} %pad_maximum_fusion), channel_id=1, source_target_pairs={{0,4},{4,0},{8,12},{12,8},{1,5},{5,1},{9,13},{13,9},{2,6},{6,2},{1... | collective-permute-start | bytes 3981320 | tf_op jit(solution)/shard_map/ppermute | solution.py:540
  109.1 28.9 %collective-permute-start.21 = (bf16[512,768]{1,0:T(8,128)(2,1)S(1)}, bf16[512,768]{1,0:T(8,128)(2,1)}, u32[]{:S(2)}, u32[]{:S(2)}) collective-permute-start(bf16[512,768]{1,0:T(8,128)(2,1)S(1)} %get-tuple-element.216.refs_0_), channel_id=1, source_target_pairs={{0,1},{1,2},{2,3},{4,5},{5,6},{6,7},{8,9},{9,10},{10,11},{12,13},{... | collective-permute-start | bytes 2359304 | tf_op jit(solution)/shard_map/ppermute | solution.py:686
  119.3 21.3 %collective-permute-start.22 = (bf16[512,768]{1,0:T(8,128)(2,1)S(1)}, bf16[512,768]{1,0:T(8,128)(2,1)}, u32[]{:S(2)}, u32[]{:S(2)}) collective-permute-start(bf16[512,768]{1,0:T(8,128)(2,1)S(1)} %get-tuple-element.216.refs_0_), channel_id=1, source_target_pairs={{1,0},{2,1},{3,2},{5,4},{6,5},{7,6},{9,8},{10,9},{11,10},{13,12},{... | collective-permute-start | bytes 2359304 | tf_op jit(solution)/shard_map/ppermute | solution.py:687
  121.2 19.5 %collective-permute-start.23 = (bf16[4,96,768]{2,1,0:T(8,128)(2,1)S(1)}, bf16[4,96,768]{2,1,0:T(8,128)(2,1)S(1)}, u32[]{:S(2)}, u32[]{:S(2)}) collective-permute-start(bf16[4,96,768]{2,1,0:T(8,128)(2,1)S(1)} %bitcast.316), channel_id=1, source_target_pairs={{0,8},{4,12},{8,0},{12,4},{1,9},{5,13},{9,1},{13,5},{2,10},{6,14},... | collective-permute-start | bytes 1769480 | tf_op jit(solution)/shard_map/ppermute | solution.py:540
  122.8 17.9 %collective-permute-start.24 = (bf16[4,96,768]{2,1,0:T(8,128)(2,1)S(1)}, bf16[4,96,768]{2,1,0:T(8,128)(2,1)S(1)}, u32[]{:S(2)}, u32[]{:S(2)}) collective-permute-start(bf16[4,96,768]{2,1,0:T(8,128)(2,1)S(1)} %bitcast.315), channel_id=1, source_target_pairs={{0,16},{16,0},{1,17},{17,1},{2,18},{18,2},{3,19},{19,3},{4,20},{20... | collective-permute-start | bytes 1769480 | tf_op jit(solution)/shard_map/ppermute | solution.py:540
  138.0 14.9 %copy-start.8 = (bf16[512,768]{1,0:T(8,128)(2,1)}, bf16[512,768]{1,0:T(8,128)(2,1)S(1)}, u32[]{:S(2)}) copy-start(bf16[512,768]{1,0:T(8,128)(2,1)S(1)} %get-tuple-element.261.low_ref) | copy-start | bytes 2359300
  140.7 4.8 %collective-permute-start.25 = (bf16[4,4,96,768]{3,2,1,0:T(8,128)(2,1)}, bf16[4,4,96,768]{3,2,1,0:T(8,128)(2,1)S(1)}, u32[]{:S(2)}, u32[]{:S(2)}) collective-permute-start(bf16[4,4,96,768]{3,2,1,0:T(8,128)(2,1)} %get-tuple-element.238), channel_id=1, source_target_pairs={{0,4},{4,0},{8,12},{12,8},{1,5},{5,1},{9,13},{13,9},{2,6},{6,2},{1... | collective-permute-start | bytes 7077896 | tf_op jit(solution)/shard_map/ppermute | solution.py:540
  146.9 27.1 %collective-permute-start.29 = (bf16[6,96,768]{2,1,0:T(8,128)(2,1)}, bf16[6,96,768]{2,1,0:T(8,128)(2,1)}, u32[]{:S(2)}, u32[]{:S(2)}) collective-permute-start(bf16[6,96,768]{2,1,0:T(8,128)(2,1)} %pad_maximum_fusion.3), channel_id=1, source_target_pairs={{0,16},{16,0},{1,17},{17,1},{2,18},{18,2},{3,19},{19,3},{4,20},{20... | collective-permute-start | bytes 2654216 | tf_op jit(solution)/shard_map/ppermute | solution.py:540
  148.9 25.1 %collective-permute-start.28 = (bf16[6,96,768]{2,1,0:T(8,128)(2,1)}, bf16[6,96,768]{2,1,0:T(8,128)(2,1)}, u32[]{:S(2)}, u32[]{:S(2)}) collective-permute-start(bf16[6,96,768]{2,1,0:T(8,128)(2,1)} %pad_maximum_fusion.2), channel_id=1, source_target_pairs={{0,8},{4,12},{8,0},{12,4},{1,9},{5,13},{9,1},{13,5},{2,10},{6,14},... | collective-permute-start | bytes 2654216 | tf_op jit(solution)/shard_map/ppermute | solution.py:540
  149.9 21.0 %collective-permute-start.26 = (bf16[512,768]{1,0:T(8,128)(2,1)}, bf16[512,768]{1,0:T(8,128)(2,1)}, u32[]{:S(2)}, u32[]{:S(2)}) collective-permute-start(bf16[512,768]{1,0:T(8,128)(2,1)} %collective-permute-done.21.refs_1_), channel_id=1, source_target_pairs={{1,2},{2,3},{5,6},{6,7},{9,10},{10,11},{13,14},{14,15},{17,18},{18... | collective-permute-start | bytes 2359304 | tf_op jit(solution)/shard_map/ppermute | solution.py:686
  151.5 22.5 %collective-permute-start.27 = (bf16[512,768]{1,0:T(8,128)(2,1)}, bf16[512,768]{1,0:T(8,128)(2,1)}, u32[]{:S(2)}, u32[]{:S(2)}) collective-permute-start(bf16[512,768]{1,0:T(8,128)(2,1)} %collective-permute-done.22.refs_4_), channel_id=1, source_target_pairs={{1,0},{2,1},{5,4},{6,5},{9,8},{10,9},{13,12},{14,13},{17,16},{18,1... | collective-permute-start | bytes 2359304 | tf_op jit(solution)/shard_map/ppermute | solution.py:687
  174.0 4.8 %collective-permute-start.30 = (bf16[4,2,96,768]{3,2,1,0:T(8,128)(2,1)}, bf16[4,2,96,768]{3,2,1,0:T(8,128)(2,1)S(1)}, u32[]{:S(2)}, u32[]{:S(2)}) collective-permute-start(bf16[4,2,96,768]{3,2,1,0:T(8,128)(2,1)} %get-tuple-element.255), channel_id=1, source_target_pairs={{0,4},{4,0},{8,12},{12,8},{1,5},{5,1},{9,13},{13,9},{2,6},{6,2},{1... | collective-permute-start | bytes 3538952 | tf_op jit(solution)/shard_map/ppermute | solution.py:540
  174.0 30.4 %collective-permute-start.31 = (bf16[512,768]{1,0:T(8,128)(2,1)}, bf16[512,768]{1,0:T(8,128)(2,1)}, u32[]{:S(2)}, u32[]{:S(2)}) collective-permute-start(bf16[512,768]{1,0:T(8,128)(2,1)} %collective-permute-done.26.refs_2_), channel_id=1, source_target_pairs={{2,3},{6,7},{10,11},{14,15},{18,19},{22,23},{26,27},{30,31}} | collective-permute-start | bytes 2359304 | tf_op jit(solution)/shard_map/ppermute | solution.py:686
  175.6 28.8 %collective-permute-start.32 = (bf16[512,768]{1,0:T(8,128)(2,1)}, bf16[512,768]{1,0:T(8,128)(2,1)}, u32[]{:S(2)}, u32[]{:S(2)}) collective-permute-start(bf16[512,768]{1,0:T(8,128)(2,1)} %collective-permute-done.27.refs_5_), channel_id=1, source_target_pairs={{1,0},{5,4},{9,8},{13,12},{17,16},{21,20},{25,24},{29,28}} | collective-permute-start | bytes 2359304 | tf_op jit(solution)/shard_map/ppermute | solution.py:687
  179.0 25.3 %collective-permute-start.34 = (bf16[4,96,768]{2,1,0:T(8,128)(2,1)S(1)}, bf16[4,96,768]{2,1,0:T(8,128)(2,1)S(1)}, u32[]{:S(2)}, u32[]{:S(2)}) collective-permute-start(bf16[4,96,768]{2,1,0:T(8,128)(2,1)S(1)} %pad_maximum_fusion.6), channel_id=1, source_target_pairs={{0,16},{16,0},{1,17},{17,1},{2,18},{18,2},{3,19},{19,3},{4,20},{20... | collective-permute-start | bytes 1769480 | tf_op jit(solution)/shard_map/ppermute | solution.py:540
  180.7 23.7 %collective-permute-start.33 = (bf16[4,96,768]{2,1,0:T(8,128)(2,1)S(1)}, bf16[4,96,768]{2,1,0:T(8,128)(2,1)}, u32[]{:S(2)}, u32[]{:S(2)}) collective-permute-start(bf16[4,96,768]{2,1,0:T(8,128)(2,1)S(1)} %pad_maximum_fusion.5), channel_id=1, source_target_pairs={{0,8},{4,12},{8,0},{12,4},{1,9},{5,13},{9,1},{13,5},{2,10},{6,14},... | collective-permute-start | bytes 1769480 | tf_op jit(solution)/shard_map/ppermute | solution.py:540
  182.8 21.5 %collective-permute-start.35 = (bf16[2,96,768]{2,1,0:T(8,128)(2,1)S(1)}, bf16[2,96,768]{2,1,0:T(8,128)(2,1)S(1)}, u32[]{:S(2)}, u32[]{:S(2)}) collective-permute-start(bf16[2,96,768]{2,1,0:T(8,128)(2,1)S(1)} %pad_maximum_fusion.18), channel_id=1, source_target_pairs={{0,1},{1,0},{2,3},{3,2},{4,5},{5,4},{6,7},{7,6},{8,9},{9,8},{10,11... | collective-permute-start | bytes 884744 | tf_op jit(solution)/shard_map/ppermute | solution.py:540
  205.2 6.3 %collective-permute-start.38 = (bf16[4,2,96,768]{3,2,1,0:T(8,128)(2,1)}, bf16[4,2,96,768]{3,2,1,0:T(8,128)(2,1)}, u32[]{:S(2)}, u32[]{:S(2)}) collective-permute-start(bf16[4,2,96,768]{3,2,1,0:T(8,128)(2,1)} %get-tuple-element.274), channel_id=1, source_target_pairs={{0,4},{4,0},{8,12},{12,8},{1,5},{5,1},{9,13},{13,9},{2,6},{6,2},{1... | collective-permute-start | bytes 3538952 | tf_op jit(solution)/shard_map/ppermute | solution.py:540
  205.5 25.2 %collective-permute-start.36 = (bf16[512,768]{1,0:T(8,128)(2,1)S(1)}, bf16[512,768]{1,0:T(8,128)(2,1)}, u32[]{:S(2)}, u32[]{:S(2)}) collective-permute-start(bf16[512,768]{1,0:T(8,128)(2,1)S(1)} %get-tuple-element.306.refs_0_.own_ref), channel_id=1, source_target_pairs={{0,1},{1,2},{2,3},{4,5},{5,6},{6,7},{8,9},{9,10},{10,11},{12,13},{... | collective-permute-start | bytes 2359304 | tf_op jit(solution)/shard_map/ppermute | solution.py:686
  208.4 22.4 %collective-permute-start.37 = (bf16[512,768]{1,0:T(8,128)(2,1)S(1)}, bf16[512,768]{1,0:T(8,128)(2,1)}, u32[]{:S(2)}, u32[]{:S(2)}) collective-permute-start(bf16[512,768]{1,0:T(8,128)(2,1)S(1)} %get-tuple-element.306.refs_0_.own_ref), channel_id=1, source_target_pairs={{1,0},{2,1},{3,2},{5,4},{6,5},{7,6},{9,8},{10,9},{11,10},{13,12},{... | collective-permute-start | bytes 2359304 | tf_op jit(solution)/shard_map/ppermute | solution.py:687
  213.6 17.1 %collective-permute-start.40 = (bf16[3,96,768]{2,1,0:T(8,128)(2,1)}, bf16[3,96,768]{2,1,0:T(8,128)(2,1)}, u32[]{:S(2)}, u32[]{:S(2)}) collective-permute-start(bf16[3,96,768]{2,1,0:T(8,128)(2,1)} %pad_maximum_fusion.15), channel_id=1, source_target_pairs={{0,16},{16,0},{1,17},{17,1},{2,18},{18,2},{3,19},{19,3},{4,20},{20... | collective-permute-start | bytes 1327112 | tf_op jit(solution)/shard_map/ppermute | solution.py:540
  215.3 15.4 %collective-permute-start.39 = (bf16[3,96,768]{2,1,0:T(8,128)(2,1)}, bf16[3,96,768]{2,1,0:T(8,128)(2,1)S(1)}, u32[]{:S(2)}, u32[]{:S(2)}) collective-permute-start(bf16[3,96,768]{2,1,0:T(8,128)(2,1)} %pad_maximum_fusion.14), channel_id=1, source_target_pairs={{0,8},{4,12},{8,0},{12,4},{1,9},{5,13},{9,1},{13,5},{2,10},{6,14},... | collective-permute-start | bytes 1327112 | tf_op jit(solution)/shard_map/ppermute | solution.py:540
  216.7 14.0 %collective-permute-start.41 = (f32[18,384]{1,0:T(8,128)S(1)}, f32[18,384]{1,0:T(8,128)S(1)}, u32[]{:S(2)}, u32[]{:S(2)}) collective-permute-start(f32[18,384]{1,0:T(8,128)S(1)} %concatenate.76), channel_id=1, source_target_pairs={{0,1},{1,0},{2,3},{3,2},{4,5},{5,4},{6,7},{7,6},{8,9},{9,8},{10,11... | collective-permute-start | bytes 82952 | tf_op jit(solution)/shard_map/ppermute | solution.py:540
  234.2 5.3 %collective-permute-start.43 = (bf16[1,96,768]{2,1,0:T(8,128)(2,1)S(1)}, bf16[1,96,768]{2,1,0:T(8,128)(2,1)S(1)}, u32[]{:S(2)}, u32[]{:S(2)}) collective-permute-start(bf16[1,96,768]{2,1,0:T(8,128)(2,1)S(1)} %get-tuple-element.343), channel_id=1, source_target_pairs={{0,8},{4,12},{8,0},{12,4},{1,9},{5,13},{9,1},{13,5},{2,10},{6,14},... | collective-permute-start | bytes 442376 | tf_op jit(solution)/shard_map/ppermute | solution.py:540
  235.8 5.1 %collective-permute-start.44 = (bf16[1,96,768]{2,1,0:T(8,128)(2,1)S(1)}, bf16[1,96,768]{2,1,0:T(8,128)(2,1)S(1)}, u32[]{:S(2)}, u32[]{:S(2)}) collective-permute-start(bf16[1,96,768]{2,1,0:T(8,128)(2,1)S(1)} %get-tuple-element.342), channel_id=1, source_target_pairs={{0,16},{16,0},{1,17},{17,1},{2,18},{18,2},{3,19},{19,3},{4,20},{20... | collective-permute-start | bytes 442376 | tf_op jit(solution)/shard_map/ppermute | solution.py:540
  236.4 10.3 %collective-permute-start.42 = (bf16[2,96,768]{2,1,0:T(8,128)(2,1)}, bf16[2,96,768]{2,1,0:T(8,128)(2,1)S(1)}, u32[]{:S(2)}, u32[]{:S(2)}) collective-permute-start(bf16[2,96,768]{2,1,0:T(8,128)(2,1)} %pad_maximum_fusion.19), channel_id=1, source_target_pairs={{0,1},{1,0},{2,3},{3,2},{4,5},{5,4},{6,7},{7,6},{8,9},{9,8},{10,11... | collective-permute-start | bytes 884744 | tf_op jit(solution)/shard_map/ppermute | solution.py:540
  236.4 13.0 %collective-permute-start.45 = (bf16[512,768]{1,0:T(8,128)(2,1)}, bf16[512,768]{1,0:T(8,128)(2,1)S(1)}, u32[]{:S(2)}, u32[]{:S(2)}) collective-permute-start(bf16[512,768]{1,0:T(8,128)(2,1)} %collective-permute-done.36.refs_1_), channel_id=1, source_target_pairs={{1,2},{2,3},{5,6},{6,7},{9,10},{10,11},{13,14},{14,15},{17,18},{18... | collective-permute-start | bytes 2359304 | tf_op jit(solution)/shard_map/ppermute | solution.py:686
  237.1 26.3 %collective-permute-start.46 = (bf16[512,768]{1,0:T(8,128)(2,1)}, bf16[512,768]{1,0:T(8,128)(2,1)S(1)}, u32[]{:S(2)}, u32[]{:S(2)}) collective-permute-start(bf16[512,768]{1,0:T(8,128)(2,1)} %collective-permute-done.37.refs_4_), channel_id=1, source_target_pairs={{1,0},{2,1},{5,4},{6,5},{9,8},{10,9},{13,12},{14,13},{17,16},{18,1... | collective-permute-start | bytes 2359304 | tf_op jit(solution)/shard_map/ppermute | solution.py:687
  242.7 31.4 %collective-permute-start.50 = (bf16[2,96,768]{2,1,0:T(8,128)(2,1)}, bf16[2,96,768]{2,1,0:T(8,128)(2,1)S(1)}, u32[]{:S(2)}, u32[]{:S(2)}) collective-permute-start(bf16[2,96,768]{2,1,0:T(8,128)(2,1)} %pad_maximum_fusion.21), channel_id=1, source_target_pairs={{0,1},{1,0},{2,3},{3,2},{4,5},{5,4},{6,7},{7,6},{8,9},{9,8},{10,11... | collective-permute-start | bytes 884744 | tf_op jit(solution)/shard_map/ppermute | solution.py:540
  249.4 18.5 %copy-start.38 = (bf16[512,768]{1,0:T(8,128)(2,1)}, bf16[512,768]{1,0:T(8,128)(2,1)S(1)}, u32[]{:S(2)}) copy-start(bf16[512,768]{1,0:T(8,128)(2,1)S(1)} %collective-permute-done.45.refs_2_.refs_3_) | copy-start | bytes 2359300
  263.4 15.3 %collective-permute-start.47 = (bf16[2,96,768]{2,1,0:T(8,128)(2,1)}, bf16[2,96,768]{2,1,0:T(8,128)(2,1)S(1)}, u32[]{:S(2)}, u32[]{:S(2)}) collective-permute-start(bf16[2,96,768]{2,1,0:T(8,128)(2,1)} %pad_maximum_fusion.20), channel_id=1, source_target_pairs={{0,2},{1,3},{2,0},{3,1},{4,6},{5,7},{6,4},{7,5},{8,10},{9,11},{10,... | collective-permute-start | bytes 884744 | tf_op jit(solution)/shard_map/ppermute | solution.py:540
  263.4 21.6 %collective-permute-start.52 = (f32[15,384]{1,0:T(8,128)S(1)}, f32[15,384]{1,0:T(8,128)S(1)}, u32[]{:S(2)}, u32[]{:S(2)}) collective-permute-start(f32[15,384]{1,0:T(8,128)S(1)} %pad_maximum_fusion.27), channel_id=1, source_target_pairs={{0,2},{1,3},{2,0},{3,1},{4,6},{5,7},{6,4},{7,5},{8,10},{9,11},{10,... | collective-permute-start | bytes 69128 | tf_op jit(solution)/shard_map/ppermute | solution.py:540
  266.3 32.0 %collective-permute-start.48 = (bf16[512,768]{1,0:T(8,128)(2,1)S(1)}, bf16[512,768]{1,0:T(8,128)(2,1)}, u32[]{:S(2)}, u32[]{:S(2)}) collective-permute-start(bf16[512,768]{1,0:T(8,128)(2,1)S(1)} %collective-permute-done.45.refs_2_.refs_3_), channel_id=1, source_target_pairs={{2,3},{6,7},{10,11},{14,15},{18,19},{22,23},{26,27},{30,31}} | collective-permute-start | bytes 2359304 | tf_op jit(solution)/shard_map/ppermute | solution.py:686
  272.8 25.6 %collective-permute-start.49 = (bf16[512,768]{1,0:T(8,128)(2,1)}, bf16[512,768]{1,0:T(8,128)(2,1)S(1)}, u32[]{:S(2)}, u32[]{:S(2)}) collective-permute-start(bf16[512,768]{1,0:T(8,128)(2,1)} %copy-done.39), channel_id=1, source_target_pairs={{1,0},{5,4},{9,8},{13,12},{17,16},{21,20},{25,24},{29,28}} | collective-permute-start | bytes 2359304 | tf_op jit(solution)/shard_map/ppermute | solution.py:687
  274.8 10.3 %collective-permute-start.51 = (bf16[96,768]{1,0:T(8,128)(2,1)}, bf16[96,768]{1,0:T(8,128)(2,1)S(1)}, u32[]{:S(2)}, u32[]{:S(2)}) collective-permute-start(bf16[96,768]{1,0:T(8,128)(2,1)} %fusion.10), channel_id=1, source_target_pairs={{0,2},{1,3},{2,0},{3,1},{4,6},{5,7},{6,4},{7,5},{8,10},{9,11},{10,... | collective-permute-start | bytes 442376 | tf_op jit(solution)/shard_map/ppermute | solution.py:540
  279.5 7.4 %collective-permute-start.56 = (bf16[2,96,768]{2,1,0:T(8,128)(2,1)}, bf16[2,96,768]{2,1,0:T(8,128)(2,1)S(1)}, u32[]{:S(2)}, u32[]{:S(2)}) collective-permute-start(bf16[2,96,768]{2,1,0:T(8,128)(2,1)} %get-tuple-element.324), channel_id=1, source_target_pairs={{0,16},{16,0},{1,17},{17,1},{2,18},{18,2},{3,19},{19,3},{4,20},{20... | collective-permute-start | bytes 884744 | tf_op jit(solution)/shard_map/ppermute | solution.py:540
  285.0 1.3 collective-permute-start.54
  285.2 6.3 %collective-permute-start.53 = (bf16[96,768]{1,0:T(8,128)(2,1)S(1)}, bf16[96,768]{1,0:T(8,128)(2,1)S(1)}, u32[]{:S(2)}, u32[]{:S(2)}) collective-permute-start(bf16[96,768]{1,0:T(8,128)(2,1)S(1)} %get-tuple-element.326), channel_id=1, source_target_pairs={{0,16},{16,0},{1,17},{17,1},{2,18},{18,2},{3,19},{19,3},{4,20},{20... | collective-permute-start | bytes 442376 | tf_op jit(solution)/shard_map/ppermute | solution.py:540
  286.3 3.8 %collective-permute-start.55 = (f32[15,384]{1,0:T(8,128)S(1)}, f32[15,384]{1,0:T(8,128)S(1)}, u32[]{:S(2)}, u32[]{:S(2)}) collective-permute-start(f32[15,384]{1,0:T(8,128)S(1)} %add.568), channel_id=1, source_target_pairs={{0,8},{4,12},{8,0},{12,4},{1,9},{5,13},{9,1},{13,5},{2,10},{6,14},... | collective-permute-start | bytes 69128 | tf_op jit(solution)/shard_map/ppermute | solution.py:540
  291.5 3.8 %collective-permute-start.57 = (f32[15,384]{1,0:T(8,128)S(1)}, f32[15,384]{1,0:T(8,128)S(1)}, u32[]{:S(2)}, u32[]{:S(2)}) collective-permute-start(f32[15,384]{1,0:T(8,128)S(1)} %add.569), channel_id=1, source_target_pairs={{0,16},{16,0},{1,17},{17,1},{2,18},{18,2},{3,19},{19,3},{4,20},{20... | collective-permute-start | bytes 69128 | tf_op jit(solution)/shard_map/ppermute | solution.py:540
  (49 other events, 236.1 us)

commit v5 on v4

--- a/solution.py
+++ b/solution.py
@@ -81,7 +81,8 @@
     return pl.BlockSpec((1, *shape), lambda i, at: (i,) + (0,) * len(shape))
 
 
-def attend_kernel(heads, scale, at_ref, x_ref, w_ref, bias_ref, seg_ref, extra_ref, *out_refs):
+def attend_kernel(heads, scale, at_ref, x_ref, w_ref, bias_ref, seg_ref, extra_ref, *refs):
+    *out_refs, q_low, k_side, v_low, sum_ref = refs
     x = x_ref[0]
     size = w_ref.shape[1] // heads
     q_t = ((dot_t(w_ref[0], x) + column(bias_ref[0:1])).astype(BF) * scale).astype(BF)
@@ -89,12 +90,18 @@
     v_t = (dot_t(w_ref[2], x) + column(bias_ref[1:2])).astype(BF)
     row = seg_ref[pl.ds(pl.program_id(0), 1)].astype(F32)
     allowed = column(row) == row
-    parts = []
+    q_low[...] = q_t.reshape(q_low.shape)
+    v_low[...] = v_t.reshape(v_low.shape)
     for h in range(heads):
-        at = slice(h * size, (h + 1) * size)
-        grown, inv = softmax_columns(dot(k[:, at], q_t[at]), allowed)
-        parts.append(dot(v_t[at], grown.astype(BF)) * inv)
-    context = jnp.concatenate(parts, 0).T.astype(BF)
+        k_side[h] = k[:, h * size : (h + 1) * size]
+
+    def one_head(h, carry):
+        grown, inv = softmax_columns(dot(k_side[h], q_low[h]), allowed)
+        sum_ref[pl.ds(pl.multiple_of(h * size, size), size)] = dot(v_low[h], grown.astype(BF)) * inv
+        return carry
+
+    lax.fori_loop(0, heads, one_head, 0)
+    context = sum_ref[...].T.astype(BF)
     count, rows, cols = len(out_refs), context.shape[0] // 2, context.shape[1]
     ahead = lax.rem(pl.program_id(0) + count - at_ref[3], count)
     for s, out_ref in enumerate(out_refs):
@@ -113,6 +120,10 @@
         [slot(length, width), const(3, cols, width), const(2, cols), const(seqs, length), const(*extra.shape)],
         [const(length // 2 + extra.shape[0], 2 * cols)] * seqs,
         [jax.ShapeDtypeStruct((length // 2 + extra.shape[0], 2 * cols), BF)] * seqs,
+        [
+            pltpu.VMEM((heads, cols // heads, length), BF), pltpu.VMEM((heads, length, cols // heads), BF),
+            pltpu.VMEM((heads, cols // heads, length), BF), pltpu.VMEM((cols, length), F32),
+        ],
     )(at, tokens, w_rows, bias, segments, extra)
 
 
@@ -168,20 +179,17 @@
 def rise_kernel(slots, at_ref, *refs):
     ctx_refs = refs[:slots]
     (w_out_ref, x_ref, gains_ref, shifts_ref, own_ref, mine_ref, theirs_ref, bias_ref,
-     hidden_ref, low_ref, norm_ref, recip_ref, act_ref, slope_ref, x_rel_ref, hidden_rel_ref, held, sems) = refs[slots:]
+     hidden_ref, low_ref, norm_ref, recip_ref, act_ref, slope_ref, x_rel_ref, hidden_rel_ref, held, sems, ctx_ref) = refs[slots:]
     step = pl.program_id(0)
     weight = fetch_slot(at_ref, (own_ref, mine_ref, theirs_ref), held, sems)
 
     @pl.when(step == 0)
     def _():
         rows, cols = low_ref.shape[0] // 2, w_out_ref.shape[1]
-        sides = []
-        for side in (slice(0, cols), slice(cols, None)):
-            share = dot(ctx_refs[0][:rows, side], w_out_ref[0])
-            for s in range(1, slots):
-                share += dot(ctx_refs[s][:rows, side], w_out_ref[s])
-            sides.append(share)
-        attention = jnp.concatenate(sides)
+        for s in range(slots):
+            ctx_ref[:rows, s * cols : (s + 1) * cols] = ctx_refs[s][:rows, :cols]
+            ctx_ref[rows:, s * cols : (s + 1) * cols] = ctx_refs[s][:rows, cols:]
+        attention = dot(ctx_ref[...], w_out_ref[...].reshape(slots * cols, -1))
         own = x_ref[0].astype(F32)
         norm, recip = normalize(own + attention + shifts_ref[0:1])
         hidden = norm * gains_ref[0:1] + shifts_ref[1:2]
@@ -192,10 +200,17 @@
         store_relative(x_rel_ref, own, at_ref)
         store_relative(hidden_rel_ref, hidden, at_ref)
 
-    pre = dot(low_ref[...], weight) + bias_ref[0]
-    cumul = 0.5 * (1.0 + lax.erf(pre * (1.0 / math.sqrt(2.0))))
-    act_ref[0] = (pre * cumul).astype(BF)
-    slope_ref[0] = (cumul + pre * jnp.exp(-0.5 * pre * pre) * (1.0 / math.sqrt(2.0 * math.pi))).astype(BF)
+    part = 256 if weight.shape[1] % 256 == 0 else weight.shape[1]
+    spots = [slice(i, i + part) for i in range(0, weight.shape[1], part)]
+    ready = dot(low_ref[...], weight[:, spots[0]])
+    for i, cols in enumerate(spots):
+        pre = ready + bias_ref[0, :, cols]
+        if i + 1 < len(spots):
+            ready = dot(low_ref[...], weight[:, spots[i + 1]])
+        cumul = 0.5 * (1.0 + lax.erf(pre * (1.0 / math.sqrt(2.0))))
+        slope = cumul + pre * jnp.exp(-0.5 * pre * pre) * (1.0 / math.sqrt(2.0 * math.pi))
+        act_ref[0, :, cols] = (pre * cumul).astype(BF)
+        slope_ref[0, :, cols] = slope.astype(BF)
 
 
 def rise(at, ctx, w_out, x, gains, shifts, w_in, bias):
@@ -222,7 +237,7 @@
             jax.ShapeDtypeStruct((width, rows), BF),
             jax.ShapeDtypeStruct((width, rows), BF),
         ],
-        held_scratch(slots, w_in),
+        held_scratch(slots, w_in) + [pltpu.VMEM((rows, slots * cols), BF)],
     )(at, *ctx, w_out, x, gains, shifts, *pieces(w_in), bias[:, None, :])
 
 
@@ -397,7 +412,6 @@
             ctx_ref[:rows] = ctx_refs[i][:rows, :cols]
             ctx_ref[rows:] = ctx_refs[i][:rows, cols:]
 
-    store_parts(keep_ref, send_ref, s < slots // 2, proj_ref.shape[1], dot(grad_rel_ref[...], ctx_ref[...]))
     x, low = x_ref[0], low_ref[...]
     cols = w_out_ref.shape[1]
     size = cols // heads
@@ -412,16 +426,24 @@
     gc = gc_t.T
     row = seg_ref[pl.ds(at_ref[3], 1)].astype(F32)
     allowed = column(row) == row
+    spot = lambda h: slice(h * size, (h + 1) * size)
+    first_of = lambda h: (dot(k[:, spot(h)], q_scaled[spot(h)]), dot(v[:, spot(h)], gc_t[spot(h)]))
+    ready = first_of(0)
     for h in range(heads):
-        at = slice(h * size, (h + 1) * size)
-        grown, inv = softmax_columns(dot(k[:, at], q_scaled[at]), allowed)
+        at = spot(h)
+        raw, grad_probs = ready
+        if h + 1 < heads:
+            ready = first_of(h + 1)
+        if h == 0:
+            whole = dot(grad_rel_ref[...], ctx_ref[...])
+            store_parts(keep_ref, send_ref, s < slots // 2, proj_ref.shape[1], whole)
+        grown, inv = softmax_columns(raw, allowed)
         probs = grown * inv
-        grad_probs = dot(v[:, at], gc_t[at])
         inner = jnp.sum(probs * grad_probs, axis=0, keepdims=True)
         grad_scores = (probs * (grad_probs - inner) * scale).astype(BF)
+        v_ref[:, at] = dot(probs.astype(BF), gc[:, at])
         q_ref[at] = dot(k_t[at], grad_scores)
         k_ref[:, at] = dot(grad_scores, q[:, at])
-        v_ref[:, at] = dot(probs.astype(BF), gc[:, at])
     grad_q = q_ref[...].T
     grad_v = v_ref[...]
     vec_ref[0, 0:1] = col_sum(grad_q)
@@ -619,23 +641,22 @@
         first = jnp.concatenate([piece_of(w_out), piece_of(w_in), piece_of(w_down)])
         first_z = [cyclic(first, s) for s in others]
         done(first)
-        piece_qkv = lax.dynamic_slice(
-            hold(flat_qkv), ((y * 2 + x) * (flat_qkv.shape[0] // 4), core * half), (flat_qkv.shape[0] // 4, half)
-        )
         biases = jnp.concatenate([b_inner.reshape(-1), b_qv.reshape(-1)])
         bias_rows = -(-biases.size // half)
         bias_pack = in_three(jnp.pad(hold(biases), (0, bias_rows * half - biases.size)).reshape(bias_rows, half))
         bias_pack = jnp.pad(bias_pack.reshape(3 * bias_rows, half), ((0, -3 * bias_rows % 16), (0, 0)))
-        extra = jnp.concatenate([bias_pack, piece_qkv])
-
-        context = attend(at, hold(tokens), qkv_rows, b_qv.reshape(2, head_cols), segments, heads, extra)
+
+        context = attend(at, hold(tokens), qkv_rows, b_qv.reshape(2, head_cols), segments, heads, bias_pack)
         (ctx_own, *ctx_send), first_z = run((context, first_z))
         ctx_z = [cyclic(v, s) for v, s in zip(ctx_send, others)]
         cut, end = w_out.shape[0] // 8, (w_out.shape[0] + w_in.shape[0]) // 8
         a, b = halves(first_z, slice(0, end))
         a1, b1 = by_x(a), by_y(b)
         c, d = halves(first_z, slice(end, None))
-        done(c, d, a1, b1)
+        piece_qkv = lax.dynamic_slice(
+            hold(flat_qkv), ((y * 2 + x) * (flat_qkv.shape[0] // 4), core * half), (flat_qkv.shape[0] // 4, half)
+        )
+        done(c, d, piece_qkv, a1, b1)
         a, b = plane_two(*hold((a, b, a1, b1)))
         a1, b1 = by_y(a), by_x(b)
         done(a, b, *ctx_z)
@@ -649,21 +670,23 @@
         b_inner_all = bias_all[:, :hidden_cols]
         b_qv_all = bias_all[:, hidden_cols:].reshape(n_tensor, 2, head_cols)
         done(b_inner_all, a1, b1)
-        a, b, a1, b1 = hold((a, b, a1, b1))
+        a, b, a1, b1, piece_qkv = hold((a, b, a1, b1, piece_qkv))
+        third_z = [cyclic(piece_qkv, s) for s in others]
         in_both = plane_three(a, b, a1, b1, slice(cut, None))
-        in_core = by_core(in_both)
         out_both = plane_three(a, b, a1, b1, slice(0, cut))
-        out_core = by_core(out_both)
-        done(in_both, out_both, c1, d1)
-        c, d = plane_two(*hold((c, d, c1, d1)))
-        c1, d1 = by_y(c), by_x(d)
-        done(c, d, out_core, in_core)
+        done(in_both, out_both, b_inner_all, c1, d1)
+        in_both, out_both, c, d, c1, d1 = hold((in_both, out_both, c, d, c1, d1))
+        in_core, out_core = by_core(in_both), by_core(out_both)
+        c, d = plane_two(c, d, c1, d1)
+        done(c, d, in_core, out_core)
+        c1, d1 = by_y(hold(c)), by_x(hold(d))
         out_got = ordered(*hold((out_both, out_core)), core, 0).transpose(3, 0, 1, 2, 4, 5)
         out_all = jnp.concatenate([w_out[None], out_got.reshape(n_tensor - 1, *w_out.shape)])
         in_parts = (w_in, in_both, in_core)
-        e = jnp.stack([p[-piece_qkv.shape[0] :] for p in ctx_z])
+        done(out_all, *third_z)
+        e = jnp.stack(hold(third_z))
         e1 = by_x(e)
-        done(out_all, in_core, e)
+        done(e)
         ctx = [ctx_own, *ctx_z]
         made = rise(at, hold(ctx), out_all, tokens, gains, shifts, in_parts, b_inner_all)
         made, c1, d1, e1 = run((made, c1, d1, e1))

time: 307 us -> 303 us (0.987)
  waiting for transfers between devices: 66.6 us -> 63.1 us
    ppermute x6, starting transfers between devices: 18.5 us -> 10.9 us  [hop(): lax.ppermute(right, 'tensor', steps[step:])]
    ppermute x6 -> x9, starting transfers between devices: 17.2 us -> 23.7 us  [local(): lax.ppermute(v, 'tensor', [(i, (i + s) % n_tensor) for i in range(n_tenso...]
    ppermute x6 -> x9, waiting for transfers between devices: 18.7 us -> 13.2 us  [local(): lax.ppermute(v, 'tensor', [(i, (i + s) % n_tensor) for i in range(n_tenso...]
    unnamed x123 -> x121, local copies, waits for them, and re-layouts: 12.7 us -> 14.3 us
  transfers between devices with their start and end apart: 58 -> 61, of which waited for: 20 -> 22; matrix products, arithmetic and copies ran while one was open for 13% -> 14% of each run, Pallas kernels for 30% -> 30%
where the time goes in v5:
time: 303 us; the launch traced here: 298 us
  Pallas kernels  91.5 us (30%)
  starting transfers between devices  82.8 us (27%)
  waiting for transfers between devices  63.1 us (21%)
  other arithmetic  35.8 us (12%)
  local copies, waits for them, and re-layouts  21.9 us (7%)
    ppermute x40, starting transfers between devices, swap(): return lax.ppermute(value, axis, [(i, i ^ bit) for i in range(size)])  40 us
    pallas_call x2, Pallas kernels, attend_back(): call(functools.partial(attend_back_kernel, first, slots, heads, (cols //...  31 us
    ppermute x40, waiting for transfers between devices, swap(): return lax.ppermute(value, axis, [(i, i ^ bit) for i in range(size)])  30.3 us
    ppermute x9, starting transfers between devices, local(): lax.ppermute(v, 'tensor', [(i, (i + s) % n_tensor) for i in range(n_tenso...  23.7 us
    ppermute x6, waiting for transfers between devices, hop(): lax.ppermute(left, 'tensor', back_steps[:len(steps) - step])  19.6 us
    pallas_call x1, Pallas kernels, back(): call(functools.partial(back_kernel, slots), 'back', at, (slots,), [const(...  14.6 us
    unnamed x121, local copies, waits for them, and re-layouts  14.3 us
    ppermute x9, waiting for transfers between devices, local(): lax.ppermute(v, 'tensor', [(i, (i + s) % n_tensor) for i in range(n_tenso...  13.2 us
  transfers between devices with their start and end apart: 61, of which 22 were waited for; matrix products, arithmetic and copies ran while one was open for 14% of the time, Pallas kernels for 30%

profile of v5, /device:TPU:0, one launch (start us, length us, event | category | flops | bytes accessed | tf_op | source)
XLA Modules:
  0.0 297.7 jit_solution(4321358630404761455)
XLA Ops:
  2.6 3.1 %collective-permute-start = (bf16[216,768]{1,0:T(8,128)(2,1)S(1)}, bf16[216,768]{1,0:T(8,128)(2,1)S(1)}, u32[]{:S(2)}, u32[]{:S(2)}) collective-permute-start(bf16[216,768]{1,0:T(8,128)(2,1)S(1)} %pad_maximum_fusion.16), channel_id=1, source_target_pairs={{0,1},{1,2},{2,3},{3,0},{4,5},{5,6},{6,7},{7,4},{8,9},{9,10},{10,1... | collective-permute-start | bytes 995336 | tf_op jit(solution)/shard_map/ppermute | solution.py:611
  5.6 2.6 collective-permute-start.1
  8.2 1.3 collective-permute-start.2
  11.4 1.9 copy-done
  14.0 12.8 %attend.1 = (bf16[272,384]{1,0:T(8,128)(2,1)S(1)}, bf16[272,384]{1,0:T(8,128)(2,1)S(1)}, bf16[272,384]{1,0:T(8,128)(2,1)S(1)}, bf16[272,384]{1,0:T(8,128)(2,1)S(1)}) custom-call(s32[4]{0:T(128)S(1)} %pad_add_fusion.at_ref, bf16[4,512,768]{2,1,0:T(8,128)(2,1)S(1)} %copy-done, bf16[3,192,768]{2,1,0:T(8,128)(2,1)S(1)} %bitcast.292, ...), custom_call_target="tpu_custom_call" | custom-call | flops 1000 | bytes 1000 | tf_op jit(solution)/shard_map/attend/pallas_call | solution.py:118
  26.8 3.0 %collective-permute-done.1 = bf16[216,768]{1,0:T(8,128)(2,1)S(1)} collective-permute-done((bf16[216,768]{1,0:T(8,128)(2,1)S(1)}, bf16[216,768]{1,0:T(8,128)(2,1)S(1)}, u32[]{:S(2)}, u32[]{:S(2)}) %collective-permute-start.1) | collective-permute-done | bytes 331808 | tf_op jit(solution)/shard_map/ppermute | solution.py:611
  30.0 1.6 collective-permute-start.7
  31.6 1.6 collective-permute-start.6
  33.2 7.6 %collective-permute-start.3 = (bf16[272,384]{1,0:T(8,128)(2,1)S(1)}, bf16[272,384]{1,0:T(8,128)(2,1)S(1)}, u32[]{:S(2)}, u32[]{:S(2)}) collective-permute-start(bf16[272,384]{1,0:T(8,128)(2,1)S(1)} %get-tuple-element.175), channel_id=1, source_target_pairs={{0,1},{1,2},{2,3},{3,0},{4,5},{5,6},{6,7},{7,4},{8,9},{9,10},{10,1... | collective-permute-start | bytes 626696 | tf_op jit(solution)/shard_map/ppermute | solution.py:611
  40.8 1.6 collective-permute-start.4
  45.5 2.5 collective-permute-done.3.refs_1_
  48.0 6.6 %collective-permute-done.4.refs_2_.refs_0_ = bf16[272,384]{1,0:T(8,128)(2,1)S(1)} collective-permute-done((bf16[272,384]{1,0:T(8,128)(2,1)S(1)}, bf16[272,384]{1,0:T(8,128)(2,1)S(1)}, u32[]{:S(2)}, u32[]{:S(2)}) %collective-permute-start.4) | collective-permute-done | bytes 208928 | tf_op jit(solution)/shard_map/ppermute | solution.py:611
  55.9 1.8 collective-permute-done.9
  57.7 1.3 collective-permute-done.8
  63.5 4.1 %collective-permute-start.10 = (bf16[144,384]{1,0:T(8,128)(2,1)S(1)}, bf16[144,384]{1,0:T(8,128)(2,1)S(1)}, u32[]{:S(2)}, u32[]{:S(2)}) collective-permute-start(bf16[144,384]{1,0:T(8,128)(2,1)S(1)} %dynamic_slice.24), channel_id=1, source_target_pairs={{0,1},{1,2},{2,3},{3,0},{4,5},{5,6},{6,7},{7,4},{8,9},{9,10},{10,1... | collective-permute-start | bytes 331784 | tf_op jit(solution)/shard_map/ppermute | solution.py:611
  68.8 1.4 collective-permute-start.12
  72.9 1.5 collective-permute-start.17
  76.8 1.3 collective-permute-start.19
  78.2 10.1 %rise.1 = (f32[512,768]{1,0:T(8,128)S(1)}, bf16[512,768]{1,0:T(8,128)(2,1)}, f32[512,768]{1,0:T(8,128)S(1)}, f32[512,1]{1,0:T(8,128)S(1)}, bf16[4,512,768]{2,1,0...) custom-call(s32[4]{0:T(128)S(1)} %pad_add_fusion.at_ref, ...), custom_call_target="tpu_custom_call" | custom-call | flops 1000 | bytes 1000 | tf_op jit(solution)/shard_map/rise/pallas_call | solution.py:219
  89.2 2.9 collective-permute-done.19
  92.8 1.6 collective-permute-start.21
  94.5 1.8 collective-permute-done.20
  96.6 11.1 %fall.1 = (bf16[512,768]{1,0:T(8,128)(2,1)S(1)}, f32[512,768]{1,0:T(8,128)S(1)}, bf16[512,768]{1,0:T(8,128)(2,1)S(1)}, f32[3,768]{1,0:T(4,128)S(1)}, bf16[4,4,96...) custom-call(s32[4]{0:T(128)S(1)} %pad_add_fusion.at_ref, bf16[4,512,768]{2,1,0:T(8,128)(2,1)S(1)} %copy-done.8, ...), custom_call_target="tpu_custom_call" | custom-call | flops 1000 | bytes 1000 | tf_op jit(solution)/shard_map/fall/pallas_call | solution.py:305
  107.8 2.4 collective-permute-done.21
  111.1 4.2 %collective-permute-start.24 = (bf16[512,768]{1,0:T(8,128)(2,1)S(1)}, bf16[512,768]{1,0:T(8,128)(2,1)}, u32[]{:S(2)}, u32[]{:S(2)}) collective-permute-start(bf16[512,768]{1,0:T(8,128)(2,1)S(1)} %get-tuple-element.232.refs_0_), channel_id=1, source_target_pairs={{0,1},{1,2},{2,3},{4,5},{5,6},{6,7},{8,9},{9,10},{10,11},{12,13},{... | collective-permute-start | bytes 2359304 | tf_op jit(solution)/shard_map/ppermute | solution.py:709
  115.3 1.5 collective-permute-start.25
  118.0 1.5 collective-permute-start.27
  119.5 14.6 %back.1 = (f32[4,1,768]{2,1,0:T(1,128)S(1)}, f32[512,768]{1,0:T(8,128)S(1)}, bf16[512,768]{1,0:T(8,128)(2,1)S(1)}, bf16[768,512]{1,0:T(8,128)(2,1)S(1)}, f32[3,7...) custom-call(s32[4]{0:T(128)S(1)} %pad_add_fusion.at_ref, ...), custom_call_target="tpu_custom_call" | custom-call | flops 1000 | bytes 1000 | tf_op jit(solution)/shard_map/back/pallas_call | solution.py:360
  134.1 2.3 collective-permute-done.25.refs_4_
  136.8 4.5 %collective-permute-done.28 = bf16[4,4,96,768]{3,2,1,0:T(8,128)(2,1)S(1)} collective-permute-done((bf16[4,4,96,768]{3,2,1,0:T(8,128)(2,1)}, bf16[4,4,96,768]{3,2,1,0:T(8,128)(2,1)S(1)}, u32[]{:S(2)}, u32[]{:S(2)}) %collective-permute-start.28) | collective-permute-done | bytes 2359328 | tf_op jit(solution)/shard_map/ppermute | solution.py:562
  142.7 1.3 collective-permute-start.32
  146.0 1.5 collective-permute-start.29
  147.6 1.3 collective-permute-start.30
  150.9 15.4 %attend_back.2 = (f32[2,2,192]{2,1,0:T(2,128)S(1)}, f32[512,768]{1,0:T(8,128)}, bf16[4,2,96,768]{3,2,1,0:T(8,128)(2,1)S(1)}, bf16[4,2,96,768]{3,2,1,0:T(8,128)(2,1)S(1)}) custom-call(s32[4]{0:T(128)S(1)} %pad_add_fusion.at_ref, bf16[4,512,768]{2,1,0:T(8,128)(2,1)} %x_ref.4, bf16[512,768]{1,0:T(8,128)(2,1)S(1)} %copy-done.12, f32[512,768]{1,0:T(8,128)} %copy-done.17, ...), custom_call_target="tpu_custom_call" | custom-call | flops 1000 | bytes 1000 | tf_op jit(solution)/shard_map/attend_back/pallas_call | solution.py:479
  166.3 3.2 %collective-permute-done.30.refs_5_ = bf16[512,768]{1,0:T(8,128)(2,1)} collective-permute-done((bf16[512,768]{1,0:T(8,128)(2,1)}, bf16[512,768]{1,0:T(8,128)(2,1)}, u32[]{:S(2)}, u32[]{:S(2)}) %collective-permute-start.30) | collective-permute-done | bytes 786464 | tf_op jit(solution)/shard_map/ppermute | solution.py:710
  169.5 1.6 collective-permute-start.34
  171.1 1.5 collective-permute-start.35
  172.6 1.6 fusion
  175.9 1.5 fusion.37
  177.5 3.6 %collective-permute-start.38 = (bf16[2,96,768]{2,1,0:T(8,128)(2,1)S(1)}, bf16[2,96,768]{2,1,0:T(8,128)(2,1)}, u32[]{:S(2)}, u32[]{:S(2)}) collective-permute-start(bf16[2,96,768]{2,1,0:T(8,128)(2,1)S(1)} %pad_maximum_fusion.18), channel_id=1, source_target_pairs={{0,1},{1,0},{2,3},{3,2},{4,5},{5,4},{6,7},{7,6},{8,9},{9,8},{10,11... | collective-permute-start | bytes 884744 | tf_op jit(solution)/shard_map/ppermute | solution.py:562
  181.1 15.6 %attend_back.3 = (f32[2,2,192]{2,1,0:T(2,128)S(1)}, bf16[512,768]{1,0:T(8,128)(2,1)S(1)}, bf16[4,2,96,768]{3,2,1,0:T(8,128)(2,1)S(1)}, bf16[4,2,96,768]{3,2,1,0:T(8,128)(2,1)}) custom-call(s32[4]{0:T(128)S(1)} %pad_add_fusion.at_ref, bf16[4,512,768]{2,1,0:T(8,128)(2,1)} %x_ref.4, bf16[512,768]{1,0:T(8,128)(2,1)S(1)} %copy-done.12, ...), custom_call_target="tpu_custom_call" | custom-call | flops 1000 | bytes 1000 | tf_op jit(solution)/shard_map/attend_back/pallas_call | solution.py:479
  197.8 1.8 collective-permute-done.38
  201.3 1.4 collective-permute-start.39
  202.6 1.3 collective-permute-start.40
  203.9 2.6 fusion.28
  211.3 2.7 collective-permute-start.44
  214.0 1.4 fusion.14
  215.4 1.7 pad_maximum_fusion.19
  217.7 7.5 %collective-permute-done.44 = f32[18,384]{1,0:T(8,128)S(1)} collective-permute-done((f32[18,384]{1,0:T(8,128)S(1)}, f32[18,384]{1,0:T(8,128)S(1)}, u32[]{:S(2)}, u32[]{:S(2)}) %collective-permute-start.44) | collective-permute-done | bytes 27680 | tf_op jit(solution)/shard_map/ppermute | solution.py:562
  227.3 1.5 fusion.22
  231.1 1.3 collective-permute-start.49
  236.6 3.1 %collective-permute-start.53 = (bf16[2,96,768]{2,1,0:T(8,128)(2,1)}, bf16[2,96,768]{2,1,0:T(8,128)(2,1)S(1)}, u32[]{:S(2)}, u32[]{:S(2)}) collective-permute-start(bf16[2,96,768]{2,1,0:T(8,128)(2,1)} %pad_maximum_fusion.21), channel_id=1, source_target_pairs={{0,1},{1,0},{2,3},{3,2},{4,5},{5,4},{6,7},{7,6},{8,9},{9,8},{10,11... | collective-permute-start | bytes 884744 | tf_op jit(solution)/shard_map/ppermute | solution.py:562
  240.8 1.9 convert_add_fusion.9
  242.8 14.0 %collective-permute-done.49.refs_5_.refs_6_ = bf16[512,768]{1,0:T(8,128)(2,1)S(1)} collective-permute-done((bf16[512,768]{1,0:T(8,128)(2,1)}, bf16[512,768]{1,0:T(8,128)(2,1)S(1)}, u32[]{:S(2)}, u32[]{:S(2)}) %collective-permute-start.49) | collective-permute-done | bytes 786464 | tf_op jit(solution)/shard_map/ppermute | solution.py:710
  256.9 2.8 collective-permute-start.55
  259.7 1.5 collective-permute-start.51
  261.3 4.8 %place.3.whole_ref = f32[4,512,768]{2,1,0:T(8,128)} custom-call(s32[4]{0:T(128)} %copy-done.31, bf16[512,768]{1,0:T(8,128)(2,1)} %copy-done.6, bf16[512,768]{1,0:T(8,128)(2,1)} %copy-done.42, bf16[512,768]{1,0:T(8,128)(2,1)} %copy-done.35, bf16[512,768]{1,0:T(8,128)(2,1)} %copy-done.35, bf16[512,768]{1,0:T(8,128)(2,1)} %collective-permute-done.40.refs_4_, ...), custom_call_target="tpu_custom_call" | custom-call | flops 1000 | bytes 1000 | tf_op jit(solution)/shard_map/place/pallas_call | solution.py:553
  266.1 1.3 collective-permute-start.52
  268.1 3.4 %collective-permute-start.54 = (bf16[96,768]{1,0:T(8,128)(2,1)}, bf16[96,768]{1,0:T(8,128)(2,1)S(1)}, u32[]{:S(2)}, u32[]{:S(2)}) collective-permute-start(bf16[96,768]{1,0:T(8,128)(2,1)} %fusion.10), channel_id=1, source_target_pairs={{0,2},{1,3},{2,0},{3,1},{4,6},{5,7},{6,4},{7,5},{8,10},{9,11},{10,... | collective-permute-start | bytes 442376 | tf_op jit(solution)/shard_map/ppermute | solution.py:562
  273.9 2.1 collective-permute-start.59
  276.0 4.0 %place.2 = bf16[4,512,768]{2,1,0:T(8,128)(2,1)} custom-call(s32[4]{0:T(128)} %copy-done.31, bf16[512,768]{1,0:T(8,128)(2,1)} %copy-done.27, bf16[512,768]{1,0:T(8,128)(2,1)} %collective-permute-done.24.refs_1_, bf16[512,768]{1,0:T(8,128)(2,1)} %collective-permute-done.29.refs_2_, bf16[512,768]{1,0:T(8,128)(2,1)} %collective-permute-done.34.refs_3_, ...), custom_call_target="tpu_custom_call" | custom-call | flops 1000 | bytes 1000 | tf_op jit(solution)/shard_map/place/pallas_call | solution.py:553
  281.3 1.3 collective-permute-start.58
  285.1 1.4 collective-permute-done.56
  294.2 3.0 %place_end.1 = f32[4,512,768]{2,1,0:T(8,128)} custom-call(s32[4]{0:T(128)} %copy-done.31, bf16[512,768]{1,0:T(8,128)(2,1)} %copy-done.6, bf16[512,768]{1,0:T(8,128)(2,1)} %collective-permute-done.51.behind_ref, bf16[512,768]{1,0:T(8,128)(2,1)} %copy-done.41, f32[4,512,768]{2,1,0:T(8,128)} %place.3.whole_ref), custom_call_target="tpu_custom_call", output_to_operand_aliasing={{}: (4, {})} | custom-call | flops 1000 | bytes 1000 | tf_op jit(solution)/shard_map/place_end/pallas_call | solution.py:537
  (317 shorter events, 63.0 us)
Async XLA Ops:
  2.6 24.3 %collective-permute-start = (bf16[216,768]{1,0:T(8,128)(2,1)S(1)}, bf16[216,768]{1,0:T(8,128)(2,1)S(1)}, u32[]{:S(2)}, u32[]{:S(2)}) collective-permute-start(bf16[216,768]{1,0:T(8,128)(2,1)S(1)} %pad_maximum_fusion.16), channel_id=1, source_target_pairs={{0,1},{1,2},{2,3},{3,0},{4,5},{5,6},{6,7},{7,4},{8,9},{9,10},{10,1... | collective-permute-start | bytes 995336 | tf_op jit(solution)/shard_map/ppermute | solution.py:611
  5.6 24.2 %collective-permute-start.1 = (bf16[216,768]{1,0:T(8,128)(2,1)S(1)}, bf16[216,768]{1,0:T(8,128)(2,1)S(1)}, u32[]{:S(2)}, u32[]{:S(2)}) collective-permute-start(bf16[216,768]{1,0:T(8,128)(2,1)S(1)} %pad_maximum_fusion.16), channel_id=1, source_target_pairs={{0,2},{1,3},{2,0},{3,1},{4,6},{5,7},{6,4},{7,5},{8,10},{9,11},{10,... | collective-permute-start | bytes 995336 | tf_op jit(solution)/shard_map/ppermute | solution.py:611
  8.2 21.6 %collective-permute-start.2 = (bf16[216,768]{1,0:T(8,128)(2,1)S(1)}, bf16[216,768]{1,0:T(8,128)(2,1)S(1)}, u32[]{:S(2)}, u32[]{:S(2)}) collective-permute-start(bf16[216,768]{1,0:T(8,128)(2,1)S(1)} %pad_maximum_fusion.16), channel_id=1, source_target_pairs={{0,3},{1,0},{2,1},{3,2},{4,7},{5,4},{6,5},{7,6},{8,11},{9,8},{10,9... | collective-permute-start | bytes 995336 | tf_op jit(solution)/shard_map/ppermute | solution.py:611
  11.4 169.7 %copy-start.31 = (s32[4]{0:T(128)}, s32[4]{0:T(128)S(1)}, u32[]{:S(2)}) copy-start(s32[4]{0:T(128)S(1)} %pad_add_fusion.at_ref) | copy-start | bytes 52
  26.8 51.3 %copy-start.25 = (bf16[272,384]{1,0:T(8,128)(2,1)}, bf16[272,384]{1,0:T(8,128)(2,1)S(1)}, u32[]{:S(2)}) copy-start(bf16[272,384]{1,0:T(8,128)(2,1)S(1)} %get-tuple-element.207.refs_0_) | copy-start | bytes 626692
  30.0 14.1 %collective-permute-start.7 = (bf16[3,120,384]{2,1,0:T(8,128)(2,1)S(1)}, bf16[3,120,384]{2,1,0:T(8,128)(2,1)S(1)}, u32[]{:S(2)}, u32[]{:S(2)}) collective-permute-start(bf16[3,120,384]{2,1,0:T(8,128)(2,1)S(1)} %pad_maximum_fusion.23), channel_id=1, source_target_pairs={{0,16},{16,0},{1,17},{17,1},{2,18},{18,2},{3,19},{19,3},{4,20},{20... | collective-permute-start | bytes 829448 | tf_op jit(solution)/shard_map/ppermute | solution.py:562
  31.6 12.4 %collective-permute-start.6 = (bf16[3,120,384]{2,1,0:T(8,128)(2,1)S(1)}, bf16[3,120,384]{2,1,0:T(8,128)(2,1)S(1)}, u32[]{:S(2)}, u32[]{:S(2)}) collective-permute-start(bf16[3,120,384]{2,1,0:T(8,128)(2,1)S(1)} %pad_maximum_fusion.22), channel_id=1, source_target_pairs={{0,8},{4,12},{8,0},{12,4},{1,9},{5,13},{9,1},{13,5},{2,10},{6,14},... | collective-permute-start | bytes 829448 | tf_op jit(solution)/shard_map/ppermute | solution.py:562
  33.2 14.8 %collective-permute-start.3 = (bf16[272,384]{1,0:T(8,128)(2,1)S(1)}, bf16[272,384]{1,0:T(8,128)(2,1)S(1)}, u32[]{:S(2)}, u32[]{:S(2)}) collective-permute-start(bf16[272,384]{1,0:T(8,128)(2,1)S(1)} %get-tuple-element.175), channel_id=1, source_target_pairs={{0,1},{1,2},{2,3},{3,0},{4,5},{5,6},{6,7},{7,4},{8,9},{9,10},{10,1... | collective-permute-start | bytes 626696 | tf_op jit(solution)/shard_map/ppermute | solution.py:611
  40.8 13.8 %collective-permute-start.4 = (bf16[272,384]{1,0:T(8,128)(2,1)S(1)}, bf16[272,384]{1,0:T(8,128)(2,1)S(1)}, u32[]{:S(2)}, u32[]{:S(2)}) collective-permute-start(bf16[272,384]{1,0:T(8,128)(2,1)S(1)} %get-tuple-element.176), channel_id=1, source_target_pairs={{0,2},{1,3},{2,0},{3,1},{4,6},{5,7},{6,4},{7,5},{8,10},{9,11},{10,... | collective-permute-start | bytes 626696 | tf_op jit(solution)/shard_map/ppermute | solution.py:611
  42.4 12.2 %collective-permute-start.5 = (bf16[272,384]{1,0:T(8,128)(2,1)S(1)}, bf16[272,384]{1,0:T(8,128)(2,1)S(1)}, u32[]{:S(2)}, u32[]{:S(2)}) collective-permute-start(bf16[272,384]{1,0:T(8,128)(2,1)S(1)} %get-tuple-element.177), channel_id=1, source_target_pairs={{0,3},{1,0},{2,1},{3,2},{4,7},{5,4},{6,5},{7,6},{8,11},{9,8},{10,9... | collective-permute-start | bytes 626696 | tf_op jit(solution)/shard_map/ppermute | solution.py:611
  44.2 13.5 %collective-permute-start.9 = (bf16[2,3,120,384]{3,2,1,0:T(8,128)(2,1)S(1)}, bf16[2,3,120,384]{3,2,1,0:T(8,128)(2,1)}, u32[]{:S(2)}, u32[]{:S(2)}) collective-permute-start(bf16[2,3,120,384]{3,2,1,0:T(8,128)(2,1)S(1)} %pad_maximum_fusion.11), channel_id=1, source_target_pairs={{0,8},{4,12},{8,0},{12,4},{1,9},{5,13},{9,1},{13,5},{2,10},{6,14},... | collective-permute-start | bytes 1658888 | tf_op jit(solution)/shard_map/ppermute | solution.py:562
  44.9 14.1 %collective-permute-start.8 = (bf16[2,3,120,384]{3,2,1,0:T(8,128)(2,1)S(1)}, bf16[2,3,120,384]{3,2,1,0:T(8,128)(2,1)}, u32[]{:S(2)}, u32[]{:S(2)}) collective-permute-start(bf16[2,3,120,384]{3,2,1,0:T(8,128)(2,1)S(1)} %pad_maximum_fusion.10), channel_id=1, source_target_pairs={{0,16},{16,0},{1,17},{17,1},{2,18},{18,2},{3,19},{19,3},{4,20},{20... | collective-permute-start | bytes 1658888 | tf_op jit(solution)/shard_map/ppermute | solution.py:562
  48.0 30.1 %copy-start.23 = (bf16[272,384]{1,0:T(8,128)(2,1)}, bf16[272,384]{1,0:T(8,128)(2,1)S(1)}, u32[]{:S(2)}) copy-start(bf16[272,384]{1,0:T(8,128)(2,1)S(1)} %collective-permute-done.3.refs_1_) | copy-start | bytes 626692
  54.7 8.7 %collective-permute-start.14 = (bf16[3,96,384]{2,1,0:T(8,128)(2,1)S(1)}, bf16[3,96,384]{2,1,0:T(8,128)(2,1)}, u32[]{:S(2)}, u32[]{:S(2)}) collective-permute-start(bf16[3,96,384]{2,1,0:T(8,128)(2,1)S(1)} %pad_maximum_fusion.25), channel_id=1, source_target_pairs={{0,16},{16,0},{1,17},{17,1},{2,18},{18,2},{3,19},{19,3},{4,20},{20... | collective-permute-start | bytes 663560 | tf_op jit(solution)/shard_map/ppermute | solution.py:562
  55.2 8.2 %collective-permute-start.13 = (bf16[3,96,384]{2,1,0:T(8,128)(2,1)}, bf16[3,96,384]{2,1,0:T(8,128)(2,1)}, u32[]{:S(2)}, u32[]{:S(2)}) collective-permute-start(bf16[3,96,384]{2,1,0:T(8,128)(2,1)} %pad_maximum_fusion.24), channel_id=1, source_target_pairs={{0,8},{4,12},{8,0},{12,4},{1,9},{5,13},{9,1},{13,5},{2,10},{6,14},... | collective-permute-start | bytes 663560 | tf_op jit(solution)/shard_map/ppermute | solution.py:562
  63.4 9.0 %collective-permute-start.16 = (bf16[2,2,3,96,768]{4,3,2,1,0:T(8,128)(2,1)S(1)}, bf16[2,2,3,96,768]{4,3,2,1,0:T(8,128)(2,1)}, u32[]{:S(2)}, u32[]{:S(2)}) collective-permute-start(bf16[2,2,3,96,768]{4,3,2,1,0:T(8,128)(2,1)S(1)} %maximum_maximum_fusion), channel_id=1, source_target_pairs={{0,4},{4,0},{8,12},{12,8},{1,5},{5,1},{9,13},{13,9},{2,6},{6,2},{1... | collective-permute-start | bytes 5308424 | tf_op jit(solution)/shard_map/ppermute | solution.py:562
  63.5 12.2 %collective-permute-start.10 = (bf16[144,384]{1,0:T(8,128)(2,1)S(1)}, bf16[144,384]{1,0:T(8,128)(2,1)S(1)}, u32[]{:S(2)}, u32[]{:S(2)}) collective-permute-start(bf16[144,384]{1,0:T(8,128)(2,1)S(1)} %dynamic_slice.24), channel_id=1, source_target_pairs={{0,1},{1,2},{2,3},{3,0},{4,5},{5,6},{6,7},{7,4},{8,9},{9,10},{10,1... | collective-permute-start | bytes 331784 | tf_op jit(solution)/shard_map/ppermute | solution.py:611
  67.6 9.1 %collective-permute-start.11 = (bf16[144,384]{1,0:T(8,128)(2,1)S(1)}, bf16[144,384]{1,0:T(8,128)(2,1)S(1)}, u32[]{:S(2)}, u32[]{:S(2)}) collective-permute-start(bf16[144,384]{1,0:T(8,128)(2,1)S(1)} %dynamic_slice.24), channel_id=1, source_target_pairs={{0,2},{1,3},{2,0},{3,1},{4,6},{5,7},{6,4},{7,5},{8,10},{9,11},{10,... | collective-permute-start | bytes 331784 | tf_op jit(solution)/shard_map/ppermute | solution.py:611
  68.8 8.0 %collective-permute-start.12 = (bf16[144,384]{1,0:T(8,128)(2,1)S(1)}, bf16[144,384]{1,0:T(8,128)(2,1)S(1)}, u32[]{:S(2)}, u32[]{:S(2)}) collective-permute-start(bf16[144,384]{1,0:T(8,128)(2,1)S(1)} %dynamic_slice.24), channel_id=1, source_target_pairs={{0,3},{1,0},{2,1},{3,2},{4,7},{5,4},{6,5},{7,6},{8,11},{9,8},{10,9... | collective-permute-start | bytes 331784 | tf_op jit(solution)/shard_map/ppermute | solution.py:611
  70.1 2.2 collective-permute-start.15
  72.3 19.8 %collective-permute-start.18 = (bf16[2,3,96,384]{3,2,1,0:T(8,128)(2,1)S(1)}, bf16[2,3,96,384]{3,2,1,0:T(8,128)(2,1)S(1)}, u32[]{:S(2)}, u32[]{:S(2)}) collective-permute-start(bf16[2,3,96,384]{3,2,1,0:T(8,128)(2,1)S(1)} %pad_maximum_fusion.13), channel_id=1, source_target_pairs={{0,8},{4,12},{8,0},{12,4},{1,9},{5,13},{9,1},{13,5},{2,10},{6,14},... | collective-permute-start | bytes 1327112 | tf_op jit(solution)/shard_map/ppermute | solution.py:562
  72.9 19.2 %collective-permute-start.17 = (bf16[2,3,96,384]{3,2,1,0:T(8,128)(2,1)S(1)}, bf16[2,3,96,384]{3,2,1,0:T(8,128)(2,1)S(1)}, u32[]{:S(2)}, u32[]{:S(2)}) collective-permute-start(bf16[2,3,96,384]{3,2,1,0:T(8,128)(2,1)S(1)} %pad_maximum_fusion.12), channel_id=1, source_target_pairs={{0,16},{16,0},{1,17},{17,1},{2,18},{18,2},{3,19},{19,3},{4,20},{20... | collective-permute-start | bytes 1327112 | tf_op jit(solution)/shard_map/ppermute | solution.py:562
  76.8 15.3 %collective-permute-start.19 = (bf16[3,144,384]{2,1,0:T(8,128)(2,1)S(1)}, bf16[3,144,384]{2,1,0:T(8,128)(2,1)S(1)}, u32[]{:S(2)}, u32[]{:S(2)}) collective-permute-start(bf16[3,144,384]{2,1,0:T(8,128)(2,1)S(1)} %pad_maximum_fusion.17), channel_id=1, source_target_pairs={{0,8},{4,12},{8,0},{12,4},{1,9},{5,13},{9,1},{13,5},{2,10},{6,14},... | collective-permute-start | bytes 995336 | tf_op jit(solution)/shard_map/ppermute | solution.py:562
  92.5 3.8 %collective-permute-start.20 = (bf16[2,2,3,96,768]{4,3,2,0,1:T(8,128)(2,1)S(1)}, bf16[2,2,3,96,768]{4,3,2,0,1:T(8,128)(2,1)S(1)}, u32[]{:S(2)}, u32[]{:S(2)}) collective-permute-start(bf16[2,2,3,96,768]{4,3,2,0,1:T(8,128)(2,1)S(1)} %maximum_maximum_fusion.1), channel_id=1, source_target_pairs={{0,4},{4,0},{8,12},{12,8},{1,5},{5,1},{9,13},{13,9},{2,6},{6,2},{1... | collective-permute-start | bytes 5308424 | tf_op jit(solution)/shard_map/ppermute | solution.py:562
  92.8 17.4 %collective-permute-start.21 = (bf16[2,3,144,384]{3,2,1,0:T(8,128)(2,1)S(1)}, bf16[2,3,144,384]{3,2,1,0:T(8,128)(2,1)S(1)}, u32[]{:S(2)}, u32[]{:S(2)}) collective-permute-start(bf16[2,3,144,384]{3,2,1,0:T(8,128)(2,1)S(1)} %pad_maximum_fusion.4), channel_id=1, source_target_pairs={{0,16},{16,0},{1,17},{17,1},{2,18},{18,2},{3,19},{19,3},{4,20},{20... | collective-permute-start | bytes 1990664 | tf_op jit(solution)/shard_map/ppermute | solution.py:562
  110.2 6.6 %collective-permute-start.22 = (bf16[4,4,96,768]{3,2,1,0:T(8,128)(2,1)S(1)}, bf16[4,4,96,768]{3,2,1,0:T(8,128)(2,1)S(1)}, u32[]{:S(2)}, u32[]{:S(2)}) collective-permute-start(bf16[4,4,96,768]{3,2,1,0:T(8,128)(2,1)S(1)} %get-tuple-element.235), channel_id=1, source_target_pairs={{0,4},{4,0},{8,12},{12,8},{1,5},{5,1},{9,13},{13,9},{2,6},{6,2},{1... | collective-permute-start | bytes 7077896 | tf_op jit(solution)/shard_map/ppermute | solution.py:562
  110.5 26.0 %collective-permute-start.23 = (bf16[2,2,3,144,384]{4,3,2,1,0:T(8,128)(2,1)S(1)}, bf16[2,2,3,144,384]{4,3,2,1,0:T(8,128)(2,1)S(1)}, u32[]{:S(2)}, u32[]{:S(2)}) collective-permute-start(bf16[2,2,3,144,384]{4,3,2,1,0:T(8,128)(2,1)S(1)} %pad_maximum_fusion), channel_id=1, source_target_pairs={{0,4},{4,0},{8,12},{12,8},{1,5},{5,1},{9,13},{13,9},{2,6},{6,2},{1... | collective-permute-start | bytes 3981320 | tf_op jit(solution)/shard_map/ppermute | solution.py:562
  111.1 23.1 %collective-permute-start.24 = (bf16[512,768]{1,0:T(8,128)(2,1)S(1)}, bf16[512,768]{1,0:T(8,128)(2,1)}, u32[]{:S(2)}, u32[]{:S(2)}) collective-permute-start(bf16[512,768]{1,0:T(8,128)(2,1)S(1)} %get-tuple-element.232.refs_0_), channel_id=1, source_target_pairs={{0,1},{1,2},{2,3},{4,5},{5,6},{6,7},{8,9},{9,10},{10,11},{12,13},{... | collective-permute-start | bytes 2359304 | tf_op jit(solution)/shard_map/ppermute | solution.py:709
  115.3 21.2 %collective-permute-start.25 = (bf16[512,768]{1,0:T(8,128)(2,1)S(1)}, bf16[512,768]{1,0:T(8,128)(2,1)}, u32[]{:S(2)}, u32[]{:S(2)}) collective-permute-start(bf16[512,768]{1,0:T(8,128)(2,1)S(1)} %get-tuple-element.232.refs_0_), channel_id=1, source_target_pairs={{1,0},{2,1},{3,2},{5,4},{6,5},{7,6},{9,8},{10,9},{11,10},{13,12},{... | collective-permute-start | bytes 2359304 | tf_op jit(solution)/shard_map/ppermute | solution.py:710
  117.1 19.3 %collective-permute-start.26 = (bf16[4,96,768]{2,1,0:T(8,128)(2,1)S(1)}, bf16[4,96,768]{2,1,0:T(8,128)(2,1)S(1)}, u32[]{:S(2)}, u32[]{:S(2)}) collective-permute-start(bf16[4,96,768]{2,1,0:T(8,128)(2,1)S(1)} %bitcast.311), channel_id=1, source_target_pairs={{0,8},{4,12},{8,0},{12,4},{1,9},{5,13},{9,1},{13,5},{2,10},{6,14},... | collective-permute-start | bytes 1769480 | tf_op jit(solution)/shard_map/ppermute | solution.py:562
  118.0 18.5 %collective-permute-start.27 = (bf16[4,96,768]{2,1,0:T(8,128)(2,1)S(1)}, bf16[4,96,768]{2,1,0:T(8,128)(2,1)S(1)}, u32[]{:S(2)}, u32[]{:S(2)}) collective-permute-start(bf16[4,96,768]{2,1,0:T(8,128)(2,1)S(1)} %bitcast.310), channel_id=1, source_target_pairs={{0,16},{16,0},{1,17},{17,1},{2,18},{18,2},{3,19},{19,3},{4,20},{20... | collective-permute-start | bytes 1769480 | tf_op jit(solution)/shard_map/ppermute | solution.py:562
  136.5 4.8 %collective-permute-start.28 = (bf16[4,4,96,768]{3,2,1,0:T(8,128)(2,1)}, bf16[4,4,96,768]{3,2,1,0:T(8,128)(2,1)S(1)}, u32[]{:S(2)}, u32[]{:S(2)}) collective-permute-start(bf16[4,4,96,768]{3,2,1,0:T(8,128)(2,1)} %get-tuple-element.254), channel_id=1, source_target_pairs={{0,4},{4,0},{8,12},{12,8},{1,5},{5,1},{9,13},{13,9},{2,6},{6,2},{1... | collective-permute-start | bytes 7077896 | tf_op jit(solution)/shard_map/ppermute | solution.py:562
  142.7 26.8 %collective-permute-start.32 = (bf16[6,96,768]{2,1,0:T(8,128)(2,1)}, bf16[6,96,768]{2,1,0:T(8,128)(2,1)}, u32[]{:S(2)}, u32[]{:S(2)}) collective-permute-start(bf16[6,96,768]{2,1,0:T(8,128)(2,1)} %pad_maximum_fusion.3), channel_id=1, source_target_pairs={{0,16},{16,0},{1,17},{17,1},{2,18},{18,2},{3,19},{19,3},{4,20},{20... | collective-permute-start | bytes 2654216 | tf_op jit(solution)/shard_map/ppermute | solution.py:562
  145.0 24.5 %collective-permute-start.31 = (bf16[6,96,768]{2,1,0:T(8,128)(2,1)}, bf16[6,96,768]{2,1,0:T(8,128)(2,1)}, u32[]{:S(2)}, u32[]{:S(2)}) collective-permute-start(bf16[6,96,768]{2,1,0:T(8,128)(2,1)} %pad_maximum_fusion.2), channel_id=1, source_target_pairs={{0,8},{4,12},{8,0},{12,4},{1,9},{5,13},{9,1},{13,5},{2,10},{6,14},... | collective-permute-start | bytes 2654216 | tf_op jit(solution)/shard_map/ppermute | solution.py:562
  146.0 20.2 %collective-permute-start.29 = (bf16[512,768]{1,0:T(8,128)(2,1)}, bf16[512,768]{1,0:T(8,128)(2,1)}, u32[]{:S(2)}, u32[]{:S(2)}) collective-permute-start(bf16[512,768]{1,0:T(8,128)(2,1)} %collective-permute-done.24.refs_1_), channel_id=1, source_target_pairs={{1,2},{2,3},{5,6},{6,7},{9,10},{10,11},{13,14},{14,15},{17,18},{18... | collective-permute-start | bytes 2359304 | tf_op jit(solution)/shard_map/ppermute | solution.py:709
  147.6 21.9 %collective-permute-start.30 = (bf16[512,768]{1,0:T(8,128)(2,1)}, bf16[512,768]{1,0:T(8,128)(2,1)}, u32[]{:S(2)}, u32[]{:S(2)}) collective-permute-start(bf16[512,768]{1,0:T(8,128)(2,1)} %collective-permute-done.25.refs_4_), channel_id=1, source_target_pairs={{1,0},{2,1},{5,4},{6,5},{9,8},{10,9},{13,12},{14,13},{17,16},{18,1... | collective-permute-start | bytes 2359304 | tf_op jit(solution)/shard_map/ppermute | solution.py:710
  169.5 4.8 %collective-permute-start.33 = (bf16[4,2,96,768]{3,2,1,0:T(8,128)(2,1)S(1)}, bf16[4,2,96,768]{3,2,1,0:T(8,128)(2,1)S(1)}, u32[]{:S(2)}, u32[]{:S(2)}) collective-permute-start(bf16[4,2,96,768]{3,2,1,0:T(8,128)(2,1)S(1)} %get-tuple-element.271), channel_id=1, source_target_pairs={{0,4},{4,0},{8,12},{12,8},{1,5},{5,1},{9,13},{13,9},{2,6},{6,2},{1... | collective-permute-start | bytes 3538952 | tf_op jit(solution)/shard_map/ppermute | solution.py:562
  169.5 30.0 %collective-permute-start.34 = (bf16[512,768]{1,0:T(8,128)(2,1)}, bf16[512,768]{1,0:T(8,128)(2,1)}, u32[]{:S(2)}, u32[]{:S(2)}) collective-permute-start(bf16[512,768]{1,0:T(8,128)(2,1)} %collective-permute-done.29.refs_2_), channel_id=1, source_target_pairs={{2,3},{6,7},{10,11},{14,15},{18,19},{22,23},{26,27},{30,31}} | collective-permute-start | bytes 2359304 | tf_op jit(solution)/shard_map/ppermute | solution.py:709
  171.1 28.5 %collective-permute-start.35 = (bf16[512,768]{1,0:T(8,128)(2,1)}, bf16[512,768]{1,0:T(8,128)(2,1)}, u32[]{:S(2)}, u32[]{:S(2)}) collective-permute-start(bf16[512,768]{1,0:T(8,128)(2,1)} %collective-permute-done.30.refs_5_), channel_id=1, source_target_pairs={{1,0},{5,4},{9,8},{13,12},{17,16},{21,20},{25,24},{29,28}} | collective-permute-start | bytes 2359304 | tf_op jit(solution)/shard_map/ppermute | solution.py:710
  174.5 25.0 %collective-permute-start.37 = (bf16[4,96,768]{2,1,0:T(8,128)(2,1)S(1)}, bf16[4,96,768]{2,1,0:T(8,128)(2,1)S(1)}, u32[]{:S(2)}, u32[]{:S(2)}) collective-permute-start(bf16[4,96,768]{2,1,0:T(8,128)(2,1)S(1)} %pad_maximum_fusion.6), channel_id=1, source_target_pairs={{0,16},{16,0},{1,17},{17,1},{2,18},{18,2},{3,19},{19,3},{4,20},{20... | collective-permute-start | bytes 1769480 | tf_op jit(solution)/shard_map/ppermute | solution.py:562
  175.3 24.3 %collective-permute-start.36 = (bf16[4,96,768]{2,1,0:T(8,128)(2,1)S(1)}, bf16[4,96,768]{2,1,0:T(8,128)(2,1)}, u32[]{:S(2)}, u32[]{:S(2)}) collective-permute-start(bf16[4,96,768]{2,1,0:T(8,128)(2,1)S(1)} %pad_maximum_fusion.5), channel_id=1, source_target_pairs={{0,8},{4,12},{8,0},{12,4},{1,9},{5,13},{9,1},{13,5},{2,10},{6,14},... | collective-permute-start | bytes 1769480 | tf_op jit(solution)/shard_map/ppermute | solution.py:562
  177.5 22.1 %collective-permute-start.38 = (bf16[2,96,768]{2,1,0:T(8,128)(2,1)S(1)}, bf16[2,96,768]{2,1,0:T(8,128)(2,1)}, u32[]{:S(2)}, u32[]{:S(2)}) collective-permute-start(bf16[2,96,768]{2,1,0:T(8,128)(2,1)S(1)} %pad_maximum_fusion.18), channel_id=1, source_target_pairs={{0,1},{1,0},{2,3},{3,2},{4,5},{5,4},{6,7},{7,6},{8,9},{9,8},{10,11... | collective-permute-start | bytes 884744 | tf_op jit(solution)/shard_map/ppermute | solution.py:562
  200.4 6.1 %collective-permute-start.41 = (bf16[4,2,96,768]{3,2,1,0:T(8,128)(2,1)}, bf16[4,2,96,768]{3,2,1,0:T(8,128)(2,1)}, u32[]{:S(2)}, u32[]{:S(2)}) collective-permute-start(bf16[4,2,96,768]{3,2,1,0:T(8,128)(2,1)} %get-tuple-element.290), channel_id=1, source_target_pairs={{0,4},{4,0},{8,12},{12,8},{1,5},{5,1},{9,13},{13,9},{2,6},{6,2},{1... | collective-permute-start | bytes 3538952 | tf_op jit(solution)/shard_map/ppermute | solution.py:562
  201.3 24.0 %collective-permute-start.39 = (bf16[512,768]{1,0:T(8,128)(2,1)S(1)}, bf16[512,768]{1,0:T(8,128)(2,1)S(1)}, u32[]{:S(2)}, u32[]{:S(2)}) collective-permute-start(bf16[512,768]{1,0:T(8,128)(2,1)S(1)} %get-tuple-element.322.refs_0_.own_ref), channel_id=1, source_target_pairs={{0,1},{1,2},{2,3},{4,5},{5,6},{6,7},{8,9},{9,10},{10,11},{12,13},{... | collective-permute-start | bytes 2359304 | tf_op jit(solution)/shard_map/ppermute | solution.py:709
  202.6 22.6 %collective-permute-start.40 = (bf16[512,768]{1,0:T(8,128)(2,1)S(1)}, bf16[512,768]{1,0:T(8,128)(2,1)}, u32[]{:S(2)}, u32[]{:S(2)}) collective-permute-start(bf16[512,768]{1,0:T(8,128)(2,1)S(1)} %get-tuple-element.322.refs_0_.own_ref), channel_id=1, source_target_pairs={{1,0},{2,1},{3,2},{5,4},{6,5},{7,6},{9,8},{10,9},{11,10},{13,12},{... | collective-permute-start | bytes 2359304 | tf_op jit(solution)/shard_map/ppermute | solution.py:710
  208.5 16.7 %collective-permute-start.43 = (bf16[3,96,768]{2,1,0:T(8,128)(2,1)}, bf16[3,96,768]{2,1,0:T(8,128)(2,1)}, u32[]{:S(2)}, u32[]{:S(2)}) collective-permute-start(bf16[3,96,768]{2,1,0:T(8,128)(2,1)} %pad_maximum_fusion.15), channel_id=1, source_target_pairs={{0,16},{16,0},{1,17},{17,1},{2,18},{18,2},{3,19},{19,3},{4,20},{20... | collective-permute-start | bytes 1327112 | tf_op jit(solution)/shard_map/ppermute | solution.py:562
  209.9 15.4 %collective-permute-start.42 = (bf16[3,96,768]{2,1,0:T(8,128)(2,1)}, bf16[3,96,768]{2,1,0:T(8,128)(2,1)S(1)}, u32[]{:S(2)}, u32[]{:S(2)}) collective-permute-start(bf16[3,96,768]{2,1,0:T(8,128)(2,1)} %pad_maximum_fusion.14), channel_id=1, source_target_pairs={{0,8},{4,12},{8,0},{12,4},{1,9},{5,13},{9,1},{13,5},{2,10},{6,14},... | collective-permute-start | bytes 1327112 | tf_op jit(solution)/shard_map/ppermute | solution.py:562
  211.3 13.9 %collective-permute-start.44 = (f32[18,384]{1,0:T(8,128)S(1)}, f32[18,384]{1,0:T(8,128)S(1)}, u32[]{:S(2)}, u32[]{:S(2)}) collective-permute-start(f32[18,384]{1,0:T(8,128)S(1)} %concatenate.72), channel_id=1, source_target_pairs={{0,1},{1,0},{2,3},{3,2},{4,5},{5,4},{6,7},{7,6},{8,9},{9,8},{10,11... | collective-permute-start | bytes 82952 | tf_op jit(solution)/shard_map/ppermute | solution.py:562
  228.8 5.6 %collective-permute-start.46 = (bf16[1,96,768]{2,1,0:T(8,128)(2,1)S(1)}, bf16[1,96,768]{2,1,0:T(8,128)(2,1)S(1)}, u32[]{:S(2)}, u32[]{:S(2)}) collective-permute-start(bf16[1,96,768]{2,1,0:T(8,128)(2,1)S(1)} %get-tuple-element.359), channel_id=1, source_target_pairs={{0,8},{4,12},{8,0},{12,4},{1,9},{5,13},{9,1},{13,5},{2,10},{6,14},... | collective-permute-start | bytes 442376 | tf_op jit(solution)/shard_map/ppermute | solution.py:562
  229.5 5.3 %collective-permute-start.47 = (bf16[1,96,768]{2,1,0:T(8,128)(2,1)S(1)}, bf16[1,96,768]{2,1,0:T(8,128)(2,1)S(1)}, u32[]{:S(2)}, u32[]{:S(2)}) collective-permute-start(bf16[1,96,768]{2,1,0:T(8,128)(2,1)S(1)} %get-tuple-element.358), channel_id=1, source_target_pairs={{0,16},{16,0},{1,17},{17,1},{2,18},{18,2},{3,19},{19,3},{4,20},{20... | collective-permute-start | bytes 442376 | tf_op jit(solution)/shard_map/ppermute | solution.py:562
  230.4 10.4 %collective-permute-start.45 = (bf16[2,96,768]{2,1,0:T(8,128)(2,1)S(1)}, bf16[2,96,768]{2,1,0:T(8,128)(2,1)S(1)}, u32[]{:S(2)}, u32[]{:S(2)}) collective-permute-start(bf16[2,96,768]{2,1,0:T(8,128)(2,1)S(1)} %copy-done.49), channel_id=1, source_target_pairs={{0,1},{1,0},{2,3},{3,2},{4,5},{5,4},{6,7},{7,6},{8,9},{9,8},{10,11... | collective-permute-start | bytes 884744 | tf_op jit(solution)/shard_map/ppermute | solution.py:562
  230.4 12.3 %collective-permute-start.48 = (bf16[512,768]{1,0:T(8,128)(2,1)}, bf16[512,768]{1,0:T(8,128)(2,1)S(1)}, u32[]{:S(2)}, u32[]{:S(2)}) collective-permute-start(bf16[512,768]{1,0:T(8,128)(2,1)} %copy-done.42), channel_id=1, source_target_pairs={{1,2},{2,3},{5,6},{6,7},{9,10},{10,11},{13,14},{14,15},{17,18},{18... | collective-permute-start | bytes 2359304 | tf_op jit(solution)/shard_map/ppermute | solution.py:709
  231.1 25.6 %collective-permute-start.49 = (bf16[512,768]{1,0:T(8,128)(2,1)}, bf16[512,768]{1,0:T(8,128)(2,1)S(1)}, u32[]{:S(2)}, u32[]{:S(2)}) collective-permute-start(bf16[512,768]{1,0:T(8,128)(2,1)} %collective-permute-done.40.refs_4_), channel_id=1, source_target_pairs={{1,0},{2,1},{5,4},{6,5},{9,8},{10,9},{13,12},{14,13},{17,16},{18,1... | collective-permute-start | bytes 2359304 | tf_op jit(solution)/shard_map/ppermute | solution.py:710
  236.6 30.8 %collective-permute-start.53 = (bf16[2,96,768]{2,1,0:T(8,128)(2,1)}, bf16[2,96,768]{2,1,0:T(8,128)(2,1)S(1)}, u32[]{:S(2)}, u32[]{:S(2)}) collective-permute-start(bf16[2,96,768]{2,1,0:T(8,128)(2,1)} %pad_maximum_fusion.21), channel_id=1, source_target_pairs={{0,1},{1,0},{2,3},{3,2},{4,5},{5,4},{6,7},{7,6},{8,9},{9,8},{10,11... | collective-permute-start | bytes 884744 | tf_op jit(solution)/shard_map/ppermute | solution.py:562
  256.8 15.4 %collective-permute-start.50 = (bf16[2,96,768]{2,1,0:T(8,128)(2,1)S(1)}, bf16[2,96,768]{2,1,0:T(8,128)(2,1)S(1)}, u32[]{:S(2)}, u32[]{:S(2)}) collective-permute-start(bf16[2,96,768]{2,1,0:T(8,128)(2,1)S(1)} %pad_maximum_fusion.20), channel_id=1, source_target_pairs={{0,2},{1,3},{2,0},{3,1},{4,6},{5,7},{6,4},{7,5},{8,10},{9,11},{10,... | collective-permute-start | bytes 884744 | tf_op jit(solution)/shard_map/ppermute | solution.py:562
  256.9 23.1 %collective-permute-start.55 = (f32[15,384]{1,0:T(8,128)S(1)}, f32[15,384]{1,0:T(8,128)S(1)}, u32[]{:S(2)}, u32[]{:S(2)}) collective-permute-start(f32[15,384]{1,0:T(8,128)S(1)} %pad_maximum_fusion.27), channel_id=1, source_target_pairs={{0,2},{1,3},{2,0},{3,1},{4,6},{5,7},{6,4},{7,5},{8,10},{9,11},{10,... | collective-permute-start | bytes 69128 | tf_op jit(solution)/shard_map/ppermute | solution.py:562
  259.7 33.6 %collective-permute-start.51 = (bf16[512,768]{1,0:T(8,128)(2,1)S(1)}, bf16[512,768]{1,0:T(8,128)(2,1)}, u32[]{:S(2)}, u32[]{:S(2)}) collective-permute-start(bf16[512,768]{1,0:T(8,128)(2,1)S(1)} %collective-permute-done.48.refs_2_.refs_3_), channel_id=1, source_target_pairs={{2,3},{6,7},{10,11},{14,15},{18,19},{22,23},{26,27},{30,31}} | collective-permute-start | bytes 2359304 | tf_op jit(solution)/shard_map/ppermute | solution.py:709
  266.1 27.2 %collective-permute-start.52 = (bf16[512,768]{1,0:T(8,128)(2,1)}, bf16[512,768]{1,0:T(8,128)(2,1)S(1)}, u32[]{:S(2)}, u32[]{:S(2)}) collective-permute-start(bf16[512,768]{1,0:T(8,128)(2,1)} %copy-done.36), channel_id=1, source_target_pairs={{1,0},{5,4},{9,8},{13,12},{17,16},{21,20},{25,24},{29,28}} | collective-permute-start | bytes 2359304 | tf_op jit(solution)/shard_map/ppermute | solution.py:710
  268.1 12.0 %collective-permute-start.54 = (bf16[96,768]{1,0:T(8,128)(2,1)}, bf16[96,768]{1,0:T(8,128)(2,1)S(1)}, u32[]{:S(2)}, u32[]{:S(2)}) collective-permute-start(bf16[96,768]{1,0:T(8,128)(2,1)} %fusion.10), channel_id=1, source_target_pairs={{0,2},{1,3},{2,0},{3,1},{4,6},{5,7},{6,4},{7,5},{8,10},{9,11},{10,... | collective-permute-start | bytes 442376 | tf_op jit(solution)/shard_map/ppermute | solution.py:562
  273.9 8.7 %collective-permute-start.59 = (bf16[2,96,768]{2,1,0:T(8,128)(2,1)S(1)}, bf16[2,96,768]{2,1,0:T(8,128)(2,1)S(1)}, u32[]{:S(2)}, u32[]{:S(2)}) collective-permute-start(bf16[2,96,768]{2,1,0:T(8,128)(2,1)S(1)} %get-tuple-element.340), channel_id=1, source_target_pairs={{0,16},{16,0},{1,17},{17,1},{2,18},{18,2},{3,19},{19,3},{4,20},{20... | collective-permute-start | bytes 884744 | tf_op jit(solution)/shard_map/ppermute | solution.py:562
  280.0 1.3 collective-permute-start.57
  280.2 6.3 %collective-permute-start.56 = (bf16[96,768]{1,0:T(8,128)(2,1)S(1)}, bf16[96,768]{1,0:T(8,128)(2,1)S(1)}, u32[]{:S(2)}, u32[]{:S(2)}) collective-permute-start(bf16[96,768]{1,0:T(8,128)(2,1)S(1)} %get-tuple-element.342), channel_id=1, source_target_pairs={{0,16},{16,0},{1,17},{17,1},{2,18},{18,2},{3,19},{19,3},{4,20},{20... | collective-permute-start | bytes 442376 | tf_op jit(solution)/shard_map/ppermute | solution.py:562
  281.3 3.8 %collective-permute-start.58 = (f32[15,384]{1,0:T(8,128)S(1)}, f32[15,384]{1,0:T(8,128)S(1)}, u32[]{:S(2)}, u32[]{:S(2)}) collective-permute-start(f32[15,384]{1,0:T(8,128)S(1)} %add.568), channel_id=1, source_target_pairs={{0,8},{4,12},{8,0},{12,4},{1,9},{5,13},{9,1},{13,5},{2,10},{6,14},... | collective-permute-start | bytes 69128 | tf_op jit(solution)/shard_map/ppermute | solution.py:562
  286.5 3.8 %collective-permute-start.60 = (f32[15,384]{1,0:T(8,128)S(1)}, f32[15,384]{1,0:T(8,128)S(1)}, u32[]{:S(2)}, u32[]{:S(2)}) collective-permute-start(f32[15,384]{1,0:T(8,128)S(1)} %add.569), channel_id=1, source_target_pairs={{0,16},{16,0},{1,17},{17,1},{2,18},{18,2},{3,19},{19,3},{4,20},{20... | collective-permute-start | bytes 69128 | tf_op jit(solution)/shard_map/ppermute | solution.py:562
  (51 other events, 334.3 us)

commit v6 on v5

--- a/solution.py
+++ b/solution.py
@@ -500,13 +500,22 @@
 def place_kernel(slots, at_ref, *refs):
     sources, (out_ref, held, sems) = refs[:-3], refs[-3:]
     here = at_ref[3]
+    end = (here == 0) | (here == slots - 1)
+    far = jnp.where(here < 2, slots - 1, 0)
 
     def each(step, act):
-        for s in range(slots):
-            for source, wanted in ((s, here - step == s),) + (((slots - 1 + s, step - here == s),) if s else ()):
-                @pl.when(wanted)
-                def _():
-                    act(pltpu.make_async_copy(sources[source], held.at[step], sems.at[step]))
+        wanted = (
+            step == here,
+            step == here + 1 - 2 * lax.rem(here, 2),
+            (step == slots - 1 - here) & (here > 0) & (here < slots - 1),
+            (step == far) & (here > 0) & (here < slots - 1),
+            (step == jnp.where(here == 0, 2, 1)) & end,
+            (step == slots - 1 - here) & end,
+        )
+        for source, now in zip(sources, wanted):
+            @pl.when(now)
+            def _():
+                act(pltpu.make_async_copy(source, held.at[step], sems.at[step]))
 
     step = pl.program_id(0)
 
@@ -519,9 +528,10 @@
     out_ref[0] = held[step].astype(out_ref.dtype)
 
 
-def place_end_kernel(slots, at_ref, own_ref, behind_ref, ahead_ref, whole_ref, out_ref, held, sem):
+def place_end_kernel(slots, at_ref, own_ref, last_ref, whole_ref, out_ref, held, sem):
     here = at_ref[3]
-    for source, wanted in ((ahead_ref, here == 0), (behind_ref, here == slots - 1), (own_ref, lax.rem(here, slots - 1) > 0)):
+    end = (here == 0) | (here == slots - 1)
+    for source, wanted in ((last_ref, end), (own_ref, jnp.logical_not(end))):
         @pl.when(wanted)
         def _():
             copy = pltpu.make_async_copy(source, held, sem)
@@ -531,25 +541,24 @@
     out_ref[0] = held[...].astype(out_ref.dtype)
 
 
-def place_end(at, own, behind, ahead, whole):
+def place_end(at, own, last, whole):
     slots = whole.shape[0]
     spot = lambda i, at: (jnp.where(at[3] == 0, slots - 1, jnp.where(at[3] == slots - 1, 0, at[3])), 0, 0)
     return pl.pallas_call(
         functools.partial(place_end_kernel, slots),
         grid_spec=pltpu.PrefetchScalarGridSpec(
-            num_scalar_prefetch=1, grid=(1,), in_specs=[FAR] * 4, out_specs=pl.BlockSpec((1, *own.shape), spot),
+            num_scalar_prefetch=1, grid=(1,), in_specs=[FAR] * 3, out_specs=pl.BlockSpec((1, *own.shape), spot),
             scratch_shapes=[pltpu.VMEM(own.shape, own.dtype), pltpu.SemaphoreType.DMA],
         ),
         out_shape=jax.ShapeDtypeStruct(whole.shape, whole.dtype),
-        input_output_aliases={4: 0},
+        input_output_aliases={3: 0},
         cost_estimate=SHORT,
         name="place_end",
-    )(at, own, behind, ahead, whole)
-
-
-def place(at, own, behind, ahead, kind):
-    slots = len(behind) + 1
-    values = [own, *behind, *ahead]
+    )(at, own, last, whole)
+
+
+def place(at, slots, values, kind):
+    own = values[0]
     return call(
         functools.partial(place_kernel, slots), "place", at, (slots,),
         [FAR] * len(values), slot(*own.shape),
@@ -701,14 +710,18 @@
         made, e1 = run((made, e1))
         output_own, grad_r2, grad_r2_low, vec_two, keep1, send1 = made
 
-        steps = [(i, i + 1) for i in range(n_tensor - 1)]
-        back_steps = [(i + 1, i) for i in range(n_tensor - 1)]
-
-        def hop(right, left, step):
-            return (
-                lax.ppermute(right, "tensor", steps[step:]),
-                lax.ppermute(left, "tensor", back_steps[: len(steps) - step]),
-            )
+        across = lambda v: swap(v, "tensor", n_tensor, 1)
+        middle = lambda v: lax.ppermute(v, "tensor", [(1, 2), (2, 1)])
+        outward = lambda v: lax.ppermute(v, "tensor", [(1, 0), (2, 3)])
+
+        def hop_one(own):
+            return across(own), middle(own)
+
+        def hop_two(partner, other):
+            return middle(partner), outward(other)
+
+        def hop_three(passed, _):
+            return (outward(passed),)
 
         block = width // 8
 
@@ -766,7 +779,7 @@
         def whole_rows(mine, got):
             return ordered(mine, got.astype(F32), y, 0).reshape(2 * block, mine.shape[-1])
 
-        out_1 = hop(output_own, output_own, 0)
+        out_1 = hop_one(output_own)
         core1 = by_core(send1)
         qkv_both = ordered(e, e1, y, 0)
         qkv_core = by_core(qkv_both)
@@ -780,7 +793,7 @@
         made, qkv_core, out_1, flight = run((made, qkv_core, out_1, flight))
         qkv_parts = (flat_qkv, qkv_both, qkv_core)
         grad_binner, grad_r1, grad_r1_low, grad_r1_rel, vec_one, keep2, send2 = made
-        out_2 = hop(*out_1, 1)
+        out_2 = hop_two(*out_1)
         core2 = by_core(send2)
         landed(flight, [h1[0]], [h1[1]])
         done(core2)
@@ -794,7 +807,7 @@
         )
         made, out_2, flight = run((made, out_2, flight))
         bqv_a, tok_a, keep_a, send_a = made
-        out_3 = hop(*out_2, 2)
+        out_3 = hop_three(*out_2)
         core_a = by_core(send_a)
         landed(flight, *groups)
         total1 = h1[0].totals() + h1[1].totals()
@@ -809,7 +822,7 @@
         )
         made, out_3, flight, near1 = run((made, out_3, flight, near1))
         bqv_b, tok_own, keep_b, send_b = made
-        tok_1 = hop(tok_own, tok_own, 0)
+        tok_1 = hop_one(tok_own)
         core_b = by_core(send_b)
         landed(flight, *groups)
 
@@ -830,7 +843,7 @@
         far1 = far1.astype(BF)
         done(*order.last, near2, far1, *tok_1, *flight, vec_got)
         tok_1, flight, vec_got, near2, far1 = hold((tok_1, flight, vec_got, near2, far1))
-        tok_2 = hop(*tok_1, 1)
+        tok_2 = hop_two(*tok_1)
         near2 = z_near(near2)
         landed(flight, *groups)
         groups = [hb[1]], [hb[0]]
@@ -849,9 +862,9 @@
         far12 = jnp.stack([far1, far2.astype(BF)])
         done(far12, *tok_2)
         tok_2, far12 = hold((tok_2, far12))
-        tok_3 = hop(*tok_2, 2)
+        tok_3 = hop_three(*tok_2)
         far12 = z_far(far12)
-        grad_tokens = place(at, tok_own, (tok_1[0], tok_2[0], tok_2[0]), (tok_1[1], tok_2[1], tok_2[1]), F32)
+        grad_tokens = place(at, n_tensor, (tok_own, *tok_1, *tok_2, tok_2[0]), F32)
         grad_tokens, near3 = run((grad_tokens, near3))
         mine3, far3 = after_near((total3[0], total3[2]), near3)
         far3 = z_far(far3.astype(BF))
@@ -860,7 +873,7 @@
         mine12 = outer_rest(jnp.stack([mine1, mine2]) + hold(far12).astype(F32))
         got12 = by_y(mine12.astype(BF))
         done(mine12)
-        output = place(at, output_own, (out_1[0], out_2[0], out_3[0]), (out_1[1], out_2[1], hold(out_3[1])), BF)
+        output = place(at, n_tensor, (output_own, *out_1, *out_2, hold(out_3[0])), BF)
         output = output.reshape(seq_count, seq_len, width)
         done(output, vec_got)
         vectors = jnp.concatenate([vec_0, common]) + hold(vec_got)
@@ -893,7 +906,7 @@
         common = part(common, width)
         grad_wqkv = done_last[:, : 3 * head_cols].reshape(width // n_local, 3, head_cols).transpose(1, 0, 2)
         done(grad_wqkv, common, binner, bqv, *tok_3)
-        grad_tokens = place_end(at, *hold((tok_own, tok_3[0], tok_3[1], grad_tokens)))
+        grad_tokens = place_end(at, *hold((tok_own, tok_3[0], grad_tokens)))
         grad_tokens = grad_tokens.reshape(seq_count, seq_len, width)
         return (
             output,

time: 303 us -> 291 us (0.960); the launches traced: 298 us -> 290 us
  waiting for transfers between devices: 63.1 us -> 55.5 us
    ppermute x12 -> x8, starting transfers between devices: 19.1 us -> 10.8 us  [the longest x4 5.4 us: local(): outward = lambda v: lax.ppermute(v, 'tensor', [(1, 0), (2, 3)])]
    ppermute x40 -> x42, starting transfers between devices: 40 us -> 47.1 us  [swap(): return lax.ppermute(value, axis, [(i, i ^ bit) for i in range(size)])]
    ppermute x40 -> x42, waiting for transfers between devices: 30.3 us -> 25.4 us  [swap(): return lax.ppermute(value, axis, [(i, i ^ bit) for i in range(size)])]
    ppermute x12 -> x8, waiting for transfers between devices: 19.6 us -> 16.8 us  [the longest x4 16.8 us: local(): outward = lambda v: lax.ppermute(v, 'tensor', [(1, 0), (2, 3)])]
    unnamed x121 -> x119, local copies, waits for them, and re-layouts: 14.3 us -> 14.3 us
  transfers between devices with their start and end apart: 61 -> 59, of which waited for: 22 -> 19; matrix products, arithmetic and copies ran while one was open for 14% -> 14% of each run, Pallas kernels for 30% -> 31%
where the time goes in v6:
time: 291 us; the launch traced here: 290 us
  Pallas kernels  91.4 us (31%)
  starting transfers between devices  81.5 us (28%)
  waiting for transfers between devices  55.5 us (19%)
  other arithmetic  37 us (13%)
  local copies, waits for them, and re-layouts  21.8 us (7%)
    ppermute x42, starting transfers between devices, swap(): return lax.ppermute(value, axis, [(i, i ^ bit) for i in range(size)])  47.1 us
    pallas_call x2, Pallas kernels, attend_back(): call(functools.partial(attend_back_kernel, first, slots, heads, (cols //...  30.9 us
    ppermute x42, waiting for transfers between devices, swap(): return lax.ppermute(value, axis, [(i, i ^ bit) for i in range(size)])  25.4 us
    ppermute x9, starting transfers between devices, local(): lax.ppermute(v, 'tensor', [(i, (i + s) % n_tensor) for i in range(n_tenso...  23.6 us
    ppermute x4, waiting for transfers between devices, local(): outward = lambda v: lax.ppermute(v, 'tensor', [(1, 0), (2, 3)])  16.8 us
    pallas_call x1, Pallas kernels, back(): call(functools.partial(back_kernel, slots), 'back', at, (slots,), [const(...  14.6 us
    unnamed x119, local copies, waits for them, and re-layouts  14.3 us
    ppermute x9, waiting for transfers between devices, local(): lax.ppermute(v, 'tensor', [(i, (i + s) % n_tensor) for i in range(n_tenso...  13.3 us
  transfers between devices with their start and end apart: 59, of which 19 were waited for; matrix products, arithmetic and copies ran while one was open for 14% of the time, Pallas kernels for 31%

profile of v6, /device:TPU:0, one launch (start us, length us, event | category | flops | bytes accessed | tf_op | source)
XLA Modules:
  0.0 289.5 jit_solution(9522639331492830071)
XLA Ops:
  2.6 3.1 %collective-permute-start = (bf16[216,768]{1,0:T(8,128)(2,1)S(1)}, bf16[216,768]{1,0:T(8,128)(2,1)S(1)}, u32[]{:S(2)}, u32[]{:S(2)}) collective-permute-start(bf16[216,768]{1,0:T(8,128)(2,1)S(1)} %pad_maximum_fusion.16), channel_id=1, source_target_pairs={{0,1},{1,2},{2,3},{3,0},{4,5},{5,6},{6,7},{7,4},{8,9},{9,10},{10,1... | collective-permute-start | bytes 995336 | tf_op jit(solution)/shard_map/ppermute | solution.py:620
  5.6 2.6 collective-permute-start.1
  8.2 1.3 collective-permute-start.2
  11.4 1.9 copy-done
  14.0 12.8 %attend.1 = (bf16[272,384]{1,0:T(8,128)(2,1)S(1)}, bf16[272,384]{1,0:T(8,128)(2,1)S(1)}, bf16[272,384]{1,0:T(8,128)(2,1)S(1)}, bf16[272,384]{1,0:T(8,128)(2,1)S(1)}) custom-call(s32[4]{0:T(128)S(1)} %pad_add_fusion.at_ref, bf16[4,512,768]{2,1,0:T(8,128)(2,1)S(1)} %copy-done, bf16[3,192,768]{2,1,0:T(8,128)(2,1)S(1)} %bitcast.292, ...), custom_call_target="tpu_custom_call" | custom-call | flops 1000 | bytes 1000 | tf_op jit(solution)/shard_map/attend/pallas_call | solution.py:118
  26.8 3.0 %collective-permute-done.1 = bf16[216,768]{1,0:T(8,128)(2,1)S(1)} collective-permute-done((bf16[216,768]{1,0:T(8,128)(2,1)S(1)}, bf16[216,768]{1,0:T(8,128)(2,1)S(1)}, u32[]{:S(2)}, u32[]{:S(2)}) %collective-permute-start.1) | collective-permute-done | bytes 331808 | tf_op jit(solution)/shard_map/ppermute | solution.py:620
  30.0 1.6 collective-permute-start.7
  31.6 1.6 collective-permute-start.6
  33.2 7.6 %collective-permute-start.3 = (bf16[272,384]{1,0:T(8,128)(2,1)S(1)}, bf16[272,384]{1,0:T(8,128)(2,1)S(1)}, u32[]{:S(2)}, u32[]{:S(2)}) collective-permute-start(bf16[272,384]{1,0:T(8,128)(2,1)S(1)} %get-tuple-element.173), channel_id=1, source_target_pairs={{0,1},{1,2},{2,3},{3,0},{4,5},{5,6},{6,7},{7,4},{8,9},{9,10},{10,1... | collective-permute-start | bytes 626696 | tf_op jit(solution)/shard_map/ppermute | solution.py:620
  40.8 1.6 collective-permute-start.4
  45.5 2.5 collective-permute-done.3.refs_1_
  48.0 6.6 %collective-permute-done.4.refs_2_.refs_0_ = bf16[272,384]{1,0:T(8,128)(2,1)S(1)} collective-permute-done((bf16[272,384]{1,0:T(8,128)(2,1)S(1)}, bf16[272,384]{1,0:T(8,128)(2,1)S(1)}, u32[]{:S(2)}, u32[]{:S(2)}) %collective-permute-start.4) | collective-permute-done | bytes 208928 | tf_op jit(solution)/shard_map/ppermute | solution.py:620
  55.9 1.8 collective-permute-done.9
  57.7 1.3 collective-permute-done.8
  63.5 4.1 %collective-permute-start.10 = (bf16[144,384]{1,0:T(8,128)(2,1)S(1)}, bf16[144,384]{1,0:T(8,128)(2,1)S(1)}, u32[]{:S(2)}, u32[]{:S(2)}) collective-permute-start(bf16[144,384]{1,0:T(8,128)(2,1)S(1)} %dynamic_slice.24), channel_id=1, source_target_pairs={{0,1},{1,2},{2,3},{3,0},{4,5},{5,6},{6,7},{7,4},{8,9},{9,10},{10,1... | collective-permute-start | bytes 331784 | tf_op jit(solution)/shard_map/ppermute | solution.py:620
  68.8 1.2 collective-permute-start.12
  72.8 1.5 collective-permute-start.17
  75.5 1.2 collective-permute-done.11
  76.8 1.3 collective-permute-start.19
  78.2 10.1 %rise.1 = (f32[512,768]{1,0:T(8,128)S(1)}, bf16[512,768]{1,0:T(8,128)(2,1)}, f32[512,768]{1,0:T(8,128)S(1)}, f32[512,1]{1,0:T(8,128)S(1)}, bf16[4,512,768]{2,1,0...) custom-call(s32[4]{0:T(128)S(1)} %pad_add_fusion.at_ref, ...), custom_call_target="tpu_custom_call" | custom-call | flops 1000 | bytes 1000 | tf_op jit(solution)/shard_map/rise/pallas_call | solution.py:219
  89.2 2.7 collective-permute-done.19
  92.6 1.6 collective-permute-start.21
  94.4 1.8 collective-permute-done.20
  96.5 11.1 %fall.1 = (bf16[512,768]{1,0:T(8,128)(2,1)S(1)}, f32[512,768]{1,0:T(8,128)S(1)}, bf16[512,768]{1,0:T(8,128)(2,1)S(1)}, f32[3,768]{1,0:T(4,128)S(1)}, bf16[4,4,96...) custom-call(s32[4]{0:T(128)S(1)} %pad_add_fusion.at_ref, bf16[4,512,768]{2,1,0:T(8,128)(2,1)S(1)} %copy-done.7, ...), custom_call_target="tpu_custom_call" | custom-call | flops 1000 | bytes 1000 | tf_op jit(solution)/shard_map/fall/pallas_call | solution.py:305
  107.6 2.4 collective-permute-done.21
  110.9 1.6 collective-permute-start.24
  112.5 1.5 collective-permute-start.25
  114.6 1.4 add_convert_fusion.2
  116.5 1.5 collective-permute-start.27
  118.0 14.6 %back.1 = (f32[4,1,768]{2,1,0:T(1,128)S(1)}, f32[512,768]{1,0:T(8,128)S(1)}, bf16[512,768]{1,0:T(8,128)(2,1)S(1)}, bf16[768,512]{1,0:T(8,128)(2,1)S(1)}, f32[3,7...) custom-call(s32[4]{0:T(128)S(1)} %pad_add_fusion.at_ref, ...), custom_call_target="tpu_custom_call" | custom-call | flops 1000 | bytes 1000 | tf_op jit(solution)/shard_map/back/pallas_call | solution.py:360
  133.0 4.5 %collective-permute-done.28 = bf16[4,4,96,768]{3,2,1,0:T(8,128)(2,1)S(1)} collective-permute-done((bf16[4,4,96,768]{3,2,1,0:T(8,128)(2,1)}, bf16[4,4,96,768]{3,2,1,0:T(8,128)(2,1)S(1)}, u32[]{:S(2)}, u32[]{:S(2)}) %collective-permute-start.28) | collective-permute-done | bytes 2359328 | tf_op jit(solution)/shard_map/ppermute | solution.py:571
  140.5 1.5 collective-permute-start.31
  142.0 1.6 collective-permute-start.29
  143.6 1.3 collective-permute-start.30
  146.9 15.4 %attend_back.2 = (f32[2,2,192]{2,1,0:T(2,128)S(1)}, f32[512,768]{1,0:T(8,128)}, bf16[4,2,96,768]{3,2,1,0:T(8,128)(2,1)S(1)}, bf16[4,2,96,768]{3,2,1,0:T(8,128)(2,1)S(1)}) custom-call(s32[4]{0:T(128)S(1)} %pad_add_fusion.at_ref, bf16[4,512,768]{2,1,0:T(8,128)(2,1)} %x_ref.4, bf16[512,768]{1,0:T(8,128)(2,1)S(1)} %copy-done.12, f32[512,768]{1,0:T(8,128)} %copy-done.17, ...), custom_call_target="tpu_custom_call" | custom-call | flops 1000 | bytes 1000 | tf_op jit(solution)/shard_map/attend_back/pallas_call | solution.py:479
  162.3 3.9 %collective-permute-done.30.refs_4_ = bf16[512,768]{1,0:T(8,128)(2,1)} collective-permute-done((bf16[512,768]{1,0:T(8,128)(2,1)}, bf16[512,768]{1,0:T(8,128)(2,1)}, u32[]{:S(2)}, u32[]{:S(2)}) %collective-permute-start.30) | collective-permute-done | bytes 786464 | tf_op jit(solution)/shard_map/ppermute | solution.py:715
  166.2 1.6 collective-permute-start.34
  167.8 1.6 fusion
  171.2 1.5 fusion.37
  172.7 3.4 %collective-permute-start.37 = (bf16[2,96,768]{2,1,0:T(8,128)(2,1)S(1)}, bf16[2,96,768]{2,1,0:T(8,128)(2,1)}, u32[]{:S(2)}, u32[]{:S(2)}) collective-permute-start(bf16[2,96,768]{2,1,0:T(8,128)(2,1)S(1)} %pad_maximum_fusion.18), channel_id=1, source_target_pairs={{0,1},{1,0},{2,3},{3,2},{4,5},{5,4},{6,7},{7,6},{8,9},{9,8},{10,11... | collective-permute-start | bytes 884744 | tf_op jit(solution)/shard_map/ppermute | solution.py:571
  176.1 15.5 %attend_back.3 = (f32[2,2,192]{2,1,0:T(2,128)S(1)}, bf16[512,768]{1,0:T(8,128)(2,1)S(1)}, bf16[4,2,96,768]{3,2,1,0:T(8,128)(2,1)S(1)}, bf16[4,2,96,768]{3,2,1,0:T(8,128)(2,1)}) custom-call(s32[4]{0:T(128)S(1)} %pad_add_fusion.at_ref, bf16[4,512,768]{2,1,0:T(8,128)(2,1)} %x_ref.4, bf16[512,768]{1,0:T(8,128)(2,1)S(1)} %copy-done.12, ...), custom_call_target="tpu_custom_call" | custom-call | flops 1000 | bytes 1000 | tf_op jit(solution)/shard_map/attend_back/pallas_call | solution.py:479
  192.7 2.0 collective-permute-done.37
  196.4 1.6 collective-permute-start.39
  198.0 2.6 fusion.28
  205.0 4.1 %collective-permute-start.43 = (f32[18,384]{1,0:T(8,128)S(1)}, f32[18,384]{1,0:T(8,128)S(1)}, u32[]{:S(2)}, u32[]{:S(2)}) collective-permute-start(f32[18,384]{1,0:T(8,128)S(1)} %concatenate.72), channel_id=1, source_target_pairs={{0,1},{1,0},{2,3},{3,2},{4,5},{5,4},{6,7},{7,6},{8,9},{9,8},{10,11... | collective-permute-start | bytes 82952 | tf_op jit(solution)/shard_map/ppermute | solution.py:571
  209.1 1.4 fusion.14
  210.5 1.7 pad_maximum_fusion.19
  212.9 4.3 %collective-permute-done.43 = f32[18,384]{1,0:T(8,128)S(1)} collective-permute-done((f32[18,384]{1,0:T(8,128)S(1)}, f32[18,384]{1,0:T(8,128)S(1)}, u32[]{:S(2)}, u32[]{:S(2)}) %collective-permute-start.43) | collective-permute-done | bytes 27680 | tf_op jit(solution)/shard_map/ppermute | solution.py:571
  219.2 1.5 fusion.22
  222.1 2.9 collective-permute-start.44
  225.7 1.3 collective-permute-start.48
  229.7 3.8 %collective-permute-start.51 = (bf16[2,96,768]{2,1,0:T(8,128)(2,1)}, bf16[2,96,768]{2,1,0:T(8,128)(2,1)S(1)}, u32[]{:S(2)}, u32[]{:S(2)}) collective-permute-start(bf16[2,96,768]{2,1,0:T(8,128)(2,1)} %pad_maximum_fusion.21), channel_id=1, source_target_pairs={{0,1},{1,0},{2,3},{3,2},{4,5},{5,4},{6,7},{7,6},{8,9},{9,8},{10,11... | collective-permute-start | bytes 884744 | tf_op jit(solution)/shard_map/ppermute | solution.py:571
  234.6 1.9 convert_add_fusion.9
  236.5 12.8 %collective-permute-done.48.refs_4_ = bf16[512,768]{1,0:T(8,128)(2,1)} collective-permute-done((bf16[512,768]{1,0:T(8,128)(2,1)}, bf16[512,768]{1,0:T(8,128)(2,1)}, u32[]{:S(2)}, u32[]{:S(2)}) %collective-permute-start.48) | collective-permute-done | bytes 786464 | tf_op jit(solution)/shard_map/ppermute | solution.py:715
  249.4 1.4 collective-permute-start.49
  250.8 1.5 collective-permute-start.53
  252.3 1.3 collective-permute-start.50
  253.6 4.9 %place.3.whole_ref = f32[4,512,768]{2,1,0:T(8,128)} custom-call(s32[4]{0:T(128)} %copy-done.31, bf16[512,768]{1,0:T(8,128)(2,1)} %copy-done.8, bf16[512,768]{1,0:T(8,128)(2,1)} %copy-done.41, bf16[512,768]{1,0:T(8,128)(2,1)} %collective-permute-done.39.refs_2_, bf16[512,768]{1,0:T(8,128)(2,1)} %copy-done.35, ...), custom_call_target="tpu_custom_call" | custom-call | flops 1000 | bytes 1000 | tf_op jit(solution)/shard_map/place/pallas_call | solution.py:562
  259.2 4.4 %collective-permute-start.52 = (bf16[96,768]{1,0:T(8,128)(2,1)}, bf16[96,768]{1,0:T(8,128)(2,1)S(1)}, u32[]{:S(2)}, u32[]{:S(2)}) collective-permute-start(bf16[96,768]{1,0:T(8,128)(2,1)} %fusion.10), channel_id=1, source_target_pairs={{0,2},{1,3},{2,0},{3,1},{4,6},{5,7},{6,4},{7,5},{8,10},{9,11},{10,... | collective-permute-start | bytes 442376 | tf_op jit(solution)/shard_map/ppermute | solution.py:571
  263.6 1.8 collective-permute-done.49
  268.1 4.0 %place.2 = bf16[4,512,768]{2,1,0:T(8,128)(2,1)} custom-call(s32[4]{0:T(128)} %copy-done.31, bf16[512,768]{1,0:T(8,128)(2,1)} %copy-done.27, bf16[512,768]{1,0:T(8,128)(2,1)} %collective-permute-done.24.refs_1_, bf16[512,768]{1,0:T(8,128)(2,1)} %collective-permute-done.25.refs_2_, bf16[512,768]{1,0:T(8,128)(2,1)} %collective-permute-done.29.refs_3_, ...), custom_call_target="tpu_custom_call" | custom-call | flops 1000 | bytes 1000 | tf_op jit(solution)/shard_map/place/pallas_call | solution.py:562
  273.4 1.5 collective-permute-start.56
  277.3 1.2 collective-permute-done.54
  286.3 3.0 %place_end.1 = f32[4,512,768]{2,1,0:T(8,128)} custom-call(s32[4]{0:T(128)} %copy-done.31, bf16[512,768]{1,0:T(8,128)(2,1)} %copy-done.8, bf16[512,768]{1,0:T(8,128)(2,1)} %copy-done.40, f32[4,512,768]{2,1,0:T(8,128)} %place.3.whole_ref), custom_call_target="tpu_custom_call", output_to_operand_aliasing={{}: (3, {})} | custom-call | flops 1000 | bytes 1000 | tf_op jit(solution)/shard_map/place_end/pallas_call | solution.py:547
  (311 shorter events, 59.7 us)
Async XLA Ops:
  2.6 24.3 %collective-permute-start = (bf16[216,768]{1,0:T(8,128)(2,1)S(1)}, bf16[216,768]{1,0:T(8,128)(2,1)S(1)}, u32[]{:S(2)}, u32[]{:S(2)}) collective-permute-start(bf16[216,768]{1,0:T(8,128)(2,1)S(1)} %pad_maximum_fusion.16), channel_id=1, source_target_pairs={{0,1},{1,2},{2,3},{3,0},{4,5},{5,6},{6,7},{7,4},{8,9},{9,10},{10,1... | collective-permute-start | bytes 995336 | tf_op jit(solution)/shard_map/ppermute | solution.py:620
  5.6 24.2 %collective-permute-start.1 = (bf16[216,768]{1,0:T(8,128)(2,1)S(1)}, bf16[216,768]{1,0:T(8,128)(2,1)S(1)}, u32[]{:S(2)}, u32[]{:S(2)}) collective-permute-start(bf16[216,768]{1,0:T(8,128)(2,1)S(1)} %pad_maximum_fusion.16), channel_id=1, source_target_pairs={{0,2},{1,3},{2,0},{3,1},{4,6},{5,7},{6,4},{7,5},{8,10},{9,11},{10,... | collective-permute-start | bytes 995336 | tf_op jit(solution)/shard_map/ppermute | solution.py:620
  8.2 21.6 %collective-permute-start.2 = (bf16[216,768]{1,0:T(8,128)(2,1)S(1)}, bf16[216,768]{1,0:T(8,128)(2,1)S(1)}, u32[]{:S(2)}, u32[]{:S(2)}) collective-permute-start(bf16[216,768]{1,0:T(8,128)(2,1)S(1)} %pad_maximum_fusion.16), channel_id=1, source_target_pairs={{0,3},{1,0},{2,1},{3,2},{4,7},{5,4},{6,5},{7,6},{8,11},{9,8},{10,9... | collective-permute-start | bytes 995336 | tf_op jit(solution)/shard_map/ppermute | solution.py:620
  11.4 164.8 %copy-start.31 = (s32[4]{0:T(128)}, s32[4]{0:T(128)S(1)}, u32[]{:S(2)}) copy-start(s32[4]{0:T(128)S(1)} %pad_add_fusion.at_ref) | copy-start | bytes 52
  26.8 51.3 %copy-start.25 = (bf16[272,384]{1,0:T(8,128)(2,1)}, bf16[272,384]{1,0:T(8,128)(2,1)S(1)}, u32[]{:S(2)}) copy-start(bf16[272,384]{1,0:T(8,128)(2,1)S(1)} %get-tuple-element.205.refs_0_) | copy-start | bytes 626692
  30.0 14.1 %collective-permute-start.7 = (bf16[3,120,384]{2,1,0:T(8,128)(2,1)S(1)}, bf16[3,120,384]{2,1,0:T(8,128)(2,1)S(1)}, u32[]{:S(2)}, u32[]{:S(2)}) collective-permute-start(bf16[3,120,384]{2,1,0:T(8,128)(2,1)S(1)} %pad_maximum_fusion.23), channel_id=1, source_target_pairs={{0,16},{16,0},{1,17},{17,1},{2,18},{18,2},{3,19},{19,3},{4,20},{20... | collective-permute-start | bytes 829448 | tf_op jit(solution)/shard_map/ppermute | solution.py:571
  31.6 12.4 %collective-permute-start.6 = (bf16[3,120,384]{2,1,0:T(8,128)(2,1)S(1)}, bf16[3,120,384]{2,1,0:T(8,128)(2,1)S(1)}, u32[]{:S(2)}, u32[]{:S(2)}) collective-permute-start(bf16[3,120,384]{2,1,0:T(8,128)(2,1)S(1)} %pad_maximum_fusion.22), channel_id=1, source_target_pairs={{0,8},{4,12},{8,0},{12,4},{1,9},{5,13},{9,1},{13,5},{2,10},{6,14},... | collective-permute-start | bytes 829448 | tf_op jit(solution)/shard_map/ppermute | solution.py:571
  33.2 14.8 %collective-permute-start.3 = (bf16[272,384]{1,0:T(8,128)(2,1)S(1)}, bf16[272,384]{1,0:T(8,128)(2,1)S(1)}, u32[]{:S(2)}, u32[]{:S(2)}) collective-permute-start(bf16[272,384]{1,0:T(8,128)(2,1)S(1)} %get-tuple-element.173), channel_id=1, source_target_pairs={{0,1},{1,2},{2,3},{3,0},{4,5},{5,6},{6,7},{7,4},{8,9},{9,10},{10,1... | collective-permute-start | bytes 626696 | tf_op jit(solution)/shard_map/ppermute | solution.py:620
  40.8 13.8 %collective-permute-start.4 = (bf16[272,384]{1,0:T(8,128)(2,1)S(1)}, bf16[272,384]{1,0:T(8,128)(2,1)S(1)}, u32[]{:S(2)}, u32[]{:S(2)}) collective-permute-start(bf16[272,384]{1,0:T(8,128)(2,1)S(1)} %get-tuple-element.174), channel_id=1, source_target_pairs={{0,2},{1,3},{2,0},{3,1},{4,6},{5,7},{6,4},{7,5},{8,10},{9,11},{10,... | collective-permute-start | bytes 626696 | tf_op jit(solution)/shard_map/ppermute | solution.py:620
  42.4 12.2 %collective-permute-start.5 = (bf16[272,384]{1,0:T(8,128)(2,1)S(1)}, bf16[272,384]{1,0:T(8,128)(2,1)S(1)}, u32[]{:S(2)}, u32[]{:S(2)}) collective-permute-start(bf16[272,384]{1,0:T(8,128)(2,1)S(1)} %get-tuple-element.175), channel_id=1, source_target_pairs={{0,3},{1,0},{2,1},{3,2},{4,7},{5,4},{6,5},{7,6},{8,11},{9,8},{10,9... | collective-permute-start | bytes 626696 | tf_op jit(solution)/shard_map/ppermute | solution.py:620
  44.2 13.5 %collective-permute-start.9 = (bf16[2,3,120,384]{3,2,1,0:T(8,128)(2,1)S(1)}, bf16[2,3,120,384]{3,2,1,0:T(8,128)(2,1)}, u32[]{:S(2)}, u32[]{:S(2)}) collective-permute-start(bf16[2,3,120,384]{3,2,1,0:T(8,128)(2,1)S(1)} %pad_maximum_fusion.11), channel_id=1, source_target_pairs={{0,8},{4,12},{8,0},{12,4},{1,9},{5,13},{9,1},{13,5},{2,10},{6,14},... | collective-permute-start | bytes 1658888 | tf_op jit(solution)/shard_map/ppermute | solution.py:571
  44.9 14.1 %collective-permute-start.8 = (bf16[2,3,120,384]{3,2,1,0:T(8,128)(2,1)S(1)}, bf16[2,3,120,384]{3,2,1,0:T(8,128)(2,1)}, u32[]{:S(2)}, u32[]{:S(2)}) collective-permute-start(bf16[2,3,120,384]{3,2,1,0:T(8,128)(2,1)S(1)} %pad_maximum_fusion.10), channel_id=1, source_target_pairs={{0,16},{16,0},{1,17},{17,1},{2,18},{18,2},{3,19},{19,3},{4,20},{20... | collective-permute-start | bytes 1658888 | tf_op jit(solution)/shard_map/ppermute | solution.py:571
  48.0 30.1 %copy-start.23 = (bf16[272,384]{1,0:T(8,128)(2,1)}, bf16[272,384]{1,0:T(8,128)(2,1)S(1)}, u32[]{:S(2)}) copy-start(bf16[272,384]{1,0:T(8,128)(2,1)S(1)} %collective-permute-done.3.refs_1_) | copy-start | bytes 626692
  54.7 23.5 %copy-start.21 = (bf16[272,384]{1,0:T(8,128)(2,1)}, bf16[272,384]{1,0:T(8,128)(2,1)S(1)}, u32[]{:S(2)}) copy-start(bf16[272,384]{1,0:T(8,128)(2,1)S(1)} %collective-permute-done.5.refs_3_.refs_1_) | copy-start | bytes 626692
  54.7 8.7 %collective-permute-start.14 = (bf16[3,96,384]{2,1,0:T(8,128)(2,1)S(1)}, bf16[3,96,384]{2,1,0:T(8,128)(2,1)}, u32[]{:S(2)}, u32[]{:S(2)}) collective-permute-start(bf16[3,96,384]{2,1,0:T(8,128)(2,1)S(1)} %pad_maximum_fusion.25), channel_id=1, source_target_pairs={{0,16},{16,0},{1,17},{17,1},{2,18},{18,2},{3,19},{19,3},{4,20},{20... | collective-permute-start | bytes 663560 | tf_op jit(solution)/shard_map/ppermute | solution.py:571
  55.2 8.2 %collective-permute-start.13 = (bf16[3,96,384]{2,1,0:T(8,128)(2,1)}, bf16[3,96,384]{2,1,0:T(8,128)(2,1)}, u32[]{:S(2)}, u32[]{:S(2)}) collective-permute-start(bf16[3,96,384]{2,1,0:T(8,128)(2,1)} %pad_maximum_fusion.24), channel_id=1, source_target_pairs={{0,8},{4,12},{8,0},{12,4},{1,9},{5,13},{9,1},{13,5},{2,10},{6,14},... | collective-permute-start | bytes 663560 | tf_op jit(solution)/shard_map/ppermute | solution.py:571
  63.4 8.8 %collective-permute-start.16 = (bf16[2,2,3,96,768]{4,3,2,1,0:T(8,128)(2,1)S(1)}, bf16[2,2,3,96,768]{4,3,2,1,0:T(8,128)(2,1)}, u32[]{:S(2)}, u32[]{:S(2)}) collective-permute-start(bf16[2,2,3,96,768]{4,3,2,1,0:T(8,128)(2,1)S(1)} %maximum_maximum_fusion), channel_id=1, source_target_pairs={{0,4},{4,0},{8,12},{12,8},{1,5},{5,1},{9,13},{13,9},{2,6},{6,2},{1... | collective-permute-start | bytes 5308424 | tf_op jit(solution)/shard_map/ppermute | solution.py:571
  63.5 12.1 %collective-permute-start.10 = (bf16[144,384]{1,0:T(8,128)(2,1)S(1)}, bf16[144,384]{1,0:T(8,128)(2,1)S(1)}, u32[]{:S(2)}, u32[]{:S(2)}) collective-permute-start(bf16[144,384]{1,0:T(8,128)(2,1)S(1)} %dynamic_slice.24), channel_id=1, source_target_pairs={{0,1},{1,2},{2,3},{3,0},{4,5},{5,6},{6,7},{7,4},{8,9},{9,10},{10,1... | collective-permute-start | bytes 331784 | tf_op jit(solution)/shard_map/ppermute | solution.py:620
  67.6 9.1 %collective-permute-start.11 = (bf16[144,384]{1,0:T(8,128)(2,1)S(1)}, bf16[144,384]{1,0:T(8,128)(2,1)S(1)}, u32[]{:S(2)}, u32[]{:S(2)}) collective-permute-start(bf16[144,384]{1,0:T(8,128)(2,1)S(1)} %dynamic_slice.24), channel_id=1, source_target_pairs={{0,2},{1,3},{2,0},{3,1},{4,6},{5,7},{6,4},{7,5},{8,10},{9,11},{10,... | collective-permute-start | bytes 331784 | tf_op jit(solution)/shard_map/ppermute | solution.py:620
  68.8 8.0 %collective-permute-start.12 = (bf16[144,384]{1,0:T(8,128)(2,1)S(1)}, bf16[144,384]{1,0:T(8,128)(2,1)S(1)}, u32[]{:S(2)}, u32[]{:S(2)}) collective-permute-start(bf16[144,384]{1,0:T(8,128)(2,1)S(1)} %dynamic_slice.24), channel_id=1, source_target_pairs={{0,3},{1,0},{2,1},{3,2},{4,7},{5,4},{6,5},{7,6},{8,11},{9,8},{10,9... | collective-permute-start | bytes 331784 | tf_op jit(solution)/shard_map/ppermute | solution.py:620
  70.0 2.2 collective-permute-start.15
  72.2 19.8 %collective-permute-start.18 = (bf16[2,3,96,384]{3,2,1,0:T(8,128)(2,1)S(1)}, bf16[2,3,96,384]{3,2,1,0:T(8,128)(2,1)S(1)}, u32[]{:S(2)}, u32[]{:S(2)}) collective-permute-start(bf16[2,3,96,384]{3,2,1,0:T(8,128)(2,1)S(1)} %pad_maximum_fusion.13), channel_id=1, source_target_pairs={{0,8},{4,12},{8,0},{12,4},{1,9},{5,13},{9,1},{13,5},{2,10},{6,14},... | collective-permute-start | bytes 1327112 | tf_op jit(solution)/shard_map/ppermute | solution.py:571
  72.8 19.2 %collective-permute-start.17 = (bf16[2,3,96,384]{3,2,1,0:T(8,128)(2,1)S(1)}, bf16[2,3,96,384]{3,2,1,0:T(8,128)(2,1)S(1)}, u32[]{:S(2)}, u32[]{:S(2)}) collective-permute-start(bf16[2,3,96,384]{3,2,1,0:T(8,128)(2,1)S(1)} %pad_maximum_fusion.12), channel_id=1, source_target_pairs={{0,16},{16,0},{1,17},{17,1},{2,18},{18,2},{3,19},{19,3},{4,20},{20... | collective-permute-start | bytes 1327112 | tf_op jit(solution)/shard_map/ppermute | solution.py:571
  76.8 15.2 %collective-permute-start.19 = (bf16[3,144,384]{2,1,0:T(8,128)(2,1)S(1)}, bf16[3,144,384]{2,1,0:T(8,128)(2,1)S(1)}, u32[]{:S(2)}, u32[]{:S(2)}) collective-permute-start(bf16[3,144,384]{2,1,0:T(8,128)(2,1)S(1)} %pad_maximum_fusion.17), channel_id=1, source_target_pairs={{0,8},{4,12},{8,0},{12,4},{1,9},{5,13},{9,1},{13,5},{2,10},{6,14},... | collective-permute-start | bytes 995336 | tf_op jit(solution)/shard_map/ppermute | solution.py:571
  92.4 3.8 %collective-permute-start.20 = (bf16[2,2,3,96,768]{4,3,2,0,1:T(8,128)(2,1)S(1)}, bf16[2,2,3,96,768]{4,3,2,0,1:T(8,128)(2,1)S(1)}, u32[]{:S(2)}, u32[]{:S(2)}) collective-permute-start(bf16[2,2,3,96,768]{4,3,2,0,1:T(8,128)(2,1)S(1)} %maximum_maximum_fusion.1), channel_id=1, source_target_pairs={{0,4},{4,0},{8,12},{12,8},{1,5},{5,1},{9,13},{13,9},{2,6},{6,2},{1... | collective-permute-start | bytes 5308424 | tf_op jit(solution)/shard_map/ppermute | solution.py:571
  92.6 17.4 %collective-permute-start.21 = (bf16[2,3,144,384]{3,2,1,0:T(8,128)(2,1)S(1)}, bf16[2,3,144,384]{3,2,1,0:T(8,128)(2,1)S(1)}, u32[]{:S(2)}, u32[]{:S(2)}) collective-permute-start(bf16[2,3,144,384]{3,2,1,0:T(8,128)(2,1)S(1)} %pad_maximum_fusion.4), channel_id=1, source_target_pairs={{0,16},{16,0},{1,17},{17,1},{2,18},{18,2},{3,19},{19,3},{4,20},{20... | collective-permute-start | bytes 1990664 | tf_op jit(solution)/shard_map/ppermute | solution.py:571
  107.6 25.2 %copy-start.16 = (bf16[4,4,96,768]{3,2,1,0:T(8,128)(2,1)}, bf16[4,4,96,768]{3,2,1,0:T(8,128)(2,1)S(1)}, u32[]{:S(2)}) copy-start(bf16[4,4,96,768]{3,2,1,0:T(8,128)(2,1)S(1)} %get-tuple-element.235) | copy-start | bytes 7077892
  110.0 4.5 %collective-permute-start.22 = (bf16[4,4,96,768]{3,2,1,0:T(8,128)(2,1)S(1)}, bf16[4,4,96,768]{3,2,1,0:T(8,128)(2,1)S(1)}, u32[]{:S(2)}, u32[]{:S(2)}) collective-permute-start(bf16[4,4,96,768]{3,2,1,0:T(8,128)(2,1)S(1)} %get-tuple-element.233), channel_id=1, source_target_pairs={{0,4},{4,0},{8,12},{12,8},{1,5},{5,1},{9,13},{13,9},{2,6},{6,2},{1... | collective-permute-start | bytes 7077896 | tf_op jit(solution)/shard_map/ppermute | solution.py:571
  110.4 22.3 %collective-permute-start.23 = (bf16[2,2,3,144,384]{4,3,2,1,0:T(8,128)(2,1)S(1)}, bf16[2,2,3,144,384]{4,3,2,1,0:T(8,128)(2,1)S(1)}, u32[]{:S(2)}, u32[]{:S(2)}) collective-permute-start(bf16[2,2,3,144,384]{4,3,2,1,0:T(8,128)(2,1)S(1)} %pad_maximum_fusion), channel_id=1, source_target_pairs={{0,4},{4,0},{8,12},{12,8},{1,5},{5,1},{9,13},{13,9},{2,6},{6,2},{1... | collective-permute-start | bytes 3981320 | tf_op jit(solution)/shard_map/ppermute | solution.py:571
  110.9 21.7 %collective-permute-start.24 = (bf16[512,768]{1,0:T(8,128)(2,1)S(1)}, bf16[512,768]{1,0:T(8,128)(2,1)}, u32[]{:S(2)}, u32[]{:S(2)}) collective-permute-start(bf16[512,768]{1,0:T(8,128)(2,1)S(1)} %get-tuple-element.230.refs_0_), channel_id=1, source_target_pairs={{0,1},{1,0},{2,3},{3,2},{4,5},{5,4},{6,7},{7,6},{8,9},{9,8},{10,11... | collective-permute-start | bytes 2359304 | tf_op jit(solution)/shard_map/ppermute | solution.py:571
  112.5 20.2 %collective-permute-start.25 = (bf16[512,768]{1,0:T(8,128)(2,1)S(1)}, bf16[512,768]{1,0:T(8,128)(2,1)}, u32[]{:S(2)}, u32[]{:S(2)}) collective-permute-start(bf16[512,768]{1,0:T(8,128)(2,1)S(1)} %get-tuple-element.230.refs_0_), channel_id=1, source_target_pairs={{1,2},{2,1},{5,6},{6,5},{9,10},{10,9},{13,14},{14,13},{17,18},{18,... | collective-permute-start | bytes 2359304 | tf_op jit(solution)/shard_map/ppermute | solution.py:714
  116.0 16.7 %collective-permute-start.26 = (bf16[4,96,768]{2,1,0:T(8,128)(2,1)}, bf16[4,96,768]{2,1,0:T(8,128)(2,1)S(1)}, u32[]{:S(2)}, u32[]{:S(2)}) collective-permute-start(bf16[4,96,768]{2,1,0:T(8,128)(2,1)} %bitcast.60), channel_id=1, source_target_pairs={{0,8},{4,12},{8,0},{12,4},{1,9},{5,13},{9,1},{13,5},{2,10},{6,14},... | collective-permute-start | bytes 1769480 | tf_op jit(solution)/shard_map/ppermute | solution.py:571
  116.5 16.2 %collective-permute-start.27 = (bf16[4,96,768]{2,1,0:T(8,128)(2,1)S(1)}, bf16[4,96,768]{2,1,0:T(8,128)(2,1)S(1)}, u32[]{:S(2)}, u32[]{:S(2)}) collective-permute-start(bf16[4,96,768]{2,1,0:T(8,128)(2,1)S(1)} %bitcast.310), channel_id=1, source_target_pairs={{0,16},{16,0},{1,17},{17,1},{2,18},{18,2},{3,19},{19,3},{4,20},{20... | collective-permute-start | bytes 1769480 | tf_op jit(solution)/shard_map/ppermute | solution.py:571
  132.7 4.8 %collective-permute-start.28 = (bf16[4,4,96,768]{3,2,1,0:T(8,128)(2,1)}, bf16[4,4,96,768]{3,2,1,0:T(8,128)(2,1)S(1)}, u32[]{:S(2)}, u32[]{:S(2)}) collective-permute-start(bf16[4,4,96,768]{3,2,1,0:T(8,128)(2,1)} %get-tuple-element.253), channel_id=1, source_target_pairs={{0,4},{4,0},{8,12},{12,8},{1,5},{5,1},{9,13},{13,9},{2,6},{6,2},{1... | collective-permute-start | bytes 7077896 | tf_op jit(solution)/shard_map/ppermute | solution.py:571
  139.0 27.3 %collective-permute-start.32 = (bf16[6,96,768]{2,1,0:T(8,128)(2,1)}, bf16[6,96,768]{2,1,0:T(8,128)(2,1)}, u32[]{:S(2)}, u32[]{:S(2)}) collective-permute-start(bf16[6,96,768]{2,1,0:T(8,128)(2,1)} %pad_maximum_fusion.3), channel_id=1, source_target_pairs={{0,16},{16,0},{1,17},{17,1},{2,18},{18,2},{3,19},{19,3},{4,20},{20... | collective-permute-start | bytes 2654216 | tf_op jit(solution)/shard_map/ppermute | solution.py:571
  140.5 25.7 %collective-permute-start.31 = (bf16[6,96,768]{2,1,0:T(8,128)(2,1)}, bf16[6,96,768]{2,1,0:T(8,128)(2,1)}, u32[]{:S(2)}, u32[]{:S(2)}) collective-permute-start(bf16[6,96,768]{2,1,0:T(8,128)(2,1)} %pad_maximum_fusion.2), channel_id=1, source_target_pairs={{0,8},{4,12},{8,0},{12,4},{1,9},{5,13},{9,1},{13,5},{2,10},{6,14},... | collective-permute-start | bytes 2654216 | tf_op jit(solution)/shard_map/ppermute | solution.py:571
  142.0 20.3 %collective-permute-start.29 = (bf16[512,768]{1,0:T(8,128)(2,1)}, bf16[512,768]{1,0:T(8,128)(2,1)}, u32[]{:S(2)}, u32[]{:S(2)}) collective-permute-start(bf16[512,768]{1,0:T(8,128)(2,1)} %collective-permute-done.24.refs_1_), channel_id=1, source_target_pairs={{1,2},{2,1},{5,6},{6,5},{9,10},{10,9},{13,14},{14,13},{17,18},{18,... | collective-permute-start | bytes 2359304 | tf_op jit(solution)/shard_map/ppermute | solution.py:714
  143.6 22.6 %collective-permute-start.30 = (bf16[512,768]{1,0:T(8,128)(2,1)}, bf16[512,768]{1,0:T(8,128)(2,1)}, u32[]{:S(2)}, u32[]{:S(2)}) collective-permute-start(bf16[512,768]{1,0:T(8,128)(2,1)} %collective-permute-done.25.refs_2_), channel_id=1, source_target_pairs={{1,0},{2,3},{5,4},{6,7},{9,8},{10,11},{13,12},{14,15},{17,16},{18,... | collective-permute-start | bytes 2359304 | tf_op jit(solution)/shard_map/ppermute | solution.py:715
  166.2 3.2 %collective-permute-start.33 = (bf16[4,2,96,768]{3,2,1,0:T(8,128)(2,1)S(1)}, bf16[4,2,96,768]{3,2,1,0:T(8,128)(2,1)S(1)}, u32[]{:S(2)}, u32[]{:S(2)}) collective-permute-start(bf16[4,2,96,768]{3,2,1,0:T(8,128)(2,1)S(1)} %get-tuple-element.270), channel_id=1, source_target_pairs={{0,4},{4,0},{8,12},{12,8},{1,5},{5,1},{9,13},{13,9},{2,6},{6,2},{1... | collective-permute-start | bytes 3538952 | tf_op jit(solution)/shard_map/ppermute | solution.py:571
  166.2 28.5 %collective-permute-start.34 = (bf16[512,768]{1,0:T(8,128)(2,1)}, bf16[512,768]{1,0:T(8,128)(2,1)}, u32[]{:S(2)}, u32[]{:S(2)}) collective-permute-start(bf16[512,768]{1,0:T(8,128)(2,1)} %collective-permute-done.29.refs_3_), channel_id=1, source_target_pairs={{1,0},{2,3},{5,4},{6,7},{9,8},{10,11},{13,12},{14,15},{17,16},{18,... | collective-permute-start | bytes 2359304 | tf_op jit(solution)/shard_map/ppermute | solution.py:715
  169.7 25.0 %collective-permute-start.36 = (bf16[4,96,768]{2,1,0:T(8,128)(2,1)S(1)}, bf16[4,96,768]{2,1,0:T(8,128)(2,1)S(1)}, u32[]{:S(2)}, u32[]{:S(2)}) collective-permute-start(bf16[4,96,768]{2,1,0:T(8,128)(2,1)S(1)} %pad_maximum_fusion.6), channel_id=1, source_target_pairs={{0,16},{16,0},{1,17},{17,1},{2,18},{18,2},{3,19},{19,3},{4,20},{20... | collective-permute-start | bytes 1769480 | tf_op jit(solution)/shard_map/ppermute | solution.py:571
  170.5 24.2 %collective-permute-start.35 = (bf16[4,96,768]{2,1,0:T(8,128)(2,1)S(1)}, bf16[4,96,768]{2,1,0:T(8,128)(2,1)}, u32[]{:S(2)}, u32[]{:S(2)}) collective-permute-start(bf16[4,96,768]{2,1,0:T(8,128)(2,1)S(1)} %pad_maximum_fusion.5), channel_id=1, source_target_pairs={{0,8},{4,12},{8,0},{12,4},{1,9},{5,13},{9,1},{13,5},{2,10},{6,14},... | collective-permute-start | bytes 1769480 | tf_op jit(solution)/shard_map/ppermute | solution.py:571
  172.7 22.0 %collective-permute-start.37 = (bf16[2,96,768]{2,1,0:T(8,128)(2,1)S(1)}, bf16[2,96,768]{2,1,0:T(8,128)(2,1)}, u32[]{:S(2)}, u32[]{:S(2)}) collective-permute-start(bf16[2,96,768]{2,1,0:T(8,128)(2,1)S(1)} %pad_maximum_fusion.18), channel_id=1, source_target_pairs={{0,1},{1,0},{2,3},{3,2},{4,5},{5,4},{6,7},{7,6},{8,9},{9,8},{10,11... | collective-permute-start | bytes 884744 | tf_op jit(solution)/shard_map/ppermute | solution.py:571
  195.5 5.1 %collective-permute-start.40 = (bf16[4,2,96,768]{3,2,1,0:T(8,128)(2,1)}, bf16[4,2,96,768]{3,2,1,0:T(8,128)(2,1)}, u32[]{:S(2)}, u32[]{:S(2)}) collective-permute-start(bf16[4,2,96,768]{3,2,1,0:T(8,128)(2,1)} %get-tuple-element.287), channel_id=1, source_target_pairs={{0,4},{4,0},{8,12},{12,8},{1,5},{5,1},{9,13},{13,9},{2,6},{6,2},{1... | collective-permute-start | bytes 3538952 | tf_op jit(solution)/shard_map/ppermute | solution.py:571
  196.4 20.7 %collective-permute-start.38 = (bf16[512,768]{1,0:T(8,128)(2,1)S(1)}, bf16[512,768]{1,0:T(8,128)(2,1)S(1)}, u32[]{:S(2)}, u32[]{:S(2)}) collective-permute-start(bf16[512,768]{1,0:T(8,128)(2,1)S(1)} %get-tuple-element.319.refs_0_.own_ref), channel_id=1, source_target_pairs={{0,1},{1,0},{2,3},{3,2},{4,5},{5,4},{6,7},{7,6},{8,9},{9,8},{10,11... | collective-permute-start | bytes 2359304 | tf_op jit(solution)/shard_map/ppermute | solution.py:571
  196.4 20.8 %collective-permute-start.39 = (bf16[512,768]{1,0:T(8,128)(2,1)S(1)}, bf16[512,768]{1,0:T(8,128)(2,1)}, u32[]{:S(2)}, u32[]{:S(2)}) collective-permute-start(bf16[512,768]{1,0:T(8,128)(2,1)S(1)} %get-tuple-element.319.refs_0_.own_ref), channel_id=1, source_target_pairs={{1,2},{2,1},{5,6},{6,5},{9,10},{10,9},{13,14},{14,13},{17,18},{18,... | collective-permute-start | bytes 2359304 | tf_op jit(solution)/shard_map/ppermute | solution.py:714
  202.6 14.5 %collective-permute-start.42 = (bf16[3,96,768]{2,1,0:T(8,128)(2,1)}, bf16[3,96,768]{2,1,0:T(8,128)(2,1)}, u32[]{:S(2)}, u32[]{:S(2)}) collective-permute-start(bf16[3,96,768]{2,1,0:T(8,128)(2,1)} %pad_maximum_fusion.15), channel_id=1, source_target_pairs={{0,16},{16,0},{1,17},{17,1},{2,18},{18,2},{3,19},{19,3},{4,20},{20... | collective-permute-start | bytes 1327112 | tf_op jit(solution)/shard_map/ppermute | solution.py:571
  203.9 13.3 %collective-permute-start.41 = (bf16[3,96,768]{2,1,0:T(8,128)(2,1)}, bf16[3,96,768]{2,1,0:T(8,128)(2,1)S(1)}, u32[]{:S(2)}, u32[]{:S(2)}) collective-permute-start(bf16[3,96,768]{2,1,0:T(8,128)(2,1)} %pad_maximum_fusion.14), channel_id=1, source_target_pairs={{0,8},{4,12},{8,0},{12,4},{1,9},{5,13},{9,1},{13,5},{2,10},{6,14},... | collective-permute-start | bytes 1327112 | tf_op jit(solution)/shard_map/ppermute | solution.py:571
  205.0 12.1 %collective-permute-start.43 = (f32[18,384]{1,0:T(8,128)S(1)}, f32[18,384]{1,0:T(8,128)S(1)}, u32[]{:S(2)}, u32[]{:S(2)}) collective-permute-start(f32[18,384]{1,0:T(8,128)S(1)} %concatenate.72), channel_id=1, source_target_pairs={{0,1},{1,0},{2,3},{3,2},{4,5},{5,4},{6,7},{7,6},{8,9},{9,8},{10,11... | collective-permute-start | bytes 82952 | tf_op jit(solution)/shard_map/ppermute | solution.py:571
  220.7 7.1 %collective-permute-start.45 = (bf16[1,96,768]{2,1,0:T(8,128)(2,1)S(1)}, bf16[1,96,768]{2,1,0:T(8,128)(2,1)S(1)}, u32[]{:S(2)}, u32[]{:S(2)}) collective-permute-start(bf16[1,96,768]{2,1,0:T(8,128)(2,1)S(1)} %get-tuple-element.355), channel_id=1, source_target_pairs={{0,8},{4,12},{8,0},{12,4},{1,9},{5,13},{9,1},{13,5},{2,10},{6,14},... | collective-permute-start | bytes 442376 | tf_op jit(solution)/shard_map/ppermute | solution.py:571
  221.3 6.5 %collective-permute-start.46 = (bf16[1,96,768]{2,1,0:T(8,128)(2,1)S(1)}, bf16[1,96,768]{2,1,0:T(8,128)(2,1)S(1)}, u32[]{:S(2)}, u32[]{:S(2)}) collective-permute-start(bf16[1,96,768]{2,1,0:T(8,128)(2,1)S(1)} %get-tuple-element.354), channel_id=1, source_target_pairs={{0,16},{16,0},{1,17},{17,1},{2,18},{18,2},{3,19},{19,3},{4,20},{20... | collective-permute-start | bytes 442376 | tf_op jit(solution)/shard_map/ppermute | solution.py:571
  222.1 12.4 %collective-permute-start.44 = (bf16[2,96,768]{2,1,0:T(8,128)(2,1)S(1)}, bf16[2,96,768]{2,1,0:T(8,128)(2,1)S(1)}, u32[]{:S(2)}, u32[]{:S(2)}) collective-permute-start(bf16[2,96,768]{2,1,0:T(8,128)(2,1)S(1)} %copy-done.48), channel_id=1, source_target_pairs={{0,1},{1,0},{2,3},{3,2},{4,5},{5,4},{6,7},{7,6},{8,9},{9,8},{10,11... | collective-permute-start | bytes 884744 | tf_op jit(solution)/shard_map/ppermute | solution.py:571
  225.0 11.5 %collective-permute-start.47 = (bf16[512,768]{1,0:T(8,128)(2,1)}, bf16[512,768]{1,0:T(8,128)(2,1)S(1)}, u32[]{:S(2)}, u32[]{:S(2)}) collective-permute-start(bf16[512,768]{1,0:T(8,128)(2,1)} %copy-done.41), channel_id=1, source_target_pairs={{1,2},{2,1},{5,6},{6,5},{9,10},{10,9},{13,14},{14,13},{17,18},{18,... | collective-permute-start | bytes 2359304 | tf_op jit(solution)/shard_map/ppermute | solution.py:714
  225.7 23.7 %collective-permute-start.48 = (bf16[512,768]{1,0:T(8,128)(2,1)}, bf16[512,768]{1,0:T(8,128)(2,1)}, u32[]{:S(2)}, u32[]{:S(2)}) collective-permute-start(bf16[512,768]{1,0:T(8,128)(2,1)} %collective-permute-done.39.refs_2_), channel_id=1, source_target_pairs={{1,0},{2,3},{5,4},{6,7},{9,8},{10,11},{13,12},{14,15},{17,16},{18,... | collective-permute-start | bytes 2359304 | tf_op jit(solution)/shard_map/ppermute | solution.py:715
  229.7 28.8 %collective-permute-start.51 = (bf16[2,96,768]{2,1,0:T(8,128)(2,1)}, bf16[2,96,768]{2,1,0:T(8,128)(2,1)S(1)}, u32[]{:S(2)}, u32[]{:S(2)}) collective-permute-start(bf16[2,96,768]{2,1,0:T(8,128)(2,1)} %pad_maximum_fusion.21), channel_id=1, source_target_pairs={{0,1},{1,0},{2,3},{3,2},{4,5},{5,4},{6,7},{7,6},{8,9},{9,8},{10,11... | collective-permute-start | bytes 884744 | tf_op jit(solution)/shard_map/ppermute | solution.py:571
  249.4 16.0 %collective-permute-start.49 = (bf16[2,96,768]{2,1,0:T(8,128)(2,1)S(1)}, bf16[2,96,768]{2,1,0:T(8,128)(2,1)S(1)}, u32[]{:S(2)}, u32[]{:S(2)}) collective-permute-start(bf16[2,96,768]{2,1,0:T(8,128)(2,1)S(1)} %pad_maximum_fusion.20), channel_id=1, source_target_pairs={{0,2},{1,3},{2,0},{3,1},{4,6},{5,7},{6,4},{7,5},{8,10},{9,11},{10,... | collective-permute-start | bytes 884744 | tf_op jit(solution)/shard_map/ppermute | solution.py:571
  250.8 21.3 %collective-permute-start.53 = (f32[15,384]{1,0:T(8,128)S(1)}, f32[15,384]{1,0:T(8,128)S(1)}, u32[]{:S(2)}, u32[]{:S(2)}) collective-permute-start(f32[15,384]{1,0:T(8,128)S(1)} %pad_maximum_fusion.27), channel_id=1, source_target_pairs={{0,2},{1,3},{2,0},{3,1},{4,6},{5,7},{6,4},{7,5},{8,10},{9,11},{10,... | collective-permute-start | bytes 69128 | tf_op jit(solution)/shard_map/ppermute | solution.py:571
  252.3 33.1 %collective-permute-start.50 = (bf16[512,768]{1,0:T(8,128)(2,1)S(1)}, bf16[512,768]{1,0:T(8,128)(2,1)S(1)}, u32[]{:S(2)}, u32[]{:S(2)}) collective-permute-start(bf16[512,768]{1,0:T(8,128)(2,1)S(1)} %collective-permute-done.47.refs_3_.refs_5_), channel_id=1, source_target_pairs={{1,0},{2,3},{5,4},{6,7},{9,8},{10,11},{13,12},{14,15},{17,16},{18,... | collective-permute-start | bytes 2359304 | tf_op jit(solution)/shard_map/ppermute | solution.py:715
  259.2 13.0 %collective-permute-start.52 = (bf16[96,768]{1,0:T(8,128)(2,1)}, bf16[96,768]{1,0:T(8,128)(2,1)S(1)}, u32[]{:S(2)}, u32[]{:S(2)}) collective-permute-start(bf16[96,768]{1,0:T(8,128)(2,1)} %fusion.10), channel_id=1, source_target_pairs={{0,2},{1,3},{2,0},{3,1},{4,6},{5,7},{6,4},{7,5},{8,10},{9,11},{10,... | collective-permute-start | bytes 442376 | tf_op jit(solution)/shard_map/ppermute | solution.py:571
  267.1 7.8 %collective-permute-start.57 = (bf16[2,96,768]{2,1,0:T(8,128)(2,1)S(1)}, bf16[2,96,768]{2,1,0:T(8,128)(2,1)S(1)}, u32[]{:S(2)}, u32[]{:S(2)}) collective-permute-start(bf16[2,96,768]{2,1,0:T(8,128)(2,1)S(1)} %get-tuple-element.336), channel_id=1, source_target_pairs={{0,16},{16,0},{1,17},{17,1},{2,18},{18,2},{3,19},{19,3},{4,20},{20... | collective-permute-start | bytes 884744 | tf_op jit(solution)/shard_map/ppermute | solution.py:571
  272.1 1.4 collective-permute-start.55
  272.3 6.3 %collective-permute-start.54 = (bf16[96,768]{1,0:T(8,128)(2,1)S(1)}, bf16[96,768]{1,0:T(8,128)(2,1)S(1)}, u32[]{:S(2)}, u32[]{:S(2)}) collective-permute-start(bf16[96,768]{1,0:T(8,128)(2,1)S(1)} %get-tuple-element.338), channel_id=1, source_target_pairs={{0,16},{16,0},{1,17},{17,1},{2,18},{18,2},{3,19},{19,3},{4,20},{20... | collective-permute-start | bytes 442376 | tf_op jit(solution)/shard_map/ppermute | solution.py:571
  273.4 3.9 %collective-permute-start.56 = (f32[15,384]{1,0:T(8,128)S(1)}, f32[15,384]{1,0:T(8,128)S(1)}, u32[]{:S(2)}, u32[]{:S(2)}) collective-permute-start(f32[15,384]{1,0:T(8,128)S(1)} %add.568), channel_id=1, source_target_pairs={{0,8},{4,12},{8,0},{12,4},{1,9},{5,13},{9,1},{13,5},{2,10},{6,14},... | collective-permute-start | bytes 69128 | tf_op jit(solution)/shard_map/ppermute | solution.py:571
  278.6 3.8 %collective-permute-start.58 = (f32[15,384]{1,0:T(8,128)S(1)}, f32[15,384]{1,0:T(8,128)S(1)}, u32[]{:S(2)}, u32[]{:S(2)}) collective-permute-start(f32[15,384]{1,0:T(8,128)S(1)} %add.569), channel_id=1, source_target_pairs={{0,16},{16,0},{1,17},{17,1},{2,18},{18,2},{3,19},{19,3},{4,20},{20... | collective-permute-start | bytes 69128 | tf_op jit(solution)/shard_map/ppermute | solution.py:571
  (48 other events, 254.3 us)

commit v7 on v6

--- a/solution.py
+++ b/solution.py
@@ -103,7 +103,7 @@
     lax.fori_loop(0, heads, one_head, 0)
     context = sum_ref[...].T.astype(BF)
     count, rows, cols = len(out_refs), context.shape[0] // 2, context.shape[1]
-    ahead = lax.rem(pl.program_id(0) + count - at_ref[3], count)
+    ahead = pl.program_id(0) ^ at_ref[3]
     for s, out_ref in enumerate(out_refs):
         @pl.when(ahead == s)
         def _():
@@ -615,9 +615,7 @@
         l_index = lax.axis_index("local")
         core, x = l_index & 1, l_index >> 1
         y = lax.axis_index("outer") & 1
-        z_from = lambda s: jnp.mod(z - s, n_tensor)
-        z_to = lambda s: jnp.mod(z + s, n_tensor)
-        cyclic = lambda v, s: lax.ppermute(v, "tensor", [(i, (i + s) % n_tensor) for i in range(n_tensor)])
+        other = lambda v, s: swap(v, "tensor", n_tensor, s)
         pick = lambda v, i: lax.dynamic_index_in_dim(v, i, 0, keepdims=False)
         others = range(1, n_tensor)
         by_x = lambda v: swap(v, "local", n_local, 2)
@@ -648,7 +646,7 @@
         flat_qkv = qkv_rows.reshape(3 * head_cols, width)
 
         first = jnp.concatenate([piece_of(w_out), piece_of(w_in), piece_of(w_down)])
-        first_z = [cyclic(first, s) for s in others]
+        first_z = [other(first, s) for s in others]
         done(first)
         biases = jnp.concatenate([b_inner.reshape(-1), b_qv.reshape(-1)])
         bias_rows = -(-biases.size // half)
@@ -657,7 +655,7 @@
 
         context = attend(at, hold(tokens), qkv_rows, b_qv.reshape(2, head_cols), segments, heads, bias_pack)
         (ctx_own, *ctx_send), first_z = run((context, first_z))
-        ctx_z = [cyclic(v, s) for v, s in zip(ctx_send, others)]
+        ctx_z = [other(v, s) for v, s in zip(ctx_send, others)]
         cut, end = w_out.shape[0] // 8, (w_out.shape[0] + w_in.shape[0]) // 8
         a, b = halves(first_z, slice(0, end))
         a1, b1 = by_x(a), by_y(b)
@@ -680,7 +678,7 @@
         b_qv_all = bias_all[:, hidden_cols:].reshape(n_tensor, 2, head_cols)
         done(b_inner_all, a1, b1)
         a, b, a1, b1, piece_qkv = hold((a, b, a1, b1, piece_qkv))
-        third_z = [cyclic(piece_qkv, s) for s in others]
+        third_z = [other(piece_qkv, s) for s in others]
         in_both = plane_three(a, b, a1, b1, slice(cut, None))
         out_both = plane_three(a, b, a1, b1, slice(0, cut))
         done(in_both, out_both, b_inner_all, c1, d1)
@@ -763,11 +761,9 @@
 
         z_near = lambda v: swap(v, "tensor", n_tensor, 1)
         z_far = lambda v: swap(v, "tensor", n_tensor, 2)
-        odd = (z & 1) == 1
 
         def after_near(values, got):
-            first, second = jnp.where(odd, got[1], got[0]), jnp.where(odd, got[0], got[1])
-            return values[0].astype(F32) + first.astype(F32), values[1].astype(F32) + second.astype(F32)
+            return values[0].astype(F32) + got[0].astype(F32), values[1].astype(F32) + got[1].astype(F32)
 
         def outer_rest(mine):
             bit = 2

time: 291 us -> 291 us (level)
  waiting for transfers between devices: 55.5 us -> 69.1 us
  starting transfers between devices: 81.5 us -> 71.1 us
    ppermute x42 -> x51, waiting for transfers between devices: 25.4 us -> 50.2 us  [swap(): return lax.ppermute(value, axis, [(i, i ^ bit) for i in range(size)])]
    ppermute x9 -> x0, starting transfers between devices: 23.6 us -> none  [local(): lax.ppermute(v, 'tensor', [(i, (i + s) % n_tensor) for i in range(n_tenso...]
    ppermute x9 -> x0, waiting for transfers between devices: 13.3 us -> none  [local(): lax.ppermute(v, 'tensor', [(i, (i + s) % n_tensor) for i in range(n_tenso...]
    ppermute x42 -> x51, starting transfers between devices: 47.1 us -> 60.4 us  [swap(): return lax.ppermute(value, axis, [(i, i ^ bit) for i in range(size)])]
    unnamed x119 -> x107, local copies, waits for them, and re-layouts: 14.3 us -> 13.6 us
  transfers between devices with their start and end apart: 59 -> 59, of which waited for: 19 -> 20; matrix products, arithmetic and copies ran while one was open for 14% -> 13% of each run, Pallas kernels for 31% -> 31%
where the time goes in v7:
time: 291 us; the launch traced here: 290 us
  Pallas kernels  92.1 us (32%)
  starting transfers between devices  71.1 us (24%)
  waiting for transfers between devices  69.1 us (24%)
  other arithmetic  35.3 us (12%)
  local copies, waits for them, and re-layouts  20.1 us (7%)
    ppermute x51, starting transfers between devices, swap(): return lax.ppermute(value, axis, [(i, i ^ bit) for i in range(size)])  60.4 us
    ppermute x51, waiting for transfers between devices, swap(): return lax.ppermute(value, axis, [(i, i ^ bit) for i in range(size)])  50.2 us
    pallas_call x2, Pallas kernels, attend_back(): call(functools.partial(attend_back_kernel, first, slots, heads, (cols //...  31.3 us
    ppermute x4, waiting for transfers between devices, local(): outward = lambda v: lax.ppermute(v, 'tensor', [(1, 0), (2, 3)])  18.8 us
    pallas_call x1, Pallas kernels, back(): call(functools.partial(back_kernel, slots), 'back', at, (slots,), [const(...  14.6 us
    unnamed x107, local copies, waits for them, and re-layouts  13.6 us
    pallas_call x1, Pallas kernels, attend(): call(functools.partial(attend_kernel, heads, (cols // heads) ** (-0.5)),...  12.8 us
    pallas_call x1, Pallas kernels, fall(): call(functools.partial(fall_kernel, slots), 'fall', at, (2 * slots,), [pl...  11.3 us
  transfers between devices with their start and end apart: 59, of which 20 were waited for; matrix products, arithmetic and copies ran while one was open for 13% of the time, Pallas kernels for 31%

profile of v7, /device:TPU:0, one launch (start us, length us, event | category | flops | bytes accessed | tf_op | source)
XLA Modules:
  0.0 289.8 jit_solution(13336051899447146958)
XLA Ops:
  2.6 3.1 %collective-permute-start = (bf16[216,768]{1,0:T(8,128)(2,1)S(1)}, bf16[216,768]{1,0:T(8,128)(2,1)S(1)}, u32[]{:S(2)}, u32[]{:S(2)}) collective-permute-start(bf16[216,768]{1,0:T(8,128)(2,1)S(1)} %pad_maximum_fusion.16), channel_id=1, source_target_pairs={{0,1},{1,0},{2,3},{3,2},{4,5},{5,4},{6,7},{7,6},{8,9},{9,8},{10,11... | collective-permute-start | bytes 995336 | tf_op jit(solution)/shard_map/ppermute | solution.py:571
  5.6 2.6 collective-permute-start.1
  10.0 1.9 copy-done
  12.6 12.8 %attend.1 = (bf16[272,384]{1,0:T(8,128)(2,1)S(1)}, bf16[272,384]{1,0:T(8,128)(2,1)S(1)}, bf16[272,384]{1,0:T(8,128)(2,1)S(1)}, bf16[272,384]{1,0:T(8,128)(2,1)S(1)}) custom-call(s32[4]{0:T(128)S(1)} %pad_add_fusion.at_ref, bf16[4,512,768]{2,1,0:T(8,128)(2,1)S(1)} %copy-done, bf16[3,192,768]{2,1,0:T(8,128)(2,1)S(1)} %bitcast.292, ...), custom_call_target="tpu_custom_call" | custom-call | flops 1000 | bytes 1000 | tf_op jit(solution)/shard_map/attend/pallas_call | solution.py:118
  25.5 6.0 %collective-permute-done.1 = bf16[216,768]{1,0:T(8,128)(2,1)S(1)} collective-permute-done((bf16[216,768]{1,0:T(8,128)(2,1)S(1)}, bf16[216,768]{1,0:T(8,128)(2,1)S(1)}, u32[]{:S(2)}, u32[]{:S(2)}) %collective-permute-start.1) | collective-permute-done | bytes 331808 | tf_op jit(solution)/shard_map/ppermute | solution.py:571
  31.7 1.6 collective-permute-start.7
  33.3 1.6 collective-permute-start.6
  34.9 6.3 %collective-permute-start.3 = (bf16[272,384]{1,0:T(8,128)(2,1)S(1)}, bf16[272,384]{1,0:T(8,128)(2,1)S(1)}, u32[]{:S(2)}, u32[]{:S(2)}) collective-permute-start(bf16[272,384]{1,0:T(8,128)(2,1)S(1)} %get-tuple-element.173), channel_id=1, source_target_pairs={{0,1},{1,0},{2,3},{3,2},{4,5},{5,4},{6,7},{7,6},{8,9},{9,8},{10,11... | collective-permute-start | bytes 626696 | tf_op jit(solution)/shard_map/ppermute | solution.py:571
  42.3 1.4 collective-permute-start.5
  45.9 1.5 collective-permute-done.3.refs_1_
  47.4 10.8 %collective-permute-done.4.refs_2_.refs_0_ = bf16[272,384]{1,0:T(8,128)(2,1)S(1)} collective-permute-done((bf16[272,384]{1,0:T(8,128)(2,1)S(1)}, bf16[272,384]{1,0:T(8,128)(2,1)S(1)}, u32[]{:S(2)}, u32[]{:S(2)}) %collective-permute-start.4) | collective-permute-done | bytes 208928 | tf_op jit(solution)/shard_map/ppermute | solution.py:571
  60.5 1.1 select_bitcast_fusion.11
  62.5 1.1 select_bitcast_fusion.9
  65.0 2.8 collective-permute-start.10
  68.8 1.5 collective-permute-start.12
  73.1 1.5 collective-permute-start.17
  75.8 3.5 %collective-permute-done.11 = bf16[144,384]{1,0:T(8,128)(2,1)S(1)} collective-permute-done((bf16[144,384]{1,0:T(8,128)(2,1)S(1)}, bf16[144,384]{1,0:T(8,128)(2,1)S(1)}, u32[]{:S(2)}, u32[]{:S(2)}) %collective-permute-start.11) | collective-permute-done | bytes 110624 | tf_op jit(solution)/shard_map/ppermute | solution.py:571
  80.1 10.2 %rise.1 = (f32[512,768]{1,0:T(8,128)S(1)}, bf16[512,768]{1,0:T(8,128)(2,1)}, f32[512,768]{1,0:T(8,128)S(1)}, f32[512,1]{1,0:T(8,128)S(1)}, bf16[4,512,768]{2,1,0...) custom-call(s32[4]{0:T(128)S(1)} %pad_add_fusion.at_ref, ...), custom_call_target="tpu_custom_call" | custom-call | flops 1000 | bytes 1000 | tf_op jit(solution)/shard_map/rise/pallas_call | solution.py:219
  93.3 1.6 collective-permute-start.21
  95.0 1.8 collective-permute-done.20
  97.1 11.3 %fall.1 = (bf16[512,768]{1,0:T(8,128)(2,1)S(1)}, f32[512,768]{1,0:T(8,128)S(1)}, bf16[512,768]{1,0:T(8,128)(2,1)S(1)}, f32[3,768]{1,0:T(4,128)S(1)}, bf16[4,4,96...) custom-call(s32[4]{0:T(128)S(1)} %pad_add_fusion.at_ref, bf16[4,512,768]{2,1,0:T(8,128)(2,1)S(1)} %copy-done.7, ...), custom_call_target="tpu_custom_call" | custom-call | flops 1000 | bytes 1000 | tf_op jit(solution)/shard_map/fall/pallas_call | solution.py:305
  108.4 2.2 collective-permute-done.21
  111.5 2.2 collective-permute-start.24
  113.8 1.5 collective-permute-start.25
  115.6 1.6 collective-permute-start.26
  117.2 1.5 collective-permute-start.27
  118.7 14.6 %back.1 = (f32[4,1,768]{2,1,0:T(1,128)S(1)}, f32[512,768]{1,0:T(8,128)S(1)}, bf16[512,768]{1,0:T(8,128)(2,1)S(1)}, bf16[768,512]{1,0:T(8,128)(2,1)S(1)}, f32[3,7...) custom-call(s32[4]{0:T(128)S(1)} %pad_add_fusion.at_ref, ...), custom_call_target="tpu_custom_call" | custom-call | flops 1000 | bytes 1000 | tf_op jit(solution)/shard_map/back/pallas_call | solution.py:360
  133.8 4.5 %collective-permute-done.28 = bf16[4,4,96,768]{3,2,1,0:T(8,128)(2,1)S(1)} collective-permute-done((bf16[4,4,96,768]{3,2,1,0:T(8,128)(2,1)}, bf16[4,4,96,768]{3,2,1,0:T(8,128)(2,1)S(1)}, u32[]{:S(2)}, u32[]{:S(2)}) %collective-permute-start.28) | collective-permute-done | bytes 2359328 | tf_op jit(solution)/shard_map/ppermute | solution.py:571
  142.0 1.5 collective-permute-start.29
  143.5 1.3 collective-permute-start.30
  146.8 15.7 %attend_back.2 = (f32[2,2,192]{2,1,0:T(2,128)S(1)}, f32[512,768]{1,0:T(8,128)}, bf16[4,2,96,768]{3,2,1,0:T(8,128)(2,1)S(1)}, bf16[4,2,96,768]{3,2,1,0:T(8,128)(2,1)S(1)}) custom-call(s32[4]{0:T(128)S(1)} %pad_add_fusion.at_ref, bf16[4,512,768]{2,1,0:T(8,128)(2,1)} %x_ref.4, bf16[512,768]{1,0:T(8,128)(2,1)S(1)} %copy-done.12, f32[512,768]{1,0:T(8,128)} %copy-done.17, ...), custom_call_target="tpu_custom_call" | custom-call | flops 1000 | bytes 1000 | tf_op jit(solution)/shard_map/attend_back/pallas_call | solution.py:479
  162.6 5.1 %collective-permute-done.30.refs_4_ = bf16[512,768]{1,0:T(8,128)(2,1)} collective-permute-done((bf16[512,768]{1,0:T(8,128)(2,1)}, bf16[512,768]{1,0:T(8,128)(2,1)}, u32[]{:S(2)}, u32[]{:S(2)}) %collective-permute-start.30) | collective-permute-done | bytes 786464 | tf_op jit(solution)/shard_map/ppermute | solution.py:713
  167.7 1.3 collective-permute-start.34
  169.0 1.6 fusion
  172.3 1.5 fusion.37
  173.8 3.6 %collective-permute-start.37 = (bf16[2,96,768]{2,1,0:T(8,128)(2,1)S(1)}, bf16[2,96,768]{2,1,0:T(8,128)(2,1)S(1)}, u32[]{:S(2)}, u32[]{:S(2)}) collective-permute-start(bf16[2,96,768]{2,1,0:T(8,128)(2,1)S(1)} %pad_maximum_fusion.18), channel_id=1, source_target_pairs={{0,1},{1,0},{2,3},{3,2},{4,5},{5,4},{6,7},{7,6},{8,9},{9,8},{10,11... | collective-permute-start | bytes 884744 | tf_op jit(solution)/shard_map/ppermute | solution.py:571
  177.4 15.6 %attend_back.3 = (f32[2,2,192]{2,1,0:T(2,128)S(1)}, bf16[512,768]{1,0:T(8,128)(2,1)S(1)}, bf16[4,2,96,768]{3,2,1,0:T(8,128)(2,1)S(1)}, bf16[4,2,96,768]{3,2,1,0:T(8,128)(2,1)}) custom-call(s32[4]{0:T(128)S(1)} %pad_add_fusion.at_ref, bf16[4,512,768]{2,1,0:T(8,128)(2,1)} %x_ref.4, bf16[512,768]{1,0:T(8,128)(2,1)S(1)} %copy-done.12, ...), custom_call_target="tpu_custom_call" | custom-call | flops 1000 | bytes 1000 | tf_op jit(solution)/shard_map/attend_back/pallas_call | solution.py:479
  194.0 2.0 collective-permute-done.37
  197.0 1.7 collective-permute-start.39
  198.7 2.8 fusion.28
  201.6 1.2 fusion.9
  205.9 3.0 %collective-permute-start.43 = (f32[18,384]{1,0:T(8,128)S(1)}, f32[18,384]{1,0:T(8,128)S(1)}, u32[]{:S(2)}, u32[]{:S(2)}) collective-permute-start(f32[18,384]{1,0:T(8,128)S(1)} %concatenate.72), channel_id=1, source_target_pairs={{0,1},{1,0},{2,3},{3,2},{4,5},{5,4},{6,7},{7,6},{8,9},{9,8},{10,11... | collective-permute-start | bytes 82952 | tf_op jit(solution)/shard_map/ppermute | solution.py:571
  208.9 1.3 fusion.14
  210.2 1.7 pad_maximum_fusion.19
  212.0 5.8 %collective-permute-done.43 = f32[18,384]{1,0:T(8,128)S(1)} collective-permute-done((f32[18,384]{1,0:T(8,128)S(1)}, f32[18,384]{1,0:T(8,128)S(1)}, u32[]{:S(2)}, u32[]{:S(2)}) %collective-permute-start.43) | collective-permute-done | bytes 27680 | tf_op jit(solution)/shard_map/ppermute | solution.py:571
  217.8 1.2 fusion.13
  219.0 1.2 fusion.22
  220.8 1.1 collective-permute-start.46
  221.9 2.5 collective-permute-start.44
  225.1 1.3 collective-permute-start.48
  228.6 3.8 %collective-permute-done.44 = bf16[2,96,768]{2,1,0:T(8,128)(2,1)S(1)} collective-permute-done((bf16[2,96,768]{2,1,0:T(8,128)(2,1)S(1)}, bf16[2,96,768]{2,1,0:T(8,128)(2,1)S(1)}, u32[]{:S(2)}, u32[]{:S(2)}) %collective-permute-start.44) | collective-permute-done | bytes 294944 | tf_op jit(solution)/shard_map/ppermute | solution.py:571
  232.3 1.7 convert_add_fusion.9
  235.6 13.7 %collective-permute-done.48.refs_4_ = bf16[512,768]{1,0:T(8,128)(2,1)} collective-permute-done((bf16[512,768]{1,0:T(8,128)(2,1)}, bf16[512,768]{1,0:T(8,128)(2,1)}, u32[]{:S(2)}, u32[]{:S(2)}) %collective-permute-start.48) | collective-permute-done | bytes 786464 | tf_op jit(solution)/shard_map/ppermute | solution.py:713
  249.3 2.9 %collective-permute-start.53 = (f32[15,384]{1,0:T(8,128)S(1)}, f32[15,384]{1,0:T(8,128)S(1)}, u32[]{:S(2)}, u32[]{:S(2)}) collective-permute-start(f32[15,384]{1,0:T(8,128)S(1)} %pad_maximum_fusion.27), channel_id=1, source_target_pairs={{0,2},{1,3},{2,0},{3,1},{4,6},{5,7},{6,4},{7,5},{8,10},{9,11},{10,... | collective-permute-start | bytes 69128 | tf_op jit(solution)/shard_map/ppermute | solution.py:571
  252.2 1.3 collective-permute-start.50
  253.5 4.9 %place.3.whole_ref = f32[4,512,768]{2,1,0:T(8,128)} custom-call(s32[4]{0:T(128)} %copy-done.31, bf16[512,768]{1,0:T(8,128)(2,1)} %copy-done.8, bf16[512,768]{1,0:T(8,128)(2,1)} %collective-permute-done.38.refs_1_, bf16[512,768]{1,0:T(8,128)(2,1)} %collective-permute-done.39.refs_2_, bf16[512,768]{1,0:T(8,128)(2,1)} %copy-done.35, ...), custom_call_target="tpu_custom_call" | custom-call | flops 1000 | bytes 1000 | tf_op jit(solution)/shard_map/place/pallas_call | solution.py:562
  258.4 3.2 %collective-permute-start.52 = (bf16[96,768]{1,0:T(8,128)(2,1)S(1)}, bf16[96,768]{1,0:T(8,128)(2,1)S(1)}, u32[]{:S(2)}, u32[]{:S(2)}) collective-permute-start(bf16[96,768]{1,0:T(8,128)(2,1)S(1)} %fusion.10), channel_id=1, source_target_pairs={{0,2},{1,3},{2,0},{3,1},{4,6},{5,7},{6,4},{7,5},{8,10},{9,11},{10,... | collective-permute-start | bytes 442376 | tf_op jit(solution)/shard_map/ppermute | solution.py:571
  261.7 2.9 %collective-permute-done.49 = bf16[2,96,768]{2,1,0:T(8,128)(2,1)S(1)} collective-permute-done((bf16[2,96,768]{2,1,0:T(8,128)(2,1)}, bf16[2,96,768]{2,1,0:T(8,128)(2,1)S(1)}, u32[]{:S(2)}, u32[]{:S(2)}) %collective-permute-start.49) | collective-permute-done | bytes 294944 | tf_op jit(solution)/shard_map/ppermute | solution.py:571
  265.3 1.7 fusion.41
  267.0 1.3 collective-permute-start.57
  268.4 4.0 %place.2 = bf16[4,512,768]{2,1,0:T(8,128)(2,1)} custom-call(s32[4]{0:T(128)} %copy-done.31, bf16[512,768]{1,0:T(8,128)(2,1)} %copy-done.27, bf16[512,768]{1,0:T(8,128)(2,1)} %collective-permute-done.24.refs_1_, bf16[512,768]{1,0:T(8,128)(2,1)} %collective-permute-done.25.refs_2_, bf16[512,768]{1,0:T(8,128)(2,1)} %collective-permute-done.29.refs_3_, ...), custom_call_target="tpu_custom_call" | custom-call | flops 1000 | bytes 1000 | tf_op jit(solution)/shard_map/place/pallas_call | solution.py:562
  273.6 1.5 collective-permute-start.56
  277.5 1.4 collective-permute-done.54
  286.5 3.0 %place_end.1 = f32[4,512,768]{2,1,0:T(8,128)} custom-call(s32[4]{0:T(128)} %copy-done.31, bf16[512,768]{1,0:T(8,128)(2,1)} %copy-done.8, bf16[512,768]{1,0:T(8,128)(2,1)} %copy-done.40, f32[4,512,768]{2,1,0:T(8,128)} %place.3.whole_ref), custom_call_target="tpu_custom_call", output_to_operand_aliasing={{}: (3, {})} | custom-call | flops 1000 | bytes 1000 | tf_op jit(solution)/shard_map/place_end/pallas_call | solution.py:547
  (299 shorter events, 52.0 us)
Async XLA Ops:
  2.6 22.9 %collective-permute-start = (bf16[216,768]{1,0:T(8,128)(2,1)S(1)}, bf16[216,768]{1,0:T(8,128)(2,1)S(1)}, u32[]{:S(2)}, u32[]{:S(2)}) collective-permute-start(bf16[216,768]{1,0:T(8,128)(2,1)S(1)} %pad_maximum_fusion.16), channel_id=1, source_target_pairs={{0,1},{1,0},{2,3},{3,2},{4,5},{5,4},{6,7},{7,6},{8,9},{9,8},{10,11... | collective-permute-start | bytes 995336 | tf_op jit(solution)/shard_map/ppermute | solution.py:571
  5.6 25.8 %collective-permute-start.1 = (bf16[216,768]{1,0:T(8,128)(2,1)S(1)}, bf16[216,768]{1,0:T(8,128)(2,1)S(1)}, u32[]{:S(2)}, u32[]{:S(2)}) collective-permute-start(bf16[216,768]{1,0:T(8,128)(2,1)S(1)} %pad_maximum_fusion.16), channel_id=1, source_target_pairs={{0,2},{1,3},{2,0},{3,1},{4,6},{5,7},{6,4},{7,5},{8,10},{9,11},{10,... | collective-permute-start | bytes 995336 | tf_op jit(solution)/shard_map/ppermute | solution.py:571
  8.2 23.3 %collective-permute-start.2 = (bf16[216,768]{1,0:T(8,128)(2,1)S(1)}, bf16[216,768]{1,0:T(8,128)(2,1)S(1)}, u32[]{:S(2)}, u32[]{:S(2)}) collective-permute-start(bf16[216,768]{1,0:T(8,128)(2,1)S(1)} %pad_maximum_fusion.16), channel_id=1, source_target_pairs={{0,3},{1,2},{2,1},{3,0},{4,7},{5,6},{6,5},{7,4},{8,11},{9,10},{10,... | collective-permute-start | bytes 995336 | tf_op jit(solution)/shard_map/ppermute | solution.py:571
  10.0 167.4 %copy-start.31 = (s32[4]{0:T(128)}, s32[4]{0:T(128)S(1)}, u32[]{:S(2)}) copy-start(s32[4]{0:T(128)S(1)} %pad_add_fusion.at_ref) | copy-start | bytes 52
  25.4 54.6 %copy-start.25 = (bf16[272,384]{1,0:T(8,128)(2,1)}, bf16[272,384]{1,0:T(8,128)(2,1)S(1)}, u32[]{:S(2)}) copy-start(bf16[272,384]{1,0:T(8,128)(2,1)S(1)} %get-tuple-element.205.refs_0_) | copy-start | bytes 626692
  31.7 12.8 %collective-permute-start.7 = (bf16[3,120,384]{2,1,0:T(8,128)(2,1)S(1)}, bf16[3,120,384]{2,1,0:T(8,128)(2,1)S(1)}, u32[]{:S(2)}, u32[]{:S(2)}) collective-permute-start(bf16[3,120,384]{2,1,0:T(8,128)(2,1)S(1)} %pad_maximum_fusion.23), channel_id=1, source_target_pairs={{0,16},{16,0},{1,17},{17,1},{2,18},{18,2},{3,19},{19,3},{4,20},{20... | collective-permute-start | bytes 829448 | tf_op jit(solution)/shard_map/ppermute | solution.py:571
  33.3 11.1 %collective-permute-start.6 = (bf16[3,120,384]{2,1,0:T(8,128)(2,1)S(1)}, bf16[3,120,384]{2,1,0:T(8,128)(2,1)S(1)}, u32[]{:S(2)}, u32[]{:S(2)}) collective-permute-start(bf16[3,120,384]{2,1,0:T(8,128)(2,1)S(1)} %pad_maximum_fusion.22), channel_id=1, source_target_pairs={{0,8},{4,12},{8,0},{12,4},{1,9},{5,13},{9,1},{13,5},{2,10},{6,14},... | collective-permute-start | bytes 829448 | tf_op jit(solution)/shard_map/ppermute | solution.py:571
  34.9 12.5 %collective-permute-start.3 = (bf16[272,384]{1,0:T(8,128)(2,1)S(1)}, bf16[272,384]{1,0:T(8,128)(2,1)S(1)}, u32[]{:S(2)}, u32[]{:S(2)}) collective-permute-start(bf16[272,384]{1,0:T(8,128)(2,1)S(1)} %get-tuple-element.173), channel_id=1, source_target_pairs={{0,1},{1,0},{2,3},{3,2},{4,5},{5,4},{6,7},{7,6},{8,9},{9,8},{10,11... | collective-permute-start | bytes 626696 | tf_op jit(solution)/shard_map/ppermute | solution.py:571
  41.2 17.0 %collective-permute-start.4 = (bf16[272,384]{1,0:T(8,128)(2,1)S(1)}, bf16[272,384]{1,0:T(8,128)(2,1)S(1)}, u32[]{:S(2)}, u32[]{:S(2)}) collective-permute-start(bf16[272,384]{1,0:T(8,128)(2,1)S(1)} %get-tuple-element.174), channel_id=1, source_target_pairs={{0,2},{1,3},{2,0},{3,1},{4,6},{5,7},{6,4},{7,5},{8,10},{9,11},{10,... | collective-permute-start | bytes 626696 | tf_op jit(solution)/shard_map/ppermute | solution.py:571
  42.3 16.0 %collective-permute-start.5 = (bf16[272,384]{1,0:T(8,128)(2,1)S(1)}, bf16[272,384]{1,0:T(8,128)(2,1)S(1)}, u32[]{:S(2)}, u32[]{:S(2)}) collective-permute-start(bf16[272,384]{1,0:T(8,128)(2,1)S(1)} %get-tuple-element.175), channel_id=1, source_target_pairs={{0,3},{1,2},{2,1},{3,0},{4,7},{5,6},{6,5},{7,4},{8,11},{9,10},{10,... | collective-permute-start | bytes 626696 | tf_op jit(solution)/shard_map/ppermute | solution.py:571
  44.6 14.9 %collective-permute-start.9 = (bf16[2,3,120,384]{3,2,1,0:T(8,128)(2,1)S(1)}, bf16[2,3,120,384]{3,2,1,0:T(8,128)(2,1)}, u32[]{:S(2)}, u32[]{:S(2)}) collective-permute-start(bf16[2,3,120,384]{3,2,1,0:T(8,128)(2,1)S(1)} %pad_maximum_fusion.11), channel_id=1, source_target_pairs={{0,8},{4,12},{8,0},{12,4},{1,9},{5,13},{9,1},{13,5},{2,10},{6,14},... | collective-permute-start | bytes 1658888 | tf_op jit(solution)/shard_map/ppermute | solution.py:571
  45.3 14.2 %collective-permute-start.8 = (bf16[2,3,120,384]{3,2,1,0:T(8,128)(2,1)S(1)}, bf16[2,3,120,384]{3,2,1,0:T(8,128)(2,1)}, u32[]{:S(2)}, u32[]{:S(2)}) collective-permute-start(bf16[2,3,120,384]{3,2,1,0:T(8,128)(2,1)S(1)} %pad_maximum_fusion.10), channel_id=1, source_target_pairs={{0,16},{16,0},{1,17},{17,1},{2,18},{18,2},{3,19},{19,3},{4,20},{20... | collective-permute-start | bytes 1658888 | tf_op jit(solution)/shard_map/ppermute | solution.py:571
  47.4 32.6 %copy-start.23 = (bf16[272,384]{1,0:T(8,128)(2,1)}, bf16[272,384]{1,0:T(8,128)(2,1)S(1)}, u32[]{:S(2)}) copy-start(bf16[272,384]{1,0:T(8,128)(2,1)S(1)} %collective-permute-done.3.refs_1_) | copy-start | bytes 626692
  58.3 21.8 %copy-start.21 = (bf16[272,384]{1,0:T(8,128)(2,1)}, bf16[272,384]{1,0:T(8,128)(2,1)S(1)}, u32[]{:S(2)}) copy-start(bf16[272,384]{1,0:T(8,128)(2,1)S(1)} %collective-permute-done.5.refs_3_.refs_1_) | copy-start | bytes 626692
  58.3 6.0 %collective-permute-start.14 = (bf16[3,96,384]{2,1,0:T(8,128)(2,1)S(1)}, bf16[3,96,384]{2,1,0:T(8,128)(2,1)}, u32[]{:S(2)}, u32[]{:S(2)}) collective-permute-start(bf16[3,96,384]{2,1,0:T(8,128)(2,1)S(1)} %pad_maximum_fusion.25), channel_id=1, source_target_pairs={{0,16},{16,0},{1,17},{17,1},{2,18},{18,2},{3,19},{19,3},{4,20},{20... | collective-permute-start | bytes 663560 | tf_op jit(solution)/shard_map/ppermute | solution.py:571
  58.8 6.2 %collective-permute-start.13 = (bf16[3,96,384]{2,1,0:T(8,128)(2,1)}, bf16[3,96,384]{2,1,0:T(8,128)(2,1)}, u32[]{:S(2)}, u32[]{:S(2)}) collective-permute-start(bf16[3,96,384]{2,1,0:T(8,128)(2,1)} %pad_maximum_fusion.24), channel_id=1, source_target_pairs={{0,8},{4,12},{8,0},{12,4},{1,9},{5,13},{9,1},{13,5},{2,10},{6,14},... | collective-permute-start | bytes 663560 | tf_op jit(solution)/shard_map/ppermute | solution.py:571
  65.0 7.5 %collective-permute-start.16 = (bf16[2,2,3,96,768]{4,3,2,1,0:T(8,128)(2,1)S(1)}, bf16[2,2,3,96,768]{4,3,2,1,0:T(8,128)(2,1)}, u32[]{:S(2)}, u32[]{:S(2)}) collective-permute-start(bf16[2,2,3,96,768]{4,3,2,1,0:T(8,128)(2,1)S(1)} %maximum_maximum_fusion), channel_id=1, source_target_pairs={{0,4},{4,0},{8,12},{12,8},{1,5},{5,1},{9,13},{13,9},{2,6},{6,2},{1... | collective-permute-start | bytes 5308424 | tf_op jit(solution)/shard_map/ppermute | solution.py:571
  65.0 10.8 %collective-permute-start.10 = (bf16[144,384]{1,0:T(8,128)(2,1)S(1)}, bf16[144,384]{1,0:T(8,128)(2,1)S(1)}, u32[]{:S(2)}, u32[]{:S(2)}) collective-permute-start(bf16[144,384]{1,0:T(8,128)(2,1)S(1)} %dynamic_slice.24), channel_id=1, source_target_pairs={{0,1},{1,0},{2,3},{3,2},{4,5},{5,4},{6,7},{7,6},{8,9},{9,8},{10,11... | collective-permute-start | bytes 331784 | tf_op jit(solution)/shard_map/ppermute | solution.py:571
  67.8 11.5 %collective-permute-start.11 = (bf16[144,384]{1,0:T(8,128)(2,1)S(1)}, bf16[144,384]{1,0:T(8,128)(2,1)S(1)}, u32[]{:S(2)}, u32[]{:S(2)}) collective-permute-start(bf16[144,384]{1,0:T(8,128)(2,1)S(1)} %dynamic_slice.24), channel_id=1, source_target_pairs={{0,2},{1,3},{2,0},{3,1},{4,6},{5,7},{6,4},{7,5},{8,10},{9,11},{10,... | collective-permute-start | bytes 331784 | tf_op jit(solution)/shard_map/ppermute | solution.py:571
  68.8 10.6 %collective-permute-start.12 = (bf16[144,384]{1,0:T(8,128)(2,1)S(1)}, bf16[144,384]{1,0:T(8,128)(2,1)S(1)}, u32[]{:S(2)}, u32[]{:S(2)}) collective-permute-start(bf16[144,384]{1,0:T(8,128)(2,1)S(1)} %dynamic_slice.24), channel_id=1, source_target_pairs={{0,3},{1,2},{2,1},{3,0},{4,7},{5,6},{6,5},{7,4},{8,11},{9,10},{10,... | collective-permute-start | bytes 331784 | tf_op jit(solution)/shard_map/ppermute | solution.py:571
  70.3 2.2 collective-permute-start.15
  72.5 19.8 %collective-permute-start.18 = (bf16[2,3,96,384]{3,2,1,0:T(8,128)(2,1)S(1)}, bf16[2,3,96,384]{3,2,1,0:T(8,128)(2,1)S(1)}, u32[]{:S(2)}, u32[]{:S(2)}) collective-permute-start(bf16[2,3,96,384]{3,2,1,0:T(8,128)(2,1)S(1)} %pad_maximum_fusion.13), channel_id=1, source_target_pairs={{0,8},{4,12},{8,0},{12,4},{1,9},{5,13},{9,1},{13,5},{2,10},{6,14},... | collective-permute-start | bytes 1327112 | tf_op jit(solution)/shard_map/ppermute | solution.py:571
  73.1 19.2 %collective-permute-start.17 = (bf16[2,3,96,384]{3,2,1,0:T(8,128)(2,1)S(1)}, bf16[2,3,96,384]{3,2,1,0:T(8,128)(2,1)S(1)}, u32[]{:S(2)}, u32[]{:S(2)}) collective-permute-start(bf16[2,3,96,384]{3,2,1,0:T(8,128)(2,1)S(1)} %pad_maximum_fusion.12), channel_id=1, source_target_pairs={{0,16},{16,0},{1,17},{17,1},{2,18},{18,2},{3,19},{19,3},{4,20},{20... | collective-permute-start | bytes 1327112 | tf_op jit(solution)/shard_map/ppermute | solution.py:571
  79.4 12.8 %collective-permute-start.19 = (bf16[3,144,384]{2,1,0:T(8,128)(2,1)S(1)}, bf16[3,144,384]{2,1,0:T(8,128)(2,1)S(1)}, u32[]{:S(2)}, u32[]{:S(2)}) collective-permute-start(bf16[3,144,384]{2,1,0:T(8,128)(2,1)S(1)} %pad_maximum_fusion.17), channel_id=1, source_target_pairs={{0,8},{4,12},{8,0},{12,4},{1,9},{5,13},{9,1},{13,5},{2,10},{6,14},... | collective-permute-start | bytes 995336 | tf_op jit(solution)/shard_map/ppermute | solution.py:571
  93.0 3.8 %collective-permute-start.20 = (bf16[2,2,3,96,768]{4,3,2,0,1:T(8,128)(2,1)S(1)}, bf16[2,2,3,96,768]{4,3,2,0,1:T(8,128)(2,1)S(1)}, u32[]{:S(2)}, u32[]{:S(2)}) collective-permute-start(bf16[2,2,3,96,768]{4,3,2,0,1:T(8,128)(2,1)S(1)} %maximum_maximum_fusion.1), channel_id=1, source_target_pairs={{0,4},{4,0},{8,12},{12,8},{1,5},{5,1},{9,13},{13,9},{2,6},{6,2},{1... | collective-permute-start | bytes 5308424 | tf_op jit(solution)/shard_map/ppermute | solution.py:571
  93.3 17.4 %collective-permute-start.21 = (bf16[2,3,144,384]{3,2,1,0:T(8,128)(2,1)S(1)}, bf16[2,3,144,384]{3,2,1,0:T(8,128)(2,1)S(1)}, u32[]{:S(2)}, u32[]{:S(2)}) collective-permute-start(bf16[2,3,144,384]{3,2,1,0:T(8,128)(2,1)S(1)} %pad_maximum_fusion.4), channel_id=1, source_target_pairs={{0,16},{16,0},{1,17},{17,1},{2,18},{18,2},{3,19},{19,3},{4,20},{20... | collective-permute-start | bytes 1990664 | tf_op jit(solution)/shard_map/ppermute | solution.py:571
  108.4 25.2 %copy-start.16 = (bf16[4,4,96,768]{3,2,1,0:T(8,128)(2,1)}, bf16[4,4,96,768]{3,2,1,0:T(8,128)(2,1)S(1)}, u32[]{:S(2)}) copy-start(bf16[4,4,96,768]{3,2,1,0:T(8,128)(2,1)S(1)} %get-tuple-element.235) | copy-start | bytes 7077892
  110.6 4.7 %collective-permute-start.22 = (bf16[4,4,96,768]{3,2,1,0:T(8,128)(2,1)S(1)}, bf16[4,4,96,768]{3,2,1,0:T(8,128)(2,1)S(1)}, u32[]{:S(2)}, u32[]{:S(2)}) collective-permute-start(bf16[4,4,96,768]{3,2,1,0:T(8,128)(2,1)S(1)} %get-tuple-element.233), channel_id=1, source_target_pairs={{0,4},{4,0},{8,12},{12,8},{1,5},{5,1},{9,13},{13,9},{2,6},{6,2},{1... | collective-permute-start | bytes 7077896 | tf_op jit(solution)/shard_map/ppermute | solution.py:571
  111.0 22.4 %collective-permute-start.23 = (bf16[2,2,3,144,384]{4,3,2,1,0:T(8,128)(2,1)S(1)}, bf16[2,2,3,144,384]{4,3,2,1,0:T(8,128)(2,1)S(1)}, u32[]{:S(2)}, u32[]{:S(2)}) collective-permute-start(bf16[2,2,3,144,384]{4,3,2,1,0:T(8,128)(2,1)S(1)} %pad_maximum_fusion), channel_id=1, source_target_pairs={{0,4},{4,0},{8,12},{12,8},{1,5},{5,1},{9,13},{13,9},{2,6},{6,2},{1... | collective-permute-start | bytes 3981320 | tf_op jit(solution)/shard_map/ppermute | solution.py:571
  111.5 21.8 %collective-permute-start.24 = (bf16[512,768]{1,0:T(8,128)(2,1)S(1)}, bf16[512,768]{1,0:T(8,128)(2,1)}, u32[]{:S(2)}, u32[]{:S(2)}) collective-permute-start(bf16[512,768]{1,0:T(8,128)(2,1)S(1)} %get-tuple-element.230.refs_0_), channel_id=1, source_target_pairs={{0,1},{1,0},{2,3},{3,2},{4,5},{5,4},{6,7},{7,6},{8,9},{9,8},{10,11... | collective-permute-start | bytes 2359304 | tf_op jit(solution)/shard_map/ppermute | solution.py:571
  113.8 19.6 %collective-permute-start.25 = (bf16[512,768]{1,0:T(8,128)(2,1)S(1)}, bf16[512,768]{1,0:T(8,128)(2,1)}, u32[]{:S(2)}, u32[]{:S(2)}) collective-permute-start(bf16[512,768]{1,0:T(8,128)(2,1)S(1)} %get-tuple-element.230.refs_0_), channel_id=1, source_target_pairs={{1,2},{2,1},{5,6},{6,5},{9,10},{10,9},{13,14},{14,13},{17,18},{18,... | collective-permute-start | bytes 2359304 | tf_op jit(solution)/shard_map/ppermute | solution.py:712
  115.6 17.8 %collective-permute-start.26 = (bf16[4,96,768]{2,1,0:T(8,128)(2,1)S(1)}, bf16[4,96,768]{2,1,0:T(8,128)(2,1)S(1)}, u32[]{:S(2)}, u32[]{:S(2)}) collective-permute-start(bf16[4,96,768]{2,1,0:T(8,128)(2,1)S(1)} %bitcast.311), channel_id=1, source_target_pairs={{0,8},{4,12},{8,0},{12,4},{1,9},{5,13},{9,1},{13,5},{2,10},{6,14},... | collective-permute-start | bytes 1769480 | tf_op jit(solution)/shard_map/ppermute | solution.py:571
  117.2 16.3 %collective-permute-start.27 = (bf16[4,96,768]{2,1,0:T(8,128)(2,1)S(1)}, bf16[4,96,768]{2,1,0:T(8,128)(2,1)S(1)}, u32[]{:S(2)}, u32[]{:S(2)}) collective-permute-start(bf16[4,96,768]{2,1,0:T(8,128)(2,1)S(1)} %bitcast.310), channel_id=1, source_target_pairs={{0,16},{16,0},{1,17},{17,1},{2,18},{18,2},{3,19},{19,3},{4,20},{20... | collective-permute-start | bytes 1769480 | tf_op jit(solution)/shard_map/ppermute | solution.py:571
  133.5 4.8 %collective-permute-start.28 = (bf16[4,4,96,768]{3,2,1,0:T(8,128)(2,1)}, bf16[4,4,96,768]{3,2,1,0:T(8,128)(2,1)S(1)}, u32[]{:S(2)}, u32[]{:S(2)}) collective-permute-start(bf16[4,4,96,768]{3,2,1,0:T(8,128)(2,1)} %get-tuple-element.253), channel_id=1, source_target_pairs={{0,4},{4,0},{8,12},{12,8},{1,5},{5,1},{9,13},{13,9},{2,6},{6,2},{1... | collective-permute-start | bytes 7077896 | tf_op jit(solution)/shard_map/ppermute | solution.py:571
  139.7 27.9 %collective-permute-start.32 = (bf16[6,96,768]{2,1,0:T(8,128)(2,1)}, bf16[6,96,768]{2,1,0:T(8,128)(2,1)}, u32[]{:S(2)}, u32[]{:S(2)}) collective-permute-start(bf16[6,96,768]{2,1,0:T(8,128)(2,1)} %pad_maximum_fusion.3), channel_id=1, source_target_pairs={{0,16},{16,0},{1,17},{17,1},{2,18},{18,2},{3,19},{19,3},{4,20},{20... | collective-permute-start | bytes 2654216 | tf_op jit(solution)/shard_map/ppermute | solution.py:571
  141.2 26.4 %collective-permute-start.31 = (bf16[6,96,768]{2,1,0:T(8,128)(2,1)}, bf16[6,96,768]{2,1,0:T(8,128)(2,1)}, u32[]{:S(2)}, u32[]{:S(2)}) collective-permute-start(bf16[6,96,768]{2,1,0:T(8,128)(2,1)} %pad_maximum_fusion.2), channel_id=1, source_target_pairs={{0,8},{4,12},{8,0},{12,4},{1,9},{5,13},{9,1},{13,5},{2,10},{6,14},... | collective-permute-start | bytes 2654216 | tf_op jit(solution)/shard_map/ppermute | solution.py:571
  142.0 20.6 %collective-permute-start.29 = (bf16[512,768]{1,0:T(8,128)(2,1)}, bf16[512,768]{1,0:T(8,128)(2,1)}, u32[]{:S(2)}, u32[]{:S(2)}) collective-permute-start(bf16[512,768]{1,0:T(8,128)(2,1)} %collective-permute-done.24.refs_1_), channel_id=1, source_target_pairs={{1,2},{2,1},{5,6},{6,5},{9,10},{10,9},{13,14},{14,13},{17,18},{18,... | collective-permute-start | bytes 2359304 | tf_op jit(solution)/shard_map/ppermute | solution.py:712
  143.5 24.1 %collective-permute-start.30 = (bf16[512,768]{1,0:T(8,128)(2,1)}, bf16[512,768]{1,0:T(8,128)(2,1)}, u32[]{:S(2)}, u32[]{:S(2)}) collective-permute-start(bf16[512,768]{1,0:T(8,128)(2,1)} %collective-permute-done.25.refs_2_), channel_id=1, source_target_pairs={{1,0},{2,3},{5,4},{6,7},{9,8},{10,11},{13,12},{14,15},{17,16},{18,... | collective-permute-start | bytes 2359304 | tf_op jit(solution)/shard_map/ppermute | solution.py:713
  167.7 2.9 %collective-permute-start.33 = (bf16[4,2,96,768]{3,2,1,0:T(8,128)(2,1)S(1)}, bf16[4,2,96,768]{3,2,1,0:T(8,128)(2,1)S(1)}, u32[]{:S(2)}, u32[]{:S(2)}) collective-permute-start(bf16[4,2,96,768]{3,2,1,0:T(8,128)(2,1)S(1)} %get-tuple-element.270), channel_id=1, source_target_pairs={{0,4},{4,0},{8,12},{12,8},{1,5},{5,1},{9,13},{13,9},{2,6},{6,2},{1... | collective-permute-start | bytes 3538952 | tf_op jit(solution)/shard_map/ppermute | solution.py:571
  167.7 28.4 %collective-permute-start.34 = (bf16[512,768]{1,0:T(8,128)(2,1)}, bf16[512,768]{1,0:T(8,128)(2,1)}, u32[]{:S(2)}, u32[]{:S(2)}) collective-permute-start(bf16[512,768]{1,0:T(8,128)(2,1)} %collective-permute-done.29.refs_3_), channel_id=1, source_target_pairs={{1,0},{2,3},{5,4},{6,7},{9,8},{10,11},{13,12},{14,15},{17,16},{18,... | collective-permute-start | bytes 2359304 | tf_op jit(solution)/shard_map/ppermute | solution.py:713
  170.8 25.2 %collective-permute-start.36 = (bf16[4,96,768]{2,1,0:T(8,128)(2,1)S(1)}, bf16[4,96,768]{2,1,0:T(8,128)(2,1)}, u32[]{:S(2)}, u32[]{:S(2)}) collective-permute-start(bf16[4,96,768]{2,1,0:T(8,128)(2,1)S(1)} %pad_maximum_fusion.6), channel_id=1, source_target_pairs={{0,16},{16,0},{1,17},{17,1},{2,18},{18,2},{3,19},{19,3},{4,20},{20... | collective-permute-start | bytes 1769480 | tf_op jit(solution)/shard_map/ppermute | solution.py:571
  171.6 24.4 %collective-permute-start.35 = (bf16[4,96,768]{2,1,0:T(8,128)(2,1)S(1)}, bf16[4,96,768]{2,1,0:T(8,128)(2,1)}, u32[]{:S(2)}, u32[]{:S(2)}) collective-permute-start(bf16[4,96,768]{2,1,0:T(8,128)(2,1)S(1)} %pad_maximum_fusion.5), channel_id=1, source_target_pairs={{0,8},{4,12},{8,0},{12,4},{1,9},{5,13},{9,1},{13,5},{2,10},{6,14},... | collective-permute-start | bytes 1769480 | tf_op jit(solution)/shard_map/ppermute | solution.py:571
  173.8 22.2 %collective-permute-start.37 = (bf16[2,96,768]{2,1,0:T(8,128)(2,1)S(1)}, bf16[2,96,768]{2,1,0:T(8,128)(2,1)S(1)}, u32[]{:S(2)}, u32[]{:S(2)}) collective-permute-start(bf16[2,96,768]{2,1,0:T(8,128)(2,1)S(1)} %pad_maximum_fusion.18), channel_id=1, source_target_pairs={{0,1},{1,0},{2,3},{3,2},{4,5},{5,4},{6,7},{7,6},{8,9},{9,8},{10,11... | collective-permute-start | bytes 884744 | tf_op jit(solution)/shard_map/ppermute | solution.py:571
  196.7 4.8 %collective-permute-start.40 = (bf16[4,2,96,768]{3,2,1,0:T(8,128)(2,1)}, bf16[4,2,96,768]{3,2,1,0:T(8,128)(2,1)}, u32[]{:S(2)}, u32[]{:S(2)}) collective-permute-start(bf16[4,2,96,768]{3,2,1,0:T(8,128)(2,1)} %get-tuple-element.287), channel_id=1, source_target_pairs={{0,4},{4,0},{8,12},{12,8},{1,5},{5,1},{9,13},{13,9},{2,6},{6,2},{1... | collective-permute-start | bytes 3538952 | tf_op jit(solution)/shard_map/ppermute | solution.py:571
  197.0 20.7 %collective-permute-start.38 = (bf16[512,768]{1,0:T(8,128)(2,1)S(1)}, bf16[512,768]{1,0:T(8,128)(2,1)}, u32[]{:S(2)}, u32[]{:S(2)}) collective-permute-start(bf16[512,768]{1,0:T(8,128)(2,1)S(1)} %get-tuple-element.319.refs_0_.own_ref), channel_id=1, source_target_pairs={{0,1},{1,0},{2,3},{3,2},{4,5},{5,4},{6,7},{7,6},{8,9},{9,8},{10,11... | collective-permute-start | bytes 2359304 | tf_op jit(solution)/shard_map/ppermute | solution.py:571
  197.0 20.7 %collective-permute-start.39 = (bf16[512,768]{1,0:T(8,128)(2,1)S(1)}, bf16[512,768]{1,0:T(8,128)(2,1)}, u32[]{:S(2)}, u32[]{:S(2)}) collective-permute-start(bf16[512,768]{1,0:T(8,128)(2,1)S(1)} %get-tuple-element.319.refs_0_.own_ref), channel_id=1, source_target_pairs={{1,2},{2,1},{5,6},{6,5},{9,10},{10,9},{13,14},{14,13},{17,18},{18,... | collective-permute-start | bytes 2359304 | tf_op jit(solution)/shard_map/ppermute | solution.py:712
  203.6 14.2 %collective-permute-start.42 = (bf16[3,96,768]{2,1,0:T(8,128)(2,1)}, bf16[3,96,768]{2,1,0:T(8,128)(2,1)}, u32[]{:S(2)}, u32[]{:S(2)}) collective-permute-start(bf16[3,96,768]{2,1,0:T(8,128)(2,1)} %pad_maximum_fusion.15), channel_id=1, source_target_pairs={{0,16},{16,0},{1,17},{17,1},{2,18},{18,2},{3,19},{19,3},{4,20},{20... | collective-permute-start | bytes 1327112 | tf_op jit(solution)/shard_map/ppermute | solution.py:571
  204.9 12.9 %collective-permute-start.41 = (bf16[3,96,768]{2,1,0:T(8,128)(2,1)}, bf16[3,96,768]{2,1,0:T(8,128)(2,1)S(1)}, u32[]{:S(2)}, u32[]{:S(2)}) collective-permute-start(bf16[3,96,768]{2,1,0:T(8,128)(2,1)} %pad_maximum_fusion.14), channel_id=1, source_target_pairs={{0,8},{4,12},{8,0},{12,4},{1,9},{5,13},{9,1},{13,5},{2,10},{6,14},... | collective-permute-start | bytes 1327112 | tf_op jit(solution)/shard_map/ppermute | solution.py:571
  205.9 11.9 %collective-permute-start.43 = (f32[18,384]{1,0:T(8,128)S(1)}, f32[18,384]{1,0:T(8,128)S(1)}, u32[]{:S(2)}, u32[]{:S(2)}) collective-permute-start(f32[18,384]{1,0:T(8,128)S(1)} %concatenate.72), channel_id=1, source_target_pairs={{0,1},{1,0},{2,3},{3,2},{4,5},{5,4},{6,7},{7,6},{8,9},{9,8},{10,11... | collective-permute-start | bytes 82952 | tf_op jit(solution)/shard_map/ppermute | solution.py:571
  220.2 6.3 %collective-permute-start.45 = (bf16[1,96,768]{2,1,0:T(8,128)(2,1)S(1)}, bf16[1,96,768]{2,1,0:T(8,128)(2,1)S(1)}, u32[]{:S(2)}, u32[]{:S(2)}) collective-permute-start(bf16[1,96,768]{2,1,0:T(8,128)(2,1)S(1)} %get-tuple-element.355), channel_id=1, source_target_pairs={{0,8},{4,12},{8,0},{12,4},{1,9},{5,13},{9,1},{13,5},{2,10},{6,14},... | collective-permute-start | bytes 442376 | tf_op jit(solution)/shard_map/ppermute | solution.py:571
  220.8 5.7 %collective-permute-start.46 = (bf16[1,96,768]{2,1,0:T(8,128)(2,1)S(1)}, bf16[1,96,768]{2,1,0:T(8,128)(2,1)S(1)}, u32[]{:S(2)}, u32[]{:S(2)}) collective-permute-start(bf16[1,96,768]{2,1,0:T(8,128)(2,1)S(1)} %get-tuple-element.354), channel_id=1, source_target_pairs={{0,16},{16,0},{1,17},{17,1},{2,18},{18,2},{3,19},{19,3},{4,20},{20... | collective-permute-start | bytes 442376 | tf_op jit(solution)/shard_map/ppermute | solution.py:571
  221.9 10.4 %collective-permute-start.44 = (bf16[2,96,768]{2,1,0:T(8,128)(2,1)S(1)}, bf16[2,96,768]{2,1,0:T(8,128)(2,1)S(1)}, u32[]{:S(2)}, u32[]{:S(2)}) collective-permute-start(bf16[2,96,768]{2,1,0:T(8,128)(2,1)S(1)} %copy-done.46), channel_id=1, source_target_pairs={{0,1},{1,0},{2,3},{3,2},{4,5},{5,4},{6,7},{7,6},{8,9},{9,8},{10,11... | collective-permute-start | bytes 884744 | tf_op jit(solution)/shard_map/ppermute | solution.py:571
  224.4 11.1 %collective-permute-start.47 = (bf16[512,768]{1,0:T(8,128)(2,1)}, bf16[512,768]{1,0:T(8,128)(2,1)S(1)}, u32[]{:S(2)}, u32[]{:S(2)}) collective-permute-start(bf16[512,768]{1,0:T(8,128)(2,1)} %collective-permute-done.38.refs_1_), channel_id=1, source_target_pairs={{1,2},{2,1},{5,6},{6,5},{9,10},{10,9},{13,14},{14,13},{17,18},{18,... | collective-permute-start | bytes 2359304 | tf_op jit(solution)/shard_map/ppermute | solution.py:712
  225.1 24.2 %collective-permute-start.48 = (bf16[512,768]{1,0:T(8,128)(2,1)}, bf16[512,768]{1,0:T(8,128)(2,1)}, u32[]{:S(2)}, u32[]{:S(2)}) collective-permute-start(bf16[512,768]{1,0:T(8,128)(2,1)} %collective-permute-done.39.refs_2_), channel_id=1, source_target_pairs={{1,0},{2,3},{5,4},{6,7},{9,8},{10,11},{13,12},{14,15},{17,16},{18,... | collective-permute-start | bytes 2359304 | tf_op jit(solution)/shard_map/ppermute | solution.py:713
  234.8 23.6 %collective-permute-start.51 = (bf16[2,96,768]{2,1,0:T(8,128)(2,1)}, bf16[2,96,768]{2,1,0:T(8,128)(2,1)S(1)}, u32[]{:S(2)}, u32[]{:S(2)}) collective-permute-start(bf16[2,96,768]{2,1,0:T(8,128)(2,1)} %pad_maximum_fusion.21), channel_id=1, source_target_pairs={{0,1},{1,0},{2,3},{3,2},{4,5},{5,4},{6,7},{7,6},{8,9},{9,8},{10,11... | collective-permute-start | bytes 884744 | tf_op jit(solution)/shard_map/ppermute | solution.py:571
  249.3 15.3 %collective-permute-start.49 = (bf16[2,96,768]{2,1,0:T(8,128)(2,1)}, bf16[2,96,768]{2,1,0:T(8,128)(2,1)S(1)}, u32[]{:S(2)}, u32[]{:S(2)}) collective-permute-start(bf16[2,96,768]{2,1,0:T(8,128)(2,1)} %pad_maximum_fusion.20), channel_id=1, source_target_pairs={{0,2},{1,3},{2,0},{3,1},{4,6},{5,7},{6,4},{7,5},{8,10},{9,11},{10,... | collective-permute-start | bytes 884744 | tf_op jit(solution)/shard_map/ppermute | solution.py:571
  249.3 23.0 %collective-permute-start.53 = (f32[15,384]{1,0:T(8,128)S(1)}, f32[15,384]{1,0:T(8,128)S(1)}, u32[]{:S(2)}, u32[]{:S(2)}) collective-permute-start(f32[15,384]{1,0:T(8,128)S(1)} %pad_maximum_fusion.27), channel_id=1, source_target_pairs={{0,2},{1,3},{2,0},{3,1},{4,6},{5,7},{6,4},{7,5},{8,10},{9,11},{10,... | collective-permute-start | bytes 69128 | tf_op jit(solution)/shard_map/ppermute | solution.py:571
  252.2 33.4 %collective-permute-start.50 = (bf16[512,768]{1,0:T(8,128)(2,1)S(1)}, bf16[512,768]{1,0:T(8,128)(2,1)S(1)}, u32[]{:S(2)}, u32[]{:S(2)}) collective-permute-start(bf16[512,768]{1,0:T(8,128)(2,1)S(1)} %collective-permute-done.47.refs_3_.refs_5_), channel_id=1, source_target_pairs={{1,0},{2,3},{5,4},{6,7},{9,8},{10,11},{13,12},{14,15},{17,16},{18,... | collective-permute-start | bytes 2359304 | tf_op jit(solution)/shard_map/ppermute | solution.py:713
  258.4 14.0 %collective-permute-start.52 = (bf16[96,768]{1,0:T(8,128)(2,1)S(1)}, bf16[96,768]{1,0:T(8,128)(2,1)S(1)}, u32[]{:S(2)}, u32[]{:S(2)}) collective-permute-start(bf16[96,768]{1,0:T(8,128)(2,1)S(1)} %fusion.10), channel_id=1, source_target_pairs={{0,2},{1,3},{2,0},{3,1},{4,6},{5,7},{6,4},{7,5},{8,10},{9,11},{10,... | collective-permute-start | bytes 442376 | tf_op jit(solution)/shard_map/ppermute | solution.py:571
  267.0 8.1 %collective-permute-start.57 = (bf16[2,96,768]{2,1,0:T(8,128)(2,1)}, bf16[2,96,768]{2,1,0:T(8,128)(2,1)S(1)}, u32[]{:S(2)}, u32[]{:S(2)}) collective-permute-start(bf16[2,96,768]{2,1,0:T(8,128)(2,1)} %get-tuple-element.336), channel_id=1, source_target_pairs={{0,16},{16,0},{1,17},{17,1},{2,18},{18,2},{3,19},{19,3},{4,20},{20... | collective-permute-start | bytes 884744 | tf_op jit(solution)/shard_map/ppermute | solution.py:571
  272.4 1.3 collective-permute-start.55
  272.5 6.3 %collective-permute-start.54 = (bf16[96,768]{1,0:T(8,128)(2,1)S(1)}, bf16[96,768]{1,0:T(8,128)(2,1)S(1)}, u32[]{:S(2)}, u32[]{:S(2)}) collective-permute-start(bf16[96,768]{1,0:T(8,128)(2,1)S(1)} %get-tuple-element.338), channel_id=1, source_target_pairs={{0,16},{16,0},{1,17},{17,1},{2,18},{18,2},{3,19},{19,3},{4,20},{20... | collective-permute-start | bytes 442376 | tf_op jit(solution)/shard_map/ppermute | solution.py:571
  273.6 3.8 %collective-permute-start.56 = (f32[15,384]{1,0:T(8,128)S(1)}, f32[15,384]{1,0:T(8,128)S(1)}, u32[]{:S(2)}, u32[]{:S(2)}) collective-permute-start(f32[15,384]{1,0:T(8,128)S(1)} %add.568), channel_id=1, source_target_pairs={{0,8},{4,12},{8,0},{12,4},{1,9},{5,13},{9,1},{13,5},{2,10},{6,14},... | collective-permute-start | bytes 69128 | tf_op jit(solution)/shard_map/ppermute | solution.py:571
  278.8 3.8 %collective-permute-start.58 = (f32[15,384]{1,0:T(8,128)S(1)}, f32[15,384]{1,0:T(8,128)S(1)}, u32[]{:S(2)}, u32[]{:S(2)}) collective-permute-start(f32[15,384]{1,0:T(8,128)S(1)} %add.569), channel_id=1, source_target_pairs={{0,16},{16,0},{1,17},{17,1},{2,18},{18,2},{3,19},{19,3},{4,20},{20... | collective-permute-start | bytes 69128 | tf_op jit(solution)/shard_map/ppermute | solution.py:571
  (42 other events, 219.4 us)
